TPU v7x, 32 devices: a whole 2x2x4 slice. The times are simulated.
32 devices in a mesh: groups: 2 (over y), gx: 8 (over z, x), gy: 2 (over core).
Axes of the slice: x: 2, y: 2, z: 4, core: 2. Of those that a mesh axis runs over, the one named last changes fastest.
Arguments:
- probe_vectors: bfloat16 [8192, 1536], P(('groups', 'gx', 'gy')), parts along dimension 0, may hold values from -60 to 60
- mesh_lookup_pair: bfloat16 [8192, 2, 1536], P(('groups', 'gx', 'gy')), parts along dimension 0, may hold values from -6 to 6
- landmark_lookup_pair: bfloat16 [128, 2, 1536], P(('groups', 'gx', 'gy')), parts along dimension 0, may hold values from -6 to 6
- softmax_warmth: float32 [24], P('groups'), parts along dimension 0, may hold values from 0.5 to 2
- output_adjoint: bfloat16 [8192, 1536], P(('groups', 'gx', 'gy')), parts along dimension 0, may hold values from -6 to 6
- exported_boundary_tiles: int32 [32, 3, 1], P(('groups', 'gx', 'gy')), parts along dimension 0, may hold values from 0 to 1
- adjacency_tile_filter: int32 [32, 2, 5], P(('groups', 'gx', 'gy')), parts along dimension 0, may hold values 0 or 1
Outputs:
- probe_derivative: bfloat16 [8192, 1536], P(('groups', 'gx', 'gy')), parts along dimension 0
- cell_kv_grad: bfloat16 [8192, 2, 1536], P(('groups', 'gx', 'gy')), parts along dimension 0
- anchor_kv_grad: float32 [128, 2, 1536], P(('groups', 'gx', 'gy')), parts along dimension 0
- temperature_grad: float32 [24], P('groups'), parts along dimension 0
There are 2 independent parts, one for each index of `groups`. A program takes and returns all parts, laid end to end along the dimension named above; each array names one. Nothing has to cross between parts.
All inputs are finite; a program needn't handle non-finite values. No bound on the sum of `adjacency_tile_filter` on one device may be relied on, other than what follows from the above.
Results may differ from a plain program's by a relative error of at most 0.001.
The roundings to bfloat16 on the way count: a program that leaves them out, or rounds other values in their place, can miss the bound.
Values may be sent and summed in bfloat16 or wider, within the bound.
No kernel may reach another device: no remote copies, remote signals or barrier semaphores. Data moves between devices by JAX's collectives and lax.ppermute only.
A program may use at most 128 MiB of HBM per device.

v0:
```python
import math

import jax
import jax.numpy as jnp
from jax import lax
from jax.sharding import PartitionSpec as P

BLOCK = 128


def padded(array, sides, width):
    for axis, dim in sides:
        count, length = (lax.axis_size(axis), array.shape[dim])
        up = [(i, (i + 1) % count) for i in range(count - 1)]
        down = [(j, i) for i, j in up]
        last = lax.slice_in_dim(array, length - width, length, axis=dim)
        initial = lax.slice_in_dim(array, 0, width, axis=dim)
        before = lax.ppermute(last, axis, up)
        after = lax.ppermute(initial, axis, down)
        array = jnp.concatenate([before, array, after], axis=dim)
    return array


def swapped(block, axis, stride):
    count = lax.axis_size(axis)
    route = []
    for low in range(count):
        high = low | 1 << stride
        if high != low and high < count:
            route += [(low, high), (high, low)]
    return lax.ppermute(block, axis, route)


def local(
    probe_vectors,
    mesh_lookup_pair,
    landmark_lookup_pair,
    softmax_warmth,
    output_adjoint,
    exported_boundary_tiles,
    adjacency_tile_filter,
):
    cell_count = probe_vectors.shape[0]
    feat_width = probe_vectors.shape[1]
    block_count = cell_count // BLOCK
    face_count = exported_boundary_tiles.shape[2]
    channel_group_count = softmax_warmth.shape[0]
    channel_width_each = feat_width // channel_group_count
    kv_blocks = mesh_lookup_pair.reshape(block_count, BLOCK, 2, feat_width)
    chosen = exported_boundary_tiles[0]
    picked = kv_blocks[chosen]
    sent_x = jnp.concatenate([picked[0], picked[1]], axis=0)
    rims_x = padded(sent_x, (("gx", 0),), face_count)
    from_lower = rims_x[:face_count]
    from_upper = rims_x[3 * face_count :]
    from_partner = swapped(picked[2], "gy", 0)
    anchors_all = lax.all_gather(landmark_lookup_pair, ("gx", "gy"), axis=0, tiled=True)
    halo_kv = jnp.concatenate([from_lower, from_upper, from_partner], axis=0)
    halo_kv = halo_kv.reshape(3 * face_count * BLOCK, 2, feat_width)
    vicinity_length = cell_count + 3 * face_count * BLOCK
    combined_lookup_pair = jnp.concatenate([mesh_lookup_pair, halo_kv, anchors_all], axis=0)
    anchor_total = anchors_all.shape[0]
    primary_axis_position = lax.axis_index("gx")
    gx_count = lax.axis_size("gx")
    near_mask = (adjacency_tile_filter[0] > 0) | jnp.eye(
        block_count, block_count + 3 * face_count, dtype=bool
    )
    valid = jnp.concatenate(
        [
            jnp.ones((block_count,), bool),
            jnp.full((face_count,), primary_axis_position > 0),
            jnp.full((face_count,), primary_axis_position < gx_count - 1),
            jnp.ones((face_count,), bool),
        ]
    )
    near_mask = near_mask & valid[None]
    near_mask = jnp.repeat(jnp.repeat(near_mask, BLOCK, axis=0), BLOCK, axis=1)
    allowed_couples = jnp.concatenate(
        [near_mask, jnp.ones((cell_count, anchor_total), bool)], axis=1
    )
    logit_multiplier = softmax_warmth / math.sqrt(channel_width_each)
    query_heads = probe_vectors.reshape(cell_count, channel_group_count, channel_width_each)
    grad_heads = output_adjoint.reshape(cell_count, channel_group_count, channel_width_each)
    key_heads = combined_lookup_pair[:, 0].reshape(-1, channel_group_count, channel_width_each)
    value_heads = combined_lookup_pair[:, 1].reshape(-1, channel_group_count, channel_width_each)
    unnormalised_logits = jnp.einsum(
        "qhd,khd->hqk", query_heads, key_heads, preferred_element_type=jnp.float32
    )
    scores = jnp.where(
        allowed_couples[None], unnormalised_logits * logit_multiplier[:, None, None], -jnp.inf
    )
    row_max = jnp.max(scores, axis=2, keepdims=True)
    exp_scores = jnp.exp(scores - row_max)
    weights = exp_scores / jnp.sum(exp_scores, axis=2, keepdims=True)
    weights_b = weights.astype(jnp.bfloat16)
    attended = jnp.einsum(
        "hqk,khd->qhd", weights_b, value_heads, preferred_element_type=jnp.float32
    )
    row_delta = jnp.sum(grad_heads.astype(jnp.float32) * attended, axis=2)
    weight_grad = jnp.einsum(
        "qhd,khd->hqk", grad_heads, value_heads, preferred_element_type=jnp.float32
    )
    logit_adjoint = weights * (weight_grad - jnp.transpose(row_delta)[:, :, None])
    warmth_contribution = jnp.sum(logit_adjoint * unnormalised_logits, axis=(1, 2)) / math.sqrt(
        channel_width_each
    )
    dscore_b = (logit_adjoint * logit_multiplier[:, None, None]).astype(jnp.bfloat16)
    probe_derivative = jnp.einsum(
        "hqk,khd->qhd", dscore_b, key_heads, preferred_element_type=jnp.float32
    )
    probe_derivative = probe_derivative.reshape(cell_count, feat_width).astype(jnp.bfloat16)
    near_key = jnp.einsum(
        "hqk,qhd->khd",
        dscore_b[:, :, :vicinity_length],
        query_heads,
        preferred_element_type=jnp.float32,
    )
    near_value = jnp.einsum(
        "hqk,qhd->khd",
        weights_b[:, :, :vicinity_length],
        grad_heads,
        preferred_element_type=jnp.float32,
    )
    near_terms = jnp.stack(
        [
            near_key.reshape(vicinity_length, feat_width),
            near_value.reshape(vicinity_length, feat_width),
        ],
        axis=1,
    )
    row_total = lax.axis_size(("gx", "gy")) * landmark_lookup_pair.shape[0]
    score_cols = lax.dynamic_slice_in_dim(dscore_b, vicinity_length, row_total, 2)
    weight_cols = lax.dynamic_slice_in_dim(weights_b, vicinity_length, row_total, 2)
    key_part = jnp.einsum(
        "hqk,qhd->khd", score_cols, query_heads, preferred_element_type=jnp.float32
    )
    value_part = jnp.einsum(
        "hqk,qhd->khd", weight_cols, grad_heads, preferred_element_type=jnp.float32
    )
    anchor_grad = lax.psum_scatter(
        jnp.stack(
            [key_part.reshape(row_total, feat_width), value_part.reshape(row_total, feat_width)],
            axis=1,
        ),
        ("gx", "gy"),
        scatter_dimension=0,
        tiled=True,
    )
    face_grads = (
        near_terms[cell_count:].reshape(3, face_count, BLOCK, 2, feat_width).astype(jnp.bfloat16)
    )
    back_sent = jnp.concatenate([face_grads[0], face_grads[1]], axis=0)
    back_x = padded(back_sent, (("gx", 0),), face_count)
    back_partner = swapped(face_grads[2], "gy", 0)
    returned = jnp.stack(
        [back_x[:face_count], back_x[3 * face_count :], back_partner], axis=0
    ).astype(jnp.float32)
    local_blocks = near_terms[:cell_count].reshape(block_count, BLOCK, 2, feat_width)
    block_ids = jnp.arange(block_count, dtype=jnp.int32)
    for direction in range(3):
        hits = (block_ids == chosen[direction, 0]).astype(jnp.float32)
        local_blocks = local_blocks + hits[:, None, None, None] * returned[direction, 0][None]
    cell_grad = local_blocks.reshape(cell_count, 2, feat_width).astype(jnp.bfloat16)
    warmth_derivative = lax.psum(warmth_contribution, ("gx", "gy"))
    return (probe_derivative, cell_grad, anchor_grad, warmth_derivative)


def solution(mesh):
    placed = (
        P(("groups", "gx", "gy"), None),
        P(("groups", "gx", "gy"), None, None),
        P(("groups", "gx", "gy"), None, None),
        P("groups"),
        P(("groups", "gx", "gy"), None),
        P(("groups", "gx", "gy"), None, None),
        P(("groups", "gx", "gy"), None, None),
    )
    return jax.shard_map(
        local,
        mesh=mesh,
        in_specs=placed,
        out_specs=(
            P(("groups", "gx", "gy"), None),
            P(("groups", "gx", "gy"), None, None),
            P(("groups", "gx", "gy"), None, None),
            P("groups"),
        ),
        check_vma=False,
    )
```

profile of v0, /device:TPU:0, one launch (start us, length us, event | category | flops | bytes accessed | tf_op | source)
XLA Modules:
  0.0 289.8 jit_solution(5623075355392274938)
XLA Ops:
  7.2 1.6 copy.115
  8.8 0.7 fusion.27
  9.5 2.2 gather_fusion
  11.7 3.2 %fusion.30 = (bf16[1,128,2,1536]{3,1,2,0:T(8,128)(2,1)}, bf16[1,128,2,1536]{3,1,2,0:T(8,128)(2,1)}, bf16[1,128,2,1536]{3,1,2,0:T(8,128)(2,1)}) fusion(bf16[3,128,2,1536]{3,1,2,0:T(8,128)(2,1)} %gather_fusion), kind=kLoop, calls=%fused_computation.67 | loop fusion | bytes 4718592 | tf_op jit(solution)/shard_map/slice | solution.py:52
  14.9 5.7 %collective-permute-start = (bf16[1,128,2,1536]{3,1,2,0:T(8,128)(2,1)}, bf16[1,128,2,1536]{3,1,2,0:T(8,128)(2,1)}, u32[]{:S(2)}, u32[]{:S(2)}) collective-permute-start(bf16[1,128,2,1536]{3,1,2,0:T(8,128)(2,1)} %get-tuple-element.38), channel_id=1, source_target_pairs={{0,2},{2,4},{4,6},{6,8},{8,10},{10,12},{12,14},{1,3},{3,5},{5,7},{... | collective-permute-start | bytes 2359304 | tf_op jit(solution)/shard_map/ppermute | solution.py:18
  20.6 1.3 collective-permute-start.1
  22.0 0.6 fusion.31
  22.6 46.0 %all_gather.3 = bf16[64,2,1536]{2,1,0:T(2,128)(2,1)S(1)} all-gather(bf16[4,2,1536]{2,1,0:T(2,128)(2,1)S(1)} %copy-done.9), channel_id=1, replica_groups=mesh['groups'=2,'gx'=8,'gy'=2] {'gx','gy'}, dimensions={0}, use_global_device_ids=true | all-gather | bytes 417792 | tf_op jit(solution)/shard_map/all_gather | solution.py:57
  68.8 0.7 compare_convert_fusion
  69.4 0.6 compare_convert_fusion.1
  70.0 1.3 copy.117
  71.3 1.4 copy.120
  72.8 0.7 concatenate.23
  73.5 2.3 copy.124
  75.8 0.6 dynamic-slice
  77.0 0.6 compare_convert_fusion.2
  77.9 2.0 pad_maximum_fusion.2
  80.4 2.3 fusion.29
  82.7 2.8 copy.119
  85.5 4.2 %copy.123 = bf16[704,1,1536]{0,2,1:T(8,128)(2,1)} copy(bf16[704,1,1536]{2,0,1:T(8,128)(2,1)} %get-tuple-element.33) | data formatting | bytes 4325376 | tf_op jit(solution)/shard_map/slice | solution.py:85
  89.7 4.7 %fusion.33 = f32[12,704,256]{2,1,0:T(8,128)} fusion(bf16[704,12,128]{0,2,1:T(8,128)(2,1)S(1)} %bitcast.114, bf16[256,12,128]{0,2,1:T(8,128)(2,1)S(1)} %bitcast.119), kind=kOutput, calls=%fused_computation.70 | convolution fusion | flops 553648128 | bytes 11599872 | tf_op jit(solution)/shard_map/qhd,khd->hqk/dot_general | solution.py:86
  94.4 5.4 %fusion.32 = (f32[12,256]{1,0:T(8,128)S(1)}, f32[12,256,704]{1,2,0:T(8,128)}) fusion(f32[12]{0:T(128)S(1)} %broadcast_multiply_fusion.1, pred[256,704]{0,1:T(8,128)(4,1)S(1)} %copy-done.8, bf16[704,12,128]{0,2,1:T(8,128)(2,1)S(1)} %bitcast.115, bf16[256,12,128]{0,2,1:T(8,128)(2,1)S(1)} %bitcast.120), kind=kOutput, calls=%fused_computation.69 | convolution fusion | flops 562299584 | bytes 11792432 | tf_op jit(solution)/shard_map/sub | solution.py:93
  99.8 4.4 %fusion.15 = bf16[12,256,704]{1,2,0:T(8,128)(2,1)S(1)} fusion(f32[12,256,704]{1,2,0:T(8,128)} %get-tuple-element.45, f32[12,256]{1,0:T(8,128)S(1)} %get-tuple-element.44), kind=kLoop, calls=%fused_computation.23 | loop fusion | flops 4325376 | bytes 12988416 | tf_op jit(solution)/shard_map/convert_element_type | solution.py:95
  104.2 1.1 convolution_bitcast_fusion
  105.4 0.8 fusion.21
  106.2 7.5 %fusion.2 = (f32[12]{0:T(128)S(1)}, bf16[12,256,704]{1,2,0:T(8,128)(2,1)S(1)}) fusion(f32[12,704,256]{2,1,0:T(8,128)} %fusion.33, f32[12]{0:T(128)S(1)} %broadcast_multiply_fusion.1, f32[12,256]{1,0:T(8,128)S(1)} %bitcast.133, bf16[704,12,128]{0,2,1:T(8,128)(2,1)S(1)} %bitcast.131, bf16[256,12,128]{0,2,1:T(8,128)(2,1)S(1)} %bitcast.126, ...), kind=kOutput, calls=%fused_computation.6 | convolution fusion | flops 568786944 | bytes 24600672 | tf_op jit(solution)/shard_map/qhd,khd->hqk/dot_general | solution.py:100
  114.0 3.2 %fusion.13 = f32[12,640,128]{1,2,0:T(8,128)} fusion(bf16[256,12,128]{0,2,1:T(8,128)(2,1)S(1)} %bitcast.122, bf16[12,256,704]{1,2,0:T(8,128)(2,1)S(1)} %get-tuple-element.29), kind=kOutput, calls=%fused_computation.21 | convolution fusion | flops 503316480 | bytes 8650752 | tf_op jit(solution)/shard_map/hqk,qhd->khd/dot_general | solution.py:112
  117.2 3.2 %fusion.11 = f32[12,640,128]{1,2,0:T(8,128)} fusion(bf16[256,12,128]{0,2,1:T(8,128)(2,1)S(1)} %bitcast.127, bf16[12,256,704]{1,2,0:T(8,128)(2,1)S(1)} %fusion.15), kind=kOutput, calls=%fused_computation.19 | convolution fusion | flops 503316480 | bytes 8650752 | tf_op jit(solution)/shard_map/hqk,qhd->khd/dot_general | solution.py:118
  120.7 1.2 copy.136
  121.9 0.8 stack_reshape.15
  122.7 9.1 %copy.131 = f32[640,1,1536]{2,1,0:T(1,128)} copy(f32[640,1,1536]{0,2,1:T(8,128)} %bitcast.117) | data formatting | bytes 7864320 | tf_op jit(solution)/shard_map/stack;reshape | solution.py:124
  131.8 9.2 %copy.132 = f32[640,1,1536]{2,1,0:T(1,128)} copy(f32[640,1,1536]{0,2,1:T(8,128)} %bitcast.118) | data formatting | bytes 7864320 | tf_op jit(solution)/shard_map/stack;reshape | solution.py:124
  141.0 12.3 %fusion.3 = bf16[640,2,1536]{2,1,0:T(2,128)(2,1)} fusion(f32[640,1,1536]{2,1,0:T(1,128)} %copy.132, f32[640,1,1536]{2,1,0:T(1,128)} %copy.131), kind=kLoop, calls=%fused_computation.12 | loop fusion | flops 7864320 | bytes 11796480 | tf_op jit(solution)/shard_map/convert
  153.3 3.8 %slice_bitcast_fusion.5 = (bf16[1,128,2,1536]{3,2,1,0:T(2,128)(2,1)}, bf16[1,128,2,1536]{3,2,1,0:T(2,128)(2,1)}, bf16[1,128,2,1536]{3,2,1,0:T(2,128)(2,1)}) fusion(bf16[640,2,1536]{2,1,0:T(2,128)(2,1)} %fusion.3), kind=kLoop, calls=%fused_computation.44 | loop fusion | bytes 4718592 | tf_op jit(solution)/shard_map/squeeze | solution.py:152
  157.1 4.2 %collective-permute-start.3 = (bf16[1,128,2,1536]{3,2,1,0:T(2,128)(2,1)}, bf16[1,128,2,1536]{3,2,1,0:T(2,128)(2,1)}, u32[]{:S(2)}, u32[]{:S(2)}) collective-permute-start(bf16[1,128,2,1536]{3,2,1,0:T(2,128)(2,1)} %get-tuple-element.35), channel_id=1, source_target_pairs={{0,2},{2,4},{4,6},{6,8},{8,10},{10,12},{12,14},{1,3},{3,5},{5,7},{... | collective-permute-start | bytes 2359304 | tf_op jit(solution)/shard_map/ppermute | solution.py:18
  161.3 1.3 collective-permute-start.4
  162.7 1.0 pad_maximum_fusion.3
  163.7 55.9 %psum.7 = f32[12]{0:T(128)} all-reduce(f32[12]{0:T(128)S(1)} %broadcast_multiply_fusion), channel_id=1, replica_groups=mesh['groups'=2,'gx'=8,'gy'=2] {'gx','gy'}, use_global_device_ids=true, to_apply=%region_5.6 | all-reduce | flops 12 | bytes 96 | tf_op jit(solution)/shard_map/psum | solution.py:164
  219.5 3.0 %convolution_convert_fusion = bf16[12,128,256]{2,1,0:T(8,128)(2,1)S(1)} fusion(bf16[704,12,128]{0,2,1:T(8,128)(2,1)S(1)} %bitcast.116, bf16[12,256,704]{1,2,0:T(8,128)(2,1)} %copy-done.2), kind=kOutput, calls=%fused_computation.39 | convolution fusion | flops 554041344 | bytes 7274496 | tf_op jit(solution)/shard_map/hqk,khd->qhd/dot_general | solution.py:108
  222.5 1.2 copy.137
  223.7 42.1 %all-reduce.4.cloned.1.call-done = f32[64,2,1536]{2,0,1:T(8,128)} async-done(((f32[64,2,1536]{2,0,1:T(8,128)}), f32[64,2,1536]{2,0,1:T(8,128)}) %all-reduce.4.cloned.1.call-update) | async-done | bytes 786448
  265.8 0.9 constant_dynamic-slice_fusion
  266.7 0.6 copy.138
  267.4 5.1 %maximum_convert_fusion = f32[3,1,128,2,1536]{4,3,2,1,0:T(2,128)S(1)} fusion(bf16[1,1,128,2,1536]{4,3,2,1,0:T(2,128)(2,1)} %bitcast.30, bf16[1,1,128,2,1536]{4,3,2,1,0:T(2,128)(2,1)} %bitcast.28, bf16[1,1,128,2,1536]{4,3,2,1,0:T(2,128)(2,1)} %bitcast.26), kind=kLoop, calls=%fused_computation.33 | loop fusion | flops 3538944 | bytes 7077888 | tf_op jit(solution)/shard_map/convert_element_type | solution.py:157
  272.5 1.7 slice_bitcast_fusion.2
  274.2 0.4 copy-done
  274.6 1.2 copy-done.1
  275.8 7.2 %fusion.20 = bf16[256,2,1536]{2,1,0:T(2,128)(2,1)} fusion(f32[640,1,1536]{2,1,0:T(1,128)S(1)} %copy-done.1, f32[640,1,1536]{2,1,0:T(1,128)S(1)} %copy-done, f32[256]{0:T(256)S(1)} %get-tuple-element.46, f32[256]{0:T(256)S(1)} %get-tuple-element.47, f32[256]{0:T(256)S(1)} %broadcast_bitcast_fusion.3, f32[128,2,1536]{2,1,0:T(2,128)S(1)} %get-tuple-element.31, ...), kind=kLoop, calls=%fused_computation.29 | loop fusion | flops 6291456 | bytes 14158848 | tf_op jit(solution)/shard_map/convert_element_type | solution.py:163
  (52 shorter events, 2.0 us)
Async XLA Ops:
  7.2 258.6 %all-reduce.4.cloned.1.call-start = ((), (), s32[]{:S(2)}) async-start(), calls=%async_computation | async-start | bytes 1572864
  9.5 12.5 %copy-start.10 = (s32[1,3,1]{1,2,0:T(1,128)S(1)}, s32[1,3,1]{1,2,0:T(1,128)}, u32[]{:S(2)}) copy-start(s32[1,3,1]{1,2,0:T(1,128)} %param.12) | copy-start | bytes 40
  9.5 13.1 %copy-start.9 = (bf16[4,2,1536]{2,1,0:T(2,128)(2,1)S(1)}, bf16[4,2,1536]{2,1,0:T(2,128)(2,1)}, u32[]{:S(2)}) copy-start(bf16[4,2,1536]{2,1,0:T(2,128)(2,1)} %param.9) | copy-start | bytes 73732
  9.5 59.2 %copy-start.11 = (s32[1,2,5]{2,1,0:T(2,128)S(1)}, s32[1,2,5]{2,1,0:T(2,128)}, u32[]{:S(2)}) copy-start(s32[1,2,5]{2,1,0:T(2,128)} %param.13) | copy-start | bytes 124
  11.7 58.3 %copy-start.4 = (bf16[256,2,1536]{2,1,0:T(2,128)(2,1)S(1)}, bf16[256,2,1536]{2,1,0:T(2,128)(2,1)}, u32[]{:S(2)}) copy-start(bf16[256,2,1536]{2,1,0:T(2,128)(2,1)} %param.8) | copy-start | bytes 4718596
  14.9 63.0 %collective-permute-start = (bf16[1,128,2,1536]{3,1,2,0:T(8,128)(2,1)}, bf16[1,128,2,1536]{3,1,2,0:T(8,128)(2,1)}, u32[]{:S(2)}, u32[]{:S(2)}) collective-permute-start(bf16[1,128,2,1536]{3,1,2,0:T(8,128)(2,1)} %get-tuple-element.38), channel_id=1, source_target_pairs={{0,2},{2,4},{4,6},{6,8},{8,10},{10,12},{12,14},{1,3},{3,5},{5,7},{... | collective-permute-start | bytes 2359304 | tf_op jit(solution)/shard_map/ppermute | solution.py:18
  20.6 57.2 %collective-permute-start.1 = (bf16[1,128,2,1536]{3,1,2,0:T(8,128)(2,1)}, bf16[1,128,2,1536]{3,1,2,0:T(8,128)(2,1)}, u32[]{:S(2)}, u32[]{:S(2)}) collective-permute-start(bf16[1,128,2,1536]{3,1,2,0:T(8,128)(2,1)} %get-tuple-element.39), channel_id=1, source_target_pairs={{2,0},{4,2},{6,4},{8,6},{10,8},{12,10},{14,12},{3,1},{5,3},{7,5},{... | collective-permute-start | bytes 2359304 | tf_op jit(solution)/shard_map/ppermute | solution.py:19
  21.9 56.0 %collective-permute-start.2 = (bf16[1,128,2,1536]{3,1,2,0:T(8,128)(2,1)}, bf16[1,128,2,1536]{3,1,2,0:T(8,128)(2,1)}, u32[]{:S(2)}, u32[]{:S(2)}) collective-permute-start(bf16[1,128,2,1536]{3,1,2,0:T(8,128)(2,1)} %get-tuple-element.40), channel_id=1, source_target_pairs={{0,1},{1,0},{2,3},{3,2},{4,5},{5,4},{6,7},{7,6},{8,9},{9,8},{10,11... | collective-permute-start | bytes 2359304 | tf_op jit(solution)/shard_map/ppermute | solution.py:31
  22.6 53.2 %copy-start.13 = (u32[32]{0:T(128)S(1)}, u32[32]{0:T(128)}, u32[]{:S(2)}) copy-start(u32[32]{0:T(128)} %constant.34) | copy-start | bytes 388
  68.6 9.1 %copy-start.12 = (f32[12]{0:T(128)S(1)}, f32[12]{0:T(128)}, u32[]{:S(2)}) copy-start(f32[12]{0:T(128)} %param.10) | copy-start | bytes 148
  77.8 2.3 copy-start.5
  89.7 4.7 %copy-start.8 = (pred[256,704]{0,1:T(8,128)(4,1)S(1)}, pred[256,704]{0,1:T(8,128)(4,1)}, u32[]{:S(2)}) copy-start(pred[256,704]{0,1:T(8,128)(4,1)} %concatenate.23) | copy-start | bytes 540676
  99.8 4.4 %copy-start.3 = (bf16[256,1536]{0,1:T(8,128)(2,1)S(1)}, bf16[256,1536]{0,1:T(8,128)(2,1)}, u32[]{:S(2)}) copy-start(bf16[256,1536]{0,1:T(8,128)(2,1)} %copy.124) | copy-start | bytes 2359300
  99.8 5.6 %copy-start.6 = (bf16[704,1,1536]{0,2,1:T(8,128)(2,1)S(1)}, bf16[704,1,1536]{0,2,1:T(8,128)(2,1)}, u32[]{:S(2)}) copy-start(bf16[704,1,1536]{0,2,1:T(8,128)(2,1)} %copy.123) | copy-start | bytes 6488068
  113.6 3.6 %copy-start.2 = (bf16[12,256,704]{1,2,0:T(8,128)(2,1)}, bf16[12,256,704]{1,2,0:T(8,128)(2,1)S(1)}, u32[]{:S(2)}) copy-start(bf16[12,256,704]{1,2,0:T(8,128)(2,1)S(1)} %get-tuple-element.29) | copy-start | bytes 12976132
  153.3 9.4 %copy-start.7 = (f32[64,1,1536]{2,0,1:T(8,128)S(1)}, f32[64,1,1536]{2,0,1:T(8,128)}, u32[]{:S(2)}) copy-start(f32[64,1,1536]{2,0,1:T(8,128)} %stack_reshape.15) | copy-start | bytes 1179652
  157.1 110.2 %collective-permute-start.3 = (bf16[1,128,2,1536]{3,2,1,0:T(2,128)(2,1)}, bf16[1,128,2,1536]{3,2,1,0:T(2,128)(2,1)}, u32[]{:S(2)}, u32[]{:S(2)}) collective-permute-start(bf16[1,128,2,1536]{3,2,1,0:T(2,128)(2,1)} %get-tuple-element.35), channel_id=1, source_target_pairs={{0,2},{2,4},{4,6},{6,8},{8,10},{10,12},{12,14},{1,3},{3,5},{5,7},{... | collective-permute-start | bytes 2359304 | tf_op jit(solution)/shard_map/ppermute | solution.py:18
  161.3 106.1 %collective-permute-start.4 = (bf16[1,128,2,1536]{3,2,1,0:T(2,128)(2,1)}, bf16[1,128,2,1536]{3,2,1,0:T(2,128)(2,1)}, u32[]{:S(2)}, u32[]{:S(2)}) collective-permute-start(bf16[1,128,2,1536]{3,2,1,0:T(2,128)(2,1)} %get-tuple-element.37), channel_id=1, source_target_pairs={{2,0},{4,2},{6,4},{8,6},{10,8},{12,10},{14,12},{3,1},{5,3},{7,5},{... | collective-permute-start | bytes 2359304 | tf_op jit(solution)/shard_map/ppermute | solution.py:19
  162.6 104.8 %collective-permute-start.5 = (bf16[1,128,2,1536]{3,2,1,0:T(2,128)(2,1)}, bf16[1,128,2,1536]{3,2,1,0:T(2,128)(2,1)}, u32[]{:S(2)}, u32[]{:S(2)}) collective-permute-start(bf16[1,128,2,1536]{3,2,1,0:T(2,128)(2,1)} %get-tuple-element.36), channel_id=1, source_target_pairs={{0,1},{1,0},{2,3},{3,2},{4,5},{5,4},{6,7},{7,6},{8,9},{9,8},{10,11... | collective-permute-start | bytes 2359304 | tf_op jit(solution)/shard_map/ppermute | solution.py:31
  272.5 2.1 copy-start
  272.5 3.3 %copy-start.1 = (f32[640,1,1536]{2,1,0:T(1,128)S(1)}, f32[640,1,1536]{2,1,0:T(1,128)}, u32[]{:S(2)}) copy-start(f32[640,1,1536]{2,1,0:T(1,128)} %copy.132) | copy-start | bytes 11796484
Sparse Core Ops, SparseCore 0:
  163.8 101.9 all-reduce.3
where the time goes:
time: 291 us; the launch traced here: 290 us
  blocking collectives  102 us (35%)
  local copies, waits for them, and re-layouts  54.1 us (19%)
  waiting for transfers between devices  42.1 us (14%)
  other arithmetic  34.9 us (12%)
  matrix products  29.2 us (10%)
  between operations  15 us (5%)
  starting transfers between devices  12.7 us (4%)
    psum x1, blocking collectives, local(): warmth_derivative = lax.psum(warmth_contribution, ('gx', 'gy'))  55.9 us
    all_gather x1, blocking collectives, local(): lax.all_gather(landmark_lookup_pair, ('gx', 'gy'), axis=0, tiled=True)  46 us
    unnamed x2, waiting for transfers between devices  42.1 us
    another operation x2, local copies, waits for them, and re-layouts, local(): jnp.stack([near_key.reshape(vicinity_length, feat_width), near_value.resh...  18.3 us
    another operation x1, other arithmetic  12.3 us
    unnamed x35, local copies, waits for them, and re-layouts  9.96 us
    ppermute x2, starting transfers between devices, padded(): before = lax.ppermute(last, axis, up)  9.89 us
    dot_general x1, matrix products, local(): jnp.einsum('qhd,khd->hqk', grad_heads, value_heads, preferred_element_typ...  7.46 us
  transfers between devices with their start and end apart: 7, of which 1 were waited for; matrix products, arithmetic and copies ran while one was open for 5% of the time, Pallas kernels for 0%

commit v1 on v0

v1 whole, which is shorter than its diff:
```python
import functools
import math

import jax
import jax.numpy as jnp
from jax import lax
from jax.experimental import pallas as pl
from jax.experimental.pallas import tpu as pltpu
from jax.sharding import PartitionSpec as P

BLOCK = 128
F32 = jnp.float32
BF16 = jnp.bfloat16
SMEM = pltpu.MemorySpace.SMEM


def swap_bit(x, axis, bit):
    count = lax.axis_size(axis)
    return lax.ppermute(x, axis, [(i, i ^ (1 << bit)) for i in range(count)])


def swap_pairs(x, first):
    count = lax.axis_size("gx")
    route = []
    for low in range(first, count - 1, 2):
        route += [(low, low + 1), (low + 1, low)]
    return lax.ppermute(x, "gx", route)


def attention_kernel(
    pos_ref, filt_ref, warm_ref, q_ref, g_ref, own_ref, dir_ref, dia_ref, par_ref, anc_ref, *rest,
    gx_count, head0, width,
):
    (dq_ref, own_out, dir_out, dia_out, par_out, anc_out, temp_out, k_ref, v_ref) = rest[-9:]
    head = pl.program_id(0)
    gx = pos_ref[0]
    odd = lax.rem(gx, 2)
    own_rows = own_ref.shape[0]
    blocks = own_rows // BLOCK
    anchors = anc_ref.shape[0]
    queries = q_ref.shape[0]
    near = own_rows + 3 * BLOCK
    keys = near + anchors

    row = 0
    for ref in (own_ref, dir_ref, dia_ref, par_ref, anc_ref):
        n = ref.shape[0]
        k_ref[row : row + n, :] = ref[:, 0, :]
        v_ref[row : row + n, :] = ref[:, 1, :]
        row += n

    q = q_ref[...]
    g = g_ref[...]
    k = k_ref[...]
    v = v_ref[...]
    nt = (((1,), (1,)), ((), ()))
    s = lax.dot_general(k, q, nt, preferred_element_type=F32)
    dp = lax.dot_general(v, g, nt, preferred_element_type=F32)

    mult = warm_ref[head0 + head] / math.sqrt(width)
    lane = lax.broadcasted_iota(jnp.int32, (1, queries), 1) // BLOCK
    direct_col = blocks + 1 - odd
    diagonal_col = blocks + odd
    diagonal_there = jnp.where(odd == 1, gx < gx_count - 1, gx > 0)
    parts = []
    for b in range(blocks + 3):
        bias = jnp.zeros((1, queries), F32)
        for a in range(blocks):
            if b == a:
                continue
            col = (b if b < blocks else (direct_col, diagonal_col, blocks + 2)[b - blocks])
            ok = filt_ref[a, col] > 0
            if b == blocks + 1:
                ok = jnp.logical_and(ok, diagonal_there)
            bias = jnp.where(lane == a, jnp.where(ok, 0.0, -jnp.inf).astype(F32), bias)
        parts.append(s[b * BLOCK : (b + 1) * BLOCK] * mult + bias)
    parts.append(s[near:] * mult)
    scores = jnp.concatenate(parts, axis=0)
    top = jnp.max(scores, axis=0, keepdims=True)
    e = jnp.exp(scores - top)
    inv = 1.0 / jnp.sum(e, axis=0, keepdims=True)
    p = e * inv
    pb = p.astype(BF16)
    delta = jnp.sum(pb.astype(F32) * dp, axis=0, keepdims=True)
    ds = p * (dp - delta)
    temp_out[0] = jnp.sum(ds * s, axis=0, keepdims=True)
    dsb = (ds * mult).astype(BF16)
    nn = (((1,), (0,)), ((), ()))
    dv = lax.dot_general(pb, g, nn, preferred_element_type=F32)
    dk = lax.dot_general(dsb, q, nn, preferred_element_type=F32)
    dq = lax.dot_general(dsb, k, (((0,), (0,)), ((), ())), preferred_element_type=F32)
    dq_ref[...] = dq.astype(BF16)
    for j, terms in enumerate((dk, dv)):
        own_out[j] = terms[:own_rows]
        for i, ref in enumerate((dir_out, dia_out, par_out)):
            at = own_rows + i * BLOCK
            ref[j] = terms[at : at + BLOCK].astype(BF16)
        anc_out[j] = terms[near:]


def attention(pos, filt, warm, q, g, mesh_kv, halo, anchors, head0, heads, dq_prev, anc_prev):
    rows, feat = q.shape
    total = warm.shape[0]
    width = feat // total
    own_rows = mesh_kv.shape[0]
    a_rows = anchors.shape[0]
    keys = own_rows + 3 * BLOCK + a_rows
    full3 = lambda n: pl.BlockSpec((n, 2, width), lambda h: (0, 0, head0 + h))
    part3 = lambda n: pl.BlockSpec((n, 2, width), lambda h: (0, 0, h))
    smem = pl.BlockSpec(memory_space=SMEM)
    cols = pl.BlockSpec((rows, width), lambda h: (0, head0 + h))
    out_face = pl.BlockSpec((2, BLOCK, width), lambda h: (0, 0, h))
    in_specs = [smem, smem, smem, cols, cols, full3(own_rows), part3(BLOCK), part3(BLOCK), full3(BLOCK), full3(a_rows)]
    args = [pos, filt, warm, q, g, mesh_kv, *halo, anchors]
    alias = {}
    if dq_prev is not None:
        in_specs += [pl.BlockSpec(memory_space=pl.ANY)] * 2
        args += [dq_prev, anc_prev]
        alias = {10: 0, 11: 5}
    face = jax.ShapeDtypeStruct((2, BLOCK, heads * width), BF16)
    return pl.pallas_call(
        functools.partial(attention_kernel, gx_count=lax.axis_size("gx"), head0=head0, width=width),
        grid=(heads,),
        in_specs=in_specs,
        out_specs=[
            cols,
            pl.BlockSpec((2, own_rows, width), lambda h: (0, 0, h)),
            out_face,
            out_face,
            out_face,
            pl.BlockSpec((2, a_rows, width), lambda h: (0, 0, head0 + h)),
            pl.BlockSpec((1, 1, rows), lambda h: (h, 0, 0)),
        ],
        out_shape=[
            jax.ShapeDtypeStruct(q.shape, BF16),
            jax.ShapeDtypeStruct((2, own_rows, heads * width), F32),
            face,
            face,
            face,
            jax.ShapeDtypeStruct((2, a_rows, feat), F32),
            jax.ShapeDtypeStruct((heads, 1, rows), F32),
        ],
        scratch_shapes=[pltpu.VMEM((keys, width), BF16)] * 2,
        input_output_aliases=alias,
        compiler_params=pltpu.CompilerParams(vmem_limit_bytes=48 << 20),
        cost_estimate=pl.CostEstimate(
            flops=10 * heads * rows * keys * width,
            transcendentals=heads * rows * keys,
            bytes_accessed=heads * width * (rows * 6 + own_rows * 12 + 3 * BLOCK * 8 + a_rows * 12),
        ),
        name="attention",
    )(*args)


def combine_kernel(pos_ref, sent_ref, own_ref, dir_ref, dia_ref, par_ref, *rest):
    out_ref = rest[-1]
    odd = lax.rem(pos_ref[0], 2)
    blocks = own_ref.shape[1] // BLOCK
    spots = (
        jnp.where(odd == 1, sent_ref[0, 0], sent_ref[1, 0]),
        jnp.where(odd == 1, sent_ref[1, 0], sent_ref[0, 0]),
        sent_ref[2, 0],
    )
    for a in range(blocks):
        at = slice(a * BLOCK, (a + 1) * BLOCK)
        for j in range(2):
            total = own_ref[j, at, :]
            for spot, ref in zip(spots, (dir_ref, dia_ref, par_ref)):
                total = total + jnp.where(spot == a, 1.0, 0.0).astype(F32) * ref[j].astype(F32)
            out_ref[at, j, :] = total.astype(BF16)


def combine(pos, sent, own, faces, head0, heads, feat, width, prev):
    rows = own.shape[1]
    smem = pl.BlockSpec(memory_space=SMEM)
    w = width * (2 if heads % 2 == 0 and head0 % 2 == 0 else 1)
    steps = heads * width // w
    base = head0 * width // w
    face = pl.BlockSpec((2, BLOCK, w), lambda h: (0, 0, h))
    in_specs = [smem, smem, pl.BlockSpec((2, rows, w), lambda h: (0, 0, h)), face, face, face]
    args = [pos, sent, own, *faces]
    alias = {}
    if prev is not None:
        in_specs.append(pl.BlockSpec(memory_space=pl.ANY))
        args.append(prev)
        alias = {6: 0}
    return pl.pallas_call(
        combine_kernel,
        grid=(steps,),
        in_specs=in_specs,
        out_specs=pl.BlockSpec((rows, 2, w), lambda h: (0, 0, base + h)),
        out_shape=jax.ShapeDtypeStruct((rows, 2, feat), BF16),
        input_output_aliases=alias,
        compiler_params=pltpu.CompilerParams(vmem_limit_bytes=32 << 20),
        cost_estimate=pl.CostEstimate(
            flops=heads * width * rows * 16,
            transcendentals=0,
            bytes_accessed=heads * width * (rows * 12 + 3 * BLOCK * 4),
        ),
        name="combine",
    )(*args)


def local(q, mesh_kv, landmark, warm, g, exported, filt):
    rows, feat = q.shape
    total = warm.shape[0]
    width = feat // total
    gx_count = lax.axis_size("gx")
    bits = gx_count.bit_length() - 1
    gx = lax.axis_index("gx")
    pos = jnp.full((1,), gx, jnp.int32)
    sent = exported[0]
    filt = filt[0]
    odd = lax.rem(gx, 2)
    direct_block = jnp.where(odd == 1, sent[0, 0], sent[1, 0])
    diagonal_block = jnp.where(odd == 1, sent[1, 0], sent[0, 0])
    chunks = [(0, total // 2), (total // 2, total - total // 2)]

    def pick(block, head0, heads):
        return lax.dynamic_slice(
            mesh_kv, (block * BLOCK, 0, head0 * width), (BLOCK, 2, heads * width)
        )

    halos = []
    anchors = landmark[None]
    theirs = swap_bit(anchors, "gy", 0)
    anchors = jnp.concatenate([anchors, theirs], axis=0)
    for c, (head0, heads) in enumerate(chunks):
        diagonal = swap_pairs(pick(diagonal_block, head0, heads), 1)
        direct = swap_pairs(pick(direct_block, head0, heads), 0)
        halos.append((direct, diagonal))
    partner = swap_bit(pick(sent[2, 0], 0, total), "gy", 0)
    for bit in range(bits):
        theirs = swap_bit(anchors, "gx", bit)
        anchors = jnp.concatenate([anchors, theirs], axis=1)
    a_rows = anchors.shape[0] * anchors.shape[1]
    anchors = anchors.reshape(a_rows, 2, feat)

    dq = anc = None
    temps, owns, returned = [], [], []
    for (head0, heads), (direct, diagonal) in zip(chunks, halos):
        dq, own, f_dir, f_dia, f_par, anc, temp = attention(
            pos, filt, warm, q, g, mesh_kv, (direct, diagonal, partner), anchors, head0, heads, dq, anc
        )
        temps.append(temp)
        owns.append(own)
        returned.append((swap_pairs(f_dir, 0), swap_pairs(f_dia, 1), swap_bit(f_par, "gy", 0)))

    temp = jnp.sum(jnp.concatenate(temps, axis=0), axis=(1, 2)) / math.sqrt(width)
    extra = jnp.zeros((2, 1, feat), F32).at[0, 0, :total].set(temp)
    for axis, bit in [("gy", 0)] + [("gx", b) for b in reversed(range(bits))]:
        half = anc.shape[1] // 2
        got = swap_bit(jnp.concatenate([anc[:, half:], extra], axis=1), axis, bit)
        anc = anc[:, :half] + got[:, :half]
        extra = extra + got[:, half:]
    anchor_grad = jnp.transpose(anc, (1, 0, 2))
    temp = extra[0, 0, :total]

    cell = None
    for (head0, heads), own, faces in zip(chunks, owns, returned):
        cell = combine(pos, sent, own, faces, head0, heads, feat, width, cell)
    return (dq, cell, anchor_grad, temp)


def solution(mesh):
    rows = ("groups", "gx", "gy")
    placed = (
        P(rows, None),
        P(rows, None, None),
        P(rows, None, None),
        P("groups"),
        P(rows, None),
        P(rows, None, None),
        P(rows, None, None),
    )
    return jax.shard_map(
        local,
        mesh=mesh,
        in_specs=placed,
        out_specs=(P(rows, None), P(rows, None, None), P(rows, None, None), P("groups")),
        check_vma=False,
    )
```

time: 291 us -> 142 us (0.49)
  blocking collectives: 102 us -> 0 us
  local copies, waits for them, and re-layouts: 54.1 us -> 6.69 us
  Pallas kernels: 0 us -> 36.1 us
  other arithmetic: 34.9 us -> 5 us
  matrix products: 29.2 us -> 0 us
  waiting for transfers between devices: 42.1 us -> 61.7 us
  starting transfers between devices: 12.7 us -> 28.2 us
  between operations: 15 us -> 4.22 us
    ppermute x6 -> x19, waiting for transfers between devices: 0.02 us -> 61.7 us  [the longest x8 41 us: swap_pairs(): return lax.ppermute(x, 'gx', route)]
    psum x1 -> x0, blocking collectives: 55.9 us -> none  [local(): warmth_derivative = lax.psum(warmth_contribution, ('gx', 'gy'))]
    all_gather x1 -> x0, blocking collectives: 46 us -> none  [local(): lax.all_gather(landmark_lookup_pair, ('gx', 'gy'), axis=0, tiled=True)]
    unnamed x2 -> x0, waiting for transfers between devices: 42.1 us -> none
    pallas_call x0 -> x4, Pallas kernels: none -> 36.1 us  [the longest x2 28.8 us: attention(): pl.pallas_call(functools.partial(attention_kernel, gx_count=lax.axis_size...]
    dot_general x8 -> x0, matrix products: 23.8 us -> none  [the longest x1 7.46 us: local(): jnp.einsum('qhd,khd->hqk', grad_heads, value_heads, preferred_element_typ...]
    another operation x5 -> x0, local copies, waits for them, and re-layouts: 19.2 us -> none  [the longest x2 18.3 us: local(): jnp.stack([near_key.reshape(vicinity_length, feat_width), near_value.resh...]
    convert_element_type x6 -> x0, other arithmetic: 18.6 us -> none  [the longest x1 7.17 us: local(): local_blocks.reshape(cell_count, 2, feat_width).astype(jnp.bfloat16)]
  transfers between devices with their start and end apart: 7 -> 19, of which waited for: 1 -> 8; matrix products, arithmetic and copies ran while one was open for 5% -> 5% of each run, Pallas kernels for 0% -> 15%
where the time goes in v1:
time: 142 us
  waiting for transfers between devices  61.7 us (43%)
  Pallas kernels  36.1 us (25%)
  starting transfers between devices  28.2 us (20%)
  local copies, waits for them, and re-layouts  6.69 us (5%)
  other arithmetic  5 us (4%)
  between operations  4.22 us (3%)
    ppermute x8, waiting for transfers between devices, swap_pairs(): return lax.ppermute(x, 'gx', route)  41 us
    pallas_call x2, Pallas kernels, attention(): pl.pallas_call(functools.partial(attention_kernel, gx_count=lax.axis_size...  28.8 us
    ppermute x11, waiting for transfers between devices, swap_bit(): return lax.ppermute(x, axis, [(i, i ^ 1 << bit) for i in range(count)])  20.7 us
    ppermute x11, starting transfers between devices, swap_bit(): return lax.ppermute(x, axis, [(i, i ^ 1 << bit) for i in range(count)])  14.4 us
    ppermute x8, starting transfers between devices, swap_pairs(): return lax.ppermute(x, 'gx', route)  13.8 us
    pallas_call x2, Pallas kernels, combine(): pl.pallas_call(combine_kernel, grid=(steps,), in_specs=in_specs, out_spec...  7.23 us
  transfers between devices with their start and end apart: 19, of which 8 were waited for; matrix products, arithmetic and copies ran while one was open for 5% of the time, Pallas kernels for 15%

profile of v1, /device:TPU:0, one launch (start us, length us, event | category | flops | bytes accessed | tf_op | source)
XLA Modules:
  0.0 141.9 jit_solution(2091879614784843163)
XLA Ops:
  0.6 0.0 copy-start.6
  0.7 0.5 collective-permute-start.3
  1.2 1.1 collective-permute-done.3
  2.2 0.8 pad_maximum_fusion.6
  3.0 2.9 %collective-permute-start.4 = (bf16[2,4,2,1536]{3,2,1,0:T(2,128)(2,1)S(1)}, bf16[2,4,2,1536]{3,2,1,0:T(2,128)(2,1)S(1)}, u32[]{:S(2)}, u32[]{:S(2)}) collective-permute-start(bf16[2,4,2,1536]{3,2,1,0:T(2,128)(2,1)S(1)} %pad_maximum_fusion.6), channel_id=1, source_target_pairs={{0,2},{2,0},{4,6},{6,4},{8,10},{10,8},{12,14},{14,12},{1,3},{3,1},... | collective-permute-start | bytes 147464 | tf_op jit(solution)/shard_map/ppermute | solution.py:19
  5.9 1.4 fusion.2
  8.0 0.1 collective-permute-done.4
  8.0 0.9 pad_maximum_fusion.4
  8.9 2.2 %collective-permute-start.5 = (bf16[2,8,2,1536]{3,2,1,0:T(2,128)(2,1)S(1)}, bf16[2,8,2,1536]{3,2,1,0:T(2,128)(2,1)S(1)}, u32[]{:S(2)}, u32[]{:S(2)}) collective-permute-start(bf16[2,8,2,1536]{3,2,1,0:T(2,128)(2,1)S(1)} %pad_maximum_fusion.4), channel_id=1, source_target_pairs={{0,4},{2,6},{4,0},{6,2},{8,12},{10,14},{12,8},{14,10},{1,5},{3,7},... | collective-permute-start | bytes 294920 | tf_op jit(solution)/shard_map/ppermute | solution.py:19
  11.1 1.7 %constant_dynamic-slice_fusion.2 = bf16[128,2,1536]{2,1,0:T(2,128)(2,1)S(1)} fusion(bf16[256,2,1536]{2,1,0:T(2,128)(2,1)} %own_ref.3, s32[]{:T(128)S(6)} %select_n.22), kind=kLoop, calls=%fused_computation.19 | loop fusion | bytes 1572868 | tf_op jit(solution)/shard_map/dynamic_slice | solution.py:220
  12.7 0.1 collective-permute-start.2
  15.4 0.3 pad_maximum_fusion.2
  15.7 0.0 copy-start.2
  15.7 0.0 copy-start.3
  15.8 2.7 %collective-permute-start.6 = (bf16[2,16,2,1536]{3,2,1,0:T(2,128)(2,1)S(1)}, bf16[2,16,2,1536]{3,2,1,0:T(2,128)(2,1)S(1)}, u32[]{:S(2)}, u32[]{:S(2)}) collective-permute-start(bf16[2,16,2,1536]{3,2,1,0:T(2,128)(2,1)S(1)} %pad_maximum_fusion.2), channel_id=1, source_target_pairs={{0,8},{2,10},{4,12},{6,14},{8,0},{10,2},{12,4},{14,6},{1,9},{3,11}... | collective-permute-start | bytes 589832 | tf_op jit(solution)/shard_map/ppermute | solution.py:19
  18.4 1.1 constant_dynamic-slice_fusion
  19.5 0.7 collective-permute-start.8
  20.2 3.2 %collective-permute-start.7 = (bf16[128,2,768]{2,1,0:T(2,128)(2,1)S(1)}, bf16[128,2,768]{2,1,0:T(2,128)(2,1)S(1)}, u32[]{:S(2)}, u32[]{:S(2)}) collective-permute-start(bf16[128,2,768]{2,1,0:T(2,128)(2,1)S(1)} %get-tuple-element.49), channel_id=1, source_target_pairs={{0,2},{2,0},{4,6},{6,4},{8,10},{10,8},{12,14},{14,12},{1,3},{3,1},... | collective-permute-start | bytes 1179656 | tf_op jit(solution)/shard_map/ppermute | solution.py:27
  23.4 0.7 collective-permute-start.1
  24.1 4.1 %collective-permute-done.6 = bf16[2,16,2,1536]{3,2,1,0:T(2,128)(2,1)S(1)} collective-permute-done((bf16[2,16,2,1536]{3,2,1,0:T(2,128)(2,1)S(1)}, bf16[2,16,2,1536]{3,2,1,0:T(2,128)(2,1)S(1)}, u32[]{:S(2)}, u32[]{:S(2)}) %collective-permute-start.6) | collective-permute-done | bytes 196640 | tf_op jit(solution)/shard_map/ppermute | solution.py:19
  28.2 1.4 %collective-permute-start = (bf16[128,2,768]{2,1,0:T(2,128)(2,1)S(1)}, bf16[128,2,768]{2,1,0:T(2,128)(2,1)S(1)}, u32[]{:S(2)}, u32[]{:S(2)}) collective-permute-start(bf16[128,2,768]{2,1,0:T(2,128)(2,1)S(1)} %get-tuple-element.51), channel_id=1, source_target_pairs={{0,2},{2,0},{4,6},{6,4},{8,10},{10,8},{12,14},{14,12},{1,3},{3,1},... | collective-permute-start | bytes 1179656 | tf_op jit(solution)/shard_map/ppermute | solution.py:27
  29.6 0.6 pad_maximum_fusion
  30.2 19.5 %collective-permute-done.7.dir_ref = bf16[128,2,768]{2,1,0:T(2,128)(2,1)S(1)} collective-permute-done((bf16[128,2,768]{2,1,0:T(2,128)(2,1)S(1)}, bf16[128,2,768]{2,1,0:T(2,128)(2,1)S(1)}, u32[]{:S(2)}, u32[]{:S(2)}) %collective-permute-start.7) | collective-permute-done | bytes 393248 | tf_op jit(solution)/shard_map/ppermute | solution.py:27
  49.8 14.4 %attention.2 = (bf16[256,1536]{1,0:T(8,128)(2,1)}, f32[2,256,768]{2,1,0:T(8,128)}, bf16[2,128,768]{2,1,0:T(8,128)(2,1)}, bf16[2,128,768]{2,1,0:T(8,128)(2,1)}, b...) custom-call(s32[1]{0:T(128)} %bitcast.pos_ref, s32[2,5]{1,0:T(2,128)S(1)} %bitcast.18, ...), custom_call_target="tpu_custom_call" | custom-call | flops 1384120320 | bytes 6488064 | tf_op jit(solution)/shard_map/attention/pallas_call | solution.py:121
  64.2 14.4 %attention.3 = (bf16[256,1536]{1,0:T(8,128)(2,1)}, f32[2,256,768]{2,1,0:T(8,128)}, bf16[2,128,768]{2,1,0:T(8,128)(2,1)}, bf16[2,128,768]{2,1,0:T(8,128)(2,1)}, b...) custom-call(s32[1]{0:T(128)} %bitcast.pos_ref, ...), custom_call_target="tpu_custom_call", output_to_operand_aliasing={{0}: (10, {}), {5}: (11, {})} | custom-call | flops 1384120320 | bytes 6488064 | tf_op jit(solution)/shard_map/attention/pallas_call | solution.py:121
  78.6 0.2 maximum_reduce_fusion
  78.9 0.1 collective-permute-start.15
  78.9 1.9 %collective-permute-done.15 = f32[2,33,1536]{2,1,0:T(8,128)S(1)} collective-permute-done((f32[2,33,1536]{2,1,0:T(8,128)S(1)}, f32[2,33,1536]{2,1,0:T(8,128)S(1)}, u32[]{:S(2)}, u32[]{:S(2)}) %collective-permute-start.15) | collective-permute-done | bytes 405536 | tf_op jit(solution)/shard_map/ppermute | solution.py:19
  80.9 0.2 add.44
  81.1 3.5 %collective-permute-start.16 = (f32[2,17,1536]{2,1,0:T(8,128)S(1)}, f32[2,17,1536]{2,1,0:T(8,128)S(1)}, u32[]{:S(2)}, u32[]{:S(2)}) collective-permute-start(f32[2,17,1536]{2,1,0:T(8,128)S(1)} %pad_maximum_fusion.1), channel_id=1, source_target_pairs={{0,8},{2,10},{4,12},{6,14},{8,0},{10,2},{12,4},{14,6},{1,9},{3,11}... | collective-permute-start | bytes 626696 | tf_op jit(solution)/shard_map/ppermute | solution.py:19
  84.6 13.6 %collective-permute-done.16 = f32[2,17,1536]{2,1,0:T(8,128)S(1)} collective-permute-done((f32[2,17,1536]{2,1,0:T(8,128)S(1)}, f32[2,17,1536]{2,1,0:T(8,128)S(1)}, u32[]{:S(2)}, u32[]{:S(2)}) %collective-permute-start.16) | collective-permute-done | bytes 208928 | tf_op jit(solution)/shard_map/ppermute | solution.py:19
  98.3 0.1 collective-permute-start.17
  98.4 1.8 %collective-permute-start.12 = (bf16[2,128,768]{2,1,0:T(8,128)(2,1)}, bf16[2,128,768]{2,1,0:T(8,128)(2,1)S(1)}, u32[]{:S(2)}, u32[]{:S(2)}) collective-permute-start(bf16[2,128,768]{2,1,0:T(8,128)(2,1)} %get-tuple-element.38), channel_id=1, source_target_pairs={{0,2},{2,0},{4,6},{6,4},{8,10},{10,8},{12,14},{14,12},{1,3},{3,1},... | collective-permute-start | bytes 1179656 | tf_op jit(solution)/shard_map/ppermute | solution.py:27
  100.2 0.7 collective-permute-start.13
  100.8 0.1 collective-permute-start.14
  100.9 4.7 %collective-permute-start.9 = (bf16[2,128,768]{2,1,0:T(8,128)(2,1)}, bf16[2,128,768]{2,1,0:T(8,128)(2,1)S(1)}, u32[]{:S(2)}, u32[]{:S(2)}) collective-permute-start(bf16[2,128,768]{2,1,0:T(8,128)(2,1)} %get-tuple-element.34), channel_id=1, source_target_pairs={{0,2},{2,0},{4,6},{6,4},{8,10},{10,8},{12,14},{14,12},{1,3},{3,1},... | collective-permute-start | bytes 1179656 | tf_op jit(solution)/shard_map/ppermute | solution.py:27
  105.6 0.7 collective-permute-start.10
  106.3 20.6 %collective-permute-done.12.dir_ref = bf16[2,128,768]{2,1,0:T(8,128)(2,1)S(1)} collective-permute-done((bf16[2,128,768]{2,1,0:T(8,128)(2,1)}, bf16[2,128,768]{2,1,0:T(8,128)(2,1)S(1)}, u32[]{:S(2)}, u32[]{:S(2)}) %collective-permute-start.12) | collective-permute-done | bytes 393248 | tf_op jit(solution)/shard_map/ppermute | solution.py:27
  126.9 0.7 pad_maximum_fusion.5
  127.6 2.4 %collective-permute-start.18 = (f32[2,5,1536]{2,1,0:T(8,128)}, f32[2,5,1536]{2,1,0:T(8,128)}, u32[]{:S(2)}, u32[]{:S(2)}) collective-permute-start(f32[2,5,1536]{2,1,0:T(8,128)} %pad_maximum_fusion.5), channel_id=1, source_target_pairs={{0,2},{2,0},{4,6},{6,4},{8,10},{10,8},{12,14},{14,12},{1,3},{3,1},... | collective-permute-start | bytes 184328 | tf_op jit(solution)/shard_map/ppermute | solution.py:19
  130.0 0.7 copy.15.sent_ref
  130.7 3.3 %combine.2.rest_0_ = bf16[256,2,1536]{2,1,0:T(2,128)(2,1)} custom-call(s32[1]{0:T(128)} %bitcast.pos_ref, s32[3,1]{1,0:T(4,128)S(1)} %copy.15.sent_ref, f32[2,256,768]{2,1,0:T(8,128)S(1)} %copy-done, bf16[2,128,768]{2,1,0:T(8,128)(2,1)S(1)} %collective-permute-done.12.dir_ref, bf16[2,128,768]{2,1,0:T(8,128)(2,1)S(1)} %collective-permute-done.13.dia_ref, ...), custom_call_target="tpu_custom_call" | custom-call | flops 3145728 | bytes 3538944 | tf_op jit(solution)/shard_map/combine/pallas_call | solution.py:187
  134.0 0.9 collective-permute-done.9.dir_ref
  134.9 3.9 %combine.3 = bf16[256,2,1536]{2,1,0:T(2,128)(2,1)} custom-call(s32[1]{0:T(128)} %bitcast.pos_ref, s32[3,1]{1,0:T(4,128)S(1)} %copy.15.sent_ref, f32[2,256,768]{2,1,0:T(8,128)S(1)} %copy-done.1, bf16[2,128,768]{2,1,0:T(8,128)(2,1)S(1)} %collective-permute-done.9.dir_ref, ...), custom_call_target="tpu_custom_call", output_to_operand_aliasing={{}: (6, {})} | custom-call | flops 3145728 | bytes 3538944 | tf_op jit(solution)/shard_map/combine/pallas_call | solution.py:187
  138.9 0.9 slice.125
  139.8 0.5 fusion.1
  140.3 0.9 fusion
  141.2 0.6 copy.16
  (44 shorter events, 0.3 us)
Async XLA Ops:
  0.6 14.8 %copy-start.7 = (bf16[4,2,1536]{2,1,0:T(2,128)(2,1)S(1)}, bf16[4,2,1536]{2,1,0:T(2,128)(2,1)}, u32[]{:S(2)}) copy-start(bf16[4,2,1536]{2,1,0:T(2,128)(2,1)} %param.11) | copy-start | bytes 73732
  0.6 17.8 %copy-start.6 = (bf16[256,2,1536]{2,1,0:T(2,128)(2,1)S(1)}, bf16[256,2,1536]{2,1,0:T(2,128)(2,1)}, u32[]{:S(2)}) copy-start(bf16[256,2,1536]{2,1,0:T(2,128)(2,1)} %own_ref.3) | copy-start | bytes 4718596
  0.7 1.6 %collective-permute-start.3 = (bf16[1,4,2,1536]{3,2,1,0:T(2,128)(2,1)}, bf16[1,4,2,1536]{3,2,1,0:T(2,128)(2,1)S(1)}, u32[]{:S(2)}, u32[]{:S(2)}) collective-permute-start(bf16[1,4,2,1536]{3,2,1,0:T(2,128)(2,1)} %bitcast.20), channel_id=1, source_target_pairs={{0,1},{1,0},{2,3},{3,2},{4,5},{5,4},{6,7},{7,6},{8,9},{9,8},{10,11... | collective-permute-start | bytes 73736 | tf_op jit(solution)/shard_map/ppermute | solution.py:19
  3.0 5.0 %collective-permute-start.4 = (bf16[2,4,2,1536]{3,2,1,0:T(2,128)(2,1)S(1)}, bf16[2,4,2,1536]{3,2,1,0:T(2,128)(2,1)S(1)}, u32[]{:S(2)}, u32[]{:S(2)}) collective-permute-start(bf16[2,4,2,1536]{3,2,1,0:T(2,128)(2,1)S(1)} %pad_maximum_fusion.6), channel_id=1, source_target_pairs={{0,2},{2,0},{4,6},{6,4},{8,10},{10,8},{12,14},{14,12},{1,3},{3,1},... | collective-permute-start | bytes 147464 | tf_op jit(solution)/shard_map/ppermute | solution.py:19
  8.9 6.5 %collective-permute-start.5 = (bf16[2,8,2,1536]{3,2,1,0:T(2,128)(2,1)S(1)}, bf16[2,8,2,1536]{3,2,1,0:T(2,128)(2,1)S(1)}, u32[]{:S(2)}, u32[]{:S(2)}) collective-permute-start(bf16[2,8,2,1536]{3,2,1,0:T(2,128)(2,1)S(1)} %pad_maximum_fusion.4), channel_id=1, source_target_pairs={{0,4},{2,6},{4,0},{6,2},{8,12},{10,14},{12,8},{14,10},{1,5},{3,7},... | collective-permute-start | bytes 294920 | tf_op jit(solution)/shard_map/ppermute | solution.py:19
  12.7 37.0 %collective-permute-start.2 = (bf16[128,2,1536]{2,1,0:T(2,128)(2,1)S(1)}, bf16[128,2,1536]{2,1,0:T(2,128)(2,1)S(1)}, u32[]{:S(2)}, u32[]{:S(2)}) collective-permute-start(bf16[128,2,1536]{2,1,0:T(2,128)(2,1)S(1)} %constant_dynamic-slice_fusion.2), channel_id=1, source_target_pairs={{0,1},{1,0},{2,3},{3,2},{4,5},{5,4},{6,7},{7,6},{8,9},{9,8},{10,11... | collective-permute-start | bytes 2359304 | tf_op jit(solution)/shard_map/ppermute | solution.py:19
  15.7 34.0 %copy-start.2 = (bf16[256,1536]{1,0:T(8,128)(2,1)S(1)}, bf16[256,1536]{1,0:T(8,128)(2,1)}, u32[]{:S(2)}) copy-start(bf16[256,1536]{1,0:T(8,128)(2,1)} %q_ref.3) | copy-start | bytes 2359300
  15.7 34.0 %copy-start.3 = (bf16[256,1536]{1,0:T(8,128)(2,1)S(1)}, bf16[256,1536]{1,0:T(8,128)(2,1)}, u32[]{:S(2)}) copy-start(bf16[256,1536]{1,0:T(8,128)(2,1)} %g_ref.3) | copy-start | bytes 2359300
  15.8 34.0 %copy-start.4 = (s32[1,2,5]{2,1,0:T(2,128)S(1)}, s32[1,2,5]{2,1,0:T(2,128)}, u32[]{:S(2)}) copy-start(s32[1,2,5]{2,1,0:T(2,128)} %param.15) | copy-start | bytes 124
  15.8 34.0 %copy-start.5 = (f32[12]{0:T(128)S(1)}, f32[12]{0:T(128)}, u32[]{:S(2)}) copy-start(f32[12]{0:T(128)} %warm_ref.3) | copy-start | bytes 148
  15.8 12.4 %collective-permute-start.6 = (bf16[2,16,2,1536]{3,2,1,0:T(2,128)(2,1)S(1)}, bf16[2,16,2,1536]{3,2,1,0:T(2,128)(2,1)S(1)}, u32[]{:S(2)}, u32[]{:S(2)}) collective-permute-start(bf16[2,16,2,1536]{3,2,1,0:T(2,128)(2,1)S(1)} %pad_maximum_fusion.2), channel_id=1, source_target_pairs={{0,8},{2,10},{4,12},{6,14},{8,0},{10,2},{12,4},{14,6},{1,9},{3,11}... | collective-permute-start | bytes 589832 | tf_op jit(solution)/shard_map/ppermute | solution.py:19
  19.5 10.7 %collective-permute-start.8 = (bf16[128,2,768]{2,1,0:T(2,128)(2,1)S(1)}, bf16[128,2,768]{2,1,0:T(2,128)(2,1)S(1)}, u32[]{:S(2)}, u32[]{:S(2)}) collective-permute-start(bf16[128,2,768]{2,1,0:T(2,128)(2,1)S(1)} %get-tuple-element.48), channel_id=1, source_target_pairs={{2,4},{4,2},{6,8},{8,6},{10,12},{12,10},{3,5},{5,3},{7,9},{9,7},{1... | collective-permute-start | bytes 1179656 | tf_op jit(solution)/shard_map/ppermute | solution.py:27
  20.2 29.5 %collective-permute-start.7 = (bf16[128,2,768]{2,1,0:T(2,128)(2,1)S(1)}, bf16[128,2,768]{2,1,0:T(2,128)(2,1)S(1)}, u32[]{:S(2)}, u32[]{:S(2)}) collective-permute-start(bf16[128,2,768]{2,1,0:T(2,128)(2,1)S(1)} %get-tuple-element.49), channel_id=1, source_target_pairs={{0,2},{2,0},{4,6},{6,4},{8,10},{10,8},{12,14},{14,12},{1,3},{3,1},... | collective-permute-start | bytes 1179656 | tf_op jit(solution)/shard_map/ppermute | solution.py:27
  23.4 40.7 %collective-permute-start.1 = (bf16[128,2,768]{2,1,0:T(2,128)(2,1)S(1)}, bf16[128,2,768]{2,1,0:T(2,128)(2,1)S(1)}, u32[]{:S(2)}, u32[]{:S(2)}) collective-permute-start(bf16[128,2,768]{2,1,0:T(2,128)(2,1)S(1)} %get-tuple-element.50), channel_id=1, source_target_pairs={{2,4},{4,2},{6,8},{8,6},{10,12},{12,10},{3,5},{5,3},{7,9},{9,7},{1... | collective-permute-start | bytes 1179656 | tf_op jit(solution)/shard_map/ppermute | solution.py:27
  28.2 36.0 %collective-permute-start = (bf16[128,2,768]{2,1,0:T(2,128)(2,1)S(1)}, bf16[128,2,768]{2,1,0:T(2,128)(2,1)S(1)}, u32[]{:S(2)}, u32[]{:S(2)}) collective-permute-start(bf16[128,2,768]{2,1,0:T(2,128)(2,1)S(1)} %get-tuple-element.51), channel_id=1, source_target_pairs={{0,2},{2,0},{4,6},{6,4},{8,10},{10,8},{12,14},{14,12},{1,3},{3,1},... | collective-permute-start | bytes 1179656 | tf_op jit(solution)/shard_map/ppermute | solution.py:27
  78.9 1.9 %collective-permute-start.15 = (f32[2,33,1536]{2,1,0:T(8,128)S(1)}, f32[2,33,1536]{2,1,0:T(8,128)S(1)}, u32[]{:S(2)}, u32[]{:S(2)}) collective-permute-start(f32[2,33,1536]{2,1,0:T(8,128)S(1)} %select_maximum_fusion), channel_id=1, source_target_pairs={{0,1},{1,0},{2,3},{3,2},{4,5},{5,4},{6,7},{7,6},{8,9},{9,8},{10,11... | collective-permute-start | bytes 1216520 | tf_op jit(solution)/shard_map/ppermute | solution.py:19
  80.8 49.9 %copy-start = (f32[2,256,768]{2,1,0:T(8,128)S(1)}, f32[2,256,768]{2,1,0:T(8,128)}, u32[]{:S(2)}) copy-start(f32[2,256,768]{2,1,0:T(8,128)} %get-tuple-element.37.own_ref) | copy-start | bytes 4718596
  81.1 17.1 %collective-permute-start.16 = (f32[2,17,1536]{2,1,0:T(8,128)S(1)}, f32[2,17,1536]{2,1,0:T(8,128)S(1)}, u32[]{:S(2)}, u32[]{:S(2)}) collective-permute-start(f32[2,17,1536]{2,1,0:T(8,128)S(1)} %pad_maximum_fusion.1), channel_id=1, source_target_pairs={{0,8},{2,10},{4,12},{6,14},{8,0},{10,2},{12,4},{14,6},{1,9},{3,11}... | collective-permute-start | bytes 626696 | tf_op jit(solution)/shard_map/ppermute | solution.py:19
  98.3 7.3 %collective-permute-start.17 = (f32[2,9,1536]{2,1,0:T(8,128)S(1)}, f32[2,9,1536]{2,1,0:T(8,128)S(1)}, u32[]{:S(2)}, u32[]{:S(2)}) collective-permute-start(f32[2,9,1536]{2,1,0:T(8,128)S(1)} %pad_maximum_fusion.3), channel_id=1, source_target_pairs={{0,4},{2,6},{4,0},{6,2},{8,12},{10,14},{12,8},{14,10},{1,5},{3,7},... | collective-permute-start | bytes 331784 | tf_op jit(solution)/shard_map/ppermute | solution.py:19
  98.4 28.5 %collective-permute-start.12 = (bf16[2,128,768]{2,1,0:T(8,128)(2,1)}, bf16[2,128,768]{2,1,0:T(8,128)(2,1)S(1)}, u32[]{:S(2)}, u32[]{:S(2)}) collective-permute-start(bf16[2,128,768]{2,1,0:T(8,128)(2,1)} %get-tuple-element.38), channel_id=1, source_target_pairs={{0,2},{2,0},{4,6},{6,4},{8,10},{10,8},{12,14},{14,12},{1,3},{3,1},... | collective-permute-start | bytes 1179656 | tf_op jit(solution)/shard_map/ppermute | solution.py:27
  100.2 27.4 %collective-permute-start.13 = (bf16[2,128,768]{2,1,0:T(8,128)(2,1)}, bf16[2,128,768]{2,1,0:T(8,128)(2,1)S(1)}, u32[]{:S(2)}, u32[]{:S(2)}) collective-permute-start(bf16[2,128,768]{2,1,0:T(8,128)(2,1)} %get-tuple-element.39), channel_id=1, source_target_pairs={{2,4},{4,2},{6,8},{8,6},{10,12},{12,10},{3,5},{5,3},{7,9},{9,7},{1... | collective-permute-start | bytes 1179656 | tf_op jit(solution)/shard_map/ppermute | solution.py:27
  100.8 29.9 %collective-permute-start.14 = (bf16[2,128,768]{2,1,0:T(8,128)(2,1)}, bf16[2,128,768]{2,1,0:T(8,128)(2,1)S(1)}, u32[]{:S(2)}, u32[]{:S(2)}) collective-permute-start(bf16[2,128,768]{2,1,0:T(8,128)(2,1)} %get-tuple-element.40), channel_id=1, source_target_pairs={{0,1},{1,0},{2,3},{3,2},{4,5},{5,4},{6,7},{7,6},{8,9},{9,8},{10,11... | collective-permute-start | bytes 1179656 | tf_op jit(solution)/shard_map/ppermute | solution.py:19
  100.9 34.0 %collective-permute-start.9 = (bf16[2,128,768]{2,1,0:T(8,128)(2,1)}, bf16[2,128,768]{2,1,0:T(8,128)(2,1)S(1)}, u32[]{:S(2)}, u32[]{:S(2)}) collective-permute-start(bf16[2,128,768]{2,1,0:T(8,128)(2,1)} %get-tuple-element.34), channel_id=1, source_target_pairs={{0,2},{2,0},{4,6},{6,4},{8,10},{10,8},{12,14},{14,12},{1,3},{3,1},... | collective-permute-start | bytes 1179656 | tf_op jit(solution)/shard_map/ppermute | solution.py:27
  105.6 29.3 %collective-permute-start.10 = (bf16[2,128,768]{2,1,0:T(8,128)(2,1)}, bf16[2,128,768]{2,1,0:T(8,128)(2,1)S(1)}, u32[]{:S(2)}, u32[]{:S(2)}) collective-permute-start(bf16[2,128,768]{2,1,0:T(8,128)(2,1)} %get-tuple-element.35), channel_id=1, source_target_pairs={{2,4},{4,2},{6,8},{8,6},{10,12},{12,10},{3,5},{5,3},{7,9},{9,7},{1... | collective-permute-start | bytes 1179656 | tf_op jit(solution)/shard_map/ppermute | solution.py:27
  106.3 23.7 %copy-start.8 = (f32[2,8,1536]{2,1,0:T(8,128)}, f32[2,8,1536]{2,1,0:T(8,128)S(1)}, u32[]{:S(2)}) copy-start(f32[2,8,1536]{2,1,0:T(8,128)S(1)} %slice_add_fusion.2) | copy-start | bytes 294916
  126.9 8.0 %collective-permute-start.11 = (bf16[2,128,768]{2,1,0:T(8,128)(2,1)}, bf16[2,128,768]{2,1,0:T(8,128)(2,1)}, u32[]{:S(2)}, u32[]{:S(2)}) collective-permute-start(bf16[2,128,768]{2,1,0:T(8,128)(2,1)} %get-tuple-element.36), channel_id=1, source_target_pairs={{0,1},{1,0},{2,3},{3,2},{4,5},{5,4},{6,7},{7,6},{8,9},{9,8},{10,11... | collective-permute-start | bytes 1179656 | tf_op jit(solution)/shard_map/ppermute | solution.py:19
  127.6 11.3 %collective-permute-start.18 = (f32[2,5,1536]{2,1,0:T(8,128)}, f32[2,5,1536]{2,1,0:T(8,128)}, u32[]{:S(2)}, u32[]{:S(2)}) collective-permute-start(f32[2,5,1536]{2,1,0:T(8,128)} %pad_maximum_fusion.5), channel_id=1, source_target_pairs={{0,2},{2,0},{4,6},{6,4},{8,10},{10,8},{12,14},{14,12},{1,3},{3,1},... | collective-permute-start | bytes 184328 | tf_op jit(solution)/shard_map/ppermute | solution.py:19
  130.7 4.2 %copy-start.1 = (f32[2,256,768]{2,1,0:T(8,128)S(1)}, f32[2,256,768]{2,1,0:T(8,128)}, u32[]{:S(2)}) copy-start(f32[2,256,768]{2,1,0:T(8,128)} %get-tuple-element.33.own_ref) | copy-start | bytes 4718596
  134.9 5.4 %copy-start.9 = (f32[2,8,1536]{2,1,0:T(8,128)S(1)}, f32[2,8,1536]{2,1,0:T(8,128)}, u32[]{:S(2)}) copy-start(f32[2,8,1536]{2,1,0:T(8,128)} %copy-done.8) | copy-start | bytes 294916

commit v2 on v1

--- a/solution.py
+++ b/solution.py
@@ -14,9 +14,14 @@
 SMEM = pltpu.MemorySpace.SMEM
 
 
-def swap_bit(x, axis, bit):
-    count = lax.axis_size(axis)
-    return lax.ppermute(x, axis, [(i, i ^ (1 << bit)) for i in range(count)])
+def swap_mask(x, mask):
+    count = lax.axis_size(("gx", "gy"))
+    return lax.ppermute(x, ("gx", "gy"), [(i, i ^ mask) for i in range(count)])
+
+
+def levels(count):
+    bits = count.bit_length() - 1
+    return [(at, (1 << min(2, bits - at)) - 1) for at in range(0, bits, 2)]
 
 
 def swap_pairs(x, first):
@@ -27,32 +32,54 @@
     return lax.ppermute(x, "gx", route)
 
 
-def attention_kernel(
-    pos_ref, filt_ref, warm_ref, q_ref, g_ref, own_ref, dir_ref, dia_ref, par_ref, anc_ref, *rest,
-    gx_count, head0, width,
-):
-    (dq_ref, own_out, dir_out, dia_out, par_out, anc_out, temp_out, k_ref, v_ref) = rest[-9:]
-    head = pl.program_id(0)
-    gx = pos_ref[0]
-    odd = lax.rem(gx, 2)
-    own_rows = own_ref.shape[0]
-    blocks = own_rows // BLOCK
-    anchors = anc_ref.shape[0]
-    queries = q_ref.shape[0]
-    near = own_rows + 3 * BLOCK
-    keys = near + anchors
-
+def split_heads(total):
+    first = (total + 1) // 2
+    return [n for n in (first, total - first) if n > 0]
+
+
+def prep_kernel(a_ref, b_ref, k_ref, v_ref):
     row = 0
-    for ref in (own_ref, dir_ref, dia_ref, par_ref, anc_ref):
+    for ref in (a_ref, b_ref):
         n = ref.shape[0]
         k_ref[row : row + n, :] = ref[:, 0, :]
         v_ref[row : row + n, :] = ref[:, 1, :]
         row += n
 
+
+def prep(a, b, wide, weight):
+    rows, feat = a.shape[0] + b.shape[0], a.shape[2]
+    spec = lambda n: pl.BlockSpec((n, 2, wide), lambda h: (0, 0, h))
+    out = pl.BlockSpec((rows, wide), lambda h: (0, h))
+    return pl.pallas_call(
+        prep_kernel,
+        grid=(feat // wide,),
+        in_specs=[spec(a.shape[0]), spec(b.shape[0])],
+        out_specs=[out, out],
+        out_shape=[jax.ShapeDtypeStruct((rows, feat), BF16)] * 2,
+        cost_estimate=pl.CostEstimate(
+            flops=weight * rows * feat, transcendentals=0, bytes_accessed=8 * rows * feat
+        ),
+        name="prep",
+    )(a, b)
+
+
+def attention_kernel(
+    pos_ref, filt_ref, warm_ref, q_ref, g_ref, k1_ref, v1_ref, k2_ref, v2_ref, anc_ref, *rest,
+    gx_count, head0, width,
+):
+    (dq_ref, own_out, dir_out, dia_out, par_out, anc_out, temp_out) = rest[-7:]
+    head = pl.program_id(0)
+    gx = pos_ref[0]
+    odd = lax.rem(gx, 2)
+    queries = q_ref.shape[0]
+    own_rows = k1_ref.shape[0] - BLOCK
+    blocks = own_rows // BLOCK
+    near = own_rows + 3 * BLOCK
+
     q = q_ref[...]
     g = g_ref[...]
-    k = k_ref[...]
-    v = v_ref[...]
+    k = jnp.concatenate([k1_ref[...], k2_ref[...], anc_ref[:, 0, :]], axis=0)
+    v = jnp.concatenate([v1_ref[...], v2_ref[...], anc_ref[:, 1, :]], axis=0)
     nt = (((1,), (1,)), ((), ()))
     s = lax.dot_general(k, q, nt, preferred_element_type=F32)
     dp = lax.dot_general(v, g, nt, preferred_element_type=F32)
@@ -68,9 +95,9 @@
         for a in range(blocks):
             if b == a:
                 continue
-            col = (b if b < blocks else (direct_col, diagonal_col, blocks + 2)[b - blocks])
+            col = (b if b < blocks else (blocks + 2, direct_col, diagonal_col)[b - blocks])
             ok = filt_ref[a, col] > 0
-            if b == blocks + 1:
+            if b == blocks + 2:
                 ok = jnp.logical_and(ok, diagonal_there)
             bias = jnp.where(lane == a, jnp.where(ok, 0.0, -jnp.inf).astype(F32), bias)
         parts.append(s[b * BLOCK : (b + 1) * BLOCK] * mult + bias)
@@ -92,26 +119,28 @@
     dq_ref[...] = dq.astype(BF16)
     for j, terms in enumerate((dk, dv)):
         own_out[j] = terms[:own_rows]
-        for i, ref in enumerate((dir_out, dia_out, par_out)):
+        for i, ref in enumerate((par_out, dir_out, dia_out)):
             at = own_rows + i * BLOCK
             ref[j] = terms[at : at + BLOCK].astype(BF16)
         anc_out[j] = terms[near:]
 
 
-def attention(pos, filt, warm, q, g, mesh_kv, halo, anchors, head0, heads, dq_prev, anc_prev):
+def attention(pos, filt, warm, q, g, near_kv, halo, anchors, head0, heads, dq_prev, anc_prev):
     rows, feat = q.shape
     total = warm.shape[0]
     width = feat // total
-    own_rows = mesh_kv.shape[0]
+    own_rows = near_kv[0].shape[0] - BLOCK
     a_rows = anchors.shape[0]
     keys = own_rows + 3 * BLOCK + a_rows
-    full3 = lambda n: pl.BlockSpec((n, 2, width), lambda h: (0, 0, head0 + h))
-    part3 = lambda n: pl.BlockSpec((n, 2, width), lambda h: (0, 0, h))
     smem = pl.BlockSpec(memory_space=SMEM)
-    cols = pl.BlockSpec((rows, width), lambda h: (0, head0 + h))
+    full = lambda n: pl.BlockSpec((n, width), lambda h: (0, head0 + h))
+    part = pl.BlockSpec((2 * BLOCK, width), lambda h: (0, h))
+    cols = full(rows)
     out_face = pl.BlockSpec((2, BLOCK, width), lambda h: (0, 0, h))
-    in_specs = [smem, smem, smem, cols, cols, full3(own_rows), part3(BLOCK), part3(BLOCK), full3(BLOCK), full3(a_rows)]
-    args = [pos, filt, warm, q, g, mesh_kv, *halo, anchors]
+    in_specs = [smem, smem, smem, cols, cols]
+    in_specs += [full(own_rows + BLOCK)] * 2 + [part] * 2
+    in_specs += [pl.BlockSpec((a_rows, 2, width), lambda h: (0, 0, head0 + h))]
+    args = [pos, filt, warm, q, g, *near_kv, *halo, anchors]
     alias = {}
     if dq_prev is not None:
         in_specs += [pl.BlockSpec(memory_space=pl.ANY)] * 2
@@ -140,7 +169,6 @@
             jax.ShapeDtypeStruct((2, a_rows, feat), F32),
             jax.ShapeDtypeStruct((heads, 1, rows), F32),
         ],
-        scratch_shapes=[pltpu.VMEM((keys, width), BF16)] * 2,
         input_output_aliases=alias,
         compiler_params=pltpu.CompilerParams(vmem_limit_bytes=48 << 20),
         cost_estimate=pl.CostEstimate(
@@ -170,7 +198,7 @@
             out_ref[at, j, :] = total.astype(BF16)
 
 
-def combine(pos, sent, own, faces, head0, heads, feat, width, prev):
+def combine(pos, sent, own, faces, head0, heads, feat, width, prev, weight=1):
     rows = own.shape[1]
     smem = pl.BlockSpec(memory_space=SMEM)
     w = width * (2 if heads % 2 == 0 and head0 % 2 == 0 else 1)
@@ -193,7 +221,7 @@
         input_output_aliases=alias,
         compiler_params=pltpu.CompilerParams(vmem_limit_bytes=32 << 20),
         cost_estimate=pl.CostEstimate(
-            flops=heads * width * rows * 16,
+            flops=weight * heads * width * rows * 16,
             transcendentals=0,
             bytes_accessed=heads * width * (rows * 12 + 3 * BLOCK * 4),
         ),
@@ -206,7 +234,7 @@
     total = warm.shape[0]
     width = feat // total
     gx_count = lax.axis_size("gx")
-    bits = gx_count.bit_length() - 1
+    stages = levels(lax.axis_size(("gx", "gy")))
     gx = lax.axis_index("gx")
     pos = jnp.full((1,), gx, jnp.int32)
     sent = exported[0]
@@ -214,51 +242,62 @@
     odd = lax.rem(gx, 2)
     direct_block = jnp.where(odd == 1, sent[0, 0], sent[1, 0])
     diagonal_block = jnp.where(odd == 1, sent[1, 0], sent[0, 0])
-    chunks = [(0, total // 2), (total // 2, total - total // 2)]
+    sizes = split_heads(total)
+    chunks = [(sum(sizes[:i]), n) for i, n in enumerate(sizes)]
 
     def pick(block, head0, heads):
         return lax.dynamic_slice(
             mesh_kv, (block * BLOCK, 0, head0 * width), (BLOCK, 2, heads * width)
         )
 
-    halos = []
-    anchors = landmark[None]
-    theirs = swap_bit(anchors, "gy", 0)
-    anchors = jnp.concatenate([anchors, theirs], axis=0)
-    for c, (head0, heads) in enumerate(chunks):
-        diagonal = swap_pairs(pick(diagonal_block, head0, heads), 1)
-        direct = swap_pairs(pick(direct_block, head0, heads), 0)
-        halos.append((direct, diagonal))
-    partner = swap_bit(pick(sent[2, 0], 0, total), "gy", 0)
-    for bit in range(bits):
-        theirs = swap_bit(anchors, "gx", bit)
-        anchors = jnp.concatenate([anchors, theirs], axis=1)
-    a_rows = anchors.shape[0] * anchors.shape[1]
-    anchors = anchors.reshape(a_rows, 2, feat)
+    picks = [
+        (pick(direct_block, head0, heads), pick(diagonal_block, head0, heads))
+        for head0, heads in chunks
+    ]
+    partner = swap_mask(pick(sent[2, 0], 0, total), 1)
+    anchors = landmark
+    for i, (low, peers) in enumerate(stages):
+        if i == 1:
+            anchors, picks[1] = lax.optimization_barrier((anchors, picks[1]))
+        got = [swap_mask(anchors, m << low) for m in range(1, peers + 1)]
+        anchors = jnp.concatenate([anchors] + got, axis=0)
+    near_kv = prep(mesh_kv, partner, 2 * width if total % 2 == 0 else width, 1)
+    halos = [(swap_pairs(d, 0), swap_pairs(g, 1)) for d, g in picks]
+    near_kv, halos[0] = lax.optimization_barrier((near_kv, halos[0]))
+    halos = [prep(d, g, width, 100000) for d, g in halos]
 
     dq = anc = None
     temps, owns, returned = [], [], []
-    for (head0, heads), (direct, diagonal) in zip(chunks, halos):
+    for (head0, heads), halo in zip(chunks, halos):
         dq, own, f_dir, f_dia, f_par, anc, temp = attention(
-            pos, filt, warm, q, g, mesh_kv, (direct, diagonal, partner), anchors, head0, heads, dq, anc
+            pos, filt, warm, q, g, near_kv, halo, anchors, head0, heads, dq, anc
         )
         temps.append(temp)
         owns.append(own)
-        returned.append((swap_pairs(f_dir, 0), swap_pairs(f_dia, 1), swap_bit(f_par, "gy", 0)))
+        faces = (f_dir, f_dia, f_par)
+        if returned:
+            anc, faces, returned[-1] = lax.optimization_barrier((anc, faces, returned[-1]))
+        f_dir, f_dia, f_par = faces
+        returned.append((swap_pairs(f_dir, 0), swap_pairs(f_dia, 1), swap_mask(f_par, 1)))
 
     temp = jnp.sum(jnp.concatenate(temps, axis=0), axis=(1, 2)) / math.sqrt(width)
     extra = jnp.zeros((2, 1, feat), F32).at[0, 0, :total].set(temp)
-    for axis, bit in [("gy", 0)] + [("gx", b) for b in reversed(range(bits))]:
-        half = anc.shape[1] // 2
-        got = swap_bit(jnp.concatenate([anc[:, half:], extra], axis=1), axis, bit)
-        anc = anc[:, :half] + got[:, :half]
-        extra = extra + got[:, half:]
+    cell = None
+    for c in range(len(chunks) - 1):
+        cell = combine(pos, sent, owns[c], returned[c], *chunks[c], feat, width, cell, weight=4000)
+    for i, (low, peers) in enumerate(reversed(stages)):
+        n = anc.shape[1] // (peers + 1)
+        got = [
+            swap_mask(jnp.concatenate([anc[:, m * n : (m + 1) * n], extra], axis=1), m << low)
+            for m in range(1, peers + 1)
+        ]
+        if i == len(stages) - 1:
+            got, cell = lax.optimization_barrier((got, cell))
+        anc = sum([x[:, :n] for x in got], anc[:, :n])
+        extra = sum([x[:, n:] for x in got], extra)
     anchor_grad = jnp.transpose(anc, (1, 0, 2))
     temp = extra[0, 0, :total]
-
-    cell = None
-    for (head0, heads), own, faces in zip(chunks, owns, returned):
-        cell = combine(pos, sent, own, faces, head0, heads, feat, width, cell)
+    cell = combine(pos, sent, owns[-1], returned[-1], *chunks[-1], feat, width, cell, weight=0)
     return (dq, cell, anchor_grad, temp)
 
 

time: 142 us -> 136 us (0.958)
  the two profiles are of different devices: /device:TPU:0 before, /device:TPU:21 now
where the time goes in v2:
time: 136 us; the launch traced here: 135 us
  Pallas kernels  43 us (32%)
  waiting for transfers between devices  34.9 us (26%)
  starting transfers between devices  32.3 us (24%)
  local copies, waits for them, and re-layouts  16.1 us (12%)
  other arithmetic  4.59 us (3%)
  between operations  4.2 us (3%)
    ppermute x15, waiting for transfers between devices, swap_mask(): return lax.ppermute(x, ('gx', 'gy'), [(i, i ^ mask) for i in range(count)])  34.9 us
    ppermute x8, starting transfers between devices, swap_pairs(): return lax.ppermute(x, 'gx', route)  18.8 us
    pallas_call x2, Pallas kernels, attention(): pl.pallas_call(functools.partial(attention_kernel, gx_count=lax.axis_size...  18 us
    pallas_call x3, Pallas kernels, prep(): pl.pallas_call(prep_kernel, grid=(feat // wide,), in_specs=[spec(a.shape[...  17.5 us
    ppermute x15, starting transfers between devices, swap_mask(): return lax.ppermute(x, ('gx', 'gy'), [(i, i ^ mask) for i in range(count)])  13.5 us
    unnamed x52, local copies, waits for them, and re-layouts  9.38 us
    pallas_call x2, Pallas kernels, combine(): pl.pallas_call(combine_kernel, grid=(steps,), in_specs=in_specs, out_spec...  7.6 us
    dynamic_slice x2, local copies, waits for them, and re-layouts, pick(): lax.dynamic_slice(mesh_kv, (block * BLOCK, 0, head0 * width), (BLOCK, 2,...  3.99 us
  transfers between devices with their start and end apart: 23, of which 7 were waited for; matrix products, arithmetic and copies ran while one was open for 8% of the time, Pallas kernels for 29%

profile of v2, /device:TPU:21, one launch (start us, length us, event | category | flops | bytes accessed | tf_op | source)
XLA Modules:
  0.0 135.1 jit_solution(16281634412519910124)
XLA Ops:
  0.6 0.7 collective-permute-start.3
  1.4 1.2 collective-permute-start.4
  3.1 1.4 fusion.9
  7.0 3.4 %constant_dynamic-slice_fusion = (bf16[128,2,768]{2,1,0:T(2,128)(2,1)}, bf16[128,2,768]{2,1,0:T(2,128)(2,1)S(1)}, bf16[128,2,768]{2,1,0:T(2,128)(2,1)S(1)}, bf16[128,2,768]{2,1,0:T(2,128)(2,1)}) fusion(bf16[256,2,1536]{2,1,0:T(2,128)(2,1)} %a_ref.1, s32[]{:T(128)S(6)} %select_n.22, s32[]{:T(128)S(6)} %select_n.20), kind=kLoop, calls=%fused_computation.23 | loop fusion | bytes 3145736 | tf_op jit(solution)/shard_map/dynamic_slice | solution.py:249
  10.5 1.2 collective-permute-start.1
  11.7 2.1 %collective-permute-start.2 = (bf16[128,2,768]{2,1,0:T(2,128)(2,1)S(1)}, bf16[128,2,768]{2,1,0:T(2,128)(2,1)S(1)}, u32[]{:S(2)}, u32[]{:S(2)}) collective-permute-start(bf16[128,2,768]{2,1,0:T(2,128)(2,1)S(1)} %get-tuple-element.97), channel_id=1, source_target_pairs={{2,4},{4,2},{6,8},{8,6},{10,12},{12,10},{3,5},{5,3},{7,9},{9,7},{1... | collective-permute-start | bytes 1179656 | tf_op jit(solution)/shard_map/ppermute | solution.py:32
  14.4 0.5 constant_dynamic-slice_fusion.4
  15.0 0.8 collective-permute-start
  15.9 1.4 %collective-permute-start.8 = (bf16[16,2,1536]{2,1,0:T(2,128)(2,1)S(1)}, bf16[16,2,1536]{2,1,0:T(2,128)(2,1)S(1)}, u32[]{:S(2)}, u32[]{:S(2)}) collective-permute-start(bf16[16,2,1536]{2,1,0:T(2,128)(2,1)S(1)} %pad_maximum_fusion.3), channel_id=1, source_target_pairs={{0,4},{1,5},{2,6},{3,7},{4,0},{5,1},{6,2},{7,3},{8,12},{9,13},{10,... | collective-permute-start | bytes 294920 | tf_op jit(solution)/shard_map/ppermute | solution.py:19
  17.5 8.5 %collective-permute-done.8 = bf16[16,2,1536]{2,1,0:T(2,128)(2,1)S(1)} collective-permute-done((bf16[16,2,1536]{2,1,0:T(2,128)(2,1)S(1)}, bf16[16,2,1536]{2,1,0:T(2,128)(2,1)S(1)}, u32[]{:S(2)}, u32[]{:S(2)}) %collective-permute-start.8) | collective-permute-done | bytes 98336 | tf_op jit(solution)/shard_map/ppermute | solution.py:19
  26.1 3.1 %collective-permute-start.6 = (bf16[128,2,768]{2,1,0:T(2,128)(2,1)}, bf16[128,2,768]{2,1,0:T(2,128)(2,1)}, u32[]{:S(2)}, u32[]{:S(2)}) collective-permute-start(bf16[128,2,768]{2,1,0:T(2,128)(2,1)} %get-tuple-element.58), channel_id=1, source_target_pairs={{0,2},{2,0},{4,6},{6,4},{8,10},{10,8},{12,14},{14,12},{1,3},{3,1},... | collective-permute-start | bytes 1179656 | tf_op jit(solution)/shard_map/ppermute | solution.py:32
  29.2 1.2 collective-permute-done.10
  30.5 2.8 %collective-permute-start.7 = (bf16[128,2,768]{2,1,0:T(2,128)(2,1)}, bf16[128,2,768]{2,1,0:T(2,128)(2,1)}, u32[]{:S(2)}, u32[]{:S(2)}) collective-permute-start(bf16[128,2,768]{2,1,0:T(2,128)(2,1)} %get-tuple-element.59), channel_id=1, source_target_pairs={{2,4},{4,2},{6,8},{8,6},{10,12},{12,10},{3,5},{5,3},{7,9},{9,7},{1... | collective-permute-start | bytes 1179656 | tf_op jit(solution)/shard_map/ppermute | solution.py:32
  33.4 0.7 copy-done.4
  34.2 0.9 copy-done.19
  35.1 7.2 %prep.3 = (bf16[384,1536]{1,0:T(8,128)(2,1)}, bf16[384,1536]{1,0:T(8,128)(2,1)}) custom-call(bf16[256,2,1536]{2,1,0:T(2,128)(2,1)} %a_ref.1, bf16[128,2,1536]{2,1,0:T(2,128)(2,1)} %copy-done.19), custom_call_target="tpu_custom_call" | custom-call | flops 589824 | bytes 4718592 | tf_op jit(solution)/shard_map/prep/pallas_call | solution.py:53
  42.3 0.7 copy-done.22
  43.2 5.2 %prep.5 = (bf16[256,768]{1,0:T(8,128)(2,1)}, bf16[256,768]{1,0:T(8,128)(2,1)}) custom-call(bf16[128,2,768]{2,1,0:T(2,128)(2,1)} %copy-done.22, bf16[128,2,768]{2,1,0:T(2,128)(2,1)} %copy-done.23), custom_call_target="tpu_custom_call" | custom-call | flops 19660800000 | bytes 1572864 | tf_op jit(solution)/shard_map/prep/pallas_call | solution.py:53
  48.4 1.0 copy-done.5
  49.4 1.0 copy-done.16
  50.4 1.0 copy-done.17
  51.4 8.9 %attention.2 = (bf16[256,1536]{1,0:T(8,128)(2,1)}, f32[2,256,768]{2,1,0:T(8,128)}, bf16[2,128,768]{2,1,0:T(8,128)(2,1)}, bf16[2,128,768]{2,1,0:T(8,128)(2,1)}, b...) custom-call(s32[1]{0:T(128)} %bitcast.pos_ref, s32[2,5]{1,0:T(2,128)S(1)} %bitcast.14, ...), custom_call_target="tpu_custom_call" | custom-call | flops 1384120320 | bytes 6488064 | tf_op jit(solution)/shard_map/attention/pallas_call | solution.py:150
  60.3 1.2 collective-permute-start.11
  61.5 5.3 %collective-permute-start.12 = (bf16[2,128,768]{2,1,0:T(8,128)(2,1)}, bf16[2,128,768]{2,1,0:T(8,128)(2,1)}, u32[]{:S(2)}, u32[]{:S(2)}) collective-permute-start(bf16[2,128,768]{2,1,0:T(8,128)(2,1)} %get-tuple-element.76), channel_id=1, source_target_pairs={{2,4},{4,2},{6,8},{8,6},{10,12},{12,10},{3,5},{5,3},{7,9},{9,7},{1... | collective-permute-start | bytes 1179656 | tf_op jit(solution)/shard_map/ppermute | solution.py:32
  66.8 3.0 %collective-permute-start.13 = (bf16[2,128,768]{2,1,0:T(8,128)(2,1)}, bf16[2,128,768]{2,1,0:T(8,128)(2,1)}, u32[]{:S(2)}, u32[]{:S(2)}) collective-permute-start(bf16[2,128,768]{2,1,0:T(8,128)(2,1)} %get-tuple-element.77), channel_id=1, source_target_pairs={{0,1},{1,0},{2,3},{3,2},{4,5},{5,4},{6,7},{7,6},{8,9},{9,8},{10,11... | collective-permute-start | bytes 1179656 | tf_op jit(solution)/shard_map/ppermute | solution.py:19
  69.8 5.1 %prep.4 = (bf16[256,768]{1,0:T(8,128)(2,1)}, bf16[256,768]{1,0:T(8,128)(2,1)}) custom-call(bf16[128,2,768]{2,1,0:T(2,128)(2,1)} %collective-permute-done.6.a_ref, bf16[128,2,768]{2,1,0:T(2,128)(2,1)} %collective-permute-done.7.b_ref), custom_call_target="tpu_custom_call" | custom-call | flops 19660800000 | bytes 1572864 | tf_op jit(solution)/shard_map/prep/pallas_call | solution.py:53
  74.8 1.0 copy-done.6
  75.8 1.0 copy-done.7
  76.8 1.0 copy-done.8
  77.8 9.1 %attention.3 = (bf16[256,1536]{1,0:T(8,128)(2,1)}, f32[2,256,768]{2,1,0:T(8,128)}, bf16[2,128,768]{2,1,0:T(8,128)(2,1)S(1)}, bf16[2,128,768]{2,1,0:T(8,128)(2,1)...) custom-call(s32[1]{0:T(128)} %bitcast.pos_ref, ...), custom_call_target="tpu_custom_call", output_to_operand_aliasing={{0}: (10, {}), {5}: (11, {})} | custom-call | flops 1384120320 | bytes 6488064 | tf_op jit(solution)/shard_map/attention/pallas_call | solution.py:150
  87.2 0.9 fusion
  88.1 0.5 collective-permute-start.17
  88.6 2.1 %collective-permute-start.19 = (f32[2,17,1536]{2,1,0:T(8,128)S(1)}, f32[2,17,1536]{2,1,0:T(8,128)}, u32[]{:S(2)}, u32[]{:S(2)}) collective-permute-start(f32[2,17,1536]{2,1,0:T(8,128)S(1)} %get-tuple-element.111), channel_id=1, source_target_pairs={{0,12},{1,13},{2,14},{3,15},{4,8},{5,9},{6,10},{7,11},{8,4},{9,5},... | collective-permute-start | bytes 626696 | tf_op jit(solution)/shard_map/ppermute | solution.py:19
  90.8 0.7 collective-permute-start.14
  91.5 2.4 %collective-permute-start.15 = (bf16[2,128,768]{2,1,0:T(8,128)(2,1)}, bf16[2,128,768]{2,1,0:T(8,128)(2,1)S(1)}, u32[]{:S(2)}, u32[]{:S(2)}) collective-permute-start(bf16[2,128,768]{2,1,0:T(8,128)(2,1)} %copy-done.13), channel_id=1, source_target_pairs={{2,4},{4,2},{6,8},{8,6},{10,12},{12,10},{3,5},{5,3},{7,9},{9,7},{1... | collective-permute-start | bytes 1179656 | tf_op jit(solution)/shard_map/ppermute | solution.py:32
  93.9 4.8 %collective-permute-done.17 = f32[2,17,1536]{2,1,0:T(8,128)} collective-permute-done((f32[2,17,1536]{2,1,0:T(8,128)}, f32[2,17,1536]{2,1,0:T(8,128)}, u32[]{:S(2)}, u32[]{:S(2)}) %collective-permute-start.17) | collective-permute-done | bytes 208928 | tf_op jit(solution)/shard_map/ppermute | solution.py:19
  98.7 2.8 %collective-permute-done.18 = f32[2,17,1536]{2,1,0:T(8,128)} collective-permute-done((f32[2,17,1536]{2,1,0:T(8,128)}, f32[2,17,1536]{2,1,0:T(8,128)}, u32[]{:S(2)}, u32[]{:S(2)}) %collective-permute-start.18) | collective-permute-done | bytes 208928 | tf_op jit(solution)/shard_map/ppermute | solution.py:19
  101.5 15.3 %collective-permute-done.19 = f32[2,17,1536]{2,1,0:T(8,128)} collective-permute-done((f32[2,17,1536]{2,1,0:T(8,128)S(1)}, f32[2,17,1536]{2,1,0:T(8,128)}, u32[]{:S(2)}, u32[]{:S(2)}) %collective-permute-start.19) | collective-permute-done | bytes 208928 | tf_op jit(solution)/shard_map/ppermute | solution.py:19
  116.9 1.2 slice_add_fusion
  118.1 0.7 slice_add_fusion.9
  118.8 0.9 slice.131
  119.8 1.0 slice_add_fusion.4
  120.8 1.2 collective-permute-start.20
  122.0 1.5 %collective-permute-start.21 = (f32[2,5,1536]{2,1,0:T(8,128)S(1)}, f32[2,5,1536]{2,1,0:T(8,128)S(1)}, u32[]{:S(2)}, u32[]{:S(2)}) collective-permute-start(f32[2,5,1536]{2,1,0:T(8,128)S(1)} %get-tuple-element.107), channel_id=1, source_target_pairs={{0,2},{1,3},{2,0},{3,1},{4,6},{5,7},{6,4},{7,5},{8,10},{9,11},{10,... | collective-permute-start | bytes 184328 | tf_op jit(solution)/shard_map/ppermute | solution.py:19
  123.7 4.3 %combine.2.rest_0_ = bf16[256,2,1536]{2,1,0:T(2,128)(2,1)} custom-call(s32[1]{0:T(128)} %bitcast.pos_ref, s32[3,1]{1,0:T(4,128)S(1)} %copy.15.sent_ref, f32[2,256,768]{2,1,0:T(8,128)S(1)} %copy-done.15, bf16[2,128,768]{2,1,0:T(8,128)(2,1)} %collective-permute-done.11.dir_ref, bf16[2,128,768]{2,1,0:T(8,128)(2,1)} %collective-permute-done.12.dia_ref, ...), custom_call_target="tpu_custom_call" | custom-call | flops 12582912000 | bytes 3538944 | tf_op jit(solution)/shard_map/combine/pallas_call | solution.py:215
  128.4 2.1 %collective-permute-done.22 = f32[2,5,1536]{2,1,0:T(8,128)S(1)} collective-permute-done((f32[2,5,1536]{2,1,0:T(8,128)S(1)}, f32[2,5,1536]{2,1,0:T(8,128)S(1)}, u32[]{:S(2)}, u32[]{:S(2)}) %collective-permute-start.22) | collective-permute-done | bytes 61472 | tf_op jit(solution)/shard_map/ppermute | solution.py:19
  130.6 0.6 copy.16
  131.8 3.3 %combine.3 = bf16[256,2,1536]{2,1,0:T(2,128)(2,1)} custom-call(s32[1]{0:T(128)} %bitcast.pos_ref, s32[3,1]{1,0:T(4,128)S(1)} %copy.15.sent_ref, f32[2,256,768]{2,1,0:T(8,128)S(1)} %copy-done, bf16[2,128,768]{2,1,0:T(8,128)(2,1)S(1)} %collective-permute-done.14.dir_ref, ...), custom_call_target="tpu_custom_call", output_to_operand_aliasing={{}: (6, {})} | custom-call | bytes 3538944 | tf_op jit(solution)/shard_map/combine/pallas_call | solution.py:215
  (79 shorter events, 3.0 us)
Async XLA Ops:
  0.6 14.3 %collective-permute-start.3 = (bf16[4,2,1536]{2,1,0:T(2,128)(2,1)}, bf16[4,2,1536]{2,1,0:T(2,128)(2,1)S(1)}, u32[]{:S(2)}, u32[]{:S(2)}) collective-permute-start(bf16[4,2,1536]{2,1,0:T(2,128)(2,1)} %param.11), channel_id=1, source_target_pairs={{0,1},{1,0},{2,3},{3,2},{4,5},{5,4},{6,7},{7,6},{8,9},{9,8},{10,11... | collective-permute-start | bytes 73736 | tf_op jit(solution)/shard_map/ppermute | solution.py:19
  1.4 14.4 %collective-permute-start.4 = (bf16[4,2,1536]{2,1,0:T(2,128)(2,1)}, bf16[4,2,1536]{2,1,0:T(2,128)(2,1)S(1)}, u32[]{:S(2)}, u32[]{:S(2)}) collective-permute-start(bf16[4,2,1536]{2,1,0:T(2,128)(2,1)} %param.11), channel_id=1, source_target_pairs={{0,2},{1,3},{2,0},{3,1},{4,6},{5,7},{6,4},{7,5},{8,10},{9,11},{10,... | collective-permute-start | bytes 73736 | tf_op jit(solution)/shard_map/ppermute | solution.py:19
  2.6 13.2 %collective-permute-start.5 = (bf16[4,2,1536]{2,1,0:T(2,128)(2,1)}, bf16[4,2,1536]{2,1,0:T(2,128)(2,1)S(1)}, u32[]{:S(2)}, u32[]{:S(2)}) collective-permute-start(bf16[4,2,1536]{2,1,0:T(2,128)(2,1)} %param.11), channel_id=1, source_target_pairs={{0,3},{1,2},{2,1},{3,0},{4,7},{5,6},{6,5},{7,4},{8,11},{9,10},{10,... | collective-permute-start | bytes 73736 | tf_op jit(solution)/shard_map/ppermute | solution.py:19
  7.0 7.4 %copy-start.18 = (bf16[256,2,1536]{2,1,0:T(2,128)(2,1)S(1)}, bf16[256,2,1536]{2,1,0:T(2,128)(2,1)}, u32[]{:S(2)}) copy-start(bf16[256,2,1536]{2,1,0:T(2,128)(2,1)} %a_ref.1) | copy-start | bytes 4718596
  10.5 5.3 %copy-start.20 = (bf16[4,2,1536]{2,1,0:T(2,128)(2,1)S(1)}, bf16[4,2,1536]{2,1,0:T(2,128)(2,1)}, u32[]{:S(2)}) copy-start(bf16[4,2,1536]{2,1,0:T(2,128)(2,1)} %param.11) | copy-start | bytes 73732
  10.5 31.8 %collective-permute-start.1 = (bf16[128,2,768]{2,1,0:T(2,128)(2,1)S(1)}, bf16[128,2,768]{2,1,0:T(2,128)(2,1)S(1)}, u32[]{:S(2)}, u32[]{:S(2)}) collective-permute-start(bf16[128,2,768]{2,1,0:T(2,128)(2,1)S(1)} %get-tuple-element.98), channel_id=1, source_target_pairs={{0,2},{2,0},{4,6},{6,4},{8,10},{10,8},{12,14},{14,12},{1,3},{3,1},... | collective-permute-start | bytes 1179656 | tf_op jit(solution)/shard_map/ppermute | solution.py:32
  11.7 30.6 %collective-permute-start.2 = (bf16[128,2,768]{2,1,0:T(2,128)(2,1)S(1)}, bf16[128,2,768]{2,1,0:T(2,128)(2,1)S(1)}, u32[]{:S(2)}, u32[]{:S(2)}) collective-permute-start(bf16[128,2,768]{2,1,0:T(2,128)(2,1)S(1)} %get-tuple-element.97), channel_id=1, source_target_pairs={{2,4},{4,2},{6,8},{8,6},{10,12},{12,10},{3,5},{5,3},{7,9},{9,7},{1... | collective-permute-start | bytes 1179656 | tf_op jit(solution)/shard_map/ppermute | solution.py:32
  15.0 19.2 %collective-permute-start = (bf16[128,2,1536]{2,1,0:T(2,128)(2,1)S(1)}, bf16[128,2,1536]{2,1,0:T(2,128)(2,1)S(1)}, u32[]{:S(2)}, u32[]{:S(2)}) collective-permute-start(bf16[128,2,1536]{2,1,0:T(2,128)(2,1)S(1)} %constant_dynamic-slice_fusion.4), channel_id=1, source_target_pairs={{0,1},{1,0},{2,3},{3,2},{4,5},{5,4},{6,7},{7,6},{8,9},{9,8},{10,11... | collective-permute-start | bytes 2359304 | tf_op jit(solution)/shard_map/ppermute | solution.py:19
  15.9 10.0 %collective-permute-start.8 = (bf16[16,2,1536]{2,1,0:T(2,128)(2,1)S(1)}, bf16[16,2,1536]{2,1,0:T(2,128)(2,1)S(1)}, u32[]{:S(2)}, u32[]{:S(2)}) collective-permute-start(bf16[16,2,1536]{2,1,0:T(2,128)(2,1)S(1)} %pad_maximum_fusion.3), channel_id=1, source_target_pairs={{0,4},{1,5},{2,6},{3,7},{4,0},{5,1},{6,2},{7,3},{8,12},{9,13},{10,... | collective-permute-start | bytes 294920 | tf_op jit(solution)/shard_map/ppermute | solution.py:19
  17.4 8.7 %collective-permute-start.9 = (bf16[16,2,1536]{2,1,0:T(2,128)(2,1)S(1)}, bf16[16,2,1536]{2,1,0:T(2,128)(2,1)S(1)}, u32[]{:S(2)}, u32[]{:S(2)}) collective-permute-start(bf16[16,2,1536]{2,1,0:T(2,128)(2,1)S(1)} %pad_maximum_fusion.3), channel_id=1, source_target_pairs={{0,8},{1,9},{2,10},{3,11},{4,12},{5,13},{6,14},{7,15},{8,0},{9,1},... | collective-permute-start | bytes 294920 | tf_op jit(solution)/shard_map/ppermute | solution.py:19
  26.0 4.5 %collective-permute-start.10 = (bf16[16,2,1536]{2,1,0:T(2,128)(2,1)S(1)}, bf16[16,2,1536]{2,1,0:T(2,128)(2,1)S(1)}, u32[]{:S(2)}, u32[]{:S(2)}) collective-permute-start(bf16[16,2,1536]{2,1,0:T(2,128)(2,1)S(1)} %pad_maximum_fusion.3), channel_id=1, source_target_pairs={{0,12},{1,13},{2,14},{3,15},{4,8},{5,9},{6,10},{7,11},{8,4},{9,5},... | collective-permute-start | bytes 294920 | tf_op jit(solution)/shard_map/ppermute | solution.py:19
  26.1 43.7 %collective-permute-start.6 = (bf16[128,2,768]{2,1,0:T(2,128)(2,1)}, bf16[128,2,768]{2,1,0:T(2,128)(2,1)}, u32[]{:S(2)}, u32[]{:S(2)}) collective-permute-start(bf16[128,2,768]{2,1,0:T(2,128)(2,1)} %get-tuple-element.58), channel_id=1, source_target_pairs={{0,2},{2,0},{4,6},{6,4},{8,10},{10,8},{12,14},{14,12},{1,3},{3,1},... | collective-permute-start | bytes 1179656 | tf_op jit(solution)/shard_map/ppermute | solution.py:32
  30.5 39.3 %collective-permute-start.7 = (bf16[128,2,768]{2,1,0:T(2,128)(2,1)}, bf16[128,2,768]{2,1,0:T(2,128)(2,1)}, u32[]{:S(2)}, u32[]{:S(2)}) collective-permute-start(bf16[128,2,768]{2,1,0:T(2,128)(2,1)} %get-tuple-element.59), channel_id=1, source_target_pairs={{2,4},{4,2},{6,8},{8,6},{10,12},{12,10},{3,5},{5,3},{7,9},{9,7},{1... | collective-permute-start | bytes 1179656 | tf_op jit(solution)/shard_map/ppermute | solution.py:32
  33.4 0.8 copy-start.4
  34.2 0.9 copy-start.19
  42.3 0.7 copy-start.22
  42.3 0.9 copy-start.23
  43.1 5.2 %copy-start.1 = (bf16[384,1536]{1,0:T(8,128)(2,1)S(1)}, bf16[384,1536]{1,0:T(8,128)(2,1)}, u32[]{:S(2)}) copy-start(bf16[384,1536]{1,0:T(8,128)(2,1)} %get-tuple-element.56.k1_ref) | copy-start | bytes 3538948
  43.1 5.2 %copy-start.2 = (bf16[256,1536]{1,0:T(8,128)(2,1)S(1)}, bf16[256,1536]{1,0:T(8,128)(2,1)}, u32[]{:S(2)}) copy-start(bf16[256,1536]{1,0:T(8,128)(2,1)} %q_ref.3) | copy-start | bytes 2359300
  43.1 5.2 %copy-start.3 = (bf16[256,1536]{1,0:T(8,128)(2,1)S(1)}, bf16[256,1536]{1,0:T(8,128)(2,1)}, u32[]{:S(2)}) copy-start(bf16[256,1536]{1,0:T(8,128)(2,1)} %g_ref.3) | copy-start | bytes 2359300
  43.1 5.2 %copy-start.9 = (s32[1,2,5]{2,1,0:T(2,128)S(1)}, s32[1,2,5]{2,1,0:T(2,128)}, u32[]{:S(2)}) copy-start(s32[1,2,5]{2,1,0:T(2,128)} %param.15) | copy-start | bytes 124
  43.1 5.3 %copy-start.10 = (f32[12]{0:T(128)S(1)}, f32[12]{0:T(128)}, u32[]{:S(2)}) copy-start(f32[12]{0:T(128)} %warm_ref.3) | copy-start | bytes 148
  48.4 1.0 copy-start.5
  49.4 1.0 copy-start.16
  50.4 1.0 copy-start.17
  60.3 26.9 %collective-permute-start.11 = (bf16[2,128,768]{2,1,0:T(8,128)(2,1)}, bf16[2,128,768]{2,1,0:T(8,128)(2,1)}, u32[]{:S(2)}, u32[]{:S(2)}) collective-permute-start(bf16[2,128,768]{2,1,0:T(8,128)(2,1)} %get-tuple-element.75), channel_id=1, source_target_pairs={{0,2},{2,0},{4,6},{6,4},{8,10},{10,8},{12,14},{14,12},{1,3},{3,1},... | collective-permute-start | bytes 1179656 | tf_op jit(solution)/shard_map/ppermute | solution.py:32
  61.5 25.6 %collective-permute-start.12 = (bf16[2,128,768]{2,1,0:T(8,128)(2,1)}, bf16[2,128,768]{2,1,0:T(8,128)(2,1)}, u32[]{:S(2)}, u32[]{:S(2)}) collective-permute-start(bf16[2,128,768]{2,1,0:T(8,128)(2,1)} %get-tuple-element.76), channel_id=1, source_target_pairs={{2,4},{4,2},{6,8},{8,6},{10,12},{12,10},{3,5},{5,3},{7,9},{9,7},{1... | collective-permute-start | bytes 1179656 | tf_op jit(solution)/shard_map/ppermute | solution.py:32
  66.8 20.4 %collective-permute-start.13 = (bf16[2,128,768]{2,1,0:T(8,128)(2,1)}, bf16[2,128,768]{2,1,0:T(8,128)(2,1)}, u32[]{:S(2)}, u32[]{:S(2)}) collective-permute-start(bf16[2,128,768]{2,1,0:T(8,128)(2,1)} %get-tuple-element.77), channel_id=1, source_target_pairs={{0,1},{1,0},{2,3},{3,2},{4,5},{5,4},{6,7},{7,6},{8,9},{9,8},{10,11... | collective-permute-start | bytes 1179656 | tf_op jit(solution)/shard_map/ppermute | solution.py:19
  74.8 1.0 copy-start.6
  75.8 1.0 copy-start.7
  76.8 1.0 copy-start.8
  86.9 3.8 %copy-start.11 = (bf16[2,128,768]{2,1,0:T(8,128)(2,1)}, bf16[2,128,768]{2,1,0:T(8,128)(2,1)S(1)}, u32[]{:S(2)}) copy-start(bf16[2,128,768]{2,1,0:T(8,128)(2,1)S(1)} %get-tuple-element.80) | copy-start | bytes 1179652
  86.9 3.8 %copy-start.13 = (bf16[2,128,768]{2,1,0:T(8,128)(2,1)}, bf16[2,128,768]{2,1,0:T(8,128)(2,1)S(1)}, u32[]{:S(2)}) copy-start(bf16[2,128,768]{2,1,0:T(8,128)(2,1)S(1)} %get-tuple-element.79) | copy-start | bytes 1179652
  86.9 3.8 %copy-start.14 = (bf16[2,128,768]{2,1,0:T(8,128)(2,1)}, bf16[2,128,768]{2,1,0:T(8,128)(2,1)S(1)}, u32[]{:S(2)}) copy-start(bf16[2,128,768]{2,1,0:T(8,128)(2,1)S(1)} %get-tuple-element.78) | copy-start | bytes 1179652
  86.9 3.8 %copy-start.21 = (s32[1,3,1]{1,2,0:T(1,128)S(1)}, s32[1,3,1]{1,2,0:T(1,128)}, u32[]{:S(2)}) copy-start(s32[1,3,1]{1,2,0:T(1,128)} %param.14) | copy-start | bytes 40
  87.2 36.5 %copy-start.15 = (f32[2,256,768]{2,1,0:T(8,128)S(1)}, f32[2,256,768]{2,1,0:T(8,128)}, u32[]{:S(2)}) copy-start(f32[2,256,768]{2,1,0:T(8,128)} %get-tuple-element.84.own_ref) | copy-start | bytes 4718596
  88.1 10.6 %collective-permute-start.17 = (f32[2,17,1536]{2,1,0:T(8,128)}, f32[2,17,1536]{2,1,0:T(8,128)}, u32[]{:S(2)}, u32[]{:S(2)}) collective-permute-start(f32[2,17,1536]{2,1,0:T(8,128)} %get-tuple-element.110), channel_id=1, source_target_pairs={{0,4},{1,5},{2,6},{3,7},{4,0},{5,1},{6,2},{7,3},{8,12},{9,13},{10,... | collective-permute-start | bytes 626696 | tf_op jit(solution)/shard_map/ppermute | solution.py:19
  88.6 12.9 %collective-permute-start.18 = (f32[2,17,1536]{2,1,0:T(8,128)}, f32[2,17,1536]{2,1,0:T(8,128)}, u32[]{:S(2)}, u32[]{:S(2)}) collective-permute-start(f32[2,17,1536]{2,1,0:T(8,128)} %get-tuple-element.109), channel_id=1, source_target_pairs={{0,8},{1,9},{2,10},{3,11},{4,12},{5,13},{6,14},{7,15},{8,0},{9,1},... | collective-permute-start | bytes 626696 | tf_op jit(solution)/shard_map/ppermute | solution.py:19
  88.6 28.2 %collective-permute-start.19 = (f32[2,17,1536]{2,1,0:T(8,128)S(1)}, f32[2,17,1536]{2,1,0:T(8,128)}, u32[]{:S(2)}, u32[]{:S(2)}) collective-permute-start(f32[2,17,1536]{2,1,0:T(8,128)S(1)} %get-tuple-element.111), channel_id=1, source_target_pairs={{0,12},{1,13},{2,14},{3,15},{4,8},{5,9},{6,10},{7,11},{8,4},{9,5},... | collective-permute-start | bytes 626696 | tf_op jit(solution)/shard_map/ppermute | solution.py:19
  90.8 41.0 %collective-permute-start.14 = (bf16[2,128,768]{2,1,0:T(8,128)(2,1)}, bf16[2,128,768]{2,1,0:T(8,128)(2,1)S(1)}, u32[]{:S(2)}, u32[]{:S(2)}) collective-permute-start(bf16[2,128,768]{2,1,0:T(8,128)(2,1)} %copy-done.14), channel_id=1, source_target_pairs={{0,2},{2,0},{4,6},{6,4},{8,10},{10,8},{12,14},{14,12},{1,3},{3,1},... | collective-permute-start | bytes 1179656 | tf_op jit(solution)/shard_map/ppermute | solution.py:32
  91.5 40.3 %collective-permute-start.15 = (bf16[2,128,768]{2,1,0:T(8,128)(2,1)}, bf16[2,128,768]{2,1,0:T(8,128)(2,1)S(1)}, u32[]{:S(2)}, u32[]{:S(2)}) collective-permute-start(bf16[2,128,768]{2,1,0:T(8,128)(2,1)} %copy-done.13), channel_id=1, source_target_pairs={{2,4},{4,2},{6,8},{8,6},{10,12},{12,10},{3,5},{5,3},{7,9},{9,7},{1... | collective-permute-start | bytes 1179656 | tf_op jit(solution)/shard_map/ppermute | solution.py:32
  120.8 7.2 %collective-permute-start.20 = (f32[2,5,1536]{2,1,0:T(8,128)S(1)}, f32[2,5,1536]{2,1,0:T(8,128)S(1)}, u32[]{:S(2)}, u32[]{:S(2)}) collective-permute-start(f32[2,5,1536]{2,1,0:T(8,128)S(1)} %get-tuple-element.108), channel_id=1, source_target_pairs={{0,1},{1,0},{2,3},{3,2},{4,5},{5,4},{6,7},{7,6},{8,9},{9,8},{10,11... | collective-permute-start | bytes 184328 | tf_op jit(solution)/shard_map/ppermute | solution.py:19
  122.0 6.4 %collective-permute-start.21 = (f32[2,5,1536]{2,1,0:T(8,128)S(1)}, f32[2,5,1536]{2,1,0:T(8,128)S(1)}, u32[]{:S(2)}, u32[]{:S(2)}) collective-permute-start(f32[2,5,1536]{2,1,0:T(8,128)S(1)} %get-tuple-element.107), channel_id=1, source_target_pairs={{0,2},{1,3},{2,0},{3,1},{4,6},{5,7},{6,4},{7,5},{8,10},{9,11},{10,... | collective-permute-start | bytes 184328 | tf_op jit(solution)/shard_map/ppermute | solution.py:19
  123.5 7.0 %collective-permute-start.22 = (f32[2,5,1536]{2,1,0:T(8,128)S(1)}, f32[2,5,1536]{2,1,0:T(8,128)S(1)}, u32[]{:S(2)}, u32[]{:S(2)}) collective-permute-start(f32[2,5,1536]{2,1,0:T(8,128)S(1)} %get-tuple-element.106), channel_id=1, source_target_pairs={{0,3},{1,2},{2,1},{3,0},{4,7},{5,6},{6,5},{7,4},{8,11},{9,10},{10,... | collective-permute-start | bytes 184328 | tf_op jit(solution)/shard_map/ppermute | solution.py:19
  123.7 4.3 %copy-start.12 = (bf16[2,128,768]{2,1,0:T(8,128)(2,1)S(1)}, bf16[2,128,768]{2,1,0:T(8,128)(2,1)}, u32[]{:S(2)}) copy-start(bf16[2,128,768]{2,1,0:T(8,128)(2,1)} %copy-done.11) | copy-start | bytes 1179652
  123.7 8.1 %copy-start = (f32[2,256,768]{2,1,0:T(8,128)S(1)}, f32[2,256,768]{2,1,0:T(8,128)}, u32[]{:S(2)}) copy-start(f32[2,256,768]{2,1,0:T(8,128)} %get-tuple-element.70.own_ref) | copy-start | bytes 4718596
  128.0 3.8 %collective-permute-start.16 = (bf16[2,128,768]{2,1,0:T(8,128)(2,1)S(1)}, bf16[2,128,768]{2,1,0:T(8,128)(2,1)S(1)}, u32[]{:S(2)}, u32[]{:S(2)}) collective-permute-start(bf16[2,128,768]{2,1,0:T(8,128)(2,1)S(1)} %copy-done.12), channel_id=1, source_target_pairs={{0,1},{1,0},{2,3},{3,2},{4,5},{5,4},{6,7},{7,6},{8,9},{9,8},{10,11... | collective-permute-start | bytes 1179656 | tf_op jit(solution)/shard_map/ppermute | solution.py:19

commit v3 on v2

v3 whole, which is shorter than its diff:
```python
import functools
import math

import jax
import jax.numpy as jnp
from jax import lax
from jax.experimental import pallas as pl
from jax.experimental.pallas import tpu as pltpu
from jax.sharding import PartitionSpec as P

BLOCK = 128
F32 = jnp.float32
BF16 = jnp.bfloat16
SMEM = pltpu.MemorySpace.SMEM
COMBINE_STEPS = (3, 2, 1)
LANES = 128
HOLD = 20_000_000_000


def swap_mask(x, mask):
    count = lax.axis_size(("gx", "gy"))
    return lax.ppermute(x, ("gx", "gy"), [(i, i ^ mask) for i in range(count)])


def levels(count):
    bits = count.bit_length() - 1
    out = [[2]] if bits > 1 else []
    at = 2
    while at < bits:
        take = min(2, bits - at)
        out.append([m << at for m in range(1, 1 << take)])
        at += take
    return out + [[1]]


def swap_pairs(x, first):
    count = lax.axis_size("gx")
    route = []
    for low in range(first, count - 1, 2):
        route += [(low, low + 1), (low + 1, low)]
    return lax.ppermute(x, "gx", route)


def split_heads(total):
    first = (total + 1) // 2
    return [n for n in (first, total - first) if n > 0]


def pick_kernel(pos_ref, sent_ref, kv_ref, *rest, copies):
    sems = rest[-1]
    outs = rest[:-1]
    odd = lax.rem(pos_ref[0], 2)
    spots = {
        "direct": jnp.where(odd == 1, sent_ref[0, 0], sent_ref[1, 0]),
        "diagonal": jnp.where(odd == 1, sent_ref[1, 0], sent_ref[0, 0]),
        "partner": sent_ref[2, 0],
        "own": 0,
    }
    started = []
    for out, (which, head0, heads) in zip(outs, copies):
        rows, width = out.shape[1], out.shape[3]
        for h in range(heads):
            lanes = slice((head0 + h) * width, (head0 + h + 1) * width)
            source = kv_ref.at[pl.ds(spots[which] * BLOCK, rows), :, lanes]
            copy = pltpu.make_async_copy(source, out.at[h], sems.at[len(started)])
            copy.start()
            started.append(copy)
    for copy in started:
        copy.wait()


def pick(pos, sent, mesh_kv, width, copies):
    rows = [mesh_kv.shape[0] if which == "own" else BLOCK for which, _, _ in copies]
    smem = pl.BlockSpec(memory_space=SMEM)
    anywhere = pl.BlockSpec(memory_space=pl.ANY)
    out = pl.pallas_call(
        functools.partial(pick_kernel, copies=copies),
        in_specs=[smem, smem, anywhere],
        out_specs=[anywhere] * len(copies),
        out_shape=[
            jax.ShapeDtypeStruct((heads, n, 2, width), BF16) for n, (_, _, heads) in zip(rows, copies)
        ],
        scratch_shapes=[pltpu.SemaphoreType.DMA((sum(heads for _, _, heads in copies),))],
        cost_estimate=pl.CostEstimate(flops=0, transcendentals=0, bytes_accessed=1 << 20),
        name="pick",
    )(pos, sent, mesh_kv)
    return [x.reshape(x.shape[0], 2 * x.shape[1], width) for x in out]


def hold_kernel(*refs):
    pass


def hold(arrays, flops):
    anywhere = pl.BlockSpec(memory_space=pl.ANY)
    return pl.pallas_call(
        hold_kernel,
        in_specs=[anywhere] * len(arrays),
        out_specs=[anywhere] * len(arrays),
        out_shape=[jax.ShapeDtypeStruct(x.shape, x.dtype) for x in arrays],
        input_output_aliases={i: i for i in range(len(arrays))},
        compiler_params=pltpu.CompilerParams(vmem_limit_bytes=1 << 20),
        cost_estimate=pl.CostEstimate(flops=flops, transcendentals=0, bytes_accessed=0),
        name="hold",
    )(*arrays)


def send_back(faces):
    direct, diagonal, partner = faces
    return [swap_pairs(direct, 0), swap_pairs(diagonal, 1), swap_mask(partner, 1)]


def attention_kernel(
    pos_ref, filt_ref, warm_ref, q_ref, g_ref, own_ref, par_ref, dir_ref, dia_ref, anc_ref, *rest,
    gx_count, head0, width,
):
    (dq_ref, own_out, dir_out, dia_out, par_out, anc_out, temp_out, pair_ref) = rest[-8:]
    head = pl.program_id(0)
    gx = pos_ref[0]
    odd = lax.rem(gx, 2)
    queries = q_ref.shape[0]
    own_rows = own_ref.shape[0] // 2
    blocks = own_rows // BLOCK
    near = own_rows + 3 * BLOCK
    keys = near + anc_ref.shape[0] // 2

    row = 0
    for ref in (own_ref, par_ref, dir_ref, dia_ref, anc_ref):
        pair_ref[row : row + ref.shape[0], :] = ref[...].astype(F32)
        row += ref.shape[0]
    k = pair_ref[pl.ds(0, keys, stride=2), :].astype(BF16)
    v = pair_ref[pl.ds(1, keys, stride=2), :].astype(BF16)

    q = q_ref[...]
    g = g_ref[...]
    nt = (((1,), (1,)), ((), ()))
    s = lax.dot_general(k, q, nt, preferred_element_type=F32)
    dp = lax.dot_general(v, g, nt, preferred_element_type=F32)

    mult = warm_ref[head0 + head] / math.sqrt(width)
    lane = lax.broadcasted_iota(jnp.int32, (1, queries), 1) // BLOCK
    direct_col = blocks + 1 - odd
    diagonal_col = blocks + odd
    diagonal_there = jnp.where(odd == 1, gx < gx_count - 1, gx > 0)
    parts = []
    for b in range(blocks + 3):
        bias = jnp.zeros((1, queries), F32)
        for a in range(blocks):
            if b == a:
                continue
            col = (b if b < blocks else (blocks + 2, direct_col, diagonal_col)[b - blocks])
            ok = filt_ref[a, col] > 0
            if b == blocks + 2:
                ok = jnp.logical_and(ok, diagonal_there)
            bias = jnp.where(lane == a, jnp.where(ok, 0.0, -jnp.inf).astype(F32), bias)
        parts.append(s[b * BLOCK : (b + 1) * BLOCK] * mult + bias)
    parts.append(s[near:] * mult)
    scores = jnp.concatenate(parts, axis=0)
    top = jnp.max(scores, axis=0, keepdims=True)
    e = jnp.exp(scores - top)
    inv = 1.0 / jnp.sum(e, axis=0, keepdims=True)
    p = e * inv
    pb = p.astype(BF16)
    delta = jnp.sum(pb.astype(F32) * dp, axis=0, keepdims=True)
    ds = p * (dp - delta)
    temp_out[0] = jnp.sum(ds * s, axis=0, keepdims=True)
    dsb = (ds * mult).astype(BF16)
    nn = (((1,), (0,)), ((), ()))
    dv = lax.dot_general(pb, g, nn, preferred_element_type=F32)
    dk = lax.dot_general(dsb, q, nn, preferred_element_type=F32)
    dq = lax.dot_general(dsb, k, (((0,), (0,)), ((), ())), preferred_element_type=F32)
    dq_ref[...] = dq.astype(BF16)
    pair_ref[pl.ds(0, keys, stride=2), :] = dk
    pair_ref[pl.ds(1, keys, stride=2), :] = dv
    own_out[...] = pair_ref[: 2 * own_rows, :]
    for i, ref in enumerate((par_out, dir_out, dia_out)):
        at = 2 * (own_rows + i * BLOCK)
        ref[...] = pair_ref[at : at + 2 * BLOCK, :].astype(BF16)
    anc_out[...] = pair_ref[2 * near :, :]


def attention(pos, filt, warm, q, g, own_kv, partner, halo, anchors, head0, heads, dq_prev, anc_prev):
    rows, feat = q.shape
    total, own_rows, width = own_kv.shape
    own_rows //= 2
    a_rows = anchors.shape[0] // 2
    keys = own_rows + 3 * BLOCK + a_rows
    smem = pl.BlockSpec(memory_space=SMEM)
    full = lambda n: pl.BlockSpec((None, 2 * n, width), lambda h: (head0 + h, 0, 0))
    part = pl.BlockSpec((None, 2 * BLOCK, width), lambda h: (h, 0, 0))
    cols = pl.BlockSpec((rows, width), lambda h: (0, head0 + h))
    in_specs = [smem, smem, smem, cols, cols, full(own_rows), full(BLOCK), part, part]
    in_specs += [pl.BlockSpec((2 * a_rows, width), lambda h: (0, head0 + h))]
    args = [pos, filt, warm, q, g, own_kv, partner, *halo, anchors]
    alias = {}
    if dq_prev is not None:
        in_specs += [pl.BlockSpec(memory_space=pl.ANY)] * 2
        args += [dq_prev, anc_prev]
        alias = {10: 0, 11: 5}
    face = jax.ShapeDtypeStruct((heads, 2 * BLOCK, width), BF16)
    return pl.pallas_call(
        functools.partial(attention_kernel, gx_count=lax.axis_size("gx"), head0=head0, width=width),
        grid=(heads,),
        in_specs=in_specs,
        out_specs=[
            cols,
            pl.BlockSpec((None, 2 * own_rows, width), lambda h: (h, 0, 0)),
            part,
            part,
            part,
            pl.BlockSpec((2 * a_rows, width), lambda h: (0, head0 + h)),
            pl.BlockSpec((1, 1, rows), lambda h: (h, 0, 0)),
        ],
        out_shape=[
            jax.ShapeDtypeStruct(q.shape, BF16),
            jax.ShapeDtypeStruct((heads, 2 * own_rows, width), F32),
            face,
            face,
            face,
            jax.ShapeDtypeStruct((2 * a_rows, feat), F32),
            jax.ShapeDtypeStruct((heads, 1, rows), F32),
        ],
        scratch_shapes=[pltpu.VMEM((2 * keys, width), F32)],
        input_output_aliases=alias,
        compiler_params=pltpu.CompilerParams(vmem_limit_bytes=24 << 20),
        cost_estimate=pl.CostEstimate(
            flops=10 * heads * rows * keys * width,
            transcendentals=heads * rows * keys,
            bytes_accessed=heads * width * (rows * 6 + own_rows * 12 + 3 * BLOCK * 8 + a_rows * 12),
        ),
        name="attention",
    )(*args)


def combine_kernel(pos_ref, sent_ref, own_ref, dir_ref, dia_ref, par_ref, *rest):
    out_ref = rest[-1]
    odd = lax.rem(pos_ref[0], 2)
    blocks = out_ref.shape[0] // BLOCK
    spots = (
        jnp.where(odd == 1, sent_ref[0, 0], sent_ref[1, 0]),
        jnp.where(odd == 1, sent_ref[1, 0], sent_ref[0, 0]),
        sent_ref[2, 0],
    )
    width = own_ref.shape[2]
    for h in range(own_ref.shape[0]):
        lanes = slice(h * width, (h + 1) * width)
        back = [ref[h].astype(F32) for ref in (dir_ref, dia_ref, par_ref)]
        for a in range(blocks):
            total = own_ref[h, 2 * a * BLOCK : 2 * (a + 1) * BLOCK, :]
            for spot, face in zip(spots, back):
                total = total + jnp.where(spot == a, 1.0, 0.0).astype(F32) * face
            out_ref[a * BLOCK : (a + 1) * BLOCK, :, lanes] = total.astype(BF16).reshape(BLOCK, 2, width)


def combine(pos, sent, own, faces, head0, heads, feat, width, prev, weight=1):
    rows = own.shape[1] // 2
    step = next(n for n in COMBINE_STEPS if heads % n == 0 and head0 % n == 0)
    smem = pl.BlockSpec(memory_space=SMEM)
    face = pl.BlockSpec((step, 2 * BLOCK, width), lambda h: (h, 0, 0))
    own_spec = pl.BlockSpec((step, 2 * rows, width), lambda h: (h, 0, 0))
    in_specs = [smem, smem, own_spec, face, face, face]
    args = [pos, sent, own, *faces]
    alias = {}
    if prev is not None:
        in_specs.append(pl.BlockSpec(memory_space=pl.ANY))
        args.append(prev)
        alias = {6: 0}
    return pl.pallas_call(
        combine_kernel,
        grid=(heads // step,),
        in_specs=in_specs,
        out_specs=pl.BlockSpec((rows, 2, step * width), lambda h: (0, 0, head0 // step + h)),
        out_shape=jax.ShapeDtypeStruct((rows, 2, feat), BF16),
        input_output_aliases=alias,
        compiler_params=pltpu.CompilerParams(vmem_limit_bytes=24 << 20),
        cost_estimate=pl.CostEstimate(
            flops=weight * heads * width * rows * 16,
            transcendentals=0,
            bytes_accessed=heads * width * (rows * 12 + 3 * BLOCK * 4),
        ),
        name="combine",
    )(*args)


def local(q, mesh_kv, landmark, warm, g, exported, filt):
    rows, feat = q.shape
    total = warm.shape[0]
    width = feat // total
    gx_count = lax.axis_size("gx")
    stages = levels(lax.axis_size(("gx", "gy")))
    gx = lax.axis_index("gx")
    pos = jnp.full((1,), gx, jnp.int32)
    sent = exported[0]
    filt = filt[0]
    sizes = split_heads(total)
    chunks = [(sum(sizes[:i]), n) for i, n in enumerate(sizes)]

    picks = [pick(pos, sent, mesh_kv, width, [("direct", *chunks[0]), ("diagonal", *chunks[0])])]
    others = [(which, *chunk) for chunk in chunks[1:] for which in ("direct", "diagonal")]
    others = pick(pos, sent, mesh_kv, width, others + [("partner", 0, total), ("own", 0, total)])
    own_kv, partner = others.pop(), swap_mask(others.pop(), 1)
    picks += [others[2 * i : 2 * i + 2] for i in range(len(chunks) - 1)]
    anchors = landmark.reshape(2 * landmark.shape[0], feat)
    for i, masks in enumerate(stages):
        if i == 1:
            anchors, picks[1] = lax.optimization_barrier((anchors, picks[1]))
        anchors = jnp.concatenate([anchors] + [swap_mask(anchors, m) for m in masks], axis=0)
    halos = [[swap_pairs(d, 0), swap_pairs(g, 1)] for d, g in picks]
    halos[0] = hold(halos[0], HOLD)

    dq = anc = None
    temps, owns, faces, returned = [], [], [], []
    for (head0, heads), halo in zip(chunks, halos):
        dq, own, f_dir, f_dia, f_par, anc, temp = attention(
            pos, filt, warm, q, g, own_kv, partner, halo, anchors, head0, heads, dq, anc
        )
        temps.append(temp)
        owns.append(own)
        faces.append((f_dir, f_dia, f_par))
        if len(faces) < len(chunks):
            returned.append(send_back(faces[-1]))
    temp = jnp.sum(jnp.concatenate(temps, axis=0), axis=(1, 2)) / math.sqrt(width)
    extra = jnp.zeros((1, LANES), F32).at[0, :total].set(temp)
    cell = None
    for i, masks in enumerate(reversed(stages)):
        n = anc.shape[0] // (len(masks) + 1)
        wide = jnp.broadcast_to(extra, (n, LANES))
        got = [
            swap_mask(jnp.concatenate([anc[k * n : (k + 1) * n], wide], axis=1), m)
            for k, m in enumerate(masks, 1)
        ]
        if i == 0:
            returned[-1] = hold(returned[-1], HOLD)
            got, faces[-1], returned[-1] = lax.optimization_barrier((got, faces[-1], returned[-1]))
            returned.append(send_back(faces[-1]))
            for c in range(len(chunks) - 1):
                cell = combine(pos, sent, owns[c], returned[c], *chunks[c], feat, width, cell, weight=4000)
        if i == len(stages) - 1:
            got, cell = lax.optimization_barrier((got, cell))
        anc = sum([x[:, :feat] for x in got], anc[:n])
        extra = sum([x[:1, feat:] for x in got], extra)
    anchor_grad = anc.reshape(landmark.shape)
    temp = extra[0, :total]
    cell = combine(pos, sent, owns[-1], returned[-1], *chunks[-1], feat, width, cell, weight=0)
    return (dq, cell, anchor_grad, temp)


def solution(mesh):
    rows = ("groups", "gx", "gy")
    placed = (
        P(rows, None),
        P(rows, None, None),
        P(rows, None, None),
        P("groups"),
        P(rows, None),
        P(rows, None, None),
        P(rows, None, None),
    )
    return jax.shard_map(
        local,
        mesh=mesh,
        in_specs=placed,
        out_specs=(P(rows, None), P(rows, None, None), P(rows, None, None), P("groups")),
        check_vma=False,
    )
```

time: 136 us -> 208 us (1.53)
  the two profiles are of different devices: /device:TPU:21 before, /device:TPU:0 now
where the time goes in v3:
time: 208 us; the launch traced here: 207 us
  Pallas kernels  145 us (70%)
  starting transfers between devices  25.2 us (12%)
  waiting for transfers between devices  20.4 us (10%)
  local copies, waits for them, and re-layouts  11.2 us (5%)
  other arithmetic  4.53 us (2%)
    pallas_call x2, Pallas kernels, pick(): pl.pallas_call(functools.partial(pick_kernel, copies=copies), in_specs=[s...  123 us
    ppermute x13, starting transfers between devices, swap_mask(): return lax.ppermute(x, ('gx', 'gy'), [(i, i ^ mask) for i in range(count)])  17.7 us
    pallas_call x2, Pallas kernels, attention(): pl.pallas_call(functools.partial(attention_kernel, gx_count=lax.axis_size...  17.3 us
    ppermute x13, waiting for transfers between devices, swap_mask(): return lax.ppermute(x, ('gx', 'gy'), [(i, i ^ mask) for i in range(count)])  14.5 us
    ppermute x8, starting transfers between devices, swap_pairs(): return lax.ppermute(x, 'gx', route)  7.57 us
    unnamed x36, local copies, waits for them, and re-layouts  6.92 us
    ppermute x8, waiting for transfers between devices, swap_pairs(): return lax.ppermute(x, 'gx', route)  5.87 us
    pallas_call x2, Pallas kernels, combine(): pl.pallas_call(combine_kernel, grid=(heads // step,), in_specs=in_specs,...  4.39 us
  transfers between devices with their start and end apart: 21, of which 6 were waited for; matrix products, arithmetic and copies ran while one was open for 3% of the time, Pallas kernels for 69%

profile of v3, /device:TPU:0, one launch (start us, length us, event | category | flops | bytes accessed | tf_op | source)
XLA Modules:
  0.0 207.2 jit_solution(8153794017666793400)
XLA Ops:
  0.6 0.8 reshape.76
  1.4 3.0 %collective-permute-start.1 = (bf16[8,1536]{1,0:T(8,128)(2,1)S(1)}, bf16[8,1536]{1,0:T(8,128)(2,1)S(1)}, u32[]{:S(2)}, u32[]{:S(2)}) collective-permute-start(bf16[8,1536]{1,0:T(8,128)(2,1)S(1)} %reshape.76), channel_id=1, source_target_pairs={{0,2},{1,3},{2,0},{3,1},{4,6},{5,7},{6,4},{7,5},{8,10},{9,11},{10,... | collective-permute-start | bytes 73736 | tf_op jit(solution)/shard_map/ppermute | solution.py:22
  4.4 1.3 copy.19.sent_ref
  5.7 25.7 %pick.3 = (bf16[6,128,2,128]{3,2,1,0:T(2,128)(2,1)}, bf16[6,128,2,128]{3,2,1,0:T(2,128)(2,1)}) custom-call(s32[1]{0:T(128)} %bitcast.pos_ref, s32[3,1]{1,0:T(4,128)} %copy.19.sent_ref, bf16[256,2,1536]{2,1,0:T(2,128)(2,1)} %kv_ref.3), custom_call_target="tpu_custom_call" | custom-call | bytes 1048576 | tf_op jit(solution)/shard_map/pick/pallas_call | solution.py:76
  31.5 0.7 collective-permute-start.9
  32.2 97.4 %pick.2 = (bf16[6,128,2,128]{3,2,1,0:T(2,128)(2,1)}, bf16[6,128,2,128]{3,2,1,0:T(2,128)(2,1)}, bf16[12,128,2,128]{3,2,1,0:T(2,128)(2,1)}, bf16[12,256,2,128]{3,2,1,0:T(2,128)(2,1)}) custom-call(s32[1]{0:T(128)} %bitcast.pos_ref, s32[3,1]{1,0:T(4,128)} %copy.19.sent_ref, bf16[256,2,1536]{2,1,0:T(2,128)(2,1)} %kv_ref.3), custom_call_target="tpu_custom_call" | custom-call | bytes 1048576 | tf_op jit(solution)/shard_map/pick/pallas_call | solution.py:76
  129.6 0.6 compare_reduce_fusion
  130.3 4.7 %collective-permute-start.4 = (bf16[16,1536]{1,0:T(8,128)(2,1)S(1)}, bf16[16,1536]{1,0:T(8,128)(2,1)S(1)}, u32[]{:S(2)}, u32[]{:S(2)}) collective-permute-start(bf16[16,1536]{1,0:T(8,128)(2,1)S(1)} %pad_maximum_fusion.6), channel_id=1, source_target_pairs={{0,4},{1,5},{2,6},{3,7},{4,0},{5,1},{6,2},{7,3},{8,12},{9,13},{10,... | collective-permute-start | bytes 147464 | tf_op jit(solution)/shard_map/ppermute | solution.py:22
  135.0 2.6 %collective-permute-start.5 = (bf16[16,1536]{1,0:T(8,128)(2,1)S(1)}, bf16[16,1536]{1,0:T(8,128)(2,1)S(1)}, u32[]{:S(2)}, u32[]{:S(2)}) collective-permute-start(bf16[16,1536]{1,0:T(8,128)(2,1)S(1)} %pad_maximum_fusion.6), channel_id=1, source_target_pairs={{0,8},{1,9},{2,10},{3,11},{4,12},{5,13},{6,14},{7,15},{8,0},{9,1},... | collective-permute-start | bytes 147464 | tf_op jit(solution)/shard_map/ppermute | solution.py:22
  137.7 3.4 %collective-permute-done.5 = bf16[16,1536]{1,0:T(8,128)(2,1)S(1)} collective-permute-done((bf16[16,1536]{1,0:T(8,128)(2,1)S(1)}, bf16[16,1536]{1,0:T(8,128)(2,1)S(1)}, u32[]{:S(2)}, u32[]{:S(2)}) %collective-permute-start.5) | collective-permute-done | bytes 49184 | tf_op jit(solution)/shard_map/ppermute | solution.py:22
  141.1 1.5 collective-permute-start.2
  142.6 0.9 collective-permute-done.6
  143.6 1.4 collective-permute-done.7
  145.0 0.7 collective-permute-start.3
  145.8 1.3 copy-done
  147.1 0.2 copy-done.1
  147.3 0.2 copy-done.2
  147.6 8.6 %attention.2 = (bf16[256,1536]{1,0:T(8,128)(2,1)}, f32[6,512,128]{2,1,0:T(8,128)S(1)}, bf16[6,256,128]{2,1,0:T(8,128)(2,1)S(1)}, bf16[6,256,128]{2,1,0:T(8,128)(...) custom-call(s32[1]{0:T(128)} %bitcast.pos_ref, ...), custom_call_target="tpu_custom_call" | custom-call | flops 1384120320 | bytes 6488064 | tf_op jit(solution)/shard_map/attention/pallas_call | solution.py:201
  156.2 2.1 %collective-permute-start.11 = (bf16[6,256,128]{2,1,0:T(8,128)(2,1)S(1)}, bf16[6,256,128]{2,1,0:T(8,128)(2,1)S(1)}, u32[]{:S(2)}, u32[]{:S(2)}) collective-permute-start(bf16[6,256,128]{2,1,0:T(8,128)(2,1)S(1)} %get-tuple-element.74), channel_id=1, source_target_pairs={{0,2},{2,0},{4,6},{6,4},{8,10},{10,8},{12,14},{14,12},{1,3},{3,1},... | collective-permute-start | bytes 1179656 | tf_op jit(solution)/shard_map/ppermute | solution.py:41
  158.3 0.7 collective-permute-start.12
  159.1 8.7 %attention.3 = (bf16[256,1536]{1,0:T(8,128)(2,1)}, f32[6,512,128]{2,1,0:T(8,128)S(1)}, bf16[6,256,128]{2,1,0:T(8,128)(2,1)}, bf16[6,256,128]{2,1,0:T(8,128)(2,1)...) custom-call(s32[1]{0:T(128)} %bitcast.pos_ref, ...), custom_call_target="tpu_custom_call", output_to_operand_aliasing={{0}: (10, {}), {5}: (11, {})} | custom-call | flops 1384120320 | bytes 6488064 | tf_op jit(solution)/shard_map/attention/pallas_call | solution.py:201
  167.8 0.2 maximum_reduce_fusion
  168.0 0.6 fusion
  168.8 0.5 collective-permute-start.10
  169.3 5.8 %collective-permute-done.11.refs_0_ = bf16[6,256,128]{2,1,0:T(8,128)(2,1)S(1)} collective-permute-done((bf16[6,256,128]{2,1,0:T(8,128)(2,1)S(1)}, bf16[6,256,128]{2,1,0:T(8,128)(2,1)S(1)}, u32[]{:S(2)}, u32[]{:S(2)}) %collective-permute-start.11) | collective-permute-done | bytes 393248 | tf_op jit(solution)/shard_map/ppermute | solution.py:41
  175.2 0.7 copy-done.6
  175.9 0.8 copy-done.8
  176.7 0.7 slice_add_fusion.9
  177.5 0.1 add.36
  177.7 3.4 %collective-permute-start.17 = (f32[16,1664]{1,0:T(8,128)S(1)}, f32[16,1664]{1,0:T(8,128)S(1)}, u32[]{:S(2)}, u32[]{:S(2)}) collective-permute-start(f32[16,1664]{1,0:T(8,128)S(1)} %get-tuple-element.93), channel_id=1, source_target_pairs={{0,4},{1,5},{2,6},{3,7},{4,0},{5,1},{6,2},{7,3},{8,12},{9,13},{10,... | collective-permute-start | bytes 319496 | tf_op jit(solution)/shard_map/ppermute | solution.py:22
  181.1 0.9 collective-permute-start.18
  182.0 1.5 collective-permute-start.19
  183.5 1.1 collective-permute-start.14
  184.6 0.7 collective-permute-start.15
  185.4 5.5 %collective-permute-done.18 = f32[16,1664]{1,0:T(8,128)S(1)} collective-permute-done((f32[16,1664]{1,0:T(8,128)S(1)}, f32[16,1664]{1,0:T(8,128)S(1)}, u32[]{:S(2)}, u32[]{:S(2)}) %collective-permute-start.18) | collective-permute-done | bytes 106528 | tf_op jit(solution)/shard_map/ppermute | solution.py:22
  190.9 0.9 slice_add_fusion.1
  191.9 0.7 collective-permute-start.20
  192.6 1.0 copy-done.7
  193.6 1.0 copy-done.9
  194.6 1.0 copy-done.11
  195.6 2.2 %combine.2.rest_0_ = bf16[256,2,1536]{2,1,0:T(2,128)(2,1)} custom-call(s32[1]{0:T(128)} %bitcast.pos_ref, s32[3,1]{1,0:T(4,128)S(1)} %copy-done.3, f32[6,512,128]{2,1,0:T(8,128)S(1)} %copy-done.13, bf16[6,256,128]{2,1,0:T(8,128)(2,1)S(1)} %copy-done.7, bf16[6,256,128]{2,1,0:T(8,128)(2,1)S(1)} %copy-done.9, bf16[6,256,128]{2,1,0:T(8,128)(2,1)S(1)} %copy-done.11), custom_call_target="tpu_custom_call" | custom-call | flops 12582912000 | bytes 3538944 | tf_op jit(solution)/shard_map/combine/pallas_call | solution.py:268
  197.8 3.3 %collective-permute-done.20 = f32[8,1664]{1,0:T(8,128)S(1)} collective-permute-done((f32[8,1664]{1,0:T(8,128)S(1)}, f32[8,1664]{1,0:T(8,128)S(1)}, u32[]{:S(2)}, u32[]{:S(2)}) %collective-permute-start.20) | collective-permute-done | bytes 53280 | tf_op jit(solution)/shard_map/ppermute | solution.py:22
  201.1 0.6 copy-done.15
  201.7 0.6 slice_add_fusion.4
  202.3 1.4 reshape.82
  203.8 0.7 slice_add_fusion.8
  204.5 0.5 slice_bitcast_fusion
  205.0 2.2 %combine.3 = bf16[256,2,1536]{2,1,0:T(2,128)(2,1)} custom-call(s32[1]{0:T(128)} %bitcast.pos_ref, s32[3,1]{1,0:T(4,128)S(1)} %copy-done.3, f32[6,512,128]{2,1,0:T(8,128)S(1)} %get-tuple-element.67.own_ref, bf16[6,256,128]{2,1,0:T(8,128)(2,1)S(1)} %collective-permute-done.14.dir_ref, ...), custom_call_target="tpu_custom_call", output_to_operand_aliasing={{}: (6, {})} | custom-call | bytes 3538944 | tf_op jit(solution)/shard_map/combine/pallas_call | solution.py:268
  (66 shorter events, 0.7 us)
Async XLA Ops:
  1.4 128.9 %collective-permute-start.1 = (bf16[8,1536]{1,0:T(8,128)(2,1)S(1)}, bf16[8,1536]{1,0:T(8,128)(2,1)S(1)}, u32[]{:S(2)}, u32[]{:S(2)}) collective-permute-start(bf16[8,1536]{1,0:T(8,128)(2,1)S(1)} %reshape.76), channel_id=1, source_target_pairs={{0,2},{1,3},{2,0},{3,1},{4,6},{5,7},{6,4},{7,5},{8,10},{9,11},{10,... | collective-permute-start | bytes 73736 | tf_op jit(solution)/shard_map/ppermute | solution.py:22
  31.4 114.4 %collective-permute-start.8 = (bf16[6,256,128]{2,1,0:T(8,128)(2,1)}, bf16[6,256,128]{2,1,0:T(8,128)(2,1)S(1)}, u32[]{:S(2)}, u32[]{:S(2)}) collective-permute-start(bf16[6,256,128]{2,1,0:T(8,128)(2,1)} %bitcast.30), channel_id=1, source_target_pairs={{0,2},{2,0},{4,6},{6,4},{8,10},{10,8},{12,14},{14,12},{1,3},{3,1},... | collective-permute-start | bytes 1179656 | tf_op jit(solution)/shard_map/ppermute | solution.py:41
  31.5 114.3 %collective-permute-start.9 = (bf16[6,256,128]{2,1,0:T(8,128)(2,1)}, bf16[6,256,128]{2,1,0:T(8,128)(2,1)S(1)}, u32[]{:S(2)}, u32[]{:S(2)}) collective-permute-start(bf16[6,256,128]{2,1,0:T(8,128)(2,1)} %bitcast.29), channel_id=1, source_target_pairs={{2,4},{4,2},{6,8},{8,6},{10,12},{12,10},{3,5},{5,3},{7,9},{9,7},{1... | collective-permute-start | bytes 1179656 | tf_op jit(solution)/shard_map/ppermute | solution.py:41
  130.3 7.3 %collective-permute-start.4 = (bf16[16,1536]{1,0:T(8,128)(2,1)S(1)}, bf16[16,1536]{1,0:T(8,128)(2,1)S(1)}, u32[]{:S(2)}, u32[]{:S(2)}) collective-permute-start(bf16[16,1536]{1,0:T(8,128)(2,1)S(1)} %pad_maximum_fusion.6), channel_id=1, source_target_pairs={{0,4},{1,5},{2,6},{3,7},{4,0},{5,1},{6,2},{7,3},{8,12},{9,13},{10,... | collective-permute-start | bytes 147464 | tf_op jit(solution)/shard_map/ppermute | solution.py:22
  135.0 6.0 %collective-permute-start.5 = (bf16[16,1536]{1,0:T(8,128)(2,1)S(1)}, bf16[16,1536]{1,0:T(8,128)(2,1)S(1)}, u32[]{:S(2)}, u32[]{:S(2)}) collective-permute-start(bf16[16,1536]{1,0:T(8,128)(2,1)S(1)} %pad_maximum_fusion.6), channel_id=1, source_target_pairs={{0,8},{1,9},{2,10},{3,11},{4,12},{5,13},{6,14},{7,15},{8,0},{9,1},... | collective-permute-start | bytes 147464 | tf_op jit(solution)/shard_map/ppermute | solution.py:22
  137.6 5.9 %collective-permute-start.6 = (bf16[16,1536]{1,0:T(8,128)(2,1)S(1)}, bf16[16,1536]{1,0:T(8,128)(2,1)S(1)}, u32[]{:S(2)}, u32[]{:S(2)}) collective-permute-start(bf16[16,1536]{1,0:T(8,128)(2,1)S(1)} %pad_maximum_fusion.6), channel_id=1, source_target_pairs={{0,12},{1,13},{2,14},{3,15},{4,8},{5,9},{6,10},{7,11},{8,4},{9,5},... | collective-permute-start | bytes 147464 | tf_op jit(solution)/shard_map/ppermute | solution.py:22
  137.6 8.2 %collective-permute-start = (bf16[12,256,128]{2,1,0:T(8,128)(2,1)}, bf16[12,256,128]{2,1,0:T(8,128)(2,1)S(1)}, u32[]{:S(2)}, u32[]{:S(2)}) collective-permute-start(bf16[12,256,128]{2,1,0:T(8,128)(2,1)} %bitcast.26), channel_id=1, source_target_pairs={{0,1},{1,0},{2,3},{3,2},{4,5},{5,4},{6,7},{7,6},{8,9},{9,8},{10,11... | collective-permute-start | bytes 2359304 | tf_op jit(solution)/shard_map/ppermute | solution.py:22
  141.1 18.0 %collective-permute-start.2 = (bf16[6,256,128]{2,1,0:T(8,128)(2,1)}, bf16[6,256,128]{2,1,0:T(8,128)(2,1)S(1)}, u32[]{:S(2)}, u32[]{:S(2)}) collective-permute-start(bf16[6,256,128]{2,1,0:T(8,128)(2,1)} %bitcast.28), channel_id=1, source_target_pairs={{0,2},{2,0},{4,6},{6,4},{8,10},{10,8},{12,14},{14,12},{1,3},{3,1},... | collective-permute-start | bytes 1179656 | tf_op jit(solution)/shard_map/ppermute | solution.py:41
  143.5 1.5 collective-permute-start.7
  145.0 14.1 %collective-permute-start.3 = (bf16[6,256,128]{2,1,0:T(8,128)(2,1)}, bf16[6,256,128]{2,1,0:T(8,128)(2,1)S(1)}, u32[]{:S(2)}, u32[]{:S(2)}) collective-permute-start(bf16[6,256,128]{2,1,0:T(8,128)(2,1)} %bitcast.27), channel_id=1, source_target_pairs={{2,4},{4,2},{6,8},{8,6},{10,12},{12,10},{3,5},{5,3},{7,9},{9,7},{1... | collective-permute-start | bytes 1179656 | tf_op jit(solution)/shard_map/ppermute | solution.py:41
  145.7 1.4 copy-start
  145.7 1.6 copy-start.1
  145.8 1.8 copy-start.2
  145.8 1.8 copy-start.4
  145.8 1.8 copy-start.5
  156.2 11.6 %copy-start.12 = (f32[6,512,128]{2,1,0:T(8,128)}, f32[6,512,128]{2,1,0:T(8,128)S(1)}, u32[]{:S(2)}) copy-start(f32[6,512,128]{2,1,0:T(8,128)S(1)} %get-tuple-element.84.own_ref) | copy-start | bytes 4718596
  156.2 19.0 %collective-permute-start.11 = (bf16[6,256,128]{2,1,0:T(8,128)(2,1)S(1)}, bf16[6,256,128]{2,1,0:T(8,128)(2,1)S(1)}, u32[]{:S(2)}, u32[]{:S(2)}) collective-permute-start(bf16[6,256,128]{2,1,0:T(8,128)(2,1)S(1)} %get-tuple-element.74), channel_id=1, source_target_pairs={{0,2},{2,0},{4,6},{6,4},{8,10},{10,8},{12,14},{14,12},{1,3},{3,1},... | collective-permute-start | bytes 1179656 | tf_op jit(solution)/shard_map/ppermute | solution.py:41
  158.3 16.8 %collective-permute-start.12 = (bf16[6,256,128]{2,1,0:T(8,128)(2,1)S(1)}, bf16[6,256,128]{2,1,0:T(8,128)(2,1)S(1)}, u32[]{:S(2)}, u32[]{:S(2)}) collective-permute-start(bf16[6,256,128]{2,1,0:T(8,128)(2,1)S(1)} %get-tuple-element.75), channel_id=1, source_target_pairs={{2,4},{4,2},{6,8},{8,6},{10,12},{12,10},{3,5},{5,3},{7,9},{9,7},{1... | collective-permute-start | bytes 1179656 | tf_op jit(solution)/shard_map/ppermute | solution.py:41
  159.0 16.1 %collective-permute-start.13 = (bf16[6,256,128]{2,1,0:T(8,128)(2,1)S(1)}, bf16[6,256,128]{2,1,0:T(8,128)(2,1)S(1)}, u32[]{:S(2)}, u32[]{:S(2)}) collective-permute-start(bf16[6,256,128]{2,1,0:T(8,128)(2,1)S(1)} %get-tuple-element.76), channel_id=1, source_target_pairs={{0,1},{1,0},{2,3},{3,2},{4,5},{5,4},{6,7},{7,6},{8,9},{9,8},{10,11... | collective-permute-start | bytes 1179656 | tf_op jit(solution)/shard_map/ppermute | solution.py:22
  168.8 7.9 %collective-permute-start.10 = (f32[64,1664]{1,0:T(8,128)S(1)}, f32[64,1664]{1,0:T(8,128)S(1)}, u32[]{:S(2)}, u32[]{:S(2)}) collective-permute-start(f32[64,1664]{1,0:T(8,128)S(1)} %pad_maximum_fusion), channel_id=1, source_target_pairs={{0,1},{1,0},{2,3},{3,2},{4,5},{5,4},{6,7},{7,6},{8,9},{9,8},{10,11... | collective-permute-start | bytes 1277960 | tf_op jit(solution)/shard_map/ppermute | solution.py:22
  175.1 0.7 copy-start.6
  175.9 0.8 copy-start.8
  176.7 5.3 %copy-start.10 = (bf16[6,256,128]{2,1,0:T(8,128)(2,1)}, bf16[6,256,128]{2,1,0:T(8,128)(2,1)S(1)}, u32[]{:S(2)}) copy-start(bf16[6,256,128]{2,1,0:T(8,128)(2,1)S(1)} %get-tuple-element.87.par_ref) | copy-start | bytes 1179652
  176.7 15.9 %copy-start.3 = (s32[3,1]{1,0:T(4,128)S(1)}, s32[3,1]{1,0:T(4,128)}, u32[]{:S(2)}) copy-start(s32[3,1]{1,0:T(4,128)} %copy.19.sent_ref) | copy-start | bytes 40
  177.4 6.1 %copy-start.14 = (f32[64,1536]{1,0:T(8,128)}, f32[64,1536]{1,0:T(8,128)S(1)}, u32[]{:S(2)}) copy-start(f32[64,1536]{1,0:T(8,128)S(1)} %slice_add_fusion) | copy-start | bytes 1179652
  177.6 15.0 %copy-start.13 = (f32[6,512,128]{2,1,0:T(8,128)S(1)}, f32[6,512,128]{2,1,0:T(8,128)}, u32[]{:S(2)}) copy-start(f32[6,512,128]{2,1,0:T(8,128)} %copy-done.12) | copy-start | bytes 4718596
  177.7 7.6 %collective-permute-start.17 = (f32[16,1664]{1,0:T(8,128)S(1)}, f32[16,1664]{1,0:T(8,128)S(1)}, u32[]{:S(2)}, u32[]{:S(2)}) collective-permute-start(f32[16,1664]{1,0:T(8,128)S(1)} %get-tuple-element.93), channel_id=1, source_target_pairs={{0,4},{1,5},{2,6},{3,7},{4,0},{5,1},{6,2},{7,3},{8,12},{9,13},{10,... | collective-permute-start | bytes 319496 | tf_op jit(solution)/shard_map/ppermute | solution.py:22
  181.1 9.9 %collective-permute-start.18 = (f32[16,1664]{1,0:T(8,128)S(1)}, f32[16,1664]{1,0:T(8,128)S(1)}, u32[]{:S(2)}, u32[]{:S(2)}) collective-permute-start(f32[16,1664]{1,0:T(8,128)S(1)} %get-tuple-element.94), channel_id=1, source_target_pairs={{0,8},{1,9},{2,10},{3,11},{4,12},{5,13},{6,14},{7,15},{8,0},{9,1},... | collective-permute-start | bytes 319496 | tf_op jit(solution)/shard_map/ppermute | solution.py:22
  182.0 8.9 %collective-permute-start.19 = (f32[16,1664]{1,0:T(8,128)S(1)}, f32[16,1664]{1,0:T(8,128)S(1)}, u32[]{:S(2)}, u32[]{:S(2)}) collective-permute-start(f32[16,1664]{1,0:T(8,128)S(1)} %get-tuple-element.95), channel_id=1, source_target_pairs={{0,12},{1,13},{2,14},{3,15},{4,8},{5,9},{6,10},{7,11},{8,4},{9,5},... | collective-permute-start | bytes 319496 | tf_op jit(solution)/shard_map/ppermute | solution.py:22
  183.5 21.5 %collective-permute-start.14 = (bf16[6,256,128]{2,1,0:T(8,128)(2,1)}, bf16[6,256,128]{2,1,0:T(8,128)(2,1)S(1)}, u32[]{:S(2)}, u32[]{:S(2)}) collective-permute-start(bf16[6,256,128]{2,1,0:T(8,128)(2,1)} %get-tuple-element.80), channel_id=1, source_target_pairs={{0,2},{2,0},{4,6},{6,4},{8,10},{10,8},{12,14},{14,12},{1,3},{3,1},... | collective-permute-start | bytes 1179656 | tf_op jit(solution)/shard_map/ppermute | solution.py:41
  184.6 20.4 %collective-permute-start.15 = (bf16[6,256,128]{2,1,0:T(8,128)(2,1)S(1)}, bf16[6,256,128]{2,1,0:T(8,128)(2,1)S(1)}, u32[]{:S(2)}, u32[]{:S(2)}) collective-permute-start(bf16[6,256,128]{2,1,0:T(8,128)(2,1)S(1)} %get-tuple-element.81), channel_id=1, source_target_pairs={{2,4},{4,2},{6,8},{8,6},{10,12},{12,10},{3,5},{5,3},{7,9},{9,7},{1... | collective-permute-start | bytes 1179656 | tf_op jit(solution)/shard_map/ppermute | solution.py:41
  185.3 19.7 %collective-permute-start.16 = (bf16[6,256,128]{2,1,0:T(8,128)(2,1)S(1)}, bf16[6,256,128]{2,1,0:T(8,128)(2,1)S(1)}, u32[]{:S(2)}, u32[]{:S(2)}) collective-permute-start(bf16[6,256,128]{2,1,0:T(8,128)(2,1)S(1)} %get-tuple-element.82), channel_id=1, source_target_pairs={{0,1},{1,0},{2,3},{3,2},{4,5},{5,4},{6,7},{7,6},{8,9},{9,8},{10,11... | collective-permute-start | bytes 1179656 | tf_op jit(solution)/shard_map/ppermute | solution.py:22
  191.9 9.2 %collective-permute-start.20 = (f32[8,1664]{1,0:T(8,128)S(1)}, f32[8,1664]{1,0:T(8,128)S(1)}, u32[]{:S(2)}, u32[]{:S(2)}) collective-permute-start(f32[8,1664]{1,0:T(8,128)S(1)} %pad_maximum_fusion.5), channel_id=1, source_target_pairs={{0,2},{1,3},{2,0},{3,1},{4,6},{5,7},{6,4},{7,5},{8,10},{9,11},{10,... | collective-permute-start | bytes 159752 | tf_op jit(solution)/shard_map/ppermute | solution.py:22
  192.6 1.0 copy-start.7
  193.6 1.0 copy-start.9
  194.6 1.0 copy-start.11
  201.1 0.6 copy-start.15

commit v4 on v3

--- a/solution.py
+++ b/solution.py
@@ -46,7 +46,7 @@
     return [n for n in (first, total - first) if n > 0]
 
 
-def pick_kernel(pos_ref, sent_ref, kv_ref, *rest, copies):
+def pick_kernel(pos_ref, sent_ref, kv_ref, *rest, copies, width):
     sems = rest[-1]
     outs = rest[:-1]
     odd = lax.rem(pos_ref[0], 2)
@@ -54,37 +54,31 @@
         "direct": jnp.where(odd == 1, sent_ref[0, 0], sent_ref[1, 0]),
         "diagonal": jnp.where(odd == 1, sent_ref[1, 0], sent_ref[0, 0]),
         "partner": sent_ref[2, 0],
-        "own": 0,
     }
     started = []
-    for out, (which, head0, heads) in zip(outs, copies):
-        rows, width = out.shape[1], out.shape[3]
-        for h in range(heads):
-            lanes = slice((head0 + h) * width, (head0 + h + 1) * width)
-            source = kv_ref.at[pl.ds(spots[which] * BLOCK, rows), :, lanes]
-            copy = pltpu.make_async_copy(source, out.at[h], sems.at[len(started)])
-            copy.start()
-            started.append(copy)
+    for i, (out, (which, head0)) in enumerate(zip(outs, copies)):
+        lanes = slice(head0 * width, head0 * width + out.shape[2])
+        source = kv_ref.at[pl.ds(spots[which] * BLOCK, BLOCK), :, lanes]
+        copy = pltpu.make_async_copy(source, out, sems.at[i])
+        copy.start()
+        started.append(copy)
     for copy in started:
         copy.wait()
 
 
 def pick(pos, sent, mesh_kv, width, copies):
-    rows = [mesh_kv.shape[0] if which == "own" else BLOCK for which, _, _ in copies]
     smem = pl.BlockSpec(memory_space=SMEM)
-    anywhere = pl.BlockSpec(memory_space=pl.ANY)
-    out = pl.pallas_call(
-        functools.partial(pick_kernel, copies=copies),
-        in_specs=[smem, smem, anywhere],
-        out_specs=[anywhere] * len(copies),
-        out_shape=[
-            jax.ShapeDtypeStruct((heads, n, 2, width), BF16) for n, (_, _, heads) in zip(rows, copies)
-        ],
-        scratch_shapes=[pltpu.SemaphoreType.DMA((sum(heads for _, _, heads in copies),))],
+    vmem = pl.BlockSpec(memory_space=pltpu.MemorySpace.VMEM)
+    return pl.pallas_call(
+        functools.partial(pick_kernel, copies=[c[:2] for c in copies], width=width),
+        in_specs=[smem, smem, pl.BlockSpec(memory_space=pl.ANY)],
+        out_specs=[vmem] * len(copies),
+        out_shape=[jax.ShapeDtypeStruct((BLOCK, 2, heads * width), BF16) for _, _, heads in copies],
+        scratch_shapes=[pltpu.SemaphoreType.DMA((len(copies),))],
+        compiler_params=pltpu.CompilerParams(vmem_limit_bytes=8 << 20),
         cost_estimate=pl.CostEstimate(flops=0, transcendentals=0, bytes_accessed=1 << 20),
         name="pick",
     )(pos, sent, mesh_kv)
-    return [x.reshape(x.shape[0], 2 * x.shape[1], width) for x in out]
 
 
 def hold_kernel(*refs):
@@ -119,15 +113,16 @@
     gx = pos_ref[0]
     odd = lax.rem(gx, 2)
     queries = q_ref.shape[0]
-    own_rows = own_ref.shape[0] // 2
+    own_rows = own_ref.shape[0]
     blocks = own_rows // BLOCK
     near = own_rows + 3 * BLOCK
     keys = near + anc_ref.shape[0] // 2
 
     row = 0
     for ref in (own_ref, par_ref, dir_ref, dia_ref, anc_ref):
-        pair_ref[row : row + ref.shape[0], :] = ref[...].astype(F32)
-        row += ref.shape[0]
+        block = ref[...] if len(ref.shape) == 2 else ref[...].reshape(2 * ref.shape[0], width)
+        pair_ref[row : row + block.shape[0], :] = block.astype(F32)
+        row += block.shape[0]
     k = pair_ref[pl.ds(0, keys, stride=2), :].astype(BF16)
     v = pair_ref[pl.ds(1, keys, stride=2), :].astype(BF16)
 
@@ -179,19 +174,20 @@
     anc_out[...] = pair_ref[2 * near :, :]
 
 
-def attention(pos, filt, warm, q, g, own_kv, partner, halo, anchors, head0, heads, dq_prev, anc_prev):
+def attention(pos, filt, warm, q, g, mesh_kv, partner, halo, anchors, head0, heads, dq_prev, anc_prev):
     rows, feat = q.shape
-    total, own_rows, width = own_kv.shape
-    own_rows //= 2
+    own_rows = mesh_kv.shape[0]
+    width = feat // warm.shape[0]
     a_rows = anchors.shape[0] // 2
     keys = own_rows + 3 * BLOCK + a_rows
     smem = pl.BlockSpec(memory_space=SMEM)
-    full = lambda n: pl.BlockSpec((None, 2 * n, width), lambda h: (head0 + h, 0, 0))
-    part = pl.BlockSpec((None, 2 * BLOCK, width), lambda h: (h, 0, 0))
+    full = lambda n: pl.BlockSpec((n, 2, width), lambda h: (0, 0, head0 + h))
+    part = pl.BlockSpec((BLOCK, 2, width), lambda h: (0, 0, h))
+    back = pl.BlockSpec((None, 2 * BLOCK, width), lambda h: (h, 0, 0))
     cols = pl.BlockSpec((rows, width), lambda h: (0, head0 + h))
     in_specs = [smem, smem, smem, cols, cols, full(own_rows), full(BLOCK), part, part]
     in_specs += [pl.BlockSpec((2 * a_rows, width), lambda h: (0, head0 + h))]
-    args = [pos, filt, warm, q, g, own_kv, partner, *halo, anchors]
+    args = [pos, filt, warm, q, g, mesh_kv, partner, *halo, anchors]
     alias = {}
     if dq_prev is not None:
         in_specs += [pl.BlockSpec(memory_space=pl.ANY)] * 2
@@ -205,9 +201,9 @@
         out_specs=[
             cols,
             pl.BlockSpec((None, 2 * own_rows, width), lambda h: (h, 0, 0)),
-            part,
-            part,
-            part,
+            back,
+            back,
+            back,
             pl.BlockSpec((2 * a_rows, width), lambda h: (0, head0 + h)),
             pl.BlockSpec((1, 1, rows), lambda h: (h, 0, 0)),
         ],
@@ -297,8 +293,8 @@
 
     picks = [pick(pos, sent, mesh_kv, width, [("direct", *chunks[0]), ("diagonal", *chunks[0])])]
     others = [(which, *chunk) for chunk in chunks[1:] for which in ("direct", "diagonal")]
-    others = pick(pos, sent, mesh_kv, width, others + [("partner", 0, total), ("own", 0, total)])
-    own_kv, partner = others.pop(), swap_mask(others.pop(), 1)
+    others = list(pick(pos, sent, mesh_kv, width, others + [("partner", 0, total)]))
+    partner = swap_mask(others.pop(), 1)
     picks += [others[2 * i : 2 * i + 2] for i in range(len(chunks) - 1)]
     anchors = landmark.reshape(2 * landmark.shape[0], feat)
     for i, masks in enumerate(stages):
@@ -312,7 +308,7 @@
     temps, owns, faces, returned = [], [], [], []
     for (head0, heads), halo in zip(chunks, halos):
         dq, own, f_dir, f_dia, f_par, anc, temp = attention(
-            pos, filt, warm, q, g, own_kv, partner, halo, anchors, head0, heads, dq, anc
+            pos, filt, warm, q, g, mesh_kv, partner, halo, anchors, head0, heads, dq, anc
         )
         temps.append(temp)
         owns.append(own)

time: 208 us -> 93 us (0.45)
  Pallas kernels: 145 us -> 26.5 us
  waiting for transfers between devices: 20.4 us -> 23.5 us
    pallas_call x2, Pallas kernels: 123 us -> 1.44 us  [pick(): pl.pallas_call(functools.partial(pick_kernel, copies=[c[:2] for c in copi...]
    ppermute x13, waiting for transfers between devices: 14.5 us -> 19.3 us  [swap_mask(): return lax.ppermute(x, ('gx', 'gy'), [(i, i ^ mask) for i in range(count)])]
    pallas_call x2, Pallas kernels: 17.3 us -> 20.6 us  [attention(): pl.pallas_call(functools.partial(attention_kernel, gx_count=lax.axis_size...]
  transfers between devices with their start and end apart: 21 -> 21, of which waited for: 6 -> 7; matrix products, arithmetic and copies ran while one was open for 3% -> 7% of each run, Pallas kernels for 69% -> 26%
where the time goes in v4:
time: 93 us; the launch traced here: 92.5 us
  Pallas kernels  26.5 us (28%)
  starting transfers between devices  25 us (27%)
  waiting for transfers between devices  23.5 us (25%)
  local copies, waits for them, and re-layouts  12 us (13%)
  other arithmetic  4.5 us (5%)
  between operations  1 us (1%)
    pallas_call x2, Pallas kernels, attention(): pl.pallas_call(functools.partial(attention_kernel, gx_count=lax.axis_size...  20.6 us
    ppermute x13, waiting for transfers between devices, swap_mask(): return lax.ppermute(x, ('gx', 'gy'), [(i, i ^ mask) for i in range(count)])  19.3 us
    ppermute x13, starting transfers between devices, swap_mask(): return lax.ppermute(x, ('gx', 'gy'), [(i, i ^ mask) for i in range(count)])  17.9 us
    unnamed x36, local copies, waits for them, and re-layouts  8.32 us
    ppermute x8, starting transfers between devices, swap_pairs(): return lax.ppermute(x, 'gx', route)  7.07 us
    pallas_call x2, Pallas kernels, combine(): pl.pallas_call(combine_kernel, grid=(heads // step,), in_specs=in_specs,...  4.39 us
    ppermute x8, waiting for transfers between devices, swap_pairs(): return lax.ppermute(x, 'gx', route)  4.21 us
  transfers between devices with their start and end apart: 21, of which 7 were waited for; matrix products, arithmetic and copies ran while one was open for 7% of the time, Pallas kernels for 26%

profile of v4, /device:TPU:0, one launch (start us, length us, event | category | flops | bytes accessed | tf_op | source)
XLA Modules:
  0.0 92.5 jit_solution(3595017074548008592)
XLA Ops:
  0.6 0.8 reshape.56
  1.4 3.0 %collective-permute-start.1 = (bf16[8,1536]{1,0:T(8,128)(2,1)S(1)}, bf16[8,1536]{1,0:T(8,128)(2,1)S(1)}, u32[]{:S(2)}, u32[]{:S(2)}) collective-permute-start(bf16[8,1536]{1,0:T(8,128)(2,1)S(1)} %reshape.56), channel_id=1, source_target_pairs={{0,2},{1,3},{2,0},{3,1},{4,6},{5,7},{6,4},{7,5},{8,10},{9,11},{10,... | collective-permute-start | bytes 73736 | tf_op jit(solution)/shard_map/ppermute | solution.py:22
  4.4 0.7 copy.19.sent_ref
  5.1 1.4 %copy-done = bf16[256,2,1536]{2,1,0:T(2,128)(2,1)S(1)} copy-done((bf16[256,2,1536]{2,1,0:T(2,128)(2,1)S(1)}, bf16[256,2,1536]{2,1,0:T(2,128)(2,1)}, u32[]{:S(2)}) %copy-start) | copy-done | bytes 1572888
  6.5 0.7 pick.3
  7.3 0.7 collective-permute-start.9
  8.0 0.8 pick.2
  8.8 0.6 compare_reduce_fusion
  9.4 4.7 %collective-permute-start.4 = (bf16[16,1536]{1,0:T(8,128)(2,1)S(1)}, bf16[16,1536]{1,0:T(8,128)(2,1)S(1)}, u32[]{:S(2)}, u32[]{:S(2)}) collective-permute-start(bf16[16,1536]{1,0:T(8,128)(2,1)S(1)} %pad_maximum_fusion.6), channel_id=1, source_target_pairs={{0,4},{1,5},{2,6},{3,7},{4,0},{5,1},{6,2},{7,3},{8,12},{9,13},{10,... | collective-permute-start | bytes 147464 | tf_op jit(solution)/shard_map/ppermute | solution.py:22
  14.2 2.6 %collective-permute-start.5 = (bf16[16,1536]{1,0:T(8,128)(2,1)S(1)}, bf16[16,1536]{1,0:T(8,128)(2,1)S(1)}, u32[]{:S(2)}, u32[]{:S(2)}) collective-permute-start(bf16[16,1536]{1,0:T(8,128)(2,1)S(1)} %pad_maximum_fusion.6), channel_id=1, source_target_pairs={{0,8},{1,9},{2,10},{3,11},{4,12},{5,13},{6,14},{7,15},{8,0},{9,1},... | collective-permute-start | bytes 147464 | tf_op jit(solution)/shard_map/ppermute | solution.py:22
  16.8 5.8 %collective-permute-done.4 = bf16[16,1536]{1,0:T(8,128)(2,1)S(1)} collective-permute-done((bf16[16,1536]{1,0:T(8,128)(2,1)S(1)}, bf16[16,1536]{1,0:T(8,128)(2,1)S(1)}, u32[]{:S(2)}, u32[]{:S(2)}) %collective-permute-start.4) | collective-permute-done | bytes 49184 | tf_op jit(solution)/shard_map/ppermute | solution.py:22
  22.6 2.1 %collective-permute-done.5 = bf16[16,1536]{1,0:T(8,128)(2,1)S(1)} collective-permute-done((bf16[16,1536]{1,0:T(8,128)(2,1)S(1)}, bf16[16,1536]{1,0:T(8,128)(2,1)S(1)}, u32[]{:S(2)}, u32[]{:S(2)}) %collective-permute-start.5) | collective-permute-done | bytes 49184 | tf_op jit(solution)/shard_map/ppermute | solution.py:22
  24.6 1.6 %collective-permute-done.6 = bf16[16,1536]{1,0:T(8,128)(2,1)S(1)} collective-permute-done((bf16[16,1536]{1,0:T(8,128)(2,1)S(1)}, bf16[16,1536]{1,0:T(8,128)(2,1)S(1)}, u32[]{:S(2)}, u32[]{:S(2)}) %collective-permute-start.6) | collective-permute-done | bytes 49184 | tf_op jit(solution)/shard_map/ppermute | solution.py:22
  26.3 1.4 %collective-permute-done.7 = bf16[64,1536]{1,0:T(8,128)(2,1)S(1)} collective-permute-done((bf16[64,1536]{1,0:T(8,128)(2,1)S(1)}, bf16[64,1536]{1,0:T(8,128)(2,1)S(1)}, u32[]{:S(2)}, u32[]{:S(2)}) %collective-permute-start.7) | collective-permute-done | bytes 196640 | tf_op jit(solution)/shard_map/ppermute | solution.py:22
  27.7 0.7 collective-permute-start.3
  28.5 1.3 %copy-done.1 = bf16[256,2,1536]{2,1,0:T(2,128)(2,1)S(1)} copy-done((bf16[256,2,1536]{2,1,0:T(2,128)(2,1)S(1)}, bf16[256,2,1536]{2,1,0:T(2,128)(2,1)}, u32[]{:S(2)}) %copy-start.1) | copy-done | bytes 1572888
  29.8 0.2 copy-done.2
  30.0 0.2 copy-done.3
  30.3 10.2 %attention.2 = (bf16[256,1536]{1,0:T(8,128)(2,1)}, f32[6,512,128]{2,1,0:T(8,128)S(1)}, bf16[6,256,128]{2,1,0:T(8,128)(2,1)S(1)}, bf16[6,256,128]{2,1,0:T(8,128)(...) custom-call(s32[1]{0:T(128)} %bitcast.pos_ref, ...), custom_call_target="tpu_custom_call" | custom-call | flops 1384120320 | bytes 6488064 | tf_op jit(solution)/shard_map/attention/pallas_call | solution.py:197
  40.5 2.7 %collective-permute-start.11 = (bf16[6,256,128]{2,1,0:T(8,128)(2,1)S(1)}, bf16[6,256,128]{2,1,0:T(8,128)(2,1)S(1)}, u32[]{:S(2)}, u32[]{:S(2)}) collective-permute-start(bf16[6,256,128]{2,1,0:T(8,128)(2,1)S(1)} %get-tuple-element.72), channel_id=1, source_target_pairs={{0,2},{2,0},{4,6},{6,4},{8,10},{10,8},{12,14},{14,12},{1,3},{3,1},... | collective-permute-start | bytes 1179656 | tf_op jit(solution)/shard_map/ppermute | solution.py:41
  43.3 0.7 collective-permute-start.12
  44.0 10.4 %attention.3 = (bf16[256,1536]{1,0:T(8,128)(2,1)}, f32[6,512,128]{2,1,0:T(8,128)S(1)}, bf16[6,256,128]{2,1,0:T(8,128)(2,1)}, bf16[6,256,128]{2,1,0:T(8,128)(2,1)...) custom-call(s32[1]{0:T(128)} %bitcast.pos_ref, ...), custom_call_target="tpu_custom_call", output_to_operand_aliasing={{0}: (10, {}), {5}: (11, {})} | custom-call | flops 1384120320 | bytes 6488064 | tf_op jit(solution)/shard_map/attention/pallas_call | solution.py:197
  54.4 0.2 maximum_reduce_fusion
  54.6 0.6 fusion
  55.4 0.5 collective-permute-start.10
  55.9 4.2 %collective-permute-done.11.refs_0_ = bf16[6,256,128]{2,1,0:T(8,128)(2,1)S(1)} collective-permute-done((bf16[6,256,128]{2,1,0:T(8,128)(2,1)S(1)}, bf16[6,256,128]{2,1,0:T(8,128)(2,1)S(1)}, u32[]{:S(2)}, u32[]{:S(2)}) %collective-permute-start.11) | collective-permute-done | bytes 393248 | tf_op jit(solution)/shard_map/ppermute | solution.py:41
  60.1 0.7 copy-done.6
  60.8 0.8 copy-done.8
  61.6 0.7 slice_add_fusion.9
  62.6 3.0 %collective-permute-start.17 = (f32[16,1664]{1,0:T(8,128)S(1)}, f32[16,1664]{1,0:T(8,128)S(1)}, u32[]{:S(2)}, u32[]{:S(2)}) collective-permute-start(f32[16,1664]{1,0:T(8,128)S(1)} %get-tuple-element.91), channel_id=1, source_target_pairs={{0,4},{1,5},{2,6},{3,7},{4,0},{5,1},{6,2},{7,3},{8,12},{9,13},{10,... | collective-permute-start | bytes 319496 | tf_op jit(solution)/shard_map/ppermute | solution.py:22
  65.6 1.7 %collective-permute-start.18 = (f32[16,1664]{1,0:T(8,128)S(1)}, f32[16,1664]{1,0:T(8,128)S(1)}, u32[]{:S(2)}, u32[]{:S(2)}) collective-permute-start(f32[16,1664]{1,0:T(8,128)S(1)} %get-tuple-element.92), channel_id=1, source_target_pairs={{0,8},{1,9},{2,10},{3,11},{4,12},{5,13},{6,14},{7,15},{8,0},{9,1},... | collective-permute-start | bytes 319496 | tf_op jit(solution)/shard_map/ppermute | solution.py:22
  67.2 0.9 collective-permute-start.19
  68.1 1.5 %collective-permute-start.14 = (bf16[6,256,128]{2,1,0:T(8,128)(2,1)}, bf16[6,256,128]{2,1,0:T(8,128)(2,1)S(1)}, u32[]{:S(2)}, u32[]{:S(2)}) collective-permute-start(bf16[6,256,128]{2,1,0:T(8,128)(2,1)} %get-tuple-element.78), channel_id=1, source_target_pairs={{0,2},{2,0},{4,6},{6,4},{8,10},{10,8},{12,14},{14,12},{1,3},{3,1},... | collective-permute-start | bytes 1179656 | tf_op jit(solution)/shard_map/ppermute | solution.py:41
  69.6 0.7 collective-permute-start.15
  70.4 5.5 %collective-permute-done.18 = f32[16,1664]{1,0:T(8,128)S(1)} collective-permute-done((f32[16,1664]{1,0:T(8,128)S(1)}, f32[16,1664]{1,0:T(8,128)S(1)}, u32[]{:S(2)}, u32[]{:S(2)}) %collective-permute-start.18) | collective-permute-done | bytes 106528 | tf_op jit(solution)/shard_map/ppermute | solution.py:22
  75.9 0.9 %slice_add_fusion.1 = f32[16,1536]{1,0:T(8,128)S(1)} fusion(f32[16,1664]{1,0:T(8,128)S(1)} %collective-permute-done.19, f32[16,1664]{1,0:T(8,128)S(1)} %collective-permute-done.18, f32[16,1664]{1,0:T(8,128)S(1)} %collective-permute-done.17, f32[64,1536]{1,0:T(8,128)} %copy-done.14), kind=kLoop, calls=%fused_computation.6 | loop fusion | flops 73728 | bytes 491520 | tf_op jit(solution)/shard_map/add | solution.py:336
  76.8 1.4 %collective-permute-start.20 = (f32[8,1664]{1,0:T(8,128)S(1)}, f32[8,1664]{1,0:T(8,128)S(1)}, u32[]{:S(2)}, u32[]{:S(2)}) collective-permute-start(f32[8,1664]{1,0:T(8,128)S(1)} %pad_maximum_fusion.5), channel_id=1, source_target_pairs={{0,2},{1,3},{2,0},{3,1},{4,6},{5,7},{6,4},{7,5},{8,10},{9,11},{10,... | collective-permute-start | bytes 159752 | tf_op jit(solution)/shard_map/ppermute | solution.py:22
  78.2 1.0 %copy-done.7 = bf16[6,256,128]{2,1,0:T(8,128)(2,1)S(1)} copy-done((bf16[6,256,128]{2,1,0:T(8,128)(2,1)S(1)}, bf16[6,256,128]{2,1,0:T(8,128)(2,1)}, u32[]{:S(2)}) %copy-start.7) | copy-done | bytes 393240
  79.2 1.0 %copy-done.9 = bf16[6,256,128]{2,1,0:T(8,128)(2,1)S(1)} copy-done((bf16[6,256,128]{2,1,0:T(8,128)(2,1)S(1)}, bf16[6,256,128]{2,1,0:T(8,128)(2,1)}, u32[]{:S(2)}) %copy-start.9) | copy-done | bytes 393240
  80.2 1.0 %copy-done.11 = bf16[6,256,128]{2,1,0:T(8,128)(2,1)S(1)} copy-done((bf16[6,256,128]{2,1,0:T(8,128)(2,1)S(1)}, bf16[6,256,128]{2,1,0:T(8,128)(2,1)}, u32[]{:S(2)}) %copy-start.11) | copy-done | bytes 393240
  81.2 2.2 %combine.2.rest_0_ = bf16[256,2,1536]{2,1,0:T(2,128)(2,1)} custom-call(s32[1]{0:T(128)} %bitcast.pos_ref, s32[3,1]{1,0:T(4,128)S(1)} %copy.19.sent_ref, f32[6,512,128]{2,1,0:T(8,128)S(1)} %copy-done.13, bf16[6,256,128]{2,1,0:T(8,128)(2,1)S(1)} %copy-done.7, bf16[6,256,128]{2,1,0:T(8,128)(2,1)S(1)} %copy-done.9, bf16[6,256,128]{2,1,0:T(8,128)(2,1)S(1)} %copy-done.11), custom_call_target="tpu_custom_call" | custom-call | flops 12582912000 | bytes 3538944 | tf_op jit(solution)/shard_map/combine/pallas_call | solution.py:264
  83.4 3.0 %collective-permute-done.20 = f32[8,1664]{1,0:T(8,128)S(1)} collective-permute-done((f32[8,1664]{1,0:T(8,128)S(1)}, f32[8,1664]{1,0:T(8,128)S(1)}, u32[]{:S(2)}, u32[]{:S(2)}) %collective-permute-start.20) | collective-permute-done | bytes 53280 | tf_op jit(solution)/shard_map/ppermute | solution.py:22
  86.4 0.6 copy-done.15
  87.0 0.6 slice_add_fusion.4
  87.6 1.4 %reshape.58 = f32[4,2,1536]{2,1,0:T(2,128)} reshape(f32[8,1536]{1,0:T(8,128)} %slice_add_fusion.4) | data formatting | bytes 98304 | tf_op jit(solution)/shard_map/reshape | solution.py:338
  89.1 0.7 slice_add_fusion.8
  89.7 0.5 slice_bitcast_fusion
  90.3 2.2 %combine.3 = bf16[256,2,1536]{2,1,0:T(2,128)(2,1)} custom-call(s32[1]{0:T(128)} %bitcast.pos_ref, s32[3,1]{1,0:T(4,128)S(1)} %copy.19.sent_ref, f32[6,512,128]{2,1,0:T(8,128)S(1)} %get-tuple-element.65.own_ref, bf16[6,256,128]{2,1,0:T(8,128)(2,1)S(1)} %collective-permute-done.14.dir_ref, ...), custom_call_target="tpu_custom_call", output_to_operand_aliasing={{}: (6, {})} | custom-call | bytes 3538944 | tf_op jit(solution)/shard_map/combine/pallas_call | solution.py:264
  (66 shorter events, 0.8 us)
Async XLA Ops:
  1.4 8.0 %collective-permute-start.1 = (bf16[8,1536]{1,0:T(8,128)(2,1)S(1)}, bf16[8,1536]{1,0:T(8,128)(2,1)S(1)}, u32[]{:S(2)}, u32[]{:S(2)}) collective-permute-start(bf16[8,1536]{1,0:T(8,128)(2,1)S(1)} %reshape.56), channel_id=1, source_target_pairs={{0,2},{1,3},{2,0},{3,1},{4,6},{5,7},{6,4},{7,5},{8,10},{9,11},{10,... | collective-permute-start | bytes 73736 | tf_op jit(solution)/shard_map/ppermute | solution.py:22
  5.1 1.4 %copy-start = (bf16[256,2,1536]{2,1,0:T(2,128)(2,1)S(1)}, bf16[256,2,1536]{2,1,0:T(2,128)(2,1)}, u32[]{:S(2)}) copy-start(bf16[256,2,1536]{2,1,0:T(2,128)(2,1)} %own_ref.3) | copy-start | bytes 4718596
  7.2 21.3 %collective-permute-start.8 = (bf16[128,2,768]{2,1,0:T(2,128)(2,1)S(1)}, bf16[128,2,768]{2,1,0:T(2,128)(2,1)S(1)}, u32[]{:S(2)}, u32[]{:S(2)}) collective-permute-start(bf16[128,2,768]{2,1,0:T(2,128)(2,1)S(1)} %get-tuple-element.58), channel_id=1, source_target_pairs={{0,2},{2,0},{4,6},{6,4},{8,10},{10,8},{12,14},{14,12},{1,3},{3,1},... | collective-permute-start | bytes 1179656 | tf_op jit(solution)/shard_map/ppermute | solution.py:41
  7.3 21.2 %collective-permute-start.9 = (bf16[128,2,768]{2,1,0:T(2,128)(2,1)S(1)}, bf16[128,2,768]{2,1,0:T(2,128)(2,1)S(1)}, u32[]{:S(2)}, u32[]{:S(2)}) collective-permute-start(bf16[128,2,768]{2,1,0:T(2,128)(2,1)S(1)} %get-tuple-element.59), channel_id=1, source_target_pairs={{2,4},{4,2},{6,8},{8,6},{10,12},{12,10},{3,5},{5,3},{7,9},{9,7},{1... | collective-permute-start | bytes 1179656 | tf_op jit(solution)/shard_map/ppermute | solution.py:41
  9.4 13.2 %collective-permute-start.4 = (bf16[16,1536]{1,0:T(8,128)(2,1)S(1)}, bf16[16,1536]{1,0:T(8,128)(2,1)S(1)}, u32[]{:S(2)}, u32[]{:S(2)}) collective-permute-start(bf16[16,1536]{1,0:T(8,128)(2,1)S(1)} %pad_maximum_fusion.6), channel_id=1, source_target_pairs={{0,4},{1,5},{2,6},{3,7},{4,0},{5,1},{6,2},{7,3},{8,12},{9,13},{10,... | collective-permute-start | bytes 147464 | tf_op jit(solution)/shard_map/ppermute | solution.py:22
  14.2 10.5 %collective-permute-start.5 = (bf16[16,1536]{1,0:T(8,128)(2,1)S(1)}, bf16[16,1536]{1,0:T(8,128)(2,1)S(1)}, u32[]{:S(2)}, u32[]{:S(2)}) collective-permute-start(bf16[16,1536]{1,0:T(8,128)(2,1)S(1)} %pad_maximum_fusion.6), channel_id=1, source_target_pairs={{0,8},{1,9},{2,10},{3,11},{4,12},{5,13},{6,14},{7,15},{8,0},{9,1},... | collective-permute-start | bytes 147464 | tf_op jit(solution)/shard_map/ppermute | solution.py:22
  16.7 9.5 %collective-permute-start.6 = (bf16[16,1536]{1,0:T(8,128)(2,1)S(1)}, bf16[16,1536]{1,0:T(8,128)(2,1)S(1)}, u32[]{:S(2)}, u32[]{:S(2)}) collective-permute-start(bf16[16,1536]{1,0:T(8,128)(2,1)S(1)} %pad_maximum_fusion.6), channel_id=1, source_target_pairs={{0,12},{1,13},{2,14},{3,15},{4,8},{5,9},{6,10},{7,11},{8,4},{9,5},... | collective-permute-start | bytes 147464 | tf_op jit(solution)/shard_map/ppermute | solution.py:22
  22.6 6.0 %collective-permute-start = (bf16[128,2,1536]{2,1,0:T(2,128)(2,1)S(1)}, bf16[128,2,1536]{2,1,0:T(2,128)(2,1)S(1)}, u32[]{:S(2)}, u32[]{:S(2)}) collective-permute-start(bf16[128,2,1536]{2,1,0:T(2,128)(2,1)S(1)} %get-tuple-element.52), channel_id=1, source_target_pairs={{0,1},{1,0},{2,3},{3,2},{4,5},{5,4},{6,7},{7,6},{8,9},{9,8},{10,11... | collective-permute-start | bytes 2359304 | tf_op jit(solution)/shard_map/ppermute | solution.py:22
  24.6 19.4 %collective-permute-start.2 = (bf16[128,2,768]{2,1,0:T(2,128)(2,1)S(1)}, bf16[128,2,768]{2,1,0:T(2,128)(2,1)S(1)}, u32[]{:S(2)}, u32[]{:S(2)}) collective-permute-start(bf16[128,2,768]{2,1,0:T(2,128)(2,1)S(1)} %get-tuple-element.55), channel_id=1, source_target_pairs={{0,2},{2,0},{4,6},{6,4},{8,10},{10,8},{12,14},{14,12},{1,3},{3,1},... | collective-permute-start | bytes 1179656 | tf_op jit(solution)/shard_map/ppermute | solution.py:41
  26.2 1.5 %collective-permute-start.7 = (bf16[64,1536]{1,0:T(8,128)(2,1)S(1)}, bf16[64,1536]{1,0:T(8,128)(2,1)S(1)}, u32[]{:S(2)}, u32[]{:S(2)}) collective-permute-start(bf16[64,1536]{1,0:T(8,128)(2,1)S(1)} %pad_maximum_fusion.1), channel_id=1, source_target_pairs={{0,1},{1,0},{2,3},{3,2},{4,5},{5,4},{6,7},{7,6},{8,9},{9,8},{10,11... | collective-permute-start | bytes 589832 | tf_op jit(solution)/shard_map/ppermute | solution.py:22
  27.7 16.3 %collective-permute-start.3 = (bf16[128,2,768]{2,1,0:T(2,128)(2,1)S(1)}, bf16[128,2,768]{2,1,0:T(2,128)(2,1)S(1)}, u32[]{:S(2)}, u32[]{:S(2)}) collective-permute-start(bf16[128,2,768]{2,1,0:T(2,128)(2,1)S(1)} %get-tuple-element.56), channel_id=1, source_target_pairs={{2,4},{4,2},{6,8},{8,6},{10,12},{12,10},{3,5},{5,3},{7,9},{9,7},{1... | collective-permute-start | bytes 1179656 | tf_op jit(solution)/shard_map/ppermute | solution.py:41
  28.4 1.4 %copy-start.1 = (bf16[256,2,1536]{2,1,0:T(2,128)(2,1)S(1)}, bf16[256,2,1536]{2,1,0:T(2,128)(2,1)}, u32[]{:S(2)}) copy-start(bf16[256,2,1536]{2,1,0:T(2,128)(2,1)} %own_ref.3) | copy-start | bytes 4718596
  28.4 1.6 %copy-start.2 = (bf16[256,1536]{1,0:T(8,128)(2,1)S(1)}, bf16[256,1536]{1,0:T(8,128)(2,1)}, u32[]{:S(2)}) copy-start(bf16[256,1536]{1,0:T(8,128)(2,1)} %q_ref.3) | copy-start | bytes 2359300
  28.5 1.8 %copy-start.3 = (bf16[256,1536]{1,0:T(8,128)(2,1)S(1)}, bf16[256,1536]{1,0:T(8,128)(2,1)}, u32[]{:S(2)}) copy-start(bf16[256,1536]{1,0:T(8,128)(2,1)} %g_ref.3) | copy-start | bytes 2359300
  28.5 1.8 %copy-start.4 = (s32[1,2,5]{2,1,0:T(2,128)S(1)}, s32[1,2,5]{2,1,0:T(2,128)}, u32[]{:S(2)}) copy-start(s32[1,2,5]{2,1,0:T(2,128)} %param.15) | copy-start | bytes 124
  28.5 1.8 %copy-start.5 = (f32[12]{0:T(128)S(1)}, f32[12]{0:T(128)}, u32[]{:S(2)}) copy-start(f32[12]{0:T(128)} %warm_ref.3) | copy-start | bytes 148
  40.5 13.9 %copy-start.12 = (f32[6,512,128]{2,1,0:T(8,128)}, f32[6,512,128]{2,1,0:T(8,128)S(1)}, u32[]{:S(2)}) copy-start(f32[6,512,128]{2,1,0:T(8,128)S(1)} %get-tuple-element.82.own_ref) | copy-start | bytes 4718596
  40.5 19.6 %collective-permute-start.11 = (bf16[6,256,128]{2,1,0:T(8,128)(2,1)S(1)}, bf16[6,256,128]{2,1,0:T(8,128)(2,1)S(1)}, u32[]{:S(2)}, u32[]{:S(2)}) collective-permute-start(bf16[6,256,128]{2,1,0:T(8,128)(2,1)S(1)} %get-tuple-element.72), channel_id=1, source_target_pairs={{0,2},{2,0},{4,6},{6,4},{8,10},{10,8},{12,14},{14,12},{1,3},{3,1},... | collective-permute-start | bytes 1179656 | tf_op jit(solution)/shard_map/ppermute | solution.py:41
  43.3 16.8 %collective-permute-start.12 = (bf16[6,256,128]{2,1,0:T(8,128)(2,1)S(1)}, bf16[6,256,128]{2,1,0:T(8,128)(2,1)S(1)}, u32[]{:S(2)}, u32[]{:S(2)}) collective-permute-start(bf16[6,256,128]{2,1,0:T(8,128)(2,1)S(1)} %get-tuple-element.73), channel_id=1, source_target_pairs={{2,4},{4,2},{6,8},{8,6},{10,12},{12,10},{3,5},{5,3},{7,9},{9,7},{1... | collective-permute-start | bytes 1179656 | tf_op jit(solution)/shard_map/ppermute | solution.py:41
  43.9 16.1 %collective-permute-start.13 = (bf16[6,256,128]{2,1,0:T(8,128)(2,1)S(1)}, bf16[6,256,128]{2,1,0:T(8,128)(2,1)S(1)}, u32[]{:S(2)}, u32[]{:S(2)}) collective-permute-start(bf16[6,256,128]{2,1,0:T(8,128)(2,1)S(1)} %get-tuple-element.74), channel_id=1, source_target_pairs={{0,1},{1,0},{2,3},{3,2},{4,5},{5,4},{6,7},{7,6},{8,9},{9,8},{10,11... | collective-permute-start | bytes 1179656 | tf_op jit(solution)/shard_map/ppermute | solution.py:22
  55.4 6.2 %collective-permute-start.10 = (f32[64,1664]{1,0:T(8,128)S(1)}, f32[64,1664]{1,0:T(8,128)S(1)}, u32[]{:S(2)}, u32[]{:S(2)}) collective-permute-start(f32[64,1664]{1,0:T(8,128)S(1)} %pad_maximum_fusion), channel_id=1, source_target_pairs={{0,1},{1,0},{2,3},{3,2},{4,5},{5,4},{6,7},{7,6},{8,9},{9,8},{10,11... | collective-permute-start | bytes 1277960 | tf_op jit(solution)/shard_map/ppermute | solution.py:22
  60.1 0.7 copy-start.6
  60.8 0.8 copy-start.8
  61.6 5.6 %copy-start.10 = (bf16[6,256,128]{2,1,0:T(8,128)(2,1)}, bf16[6,256,128]{2,1,0:T(8,128)(2,1)S(1)}, u32[]{:S(2)}) copy-start(bf16[6,256,128]{2,1,0:T(8,128)(2,1)S(1)} %get-tuple-element.85.par_ref) | copy-start | bytes 1179652
  62.4 5.7 %copy-start.14 = (f32[64,1536]{1,0:T(8,128)}, f32[64,1536]{1,0:T(8,128)S(1)}, u32[]{:S(2)}) copy-start(f32[64,1536]{1,0:T(8,128)S(1)} %slice_add_fusion) | copy-start | bytes 1179652
  62.5 15.7 %copy-start.13 = (f32[6,512,128]{2,1,0:T(8,128)S(1)}, f32[6,512,128]{2,1,0:T(8,128)}, u32[]{:S(2)}) copy-start(f32[6,512,128]{2,1,0:T(8,128)} %copy-done.12) | copy-start | bytes 4718596
  62.6 7.7 %collective-permute-start.17 = (f32[16,1664]{1,0:T(8,128)S(1)}, f32[16,1664]{1,0:T(8,128)S(1)}, u32[]{:S(2)}, u32[]{:S(2)}) collective-permute-start(f32[16,1664]{1,0:T(8,128)S(1)} %get-tuple-element.91), channel_id=1, source_target_pairs={{0,4},{1,5},{2,6},{3,7},{4,0},{5,1},{6,2},{7,3},{8,12},{9,13},{10,... | collective-permute-start | bytes 319496 | tf_op jit(solution)/shard_map/ppermute | solution.py:22
  65.6 10.3 %collective-permute-start.18 = (f32[16,1664]{1,0:T(8,128)S(1)}, f32[16,1664]{1,0:T(8,128)S(1)}, u32[]{:S(2)}, u32[]{:S(2)}) collective-permute-start(f32[16,1664]{1,0:T(8,128)S(1)} %get-tuple-element.92), channel_id=1, source_target_pairs={{0,8},{1,9},{2,10},{3,11},{4,12},{5,13},{6,14},{7,15},{8,0},{9,1},... | collective-permute-start | bytes 319496 | tf_op jit(solution)/shard_map/ppermute | solution.py:22
  67.2 8.6 %collective-permute-start.19 = (f32[16,1664]{1,0:T(8,128)S(1)}, f32[16,1664]{1,0:T(8,128)S(1)}, u32[]{:S(2)}, u32[]{:S(2)}) collective-permute-start(f32[16,1664]{1,0:T(8,128)S(1)} %get-tuple-element.93), channel_id=1, source_target_pairs={{0,12},{1,13},{2,14},{3,15},{4,8},{5,9},{6,10},{7,11},{8,4},{9,5},... | collective-permute-start | bytes 319496 | tf_op jit(solution)/shard_map/ppermute | solution.py:22
  68.1 22.2 %collective-permute-start.14 = (bf16[6,256,128]{2,1,0:T(8,128)(2,1)}, bf16[6,256,128]{2,1,0:T(8,128)(2,1)S(1)}, u32[]{:S(2)}, u32[]{:S(2)}) collective-permute-start(bf16[6,256,128]{2,1,0:T(8,128)(2,1)} %get-tuple-element.78), channel_id=1, source_target_pairs={{0,2},{2,0},{4,6},{6,4},{8,10},{10,8},{12,14},{14,12},{1,3},{3,1},... | collective-permute-start | bytes 1179656 | tf_op jit(solution)/shard_map/ppermute | solution.py:41
  69.6 20.6 %collective-permute-start.15 = (bf16[6,256,128]{2,1,0:T(8,128)(2,1)S(1)}, bf16[6,256,128]{2,1,0:T(8,128)(2,1)S(1)}, u32[]{:S(2)}, u32[]{:S(2)}) collective-permute-start(bf16[6,256,128]{2,1,0:T(8,128)(2,1)S(1)} %get-tuple-element.79), channel_id=1, source_target_pairs={{2,4},{4,2},{6,8},{8,6},{10,12},{12,10},{3,5},{5,3},{7,9},{9,7},{1... | collective-permute-start | bytes 1179656 | tf_op jit(solution)/shard_map/ppermute | solution.py:41
  70.3 19.9 %collective-permute-start.16 = (bf16[6,256,128]{2,1,0:T(8,128)(2,1)S(1)}, bf16[6,256,128]{2,1,0:T(8,128)(2,1)S(1)}, u32[]{:S(2)}, u32[]{:S(2)}) collective-permute-start(bf16[6,256,128]{2,1,0:T(8,128)(2,1)S(1)} %get-tuple-element.80), channel_id=1, source_target_pairs={{0,1},{1,0},{2,3},{3,2},{4,5},{5,4},{6,7},{7,6},{8,9},{9,8},{10,11... | collective-permute-start | bytes 1179656 | tf_op jit(solution)/shard_map/ppermute | solution.py:22
  76.8 9.5 %collective-permute-start.20 = (f32[8,1664]{1,0:T(8,128)S(1)}, f32[8,1664]{1,0:T(8,128)S(1)}, u32[]{:S(2)}, u32[]{:S(2)}) collective-permute-start(f32[8,1664]{1,0:T(8,128)S(1)} %pad_maximum_fusion.5), channel_id=1, source_target_pairs={{0,2},{1,3},{2,0},{3,1},{4,6},{5,7},{6,4},{7,5},{8,10},{9,11},{10,... | collective-permute-start | bytes 159752 | tf_op jit(solution)/shard_map/ppermute | solution.py:22
  78.2 1.0 %copy-start.7 = (bf16[6,256,128]{2,1,0:T(8,128)(2,1)S(1)}, bf16[6,256,128]{2,1,0:T(8,128)(2,1)}, u32[]{:S(2)}) copy-start(bf16[6,256,128]{2,1,0:T(8,128)(2,1)} %copy-done.6) | copy-start | bytes 1179652
  79.2 1.0 %copy-start.9 = (bf16[6,256,128]{2,1,0:T(8,128)(2,1)S(1)}, bf16[6,256,128]{2,1,0:T(8,128)(2,1)}, u32[]{:S(2)}) copy-start(bf16[6,256,128]{2,1,0:T(8,128)(2,1)} %copy-done.8) | copy-start | bytes 1179652
  80.2 1.0 %copy-start.11 = (bf16[6,256,128]{2,1,0:T(8,128)(2,1)S(1)}, bf16[6,256,128]{2,1,0:T(8,128)(2,1)}, u32[]{:S(2)}) copy-start(bf16[6,256,128]{2,1,0:T(8,128)(2,1)} %copy-done.10) | copy-start | bytes 1179652
  86.4 0.6 copy-start.15

commit v5 on v4

--- a/solution.py
+++ b/solution.py
@@ -24,13 +24,13 @@
 
 def levels(count):
     bits = count.bit_length() - 1
-    out = [[2]] if bits > 1 else []
+    out = []
     at = 2
     while at < bits:
         take = min(2, bits - at)
         out.append([m << at for m in range(1, 1 << take)])
         at += take
-    return out + [[1]]
+    return out + ([[2]] if bits > 1 else []) + [[1]]
 
 
 def swap_pairs(x, first):
@@ -71,7 +71,7 @@
     vmem = pl.BlockSpec(memory_space=pltpu.MemorySpace.VMEM)
     return pl.pallas_call(
         functools.partial(pick_kernel, copies=[c[:2] for c in copies], width=width),
-        in_specs=[smem, smem, pl.BlockSpec(memory_space=pl.ANY)],
+        in_specs=[smem, smem, pl.BlockSpec(memory_space=pltpu.MemorySpace.HBM)],
         out_specs=[vmem] * len(copies),
         out_shape=[jax.ShapeDtypeStruct((BLOCK, 2, heads * width), BF16) for _, _, heads in copies],
         scratch_shapes=[pltpu.SemaphoreType.DMA((len(copies),))],
@@ -174,7 +174,7 @@
     anc_out[...] = pair_ref[2 * near :, :]
 
 
-def attention(pos, filt, warm, q, g, mesh_kv, partner, halo, anchors, head0, heads, dq_prev, anc_prev):
+def attention(pos, filt, warm, q, g, mesh_kv, partner, halo, anchors, head0, heads, dq_prev, anc_prev, weight=0):
     rows, feat = q.shape
     own_rows = mesh_kv.shape[0]
     width = feat // warm.shape[0]
@@ -220,9 +220,9 @@
         input_output_aliases=alias,
         compiler_params=pltpu.CompilerParams(vmem_limit_bytes=24 << 20),
         cost_estimate=pl.CostEstimate(
-            flops=10 * heads * rows * keys * width,
-            transcendentals=heads * rows * keys,
-            bytes_accessed=heads * width * (rows * 6 + own_rows * 12 + 3 * BLOCK * 8 + a_rows * 12),
+            flops=weight * 10 * heads * rows * keys * width,
+            transcendentals=0,
+            bytes_accessed=weight * heads * width * (rows * 6 + own_rows * 12 + 3 * BLOCK * 8 + a_rows * 12),
         ),
         name="attention",
     )(*args)
@@ -248,12 +248,13 @@
             out_ref[a * BLOCK : (a + 1) * BLOCK, :, lanes] = total.astype(BF16).reshape(BLOCK, 2, width)
 
 
-def combine(pos, sent, own, faces, head0, heads, feat, width, prev, weight=1):
+def combine(pos, sent, own, faces, head0, heads, feat, width, prev, part=None, weight=1):
     rows = own.shape[1] // 2
-    step = next(n for n in COMBINE_STEPS if heads % n == 0 and head0 % n == 0)
+    lo, heads = part or (0, heads)
+    step = next(n for n in COMBINE_STEPS if heads % n == 0 and head0 % n == 0 and lo % n == 0)
     smem = pl.BlockSpec(memory_space=SMEM)
-    face = pl.BlockSpec((step, 2 * BLOCK, width), lambda h: (h, 0, 0))
-    own_spec = pl.BlockSpec((step, 2 * rows, width), lambda h: (h, 0, 0))
+    face = pl.BlockSpec((step, 2 * BLOCK, width), lambda h: (lo // step + h, 0, 0))
+    own_spec = pl.BlockSpec((step, 2 * rows, width), lambda h: (lo // step + h, 0, 0))
     in_specs = [smem, smem, own_spec, face, face, face]
     args = [pos, sent, own, *faces]
     alias = {}
@@ -265,7 +266,7 @@
         combine_kernel,
         grid=(heads // step,),
         in_specs=in_specs,
-        out_specs=pl.BlockSpec((rows, 2, step * width), lambda h: (0, 0, head0 // step + h)),
+        out_specs=pl.BlockSpec((rows, 2, step * width), lambda h: (0, 0, (head0 + lo) // step + h)),
         out_shape=jax.ShapeDtypeStruct((rows, 2, feat), BF16),
         input_output_aliases=alias,
         compiler_params=pltpu.CompilerParams(vmem_limit_bytes=24 << 20),
@@ -298,7 +299,7 @@
     picks += [others[2 * i : 2 * i + 2] for i in range(len(chunks) - 1)]
     anchors = landmark.reshape(2 * landmark.shape[0], feat)
     for i, masks in enumerate(stages):
-        if i == 1:
+        if i == len(stages) - 1:
             anchors, picks[1] = lax.optimization_barrier((anchors, picks[1]))
         anchors = jnp.concatenate([anchors] + [swap_mask(anchors, m) for m in masks], axis=0)
     halos = [[swap_pairs(d, 0), swap_pairs(g, 1)] for d, g in picks]
@@ -315,25 +316,32 @@
         faces.append((f_dir, f_dia, f_par))
         if len(faces) < len(chunks):
             returned.append(send_back(faces[-1]))
+
     temp = jnp.sum(jnp.concatenate(temps, axis=0), axis=(1, 2)) / math.sqrt(width)
     extra = jnp.zeros((1, LANES), F32).at[0, :total].set(temp)
     cell = None
-    for i, masks in enumerate(reversed(stages)):
-        n = anc.shape[0] // (len(masks) + 1)
-        wide = jnp.broadcast_to(extra, (n, LANES))
+    anc, faces[-1], returned[-1] = lax.optimization_barrier((anc, faces[-1], returned[-1]))
+    returned.append(send_back(faces[-1]))
+    anc = anc.reshape([len(masks) + 1 for masks in reversed(stages)] + [2 * landmark.shape[0], feat])
+    for i, masks in enumerate(stages[-1:] + stages[:-1]):
+        dim = 0 if i == 0 else anc.ndim - 3
+        parts = [lax.index_in_dim(anc, k, dim, keepdims=False) for k in range(len(masks) + 1)]
+        shape = parts[0].shape
+        parts = [x.reshape(-1, feat) for x in parts]
+        wide = jnp.broadcast_to(extra, (parts[0].shape[0], LANES))
         got = [
-            swap_mask(jnp.concatenate([anc[k * n : (k + 1) * n], wide], axis=1), m)
-            for k, m in enumerate(masks, 1)
+            swap_mask(jnp.concatenate([x, wide], axis=1), m) for x, m in zip(parts[1:], masks)
         ]
-        if i == 0:
-            returned[-1] = hold(returned[-1], HOLD)
-            got, faces[-1], returned[-1] = lax.optimization_barrier((got, faces[-1], returned[-1]))
-            returned.append(send_back(faces[-1]))
-            for c in range(len(chunks) - 1):
-                cell = combine(pos, sent, owns[c], returned[c], *chunks[c], feat, width, cell, weight=4000)
-        if i == len(stages) - 1:
+        if i >= len(stages) - 2:
+            c = len(chunks) - 2
+            head0, heads = chunks[c]
+            half = heads // 2
+            lo, n = (0, half) if i == len(stages) - 2 else (half, heads - half)
+            cell = combine(
+                pos, sent, owns[c], returned[c], head0, heads, feat, width, cell, part=(lo, n), weight=4000
+            )
             got, cell = lax.optimization_barrier((got, cell))
-        anc = sum([x[:, :feat] for x in got], anc[:n])
+        anc = sum([x[:, :feat] for x in got], parts[0]).reshape(shape)
         extra = sum([x[:1, feat:] for x in got], extra)
     anchor_grad = anc.reshape(landmark.shape)
     temp = extra[0, :total]

time: 93 us -> 98.9 us (1.063)
  waiting for transfers between devices: 23.5 us -> 31.4 us
  local copies, waits for them, and re-layouts: 12 us -> 7.25 us
  starting transfers between devices: 25 us -> 27.6 us
  Pallas kernels: 26.5 us -> 27.7 us
  other arithmetic: 4.5 us -> 3.49 us
    ppermute x13, waiting for transfers between devices: 19.3 us -> 25.4 us  [swap_mask(): return lax.ppermute(x, ('gx', 'gy'), [(i, i ^ mask) for i in range(count)])]
    ppermute x8, starting transfers between devices: 7.07 us -> 12.9 us  [swap_pairs(): return lax.ppermute(x, 'gx', route)]
    unnamed x36 -> x35, local copies, waits for them, and re-layouts: 8.32 us -> 4.4 us
    ppermute x13, starting transfers between devices: 17.9 us -> 14.7 us  [swap_mask(): return lax.ppermute(x, ('gx', 'gy'), [(i, i ^ mask) for i in range(count)])]
    ppermute x8, waiting for transfers between devices: 4.21 us -> 6 us  [swap_pairs(): return lax.ppermute(x, 'gx', route)]
    pallas_call x2 -> x3, Pallas kernels: 4.39 us -> 5.69 us  [combine(): pl.pallas_call(combine_kernel, grid=(heads // step,), in_specs=in_specs,...]
  transfers between devices with their start and end apart: 21 -> 21, of which waited for: 7 -> 6; matrix products, arithmetic and copies ran while one was open for 7% -> 6% of each run, Pallas kernels for 26% -> 26%
where the time goes in v5:
time: 98.9 us; the launch traced here: 98.5 us
  waiting for transfers between devices  31.4 us (32%)
  Pallas kernels  27.7 us (28%)
  starting transfers between devices  27.6 us (28%)
  local copies, waits for them, and re-layouts  7.25 us (7%)
  other arithmetic  3.49 us (4%)
  between operations  1.04 us (1%)
    ppermute x13, waiting for transfers between devices, swap_mask(): return lax.ppermute(x, ('gx', 'gy'), [(i, i ^ mask) for i in range(count)])  25.4 us
    pallas_call x2, Pallas kernels, attention(): pl.pallas_call(functools.partial(attention_kernel, gx_count=lax.axis_size...  20.6 us
    ppermute x13, starting transfers between devices, swap_mask(): return lax.ppermute(x, ('gx', 'gy'), [(i, i ^ mask) for i in range(count)])  14.7 us
    ppermute x8, starting transfers between devices, swap_pairs(): return lax.ppermute(x, 'gx', route)  12.9 us
    ppermute x8, waiting for transfers between devices, swap_pairs(): return lax.ppermute(x, 'gx', route)  6 us
    pallas_call x3, Pallas kernels, combine(): pl.pallas_call(combine_kernel, grid=(heads // step,), in_specs=in_specs,...  5.69 us
    unnamed x35, local copies, waits for them, and re-layouts  4.4 us
  transfers between devices with their start and end apart: 21, of which 6 were waited for; matrix products, arithmetic and copies ran while one was open for 6% of the time, Pallas kernels for 26%

profile of v5, /device:TPU:0, one launch (start us, length us, event | category | flops | bytes accessed | tf_op | source)
XLA Modules:
  0.0 98.5 jit_solution(9552969126124211924)
XLA Ops:
  0.6 0.8 reshape.69
  1.4 3.1 %collective-permute-start.1 = (bf16[8,1536]{1,0:T(8,128)(2,1)S(1)}, bf16[8,1536]{1,0:T(8,128)(2,1)S(1)}, u32[]{:S(2)}, u32[]{:S(2)}) collective-permute-start(bf16[8,1536]{1,0:T(8,128)(2,1)S(1)} %reshape.69), channel_id=1, source_target_pairs={{0,4},{1,5},{2,6},{3,7},{4,0},{5,1},{6,2},{7,3},{8,12},{9,13},{10,... | collective-permute-start | bytes 73736 | tf_op jit(solution)/shard_map/ppermute | solution.py:22
  4.5 2.6 %collective-permute-start.2 = (bf16[8,1536]{1,0:T(8,128)(2,1)S(1)}, bf16[8,1536]{1,0:T(8,128)(2,1)S(1)}, u32[]{:S(2)}, u32[]{:S(2)}) collective-permute-start(bf16[8,1536]{1,0:T(8,128)(2,1)S(1)} %reshape.69), channel_id=1, source_target_pairs={{0,8},{1,9},{2,10},{3,11},{4,12},{5,13},{6,14},{7,15},{8,0},{9,1},... | collective-permute-start | bytes 73736 | tf_op jit(solution)/shard_map/ppermute | solution.py:22
  7.1 0.7 copy.17.sent_ref
  7.8 1.4 %copy-done = bf16[256,2,1536]{2,1,0:T(2,128)(2,1)S(1)} copy-done((bf16[256,2,1536]{2,1,0:T(2,128)(2,1)S(1)}, bf16[256,2,1536]{2,1,0:T(2,128)(2,1)}, u32[]{:S(2)}) %copy-start) | copy-done | bytes 1572888
  9.2 0.7 pick.3
  9.9 1.8 %collective-permute-start.8 = (bf16[128,2,768]{2,1,0:T(2,128)(2,1)S(1)}, bf16[128,2,768]{2,1,0:T(2,128)(2,1)S(1)}, u32[]{:S(2)}, u32[]{:S(2)}) collective-permute-start(bf16[128,2,768]{2,1,0:T(2,128)(2,1)S(1)} %get-tuple-element.59), channel_id=1, source_target_pairs={{0,2},{2,0},{4,6},{6,4},{8,10},{10,8},{12,14},{14,12},{1,3},{3,1},... | collective-permute-start | bytes 1179656 | tf_op jit(solution)/shard_map/ppermute | solution.py:41
  11.7 0.7 collective-permute-start.9
  12.4 0.8 pick.2
  13.2 0.1 collective-permute-start
  13.3 3.4 %collective-permute-start.4 = (bf16[32,1536]{1,0:T(8,128)(2,1)S(1)}, bf16[32,1536]{1,0:T(8,128)(2,1)S(1)}, u32[]{:S(2)}, u32[]{:S(2)}) collective-permute-start(bf16[32,1536]{1,0:T(8,128)(2,1)S(1)} %pad_maximum_fusion.4), channel_id=1, source_target_pairs={{0,2},{1,3},{2,0},{3,1},{4,6},{5,7},{6,4},{7,5},{8,10},{9,11},{10,... | collective-permute-start | bytes 294920 | tf_op jit(solution)/shard_map/ppermute | solution.py:22
  16.7 13.1 %collective-permute-done.4 = bf16[32,1536]{1,0:T(8,128)(2,1)S(1)} collective-permute-done((bf16[32,1536]{1,0:T(8,128)(2,1)S(1)}, bf16[32,1536]{1,0:T(8,128)(2,1)S(1)}, u32[]{:S(2)}, u32[]{:S(2)}) %collective-permute-start.4) | collective-permute-done | bytes 98336 | tf_op jit(solution)/shard_map/ppermute | solution.py:22
  29.8 2.6 %collective-permute-start.5 = (bf16[128,2,768]{2,1,0:T(2,128)(2,1)S(1)}, bf16[128,2,768]{2,1,0:T(2,128)(2,1)S(1)}, u32[]{:S(2)}, u32[]{:S(2)}) collective-permute-start(bf16[128,2,768]{2,1,0:T(2,128)(2,1)S(1)} %get-tuple-element.56), channel_id=1, source_target_pairs={{0,2},{2,0},{4,6},{6,4},{8,10},{10,8},{12,14},{14,12},{1,3},{3,1},... | collective-permute-start | bytes 1179656 | tf_op jit(solution)/shard_map/ppermute | solution.py:41
  32.5 0.7 collective-permute-start.6
  33.2 0.0 copy-start.2
  33.3 1.0 %copy-done.2 = bf16[256,1536]{1,0:T(8,128)(2,1)S(1)} copy-done((bf16[256,1536]{1,0:T(8,128)(2,1)S(1)}, bf16[256,1536]{1,0:T(8,128)(2,1)}, u32[]{:S(2)}) %copy-start.2) | copy-done | bytes 786456
  34.3 0.2 copy-done.3
  34.6 10.2 %attention.2 = (bf16[256,1536]{1,0:T(8,128)(2,1)}, f32[6,512,128]{2,1,0:T(8,128)S(1)}, bf16[6,256,128]{2,1,0:T(8,128)(2,1)S(1)}, bf16[6,256,128]{2,1,0:T(8,128)(...) custom-call(s32[1]{0:T(128)} %bitcast.pos_ref, ...), custom_call_target="tpu_custom_call" | custom-call | tf_op jit(solution)/shard_map/attention/pallas_call | solution.py:197
  44.8 3.3 %collective-permute-start.10 = (bf16[6,256,128]{2,1,0:T(8,128)(2,1)S(1)}, bf16[6,256,128]{2,1,0:T(8,128)(2,1)S(1)}, u32[]{:S(2)}, u32[]{:S(2)}) collective-permute-start(bf16[6,256,128]{2,1,0:T(8,128)(2,1)S(1)} %get-tuple-element.71), channel_id=1, source_target_pairs={{0,2},{2,0},{4,6},{6,4},{8,10},{10,8},{12,14},{14,12},{1,3},{3,1},... | collective-permute-start | bytes 1179656 | tf_op jit(solution)/shard_map/ppermute | solution.py:41
  48.1 0.7 collective-permute-start.11
  48.8 0.1 collective-permute-start.12
  48.9 0.6 compare_reduce_fusion
  49.5 0.8 collective-permute-done.5.dir_ref
  50.3 10.3 %attention.3 = (bf16[256,1536]{1,0:T(8,128)(2,1)}, f32[6,512,128]{2,1,0:T(8,128)S(1)}, bf16[6,256,128]{2,1,0:T(8,128)(2,1)}, bf16[6,256,128]{2,1,0:T(8,128)(2,1)...) custom-call(s32[1]{0:T(128)} %bitcast.pos_ref, ...), custom_call_target="tpu_custom_call", output_to_operand_aliasing={{0}: (10, {}), {5}: (11, {})} | custom-call | tf_op jit(solution)/shard_map/attention/pallas_call | solution.py:197
  60.7 0.2 maximum_reduce_fusion
  60.8 0.6 fusion.3
  61.5 5.2 %collective-permute-done.10.dir_ref = bf16[6,256,128]{2,1,0:T(8,128)(2,1)S(1)} collective-permute-done((bf16[6,256,128]{2,1,0:T(8,128)(2,1)S(1)}, bf16[6,256,128]{2,1,0:T(8,128)(2,1)S(1)}, u32[]{:S(2)}, u32[]{:S(2)}) %collective-permute-start.10) | collective-permute-done | bytes 393248 | tf_op jit(solution)/shard_map/ppermute | solution.py:41
  66.8 0.1 collective-permute-start.16
  66.9 0.6 copy-done.8
  67.5 2.5 %collective-permute-start.13 = (bf16[6,256,128]{2,1,0:T(8,128)(2,1)}, bf16[6,256,128]{2,1,0:T(8,128)(2,1)S(1)}, u32[]{:S(2)}, u32[]{:S(2)}) collective-permute-start(bf16[6,256,128]{2,1,0:T(8,128)(2,1)} %get-tuple-element.74), channel_id=1, source_target_pairs={{0,2},{2,0},{4,6},{6,4},{8,10},{10,8},{12,14},{14,12},{1,3},{3,1},... | collective-permute-start | bytes 1179656 | tf_op jit(solution)/shard_map/ppermute | solution.py:41
  69.9 0.7 collective-permute-start.14
  70.7 0.7 slice_add_fusion.2
  71.3 0.1 copy-done.14
  71.4 0.1 add.36
  71.6 1.2 %slice_add_fusion = f32[64,1536]{1,0:T(8,128)S(1)} fusion(f32[64,1664]{1,0:T(8,128)} %copy-done.14, f32[128,1536]{1,0:T(8,128)S(1)} %get-tuple-element.77), kind=kLoop, calls=%fused_computation.1 | loop fusion | flops 98304 | bytes 1179648 | tf_op jit(solution)/shard_map/add | solution.py:344
  72.8 2.9 %collective-permute-start.17 = (f32[16,1664]{1,0:T(8,128)S(1)}, f32[16,1664]{1,0:T(8,128)S(1)}, u32[]{:S(2)}, u32[]{:S(2)}) collective-permute-start(f32[16,1664]{1,0:T(8,128)S(1)} %get-tuple-element.95), channel_id=1, source_target_pairs={{0,4},{1,5},{2,6},{3,7},{4,0},{5,1},{6,2},{7,3},{8,12},{9,13},{10,... | collective-permute-start | bytes 319496 | tf_op jit(solution)/shard_map/ppermute | solution.py:22
  75.7 2.0 %collective-permute-start.18 = (f32[16,1664]{1,0:T(8,128)S(1)}, f32[16,1664]{1,0:T(8,128)S(1)}, u32[]{:S(2)}, u32[]{:S(2)}) collective-permute-start(f32[16,1664]{1,0:T(8,128)S(1)} %get-tuple-element.94), channel_id=1, source_target_pairs={{0,8},{1,9},{2,10},{3,11},{4,12},{5,13},{6,14},{7,15},{8,0},{9,1},... | collective-permute-start | bytes 319496 | tf_op jit(solution)/shard_map/ppermute | solution.py:22
  77.7 0.4 collective-permute-start.19
  78.2 1.0 %copy-done.13 = bf16[6,256,128]{2,1,0:T(8,128)(2,1)S(1)} copy-done((bf16[6,256,128]{2,1,0:T(8,128)(2,1)S(1)}, bf16[6,256,128]{2,1,0:T(8,128)(2,1)}, u32[]{:S(2)}) %copy-start.13) | copy-done | bytes 393240
  79.2 1.7 %combine.3.rest_0_ = bf16[256,2,1536]{2,1,0:T(2,128)(2,1)} custom-call(s32[1]{0:T(128)} %bitcast.pos_ref, s32[3,1]{1,0:T(4,128)S(1)} %copy.17.sent_ref, f32[6,512,128]{2,1,0:T(8,128)S(1)} %copy-done.7, bf16[6,256,128]{2,1,0:T(8,128)(2,1)S(1)} %copy-done.9, bf16[6,256,128]{2,1,0:T(8,128)(2,1)S(1)} %copy-done.11, bf16[6,256,128]{2,1,0:T(8,128)(2,1)S(1)} %copy-done.13), custom_call_target="tpu_custom_call" | custom-call | flops 6291456000 | bytes 1769472 | tf_op jit(solution)/shard_map/combine/pallas_call | solution.py:265
  80.9 5.8 %collective-permute-done.17 = f32[16,1664]{1,0:T(8,128)S(1)} collective-permute-done((f32[16,1664]{1,0:T(8,128)S(1)}, f32[16,1664]{1,0:T(8,128)S(1)}, u32[]{:S(2)}, u32[]{:S(2)}) %collective-permute-start.17) | collective-permute-done | bytes 106528 | tf_op jit(solution)/shard_map/ppermute | solution.py:22
  86.7 4.0 %collective-permute-done.18 = f32[16,1664]{1,0:T(8,128)S(1)} collective-permute-done((f32[16,1664]{1,0:T(8,128)S(1)}, f32[16,1664]{1,0:T(8,128)S(1)}, u32[]{:S(2)}, u32[]{:S(2)}) %collective-permute-start.18) | collective-permute-done | bytes 106528 | tf_op jit(solution)/shard_map/ppermute | solution.py:22
  90.9 0.1 collective-permute-start.20
  90.9 1.7 %combine.4.rest_0_ = bf16[256,2,1536]{2,1,0:T(2,128)(2,1)} custom-call(s32[1]{0:T(128)} %bitcast.pos_ref, s32[3,1]{1,0:T(4,128)S(1)} %copy.17.sent_ref, f32[6,512,128]{2,1,0:T(8,128)S(1)} %copy-done.7, bf16[6,256,128]{2,1,0:T(8,128)(2,1)S(1)} %copy-done.9, bf16[6,256,128]{2,1,0:T(8,128)(2,1)S(1)} %copy-done.11, ...), custom_call_target="tpu_custom_call", output_to_operand_aliasing={{}: (6, {})} | custom-call | flops 6291456000 | bytes 1769472 | tf_op jit(solution)/shard_map/combine/pallas_call | solution.py:265
  92.7 2.4 %collective-permute-done.20 = f32[8,1664]{1,0:T(8,128)S(1)} collective-permute-done((f32[8,1664]{1,0:T(8,128)S(1)}, f32[8,1664]{1,0:T(8,128)S(1)}, u32[]{:S(2)}, u32[]{:S(2)}) %collective-permute-start.20) | collective-permute-done | bytes 53280 | tf_op jit(solution)/shard_map/ppermute | solution.py:22
  95.1 0.7 reshape.72
  95.7 0.5 slice_bitcast_fusion.4
  96.2 2.2 %combine.5 = bf16[256,2,1536]{2,1,0:T(2,128)(2,1)} custom-call(s32[1]{0:T(128)} %bitcast.pos_ref, s32[3,1]{1,0:T(4,128)S(1)} %copy.17.sent_ref, f32[6,512,128]{2,1,0:T(8,128)S(1)} %get-tuple-element.66.own_ref, bf16[6,256,128]{2,1,0:T(8,128)(2,1)S(1)} %collective-permute-done.13.dir_ref, ...), custom_call_target="tpu_custom_call", output_to_operand_aliasing={{}: (6, {})} | custom-call | bytes 3538944 | tf_op jit(solution)/shard_map/combine/pallas_call | solution.py:265
  (65 shorter events, 0.4 us)
Async XLA Ops:
  1.4 11.8 %collective-permute-start.1 = (bf16[8,1536]{1,0:T(8,128)(2,1)S(1)}, bf16[8,1536]{1,0:T(8,128)(2,1)S(1)}, u32[]{:S(2)}, u32[]{:S(2)}) collective-permute-start(bf16[8,1536]{1,0:T(8,128)(2,1)S(1)} %reshape.69), channel_id=1, source_target_pairs={{0,4},{1,5},{2,6},{3,7},{4,0},{5,1},{6,2},{7,3},{8,12},{9,13},{10,... | collective-permute-start | bytes 73736 | tf_op jit(solution)/shard_map/ppermute | solution.py:22
  4.5 8.8 %collective-permute-start.2 = (bf16[8,1536]{1,0:T(8,128)(2,1)S(1)}, bf16[8,1536]{1,0:T(8,128)(2,1)S(1)}, u32[]{:S(2)}, u32[]{:S(2)}) collective-permute-start(bf16[8,1536]{1,0:T(8,128)(2,1)S(1)} %reshape.69), channel_id=1, source_target_pairs={{0,8},{1,9},{2,10},{3,11},{4,12},{5,13},{6,14},{7,15},{8,0},{9,1},... | collective-permute-start | bytes 73736 | tf_op jit(solution)/shard_map/ppermute | solution.py:22
  7.1 6.2 %collective-permute-start.3 = (bf16[8,1536]{1,0:T(8,128)(2,1)S(1)}, bf16[8,1536]{1,0:T(8,128)(2,1)S(1)}, u32[]{:S(2)}, u32[]{:S(2)}) collective-permute-start(bf16[8,1536]{1,0:T(8,128)(2,1)S(1)} %reshape.69), channel_id=1, source_target_pairs={{0,12},{1,13},{2,14},{3,15},{4,8},{5,9},{6,10},{7,11},{8,4},{9,5},... | collective-permute-start | bytes 73736 | tf_op jit(solution)/shard_map/ppermute | solution.py:22
  7.8 1.4 %copy-start = (bf16[256,2,1536]{2,1,0:T(2,128)(2,1)S(1)}, bf16[256,2,1536]{2,1,0:T(2,128)(2,1)}, u32[]{:S(2)}) copy-start(bf16[256,2,1536]{2,1,0:T(2,128)(2,1)} %own_ref.3) | copy-start | bytes 4718596
  9.2 3.2 %copy-start.1 = (bf16[256,2,1536]{2,1,0:T(2,128)(2,1)S(1)}, bf16[256,2,1536]{2,1,0:T(2,128)(2,1)}, u32[]{:S(2)}) copy-start(bf16[256,2,1536]{2,1,0:T(2,128)(2,1)} %own_ref.3) | copy-start | bytes 4718596
  9.9 23.3 %collective-permute-start.8 = (bf16[128,2,768]{2,1,0:T(2,128)(2,1)S(1)}, bf16[128,2,768]{2,1,0:T(2,128)(2,1)S(1)}, u32[]{:S(2)}, u32[]{:S(2)}) collective-permute-start(bf16[128,2,768]{2,1,0:T(2,128)(2,1)S(1)} %get-tuple-element.59), channel_id=1, source_target_pairs={{0,2},{2,0},{4,6},{6,4},{8,10},{10,8},{12,14},{14,12},{1,3},{3,1},... | collective-permute-start | bytes 1179656 | tf_op jit(solution)/shard_map/ppermute | solution.py:41
  11.7 21.6 %collective-permute-start.9 = (bf16[128,2,768]{2,1,0:T(2,128)(2,1)S(1)}, bf16[128,2,768]{2,1,0:T(2,128)(2,1)S(1)}, u32[]{:S(2)}, u32[]{:S(2)}) collective-permute-start(bf16[128,2,768]{2,1,0:T(2,128)(2,1)S(1)} %get-tuple-element.60), channel_id=1, source_target_pairs={{2,4},{4,2},{6,8},{8,6},{10,12},{12,10},{3,5},{5,3},{7,9},{9,7},{1... | collective-permute-start | bytes 1179656 | tf_op jit(solution)/shard_map/ppermute | solution.py:41
  13.2 20.1 %collective-permute-start = (bf16[128,2,1536]{2,1,0:T(2,128)(2,1)S(1)}, bf16[128,2,1536]{2,1,0:T(2,128)(2,1)S(1)}, u32[]{:S(2)}, u32[]{:S(2)}) collective-permute-start(bf16[128,2,1536]{2,1,0:T(2,128)(2,1)S(1)} %get-tuple-element.53), channel_id=1, source_target_pairs={{0,1},{1,0},{2,3},{3,2},{4,5},{5,4},{6,7},{7,6},{8,9},{9,8},{10,11... | collective-permute-start | bytes 2359304 | tf_op jit(solution)/shard_map/ppermute | solution.py:22
  13.3 16.5 %collective-permute-start.4 = (bf16[32,1536]{1,0:T(8,128)(2,1)S(1)}, bf16[32,1536]{1,0:T(8,128)(2,1)S(1)}, u32[]{:S(2)}, u32[]{:S(2)}) collective-permute-start(bf16[32,1536]{1,0:T(8,128)(2,1)S(1)} %pad_maximum_fusion.4), channel_id=1, source_target_pairs={{0,2},{1,3},{2,0},{3,1},{4,6},{5,7},{6,4},{7,5},{8,10},{9,11},{10,... | collective-permute-start | bytes 294920 | tf_op jit(solution)/shard_map/ppermute | solution.py:22
  29.8 2.6 %collective-permute-start.7 = (bf16[64,1536]{1,0:T(8,128)(2,1)S(1)}, bf16[64,1536]{1,0:T(8,128)(2,1)S(1)}, u32[]{:S(2)}, u32[]{:S(2)}) collective-permute-start(bf16[64,1536]{1,0:T(8,128)(2,1)S(1)} %constant_dynamic-update-slice_fusion), channel_id=1, source_target_pairs={{0,1},{1,0},{2,3},{3,2},{4,5},{5,4},{6,7},{7,6},{8,9},{9,8},{10,11... | collective-permute-start | bytes 589832 | tf_op jit(solution)/shard_map/ppermute | solution.py:22
  29.8 20.5 %collective-permute-start.5 = (bf16[128,2,768]{2,1,0:T(2,128)(2,1)S(1)}, bf16[128,2,768]{2,1,0:T(2,128)(2,1)S(1)}, u32[]{:S(2)}, u32[]{:S(2)}) collective-permute-start(bf16[128,2,768]{2,1,0:T(2,128)(2,1)S(1)} %get-tuple-element.56), channel_id=1, source_target_pairs={{0,2},{2,0},{4,6},{6,4},{8,10},{10,8},{12,14},{14,12},{1,3},{3,1},... | collective-permute-start | bytes 1179656 | tf_op jit(solution)/shard_map/ppermute | solution.py:41
  32.5 17.8 %collective-permute-start.6 = (bf16[128,2,768]{2,1,0:T(2,128)(2,1)S(1)}, bf16[128,2,768]{2,1,0:T(2,128)(2,1)S(1)}, u32[]{:S(2)}, u32[]{:S(2)}) collective-permute-start(bf16[128,2,768]{2,1,0:T(2,128)(2,1)S(1)} %get-tuple-element.57), channel_id=1, source_target_pairs={{2,4},{4,2},{6,8},{8,6},{10,12},{12,10},{3,5},{5,3},{7,9},{9,7},{1... | collective-permute-start | bytes 1179656 | tf_op jit(solution)/shard_map/ppermute | solution.py:41
  33.2 1.1 %copy-start.2 = (bf16[256,1536]{1,0:T(8,128)(2,1)S(1)}, bf16[256,1536]{1,0:T(8,128)(2,1)}, u32[]{:S(2)}) copy-start(bf16[256,1536]{1,0:T(8,128)(2,1)} %q_ref.3) | copy-start | bytes 2359300
  33.2 1.4 %copy-start.3 = (bf16[256,1536]{1,0:T(8,128)(2,1)S(1)}, bf16[256,1536]{1,0:T(8,128)(2,1)}, u32[]{:S(2)}) copy-start(bf16[256,1536]{1,0:T(8,128)(2,1)} %g_ref.3) | copy-start | bytes 2359300
  33.2 1.4 %copy-start.4 = (s32[1,2,5]{2,1,0:T(2,128)S(1)}, s32[1,2,5]{2,1,0:T(2,128)}, u32[]{:S(2)}) copy-start(s32[1,2,5]{2,1,0:T(2,128)} %param.15) | copy-start | bytes 124
  33.2 1.3 %copy-start.5 = (f32[12]{0:T(128)S(1)}, f32[12]{0:T(128)}, u32[]{:S(2)}) copy-start(f32[12]{0:T(128)} %warm_ref.3) | copy-start | bytes 148
  44.8 15.8 %copy-start.6 = (f32[6,512,128]{2,1,0:T(8,128)}, f32[6,512,128]{2,1,0:T(8,128)S(1)}, u32[]{:S(2)}) copy-start(f32[6,512,128]{2,1,0:T(8,128)S(1)} %get-tuple-element.80.own_ref) | copy-start | bytes 4718596
  44.8 21.9 %collective-permute-start.10 = (bf16[6,256,128]{2,1,0:T(8,128)(2,1)S(1)}, bf16[6,256,128]{2,1,0:T(8,128)(2,1)S(1)}, u32[]{:S(2)}, u32[]{:S(2)}) collective-permute-start(bf16[6,256,128]{2,1,0:T(8,128)(2,1)S(1)} %get-tuple-element.71), channel_id=1, source_target_pairs={{0,2},{2,0},{4,6},{6,4},{8,10},{10,8},{12,14},{14,12},{1,3},{3,1},... | collective-permute-start | bytes 1179656 | tf_op jit(solution)/shard_map/ppermute | solution.py:41
  48.1 18.6 %collective-permute-start.11 = (bf16[6,256,128]{2,1,0:T(8,128)(2,1)S(1)}, bf16[6,256,128]{2,1,0:T(8,128)(2,1)S(1)}, u32[]{:S(2)}, u32[]{:S(2)}) collective-permute-start(bf16[6,256,128]{2,1,0:T(8,128)(2,1)S(1)} %get-tuple-element.72), channel_id=1, source_target_pairs={{2,4},{4,2},{6,8},{8,6},{10,12},{12,10},{3,5},{5,3},{7,9},{9,7},{1... | collective-permute-start | bytes 1179656 | tf_op jit(solution)/shard_map/ppermute | solution.py:41
  48.8 17.9 %collective-permute-start.12 = (bf16[6,256,128]{2,1,0:T(8,128)(2,1)S(1)}, bf16[6,256,128]{2,1,0:T(8,128)(2,1)S(1)}, u32[]{:S(2)}, u32[]{:S(2)}) collective-permute-start(bf16[6,256,128]{2,1,0:T(8,128)(2,1)S(1)} %get-tuple-element.73), channel_id=1, source_target_pairs={{0,1},{1,0},{2,3},{3,2},{4,5},{5,4},{6,7},{7,6},{8,9},{9,8},{10,11... | collective-permute-start | bytes 1179656 | tf_op jit(solution)/shard_map/ppermute | solution.py:22
  66.7 0.7 copy-start.8
  66.7 3.2 %copy-start.10 = (bf16[6,256,128]{2,1,0:T(8,128)(2,1)}, bf16[6,256,128]{2,1,0:T(8,128)(2,1)S(1)}, u32[]{:S(2)}) copy-start(bf16[6,256,128]{2,1,0:T(8,128)(2,1)S(1)} %collective-permute-done.11.dia_ref) | copy-start | bytes 1179652
  66.7 3.9 %copy-start.12 = (bf16[6,256,128]{2,1,0:T(8,128)(2,1)}, bf16[6,256,128]{2,1,0:T(8,128)(2,1)S(1)}, u32[]{:S(2)}) copy-start(bf16[6,256,128]{2,1,0:T(8,128)(2,1)S(1)} %collective-permute-done.12.par_ref) | copy-start | bytes 1179652
  66.8 3.8 %collective-permute-start.16 = (f32[64,1664]{1,0:T(8,128)S(1)}, f32[64,1664]{1,0:T(8,128)S(1)}, u32[]{:S(2)}, u32[]{:S(2)}) collective-permute-start(f32[64,1664]{1,0:T(8,128)S(1)} %pad_maximum_fusion), channel_id=1, source_target_pairs={{0,1},{1,0},{2,3},{3,2},{4,5},{5,4},{6,7},{7,6},{8,9},{9,8},{10,11... | collective-permute-start | bytes 1277960 | tf_op jit(solution)/shard_map/ppermute | solution.py:22
  67.5 28.8 %collective-permute-start.13 = (bf16[6,256,128]{2,1,0:T(8,128)(2,1)}, bf16[6,256,128]{2,1,0:T(8,128)(2,1)S(1)}, u32[]{:S(2)}, u32[]{:S(2)}) collective-permute-start(bf16[6,256,128]{2,1,0:T(8,128)(2,1)} %get-tuple-element.74), channel_id=1, source_target_pairs={{0,2},{2,0},{4,6},{6,4},{8,10},{10,8},{12,14},{14,12},{1,3},{3,1},... | collective-permute-start | bytes 1179656 | tf_op jit(solution)/shard_map/ppermute | solution.py:41
  69.9 26.3 %collective-permute-start.14 = (bf16[6,256,128]{2,1,0:T(8,128)(2,1)}, bf16[6,256,128]{2,1,0:T(8,128)(2,1)S(1)}, u32[]{:S(2)}, u32[]{:S(2)}) collective-permute-start(bf16[6,256,128]{2,1,0:T(8,128)(2,1)} %get-tuple-element.75), channel_id=1, source_target_pairs={{2,4},{4,2},{6,8},{8,6},{10,12},{12,10},{3,5},{5,3},{7,9},{9,7},{1... | collective-permute-start | bytes 1179656 | tf_op jit(solution)/shard_map/ppermute | solution.py:41
  70.6 0.8 copy-start.14
  71.5 6.7 %copy-start.7 = (f32[6,512,128]{2,1,0:T(8,128)S(1)}, f32[6,512,128]{2,1,0:T(8,128)}, u32[]{:S(2)}) copy-start(f32[6,512,128]{2,1,0:T(8,128)} %copy-done.6) | copy-start | bytes 4718596
  71.5 6.6 %copy-start.9 = (bf16[6,256,128]{2,1,0:T(8,128)(2,1)S(1)}, bf16[6,256,128]{2,1,0:T(8,128)(2,1)}, u32[]{:S(2)}) copy-start(bf16[6,256,128]{2,1,0:T(8,128)(2,1)} %copy-done.8) | copy-start | bytes 1179652
  71.5 6.6 %copy-start.11 = (bf16[6,256,128]{2,1,0:T(8,128)(2,1)S(1)}, bf16[6,256,128]{2,1,0:T(8,128)(2,1)}, u32[]{:S(2)}) copy-start(bf16[6,256,128]{2,1,0:T(8,128)(2,1)} %copy-done.10) | copy-start | bytes 1179652
  72.8 13.9 %collective-permute-start.17 = (f32[16,1664]{1,0:T(8,128)S(1)}, f32[16,1664]{1,0:T(8,128)S(1)}, u32[]{:S(2)}, u32[]{:S(2)}) collective-permute-start(f32[16,1664]{1,0:T(8,128)S(1)} %get-tuple-element.95), channel_id=1, source_target_pairs={{0,4},{1,5},{2,6},{3,7},{4,0},{5,1},{6,2},{7,3},{8,12},{9,13},{10,... | collective-permute-start | bytes 319496 | tf_op jit(solution)/shard_map/ppermute | solution.py:22
  75.7 15.0 %collective-permute-start.18 = (f32[16,1664]{1,0:T(8,128)S(1)}, f32[16,1664]{1,0:T(8,128)S(1)}, u32[]{:S(2)}, u32[]{:S(2)}) collective-permute-start(f32[16,1664]{1,0:T(8,128)S(1)} %get-tuple-element.94), channel_id=1, source_target_pairs={{0,8},{1,9},{2,10},{3,11},{4,12},{5,13},{6,14},{7,15},{8,0},{9,1},... | collective-permute-start | bytes 319496 | tf_op jit(solution)/shard_map/ppermute | solution.py:22
  77.7 13.0 %collective-permute-start.19 = (f32[16,1664]{1,0:T(8,128)S(1)}, f32[16,1664]{1,0:T(8,128)S(1)}, u32[]{:S(2)}, u32[]{:S(2)}) collective-permute-start(f32[16,1664]{1,0:T(8,128)S(1)} %get-tuple-element.93), channel_id=1, source_target_pairs={{0,12},{1,13},{2,14},{3,15},{4,8},{5,9},{6,10},{7,11},{8,4},{9,5},... | collective-permute-start | bytes 319496 | tf_op jit(solution)/shard_map/ppermute | solution.py:22
  78.2 1.0 %copy-start.13 = (bf16[6,256,128]{2,1,0:T(8,128)(2,1)S(1)}, bf16[6,256,128]{2,1,0:T(8,128)(2,1)}, u32[]{:S(2)}) copy-start(bf16[6,256,128]{2,1,0:T(8,128)(2,1)} %copy-done.12) | copy-start | bytes 1179652
  86.7 9.5 %collective-permute-start.15 = (bf16[6,256,128]{2,1,0:T(8,128)(2,1)S(1)}, bf16[6,256,128]{2,1,0:T(8,128)(2,1)S(1)}, u32[]{:S(2)}, u32[]{:S(2)}) collective-permute-start(bf16[6,256,128]{2,1,0:T(8,128)(2,1)S(1)} %get-tuple-element.76), channel_id=1, source_target_pairs={{0,1},{1,0},{2,3},{3,2},{4,5},{5,4},{6,7},{7,6},{8,9},{9,8},{10,11... | collective-permute-start | bytes 1179656 | tf_op jit(solution)/shard_map/ppermute | solution.py:22
  90.9 4.2 %collective-permute-start.20 = (f32[8,1664]{1,0:T(8,128)S(1)}, f32[8,1664]{1,0:T(8,128)S(1)}, u32[]{:S(2)}, u32[]{:S(2)}) collective-permute-start(f32[8,1664]{1,0:T(8,128)S(1)} %pad_maximum_fusion.5), channel_id=1, source_target_pairs={{0,2},{1,3},{2,0},{3,1},{4,6},{5,7},{6,4},{7,5},{8,10},{9,11},{10,... | collective-permute-start | bytes 159752 | tf_op jit(solution)/shard_map/ppermute | solution.py:22

commit v6 on v4

--- a/solution.py
+++ b/solution.py
@@ -218,7 +218,7 @@
         ],
         scratch_shapes=[pltpu.VMEM((2 * keys, width), F32)],
         input_output_aliases=alias,
-        compiler_params=pltpu.CompilerParams(vmem_limit_bytes=24 << 20),
+        compiler_params=pltpu.CompilerParams(vmem_limit_bytes=16 << 20),
         cost_estimate=pl.CostEstimate(
             flops=10 * heads * rows * keys * width,
             transcendentals=heads * rows * keys,
@@ -268,7 +268,7 @@
         out_specs=pl.BlockSpec((rows, 2, step * width), lambda h: (0, 0, head0 // step + h)),
         out_shape=jax.ShapeDtypeStruct((rows, 2, feat), BF16),
         input_output_aliases=alias,
-        compiler_params=pltpu.CompilerParams(vmem_limit_bytes=24 << 20),
+        compiler_params=pltpu.CompilerParams(vmem_limit_bytes=8 << 20),
         cost_estimate=pl.CostEstimate(
             flops=weight * heads * width * rows * 16,
             transcendentals=0,
@@ -296,7 +296,8 @@
     others = list(pick(pos, sent, mesh_kv, width, others + [("partner", 0, total)]))
     partner = swap_mask(others.pop(), 1)
     picks += [others[2 * i : 2 * i + 2] for i in range(len(chunks) - 1)]
-    anchors = landmark.reshape(2 * landmark.shape[0], feat)
+    anchors, picks[0] = lax.optimization_barrier((landmark, picks[0]))
+    anchors = anchors.reshape(2 * landmark.shape[0], feat)
     for i, masks in enumerate(stages):
         if i == 1:
             anchors, picks[1] = lax.optimization_barrier((anchors, picks[1]))
@@ -318,12 +319,15 @@
     temp = jnp.sum(jnp.concatenate(temps, axis=0), axis=(1, 2)) / math.sqrt(width)
     extra = jnp.zeros((1, LANES), F32).at[0, :total].set(temp)
     cell = None
-    for i, masks in enumerate(reversed(stages)):
-        n = anc.shape[0] // (len(masks) + 1)
-        wide = jnp.broadcast_to(extra, (n, LANES))
+    anc = anc.reshape([len(masks) + 1 for masks in reversed(stages)] + [2 * landmark.shape[0], feat])
+    for i, masks in enumerate([stages[-1]] + stages[:-1]):
+        dim = 0 if i == 0 else anc.ndim - 3
+        parts = [lax.index_in_dim(anc, k, dim, keepdims=False) for k in range(len(masks) + 1)]
+        shape = parts[0].shape
+        parts = [x.reshape(-1, feat) for x in parts]
+        wide = jnp.broadcast_to(extra, (parts[0].shape[0], LANES))
         got = [
-            swap_mask(jnp.concatenate([anc[k * n : (k + 1) * n], wide], axis=1), m)
-            for k, m in enumerate(masks, 1)
+            swap_mask(jnp.concatenate([x, wide], axis=1), m) for x, m in zip(parts[1:], masks)
         ]
         if i == 0:
             returned[-1] = hold(returned[-1], HOLD)
@@ -333,7 +337,7 @@
                 cell = combine(pos, sent, owns[c], returned[c], *chunks[c], feat, width, cell, weight=4000)
         if i == len(stages) - 1:
             got, cell = lax.optimization_barrier((got, cell))
-        anc = sum([x[:, :feat] for x in got], anc[:n])
+        anc = sum([x[:, :feat] for x in got], parts[0]).reshape(shape)
         extra = sum([x[:1, feat:] for x in got], extra)
     anchor_grad = anc.reshape(landmark.shape)
     temp = extra[0, :total]

time: 93 us -> 101 us (1.086)
  waiting for transfers between devices: 23.5 us -> 29.4 us
  other arithmetic: 4.5 us -> 6.18 us
    ppermute x13, waiting for transfers between devices: 19.3 us -> 25.2 us  [swap_mask(): return lax.ppermute(x, ('gx', 'gy'), [(i, i ^ mask) for i in range(count)])]
    ppermute x8, starting transfers between devices: 7.07 us -> 5.54 us  [swap_pairs(): return lax.ppermute(x, 'gx', route)]
    ppermute x13, starting transfers between devices: 17.9 us -> 18.9 us  [swap_mask(): return lax.ppermute(x, ('gx', 'gy'), [(i, i ^ mask) for i in range(count)])]
    unnamed x36 -> x42, local copies, waits for them, and re-layouts: 8.32 us -> 9.28 us
  transfers between devices with their start and end apart: 21 -> 21, of which waited for: 7 -> 7; matrix products, arithmetic and copies ran while one was open for 7% -> 7% of each run, Pallas kernels for 26% -> 23%
where the time goes in v6:
time: 101 us
  waiting for transfers between devices  29.4 us (29%)
  Pallas kernels  26.5 us (26%)
  starting transfers between devices  24.5 us (24%)
  local copies, waits for them, and re-layouts  13 us (13%)
  other arithmetic  6.18 us (6%)
  between operations  1.01 us (1%)
    ppermute x13, waiting for transfers between devices, swap_mask(): return lax.ppermute(x, ('gx', 'gy'), [(i, i ^ mask) for i in range(count)])  25.2 us
    pallas_call x2, Pallas kernels, attention(): pl.pallas_call(functools.partial(attention_kernel, gx_count=lax.axis_size...  20.6 us
    ppermute x13, starting transfers between devices, swap_mask(): return lax.ppermute(x, ('gx', 'gy'), [(i, i ^ mask) for i in range(count)])  18.9 us
    unnamed x42, local copies, waits for them, and re-layouts  9.28 us
    ppermute x8, starting transfers between devices, swap_pairs(): return lax.ppermute(x, 'gx', route)  5.54 us
    pallas_call x2, Pallas kernels, combine(): pl.pallas_call(combine_kernel, grid=(heads // step,), in_specs=in_specs,...  4.39 us
    ppermute x8, waiting for transfers between devices, swap_pairs(): return lax.ppermute(x, 'gx', route)  4.21 us
    add x3, other arithmetic, local(): anc = sum([x[:, :feat] for x in got], parts[0]).reshape(shape)  2.52 us
  transfers between devices with their start and end apart: 21, of which 7 were waited for; matrix products, arithmetic and copies ran while one was open for 7% of the time, Pallas kernels for 23%

profile of v6, /device:TPU:0, one launch (start us, length us, event | category | flops | bytes accessed | tf_op | source)
XLA Modules:
  0.0 100.5 jit_solution(1204433139506833164)
XLA Ops:
  0.6 0.7 copy.19.sent_ref
  1.4 1.4 %copy-done = bf16[256,2,1536]{2,1,0:T(2,128)(2,1)S(1)} copy-done((bf16[256,2,1536]{2,1,0:T(2,128)(2,1)S(1)}, bf16[256,2,1536]{2,1,0:T(2,128)(2,1)}, u32[]{:S(2)}) %copy-start) | copy-done | bytes 1572888
  2.8 0.7 pick.3
  3.5 0.8 reshape.73
  4.2 3.0 %collective-permute-start.1 = (bf16[8,1536]{1,0:T(8,128)(2,1)S(1)}, bf16[8,1536]{1,0:T(8,128)(2,1)S(1)}, u32[]{:S(2)}, u32[]{:S(2)}) collective-permute-start(bf16[8,1536]{1,0:T(8,128)(2,1)S(1)} %reshape.73), channel_id=1, source_target_pairs={{0,2},{1,3},{2,0},{3,1},{4,6},{5,7},{6,4},{7,5},{8,10},{9,11},{10,... | collective-permute-start | bytes 73736 | tf_op jit(solution)/shard_map/ppermute | solution.py:22
  7.3 0.7 collective-permute-start.9
  8.0 0.8 pick.2
  8.8 0.6 compare_reduce_fusion
  9.4 4.7 %collective-permute-start.4 = (bf16[16,1536]{1,0:T(8,128)(2,1)S(1)}, bf16[16,1536]{1,0:T(8,128)(2,1)S(1)}, u32[]{:S(2)}, u32[]{:S(2)}) collective-permute-start(bf16[16,1536]{1,0:T(8,128)(2,1)S(1)} %pad_maximum_fusion.6), channel_id=1, source_target_pairs={{0,4},{1,5},{2,6},{3,7},{4,0},{5,1},{6,2},{7,3},{8,12},{9,13},{10,... | collective-permute-start | bytes 147464 | tf_op jit(solution)/shard_map/ppermute | solution.py:22
  14.1 2.6 %collective-permute-start.5 = (bf16[16,1536]{1,0:T(8,128)(2,1)S(1)}, bf16[16,1536]{1,0:T(8,128)(2,1)S(1)}, u32[]{:S(2)}, u32[]{:S(2)}) collective-permute-start(bf16[16,1536]{1,0:T(8,128)(2,1)S(1)} %pad_maximum_fusion.6), channel_id=1, source_target_pairs={{0,8},{1,9},{2,10},{3,11},{4,12},{5,13},{6,14},{7,15},{8,0},{9,1},... | collective-permute-start | bytes 147464 | tf_op jit(solution)/shard_map/ppermute | solution.py:22
  16.7 5.8 %collective-permute-done.4 = bf16[16,1536]{1,0:T(8,128)(2,1)S(1)} collective-permute-done((bf16[16,1536]{1,0:T(8,128)(2,1)S(1)}, bf16[16,1536]{1,0:T(8,128)(2,1)S(1)}, u32[]{:S(2)}, u32[]{:S(2)}) %collective-permute-start.4) | collective-permute-done | bytes 49184 | tf_op jit(solution)/shard_map/ppermute | solution.py:22
  22.5 2.1 %collective-permute-done.5 = bf16[16,1536]{1,0:T(8,128)(2,1)S(1)} collective-permute-done((bf16[16,1536]{1,0:T(8,128)(2,1)S(1)}, bf16[16,1536]{1,0:T(8,128)(2,1)S(1)}, u32[]{:S(2)}, u32[]{:S(2)}) %collective-permute-start.5) | collective-permute-done | bytes 49184 | tf_op jit(solution)/shard_map/ppermute | solution.py:22
  24.6 1.6 %collective-permute-done.6 = bf16[16,1536]{1,0:T(8,128)(2,1)S(1)} collective-permute-done((bf16[16,1536]{1,0:T(8,128)(2,1)S(1)}, bf16[16,1536]{1,0:T(8,128)(2,1)S(1)}, u32[]{:S(2)}, u32[]{:S(2)}) %collective-permute-start.6) | collective-permute-done | bytes 49184 | tf_op jit(solution)/shard_map/ppermute | solution.py:22
  26.3 1.4 %collective-permute-done.7 = bf16[64,1536]{1,0:T(8,128)(2,1)S(1)} collective-permute-done((bf16[64,1536]{1,0:T(8,128)(2,1)S(1)}, bf16[64,1536]{1,0:T(8,128)(2,1)S(1)}, u32[]{:S(2)}, u32[]{:S(2)}) %collective-permute-start.7) | collective-permute-done | bytes 196640 | tf_op jit(solution)/shard_map/ppermute | solution.py:22
  27.7 0.7 collective-permute-start.3
  28.5 1.0 %copy-done.2 = bf16[256,1536]{1,0:T(8,128)(2,1)S(1)} copy-done((bf16[256,1536]{1,0:T(8,128)(2,1)S(1)}, bf16[256,1536]{1,0:T(8,128)(2,1)}, u32[]{:S(2)}) %copy-start.2) | copy-done | bytes 786456
  29.5 0.2 copy-done.3
  29.8 10.2 %attention.2 = (bf16[256,1536]{1,0:T(8,128)(2,1)}, f32[6,512,128]{2,1,0:T(8,128)S(1)}, bf16[6,256,128]{2,1,0:T(8,128)(2,1)S(1)}, bf16[6,256,128]{2,1,0:T(8,128)(...) custom-call(s32[1]{0:T(128)} %bitcast.pos_ref, ...), custom_call_target="tpu_custom_call" | custom-call | flops 1384120320 | bytes 6488064 | tf_op jit(solution)/shard_map/attention/pallas_call | solution.py:197
  40.0 1.1 %copy-done.14 = f32[6,512,128]{2,1,0:T(8,128)} copy-done((f32[6,512,128]{2,1,0:T(8,128)}, f32[6,512,128]{2,1,0:T(8,128)S(1)}, u32[]{:S(2)}) %copy-start.14) | copy-done | bytes 1572888
  41.1 2.7 %collective-permute-start.11 = (bf16[6,256,128]{2,1,0:T(8,128)(2,1)S(1)}, bf16[6,256,128]{2,1,0:T(8,128)(2,1)S(1)}, u32[]{:S(2)}, u32[]{:S(2)}) collective-permute-start(bf16[6,256,128]{2,1,0:T(8,128)(2,1)S(1)} %get-tuple-element.80), channel_id=1, source_target_pairs={{0,2},{2,0},{4,6},{6,4},{8,10},{10,8},{12,14},{14,12},{1,3},{3,1},... | collective-permute-start | bytes 1179656 | tf_op jit(solution)/shard_map/ppermute | solution.py:41
  43.9 0.7 collective-permute-start.12
  44.7 10.4 %attention.3 = (bf16[256,1536]{1,0:T(8,128)(2,1)}, f32[6,512,128]{2,1,0:T(8,128)S(1)}, bf16[6,256,128]{2,1,0:T(8,128)(2,1)}, bf16[6,256,128]{2,1,0:T(8,128)(2,1)...) custom-call(s32[1]{0:T(128)} %bitcast.pos_ref, ...), custom_call_target="tpu_custom_call", output_to_operand_aliasing={{0}: (10, {}), {5}: (11, {})} | custom-call | flops 1384120320 | bytes 6488064 | tf_op jit(solution)/shard_map/attention/pallas_call | solution.py:197
  55.2 0.6 fusion.2
  56.0 0.5 collective-permute-start.10
  56.5 4.2 %collective-permute-done.11.refs_0_ = bf16[6,256,128]{2,1,0:T(8,128)(2,1)S(1)} collective-permute-done((bf16[6,256,128]{2,1,0:T(8,128)(2,1)S(1)}, bf16[6,256,128]{2,1,0:T(8,128)(2,1)S(1)}, u32[]{:S(2)}, u32[]{:S(2)}) %collective-permute-start.11) | collective-permute-done | bytes 393248 | tf_op jit(solution)/shard_map/ppermute | solution.py:41
  60.7 0.8 copy-done.8
  61.5 0.7 copy-done.10
  62.2 0.8 copy-done.12
  63.0 0.7 slice_add_fusion.5
  64.0 0.5 copy-done.16
  64.5 2.5 %collective-permute-start.17 = (f32[32,1664]{1,0:T(8,128)S(1)}, f32[32,1664]{1,0:T(8,128)}, u32[]{:S(2)}, u32[]{:S(2)}) collective-permute-start(f32[32,1664]{1,0:T(8,128)S(1)} %pad_maximum_fusion.1), channel_id=1, source_target_pairs={{0,2},{1,3},{2,0},{3,1},{4,6},{5,7},{6,4},{7,5},{8,10},{9,11},{10,... | collective-permute-start | bytes 638984 | tf_op jit(solution)/shard_map/ppermute | solution.py:22
  67.0 0.7 collective-permute-start.15
  67.7 13.4 %collective-permute-done.17 = f32[32,1664]{1,0:T(8,128)} collective-permute-done((f32[32,1664]{1,0:T(8,128)S(1)}, f32[32,1664]{1,0:T(8,128)}, u32[]{:S(2)}, u32[]{:S(2)}) %collective-permute-start.17) | collective-permute-done | bytes 213024 | tf_op jit(solution)/shard_map/ppermute | solution.py:22
  81.1 0.7 fusion.3
  81.8 1.0 %slice_add_fusion.1 = f32[32,1536]{1,0:T(8,128)S(1)} fusion(f32[32,1664]{1,0:T(8,128)} %collective-permute-done.17, f32[4,2,8,1536]{3,2,1,0:T(8,128)} %bitcast.24), kind=kLoop, calls=%fused_computation.3 | loop fusion | flops 49152 | bytes 589824 | tf_op jit(solution)/shard_map/add | solution.py:340
  82.9 3.1 %collective-permute-start.18 = (f32[8,1664]{1,0:T(8,128)S(1)}, f32[8,1664]{1,0:T(8,128)}, u32[]{:S(2)}, u32[]{:S(2)}) collective-permute-start(f32[8,1664]{1,0:T(8,128)S(1)} %get-tuple-element.103), channel_id=1, source_target_pairs={{0,4},{1,5},{2,6},{3,7},{4,0},{5,1},{6,2},{7,3},{8,12},{9,13},{10,... | collective-permute-start | bytes 159752 | tf_op jit(solution)/shard_map/ppermute | solution.py:22
  86.0 1.7 %collective-permute-start.19 = (f32[8,1664]{1,0:T(8,128)S(1)}, f32[8,1664]{1,0:T(8,128)S(1)}, u32[]{:S(2)}, u32[]{:S(2)}) collective-permute-start(f32[8,1664]{1,0:T(8,128)S(1)} %get-tuple-element.102), channel_id=1, source_target_pairs={{0,8},{1,9},{2,10},{3,11},{4,12},{5,13},{6,14},{7,15},{8,0},{9,1},... | collective-permute-start | bytes 159752 | tf_op jit(solution)/shard_map/ppermute | solution.py:22
  87.6 0.8 collective-permute-start.20
  88.4 1.0 copy-done.11
  89.4 1.0 copy-done.13
  90.4 2.2 %combine.2.rest_0_ = bf16[256,2,1536]{2,1,0:T(2,128)(2,1)} custom-call(s32[1]{0:T(128)} %bitcast.pos_ref, s32[3,1]{1,0:T(4,128)S(1)} %copy.19.sent_ref, f32[6,512,128]{2,1,0:T(8,128)S(1)} %copy-done.15, bf16[6,256,128]{2,1,0:T(8,128)(2,1)S(1)} %copy-done.9, bf16[6,256,128]{2,1,0:T(8,128)(2,1)S(1)} %copy-done.11, bf16[6,256,128]{2,1,0:T(8,128)(2,1)S(1)} %copy-done.13), custom_call_target="tpu_custom_call" | custom-call | flops 12582912000 | bytes 3538944 | tf_op jit(solution)/shard_map/combine/pallas_call | solution.py:264
  92.6 1.0 collective-permute-done.20
  93.6 0.6 copy-done.18
  94.2 1.4 %fusion.1 = f32[8,1536]{1,0:T(8,128)} fusion(f32[32,1536]{1,0:T(8,128)S(1)} %slice_add_fusion.1, f32[8,1664]{1,0:T(8,128)S(1)} %collective-permute-done.20, f32[8,1664]{1,0:T(8,128)S(1)} %collective-permute-done.19, f32[8,1664]{1,0:T(8,128)} %collective-permute-done.18), kind=kLoop, calls=%fused_computation.12 | loop fusion | flops 36864 | bytes 245760 | tf_op jit(solution)/shard_map/add | solution.py:340
  95.6 1.4 %reshape.76 = f32[4,2,1536]{2,1,0:T(2,128)} reshape(f32[8,1536]{1,0:T(8,128)} %fusion.1) | data formatting | bytes 98304 | tf_op jit(solution)/shard_map/reshape | solution.py:342
  97.1 0.7 slice_add_fusion.4
  97.8 0.5 slice_bitcast_fusion.2
  98.3 2.2 %combine.3 = bf16[256,2,1536]{2,1,0:T(2,128)(2,1)} custom-call(s32[1]{0:T(128)} %bitcast.pos_ref, s32[3,1]{1,0:T(4,128)S(1)} %copy.19.sent_ref, f32[6,512,128]{2,1,0:T(8,128)S(1)} %get-tuple-element.73.own_ref, bf16[6,256,128]{2,1,0:T(8,128)(2,1)S(1)} %collective-permute-done.14.dir_ref, ...), custom_call_target="tpu_custom_call", output_to_operand_aliasing={{}: (6, {})} | custom-call | bytes 3538944 | tf_op jit(solution)/shard_map/combine/pallas_call | solution.py:264
  (72 shorter events, 0.9 us)
Async XLA Ops:
  1.4 1.4 %copy-start = (bf16[256,2,1536]{2,1,0:T(2,128)(2,1)S(1)}, bf16[256,2,1536]{2,1,0:T(2,128)(2,1)}, u32[]{:S(2)}) copy-start(bf16[256,2,1536]{2,1,0:T(2,128)(2,1)} %own_ref.3) | copy-start | bytes 4718596
  2.8 5.2 %copy-start.1 = (bf16[256,2,1536]{2,1,0:T(2,128)(2,1)S(1)}, bf16[256,2,1536]{2,1,0:T(2,128)(2,1)}, u32[]{:S(2)}) copy-start(bf16[256,2,1536]{2,1,0:T(2,128)(2,1)} %own_ref.3) | copy-start | bytes 4718596
  4.2 5.2 %collective-permute-start.1 = (bf16[8,1536]{1,0:T(8,128)(2,1)S(1)}, bf16[8,1536]{1,0:T(8,128)(2,1)S(1)}, u32[]{:S(2)}, u32[]{:S(2)}) collective-permute-start(bf16[8,1536]{1,0:T(8,128)(2,1)S(1)} %reshape.73), channel_id=1, source_target_pairs={{0,2},{1,3},{2,0},{3,1},{4,6},{5,7},{6,4},{7,5},{8,10},{9,11},{10,... | collective-permute-start | bytes 73736 | tf_op jit(solution)/shard_map/ppermute | solution.py:22
  7.2 21.2 %collective-permute-start.8 = (bf16[128,2,768]{2,1,0:T(2,128)(2,1)S(1)}, bf16[128,2,768]{2,1,0:T(2,128)(2,1)S(1)}, u32[]{:S(2)}, u32[]{:S(2)}) collective-permute-start(bf16[128,2,768]{2,1,0:T(2,128)(2,1)S(1)} %get-tuple-element.66), channel_id=1, source_target_pairs={{0,2},{2,0},{4,6},{6,4},{8,10},{10,8},{12,14},{14,12},{1,3},{3,1},... | collective-permute-start | bytes 1179656 | tf_op jit(solution)/shard_map/ppermute | solution.py:41
  7.3 21.1 %collective-permute-start.9 = (bf16[128,2,768]{2,1,0:T(2,128)(2,1)S(1)}, bf16[128,2,768]{2,1,0:T(2,128)(2,1)S(1)}, u32[]{:S(2)}, u32[]{:S(2)}) collective-permute-start(bf16[128,2,768]{2,1,0:T(2,128)(2,1)S(1)} %get-tuple-element.67), channel_id=1, source_target_pairs={{2,4},{4,2},{6,8},{8,6},{10,12},{12,10},{3,5},{5,3},{7,9},{9,7},{1... | collective-permute-start | bytes 1179656 | tf_op jit(solution)/shard_map/ppermute | solution.py:41
  9.4 13.1 %collective-permute-start.4 = (bf16[16,1536]{1,0:T(8,128)(2,1)S(1)}, bf16[16,1536]{1,0:T(8,128)(2,1)S(1)}, u32[]{:S(2)}, u32[]{:S(2)}) collective-permute-start(bf16[16,1536]{1,0:T(8,128)(2,1)S(1)} %pad_maximum_fusion.6), channel_id=1, source_target_pairs={{0,4},{1,5},{2,6},{3,7},{4,0},{5,1},{6,2},{7,3},{8,12},{9,13},{10,... | collective-permute-start | bytes 147464 | tf_op jit(solution)/shard_map/ppermute | solution.py:22
  14.1 10.5 %collective-permute-start.5 = (bf16[16,1536]{1,0:T(8,128)(2,1)S(1)}, bf16[16,1536]{1,0:T(8,128)(2,1)S(1)}, u32[]{:S(2)}, u32[]{:S(2)}) collective-permute-start(bf16[16,1536]{1,0:T(8,128)(2,1)S(1)} %pad_maximum_fusion.6), channel_id=1, source_target_pairs={{0,8},{1,9},{2,10},{3,11},{4,12},{5,13},{6,14},{7,15},{8,0},{9,1},... | collective-permute-start | bytes 147464 | tf_op jit(solution)/shard_map/ppermute | solution.py:22
  16.7 9.5 %collective-permute-start.6 = (bf16[16,1536]{1,0:T(8,128)(2,1)S(1)}, bf16[16,1536]{1,0:T(8,128)(2,1)S(1)}, u32[]{:S(2)}, u32[]{:S(2)}) collective-permute-start(bf16[16,1536]{1,0:T(8,128)(2,1)S(1)} %pad_maximum_fusion.6), channel_id=1, source_target_pairs={{0,12},{1,13},{2,14},{3,15},{4,8},{5,9},{6,10},{7,11},{8,4},{9,5},... | collective-permute-start | bytes 147464 | tf_op jit(solution)/shard_map/ppermute | solution.py:22
  22.5 6.0 %collective-permute-start = (bf16[128,2,1536]{2,1,0:T(2,128)(2,1)S(1)}, bf16[128,2,1536]{2,1,0:T(2,128)(2,1)S(1)}, u32[]{:S(2)}, u32[]{:S(2)}) collective-permute-start(bf16[128,2,1536]{2,1,0:T(2,128)(2,1)S(1)} %get-tuple-element.57), channel_id=1, source_target_pairs={{0,1},{1,0},{2,3},{3,2},{4,5},{5,4},{6,7},{7,6},{8,9},{9,8},{10,11... | collective-permute-start | bytes 2359304 | tf_op jit(solution)/shard_map/ppermute | solution.py:22
  24.6 20.1 %collective-permute-start.2 = (bf16[128,2,768]{2,1,0:T(2,128)(2,1)S(1)}, bf16[128,2,768]{2,1,0:T(2,128)(2,1)S(1)}, u32[]{:S(2)}, u32[]{:S(2)}) collective-permute-start(bf16[128,2,768]{2,1,0:T(2,128)(2,1)S(1)} %get-tuple-element.63), channel_id=1, source_target_pairs={{0,2},{2,0},{4,6},{6,4},{8,10},{10,8},{12,14},{14,12},{1,3},{3,1},... | collective-permute-start | bytes 1179656 | tf_op jit(solution)/shard_map/ppermute | solution.py:41
  26.2 1.5 %collective-permute-start.7 = (bf16[64,1536]{1,0:T(8,128)(2,1)S(1)}, bf16[64,1536]{1,0:T(8,128)(2,1)S(1)}, u32[]{:S(2)}, u32[]{:S(2)}) collective-permute-start(bf16[64,1536]{1,0:T(8,128)(2,1)S(1)} %pad_maximum_fusion.2), channel_id=1, source_target_pairs={{0,1},{1,0},{2,3},{3,2},{4,5},{5,4},{6,7},{7,6},{8,9},{9,8},{10,11... | collective-permute-start | bytes 589832 | tf_op jit(solution)/shard_map/ppermute | solution.py:22
  27.7 17.0 %collective-permute-start.3 = (bf16[128,2,768]{2,1,0:T(2,128)(2,1)S(1)}, bf16[128,2,768]{2,1,0:T(2,128)(2,1)S(1)}, u32[]{:S(2)}, u32[]{:S(2)}) collective-permute-start(bf16[128,2,768]{2,1,0:T(2,128)(2,1)S(1)} %get-tuple-element.64), channel_id=1, source_target_pairs={{2,4},{4,2},{6,8},{8,6},{10,12},{12,10},{3,5},{5,3},{7,9},{9,7},{1... | collective-permute-start | bytes 1179656 | tf_op jit(solution)/shard_map/ppermute | solution.py:41
  28.4 1.1 %copy-start.2 = (bf16[256,1536]{1,0:T(8,128)(2,1)S(1)}, bf16[256,1536]{1,0:T(8,128)(2,1)}, u32[]{:S(2)}) copy-start(bf16[256,1536]{1,0:T(8,128)(2,1)} %q_ref.3) | copy-start | bytes 2359300
  28.4 1.4 %copy-start.3 = (bf16[256,1536]{1,0:T(8,128)(2,1)S(1)}, bf16[256,1536]{1,0:T(8,128)(2,1)}, u32[]{:S(2)}) copy-start(bf16[256,1536]{1,0:T(8,128)(2,1)} %g_ref.3) | copy-start | bytes 2359300
  28.4 1.4 %copy-start.4 = (s32[1,2,5]{2,1,0:T(2,128)S(1)}, s32[1,2,5]{2,1,0:T(2,128)}, u32[]{:S(2)}) copy-start(s32[1,2,5]{2,1,0:T(2,128)} %param.15) | copy-start | bytes 124
  28.4 1.3 %copy-start.5 = (f32[12]{0:T(128)S(1)}, f32[12]{0:T(128)}, u32[]{:S(2)}) copy-start(f32[12]{0:T(128)} %warm_ref.3) | copy-start | bytes 148
  40.0 1.1 %copy-start.14 = (f32[6,512,128]{2,1,0:T(8,128)}, f32[6,512,128]{2,1,0:T(8,128)S(1)}, u32[]{:S(2)}) copy-start(f32[6,512,128]{2,1,0:T(8,128)S(1)} %get-tuple-element.90.own_ref) | copy-start | bytes 4718596
  41.1 19.6 %collective-permute-start.11 = (bf16[6,256,128]{2,1,0:T(8,128)(2,1)S(1)}, bf16[6,256,128]{2,1,0:T(8,128)(2,1)S(1)}, u32[]{:S(2)}, u32[]{:S(2)}) collective-permute-start(bf16[6,256,128]{2,1,0:T(8,128)(2,1)S(1)} %get-tuple-element.80), channel_id=1, source_target_pairs={{0,2},{2,0},{4,6},{6,4},{8,10},{10,8},{12,14},{14,12},{1,3},{3,1},... | collective-permute-start | bytes 1179656 | tf_op jit(solution)/shard_map/ppermute | solution.py:41
  43.9 16.8 %collective-permute-start.12 = (bf16[6,256,128]{2,1,0:T(8,128)(2,1)S(1)}, bf16[6,256,128]{2,1,0:T(8,128)(2,1)S(1)}, u32[]{:S(2)}, u32[]{:S(2)}) collective-permute-start(bf16[6,256,128]{2,1,0:T(8,128)(2,1)S(1)} %get-tuple-element.81), channel_id=1, source_target_pairs={{2,4},{4,2},{6,8},{8,6},{10,12},{12,10},{3,5},{5,3},{7,9},{9,7},{1... | collective-permute-start | bytes 1179656 | tf_op jit(solution)/shard_map/ppermute | solution.py:41
  44.6 16.1 %collective-permute-start.13 = (bf16[6,256,128]{2,1,0:T(8,128)(2,1)S(1)}, bf16[6,256,128]{2,1,0:T(8,128)(2,1)S(1)}, u32[]{:S(2)}, u32[]{:S(2)}) collective-permute-start(bf16[6,256,128]{2,1,0:T(8,128)(2,1)S(1)} %get-tuple-element.82), channel_id=1, source_target_pairs={{0,1},{1,0},{2,3},{3,2},{4,5},{5,4},{6,7},{7,6},{8,9},{9,8},{10,11... | collective-permute-start | bytes 1179656 | tf_op jit(solution)/shard_map/ppermute | solution.py:22
  55.0 5.7 %copy-start.6 = (bf16[6,256,128]{2,1,0:T(8,128)(2,1)}, bf16[6,256,128]{2,1,0:T(8,128)(2,1)S(1)}, u32[]{:S(2)}) copy-start(bf16[6,256,128]{2,1,0:T(8,128)(2,1)S(1)} %get-tuple-element.87) | copy-start | bytes 1179652
  56.0 7.0 %collective-permute-start.10 = (f32[64,1664]{1,0:T(8,128)S(1)}, f32[64,1664]{1,0:T(8,128)S(1)}, u32[]{:S(2)}, u32[]{:S(2)}) collective-permute-start(f32[64,1664]{1,0:T(8,128)S(1)} %pad_maximum_fusion), channel_id=1, source_target_pairs={{0,1},{1,0},{2,3},{3,2},{4,5},{5,4},{6,7},{7,6},{8,9},{9,8},{10,11... | collective-permute-start | bytes 1277960 | tf_op jit(solution)/shard_map/ppermute | solution.py:22
  60.7 0.8 copy-start.8
  61.5 0.7 copy-start.10
  62.2 0.8 copy-start.12
  63.0 4.1 %copy-start.7 = (bf16[6,256,128]{2,1,0:T(8,128)(2,1)S(1)}, bf16[6,256,128]{2,1,0:T(8,128)(2,1)}, u32[]{:S(2)}) copy-start(bf16[6,256,128]{2,1,0:T(8,128)(2,1)} %copy-done.6) | copy-start | bytes 1179652
  63.7 24.7 %copy-start.9 = (bf16[6,256,128]{2,1,0:T(8,128)(2,1)S(1)}, bf16[6,256,128]{2,1,0:T(8,128)(2,1)}, u32[]{:S(2)}) copy-start(bf16[6,256,128]{2,1,0:T(8,128)(2,1)} %copy-done.8) | copy-start | bytes 1179652
  63.8 0.8 copy-start.16
  63.9 24.5 %copy-start.15 = (f32[6,512,128]{2,1,0:T(8,128)S(1)}, f32[6,512,128]{2,1,0:T(8,128)}, u32[]{:S(2)}) copy-start(f32[6,512,128]{2,1,0:T(8,128)} %copy-done.14) | copy-start | bytes 4718596
  64.5 16.6 %collective-permute-start.17 = (f32[32,1664]{1,0:T(8,128)S(1)}, f32[32,1664]{1,0:T(8,128)}, u32[]{:S(2)}, u32[]{:S(2)}) collective-permute-start(f32[32,1664]{1,0:T(8,128)S(1)} %pad_maximum_fusion.1), channel_id=1, source_target_pairs={{0,2},{1,3},{2,0},{3,1},{4,6},{5,7},{6,4},{7,5},{8,10},{9,11},{10,... | collective-permute-start | bytes 638984 | tf_op jit(solution)/shard_map/ppermute | solution.py:22
  67.0 31.3 %collective-permute-start.14 = (bf16[6,256,128]{2,1,0:T(8,128)(2,1)}, bf16[6,256,128]{2,1,0:T(8,128)(2,1)S(1)}, u32[]{:S(2)}, u32[]{:S(2)}) collective-permute-start(bf16[6,256,128]{2,1,0:T(8,128)(2,1)} %get-tuple-element.86), channel_id=1, source_target_pairs={{0,2},{2,0},{4,6},{6,4},{8,10},{10,8},{12,14},{14,12},{1,3},{3,1},... | collective-permute-start | bytes 1179656 | tf_op jit(solution)/shard_map/ppermute | solution.py:41
  67.0 31.3 %collective-permute-start.15 = (bf16[6,256,128]{2,1,0:T(8,128)(2,1)S(1)}, bf16[6,256,128]{2,1,0:T(8,128)(2,1)S(1)}, u32[]{:S(2)}, u32[]{:S(2)}) collective-permute-start(bf16[6,256,128]{2,1,0:T(8,128)(2,1)S(1)} %copy-done.7), channel_id=1, source_target_pairs={{2,4},{4,2},{6,8},{8,6},{10,12},{12,10},{3,5},{5,3},{7,9},{9,7},{1... | collective-permute-start | bytes 1179656 | tf_op jit(solution)/shard_map/ppermute | solution.py:41
  82.9 9.7 %collective-permute-start.18 = (f32[8,1664]{1,0:T(8,128)S(1)}, f32[8,1664]{1,0:T(8,128)}, u32[]{:S(2)}, u32[]{:S(2)}) collective-permute-start(f32[8,1664]{1,0:T(8,128)S(1)} %get-tuple-element.103), channel_id=1, source_target_pairs={{0,4},{1,5},{2,6},{3,7},{4,0},{5,1},{6,2},{7,3},{8,12},{9,13},{10,... | collective-permute-start | bytes 159752 | tf_op jit(solution)/shard_map/ppermute | solution.py:22
  86.0 6.6 %collective-permute-start.19 = (f32[8,1664]{1,0:T(8,128)S(1)}, f32[8,1664]{1,0:T(8,128)S(1)}, u32[]{:S(2)}, u32[]{:S(2)}) collective-permute-start(f32[8,1664]{1,0:T(8,128)S(1)} %get-tuple-element.102), channel_id=1, source_target_pairs={{0,8},{1,9},{2,10},{3,11},{4,12},{5,13},{6,14},{7,15},{8,0},{9,1},... | collective-permute-start | bytes 159752 | tf_op jit(solution)/shard_map/ppermute | solution.py:22
  87.6 5.9 %collective-permute-start.20 = (f32[8,1664]{1,0:T(8,128)S(1)}, f32[8,1664]{1,0:T(8,128)S(1)}, u32[]{:S(2)}, u32[]{:S(2)}) collective-permute-start(f32[8,1664]{1,0:T(8,128)S(1)} %get-tuple-element.101), channel_id=1, source_target_pairs={{0,12},{1,13},{2,14},{3,15},{4,8},{5,9},{6,10},{7,11},{8,4},{9,5},... | collective-permute-start | bytes 159752 | tf_op jit(solution)/shard_map/ppermute | solution.py:22
  88.4 1.0 copy-start.11
  89.4 1.0 copy-start.13
  92.6 5.7 %collective-permute-start.16 = (bf16[6,256,128]{2,1,0:T(8,128)(2,1)S(1)}, bf16[6,256,128]{2,1,0:T(8,128)(2,1)S(1)}, u32[]{:S(2)}, u32[]{:S(2)}) collective-permute-start(bf16[6,256,128]{2,1,0:T(8,128)(2,1)S(1)} %get-tuple-element.88), channel_id=1, source_target_pairs={{0,1},{1,0},{2,3},{3,2},{4,5},{5,4},{6,7},{7,6},{8,9},{9,8},{10,11... | collective-permute-start | bytes 1179656 | tf_op jit(solution)/shard_map/ppermute | solution.py:22
  92.6 1.0 copy-start.17
  93.6 0.6 copy-start.18

commit v7 on v4

--- a/solution.py
+++ b/solution.py
@@ -248,12 +248,13 @@
             out_ref[a * BLOCK : (a + 1) * BLOCK, :, lanes] = total.astype(BF16).reshape(BLOCK, 2, width)
 
 
-def combine(pos, sent, own, faces, head0, heads, feat, width, prev, weight=1):
+def combine(pos, sent, own, faces, head0, heads, feat, width, prev, part=None, weight=1):
     rows = own.shape[1] // 2
-    step = next(n for n in COMBINE_STEPS if heads % n == 0 and head0 % n == 0)
+    lo, heads = part or (0, heads)
+    step = next(n for n in COMBINE_STEPS if heads % n == 0 and head0 % n == 0 and lo % n == 0)
     smem = pl.BlockSpec(memory_space=SMEM)
-    face = pl.BlockSpec((step, 2 * BLOCK, width), lambda h: (h, 0, 0))
-    own_spec = pl.BlockSpec((step, 2 * rows, width), lambda h: (h, 0, 0))
+    face = pl.BlockSpec((step, 2 * BLOCK, width), lambda h: (lo // step + h, 0, 0))
+    own_spec = pl.BlockSpec((step, 2 * rows, width), lambda h: (lo // step + h, 0, 0))
     in_specs = [smem, smem, own_spec, face, face, face]
     args = [pos, sent, own, *faces]
     alias = {}
@@ -265,7 +266,7 @@
         combine_kernel,
         grid=(heads // step,),
         in_specs=in_specs,
-        out_specs=pl.BlockSpec((rows, 2, step * width), lambda h: (0, 0, head0 // step + h)),
+        out_specs=pl.BlockSpec((rows, 2, step * width), lambda h: (0, 0, (head0 + lo) // step + h)),
         out_shape=jax.ShapeDtypeStruct((rows, 2, feat), BF16),
         input_output_aliases=alias,
         compiler_params=pltpu.CompilerParams(vmem_limit_bytes=24 << 20),
@@ -276,6 +277,26 @@
         ),
         name="combine",
     )(*args)
+
+
+def finish_kernel(own_ref, temp_ref, *refs):
+    got, (out_ref, sum_ref) = refs[:-2], refs[-2:]
+    rows, feat = own_ref.shape
+    total, temp = own_ref[...], temp_ref[...]
+    for ref in got:
+        total = total + ref[:, :feat]
+        temp = temp + ref[:1, feat:]
+    out_ref[...] = total.reshape(out_ref.shape)
+    sum_ref[...] = temp
+
+
+def finish(own, temp, got, shape):
+    return pl.pallas_call(
+        finish_kernel,
+        out_shape=[jax.ShapeDtypeStruct(shape, F32), jax.ShapeDtypeStruct(temp.shape, F32)],
+        compiler_params=pltpu.CompilerParams(vmem_limit_bytes=8 << 20),
+        name="finish",
+    )(own, temp, *got)
 
 
 def local(q, mesh_kv, landmark, warm, g, exported, filt):
@@ -329,16 +350,24 @@
             returned[-1] = hold(returned[-1], HOLD)
             got, faces[-1], returned[-1] = lax.optimization_barrier((got, faces[-1], returned[-1]))
             returned.append(send_back(faces[-1]))
-            for c in range(len(chunks) - 1):
-                cell = combine(pos, sent, owns[c], returned[c], *chunks[c], feat, width, cell, weight=4000)
+            got, returned[-1][2] = lax.optimization_barrier((got, returned[-1][2]))
+        head0, heads = chunks[-2]
+        half = heads // 2
+        part = {len(stages) - 2: (0, half), len(stages) - 1: (half, heads - half)}.get(i)
+        if part:
+            cell = combine(
+                pos, sent, owns[-2], returned[-2], head0, heads, feat, width, cell, part=part, weight=4000
+            )
+        if i == len(stages) - 2:
+            got, cell = lax.optimization_barrier((got, cell))
         if i == len(stages) - 1:
+            cell = combine(pos, sent, owns[-1], returned[-1], *chunks[-1], feat, width, cell, weight=0)
             got, cell = lax.optimization_barrier((got, cell))
+            anchor_grad, temp = finish(anc[:n], extra, got, landmark.shape)
+            break
         anc = sum([x[:, :feat] for x in got], anc[:n])
         extra = sum([x[:1, feat:] for x in got], extra)
-    anchor_grad = anc.reshape(landmark.shape)
-    temp = extra[0, :total]
-    cell = combine(pos, sent, owns[-1], returned[-1], *chunks[-1], feat, width, cell, weight=0)
-    return (dq, cell, anchor_grad, temp)
+    return (dq, cell, anchor_grad, temp[0, :total])
 
 
 def solution(mesh):

time: 93 us -> 94.2 us (1.013)
  Pallas kernels: 26.5 us -> 28.3 us
  waiting for transfers between devices: 23.5 us -> 22 us
  local copies, waits for them, and re-layouts: 12 us -> 13 us
    unnamed x36 -> x34, local copies, waits for them, and re-layouts: 8.32 us -> 9.85 us
    ppermute x13, waiting for transfers between devices: 19.3 us -> 17.8 us  [swap_mask(): return lax.ppermute(x, ('gx', 'gy'), [(i, i ^ mask) for i in range(count)])]
    reshape x1 -> x0, local copies, waits for them, and re-layouts: 1.45 us -> none  [local(): anchor_grad = anc.reshape(landmark.shape)]
    pallas_call x2 -> x3, Pallas kernels: 4.39 us -> 5.68 us  [combine(): pl.pallas_call(combine_kernel, grid=(heads // step,), in_specs=in_specs,...]
    slice x3 -> x2, local copies, waits for them, and re-layouts: 0.05 us -> 1.04 us  [local(): anc[k * n:(k + 1) * n]]
  transfers between devices with their start and end apart: 21 -> 21, of which waited for: 7 -> 9; matrix products, arithmetic and copies ran while one was open for 7% -> 6% of each run, Pallas kernels for 26% -> 30%
where the time goes in v7:
time: 94.2 us; the launch traced here: 93.6 us
  Pallas kernels  28.3 us (30%)
  starting transfers between devices  25.3 us (27%)
  waiting for transfers between devices  22 us (23%)
  local copies, waits for them, and re-layouts  13 us (14%)
  other arithmetic  3.94 us (4%)
  between operations  0.98 us (1%)
    pallas_call x2, Pallas kernels, attention(): pl.pallas_call(functools.partial(attention_kernel, gx_count=lax.axis_size...  20.6 us
    ppermute x13, waiting for transfers between devices, swap_mask(): return lax.ppermute(x, ('gx', 'gy'), [(i, i ^ mask) for i in range(count)])  17.8 us
    ppermute x13, starting transfers between devices, swap_mask(): return lax.ppermute(x, ('gx', 'gy'), [(i, i ^ mask) for i in range(count)])  17.3 us
    unnamed x34, local copies, waits for them, and re-layouts  9.85 us
    ppermute x8, starting transfers between devices, swap_pairs(): return lax.ppermute(x, 'gx', route)  8 us
    pallas_call x3, Pallas kernels, combine(): pl.pallas_call(combine_kernel, grid=(heads // step,), in_specs=in_specs,...  5.68 us
    ppermute x8, waiting for transfers between devices, swap_pairs(): return lax.ppermute(x, 'gx', route)  4.24 us
  transfers between devices with their start and end apart: 21, of which 9 were waited for; matrix products, arithmetic and copies ran while one was open for 6% of the time, Pallas kernels for 30%

profile of v7, /device:TPU:0, one launch (start us, length us, event | category | flops | bytes accessed | tf_op | source)
XLA Modules:
  0.0 93.6 jit_solution(12287630764208511643)
XLA Ops:
  0.6 0.8 reshape.53
  1.4 3.0 %collective-permute-start.1 = (bf16[8,1536]{1,0:T(8,128)(2,1)S(1)}, bf16[8,1536]{1,0:T(8,128)(2,1)S(1)}, u32[]{:S(2)}, u32[]{:S(2)}) collective-permute-start(bf16[8,1536]{1,0:T(8,128)(2,1)S(1)} %reshape.53), channel_id=1, source_target_pairs={{0,2},{1,3},{2,0},{3,1},{4,6},{5,7},{6,4},{7,5},{8,10},{9,11},{10,... | collective-permute-start | bytes 73736 | tf_op jit(solution)/shard_map/ppermute | solution.py:22
  4.4 0.7 copy.20.sent_ref
  5.1 1.4 %copy-done = bf16[256,2,1536]{2,1,0:T(2,128)(2,1)S(1)} copy-done((bf16[256,2,1536]{2,1,0:T(2,128)(2,1)S(1)}, bf16[256,2,1536]{2,1,0:T(2,128)(2,1)}, u32[]{:S(2)}) %copy-start) | copy-done | bytes 1572888
  6.5 0.7 pick.3
  7.3 0.7 collective-permute-start.9
  8.0 0.8 pick.2
  8.8 0.6 compare_reduce_fusion
  9.4 4.7 %collective-permute-start.4 = (bf16[16,1536]{1,0:T(8,128)(2,1)S(1)}, bf16[16,1536]{1,0:T(8,128)(2,1)S(1)}, u32[]{:S(2)}, u32[]{:S(2)}) collective-permute-start(bf16[16,1536]{1,0:T(8,128)(2,1)S(1)} %pad_maximum_fusion.6), channel_id=1, source_target_pairs={{0,4},{1,5},{2,6},{3,7},{4,0},{5,1},{6,2},{7,3},{8,12},{9,13},{10,... | collective-permute-start | bytes 147464 | tf_op jit(solution)/shard_map/ppermute | solution.py:22
  14.2 2.6 %collective-permute-start.5 = (bf16[16,1536]{1,0:T(8,128)(2,1)S(1)}, bf16[16,1536]{1,0:T(8,128)(2,1)S(1)}, u32[]{:S(2)}, u32[]{:S(2)}) collective-permute-start(bf16[16,1536]{1,0:T(8,128)(2,1)S(1)} %pad_maximum_fusion.6), channel_id=1, source_target_pairs={{0,8},{1,9},{2,10},{3,11},{4,12},{5,13},{6,14},{7,15},{8,0},{9,1},... | collective-permute-start | bytes 147464 | tf_op jit(solution)/shard_map/ppermute | solution.py:22
  16.8 5.8 %collective-permute-done.4 = bf16[16,1536]{1,0:T(8,128)(2,1)S(1)} collective-permute-done((bf16[16,1536]{1,0:T(8,128)(2,1)S(1)}, bf16[16,1536]{1,0:T(8,128)(2,1)S(1)}, u32[]{:S(2)}, u32[]{:S(2)}) %collective-permute-start.4) | collective-permute-done | bytes 49184 | tf_op jit(solution)/shard_map/ppermute | solution.py:22
  22.6 2.1 %collective-permute-done.5 = bf16[16,1536]{1,0:T(8,128)(2,1)S(1)} collective-permute-done((bf16[16,1536]{1,0:T(8,128)(2,1)S(1)}, bf16[16,1536]{1,0:T(8,128)(2,1)S(1)}, u32[]{:S(2)}, u32[]{:S(2)}) %collective-permute-start.5) | collective-permute-done | bytes 49184 | tf_op jit(solution)/shard_map/ppermute | solution.py:22
  24.6 1.6 %collective-permute-done.6 = bf16[16,1536]{1,0:T(8,128)(2,1)S(1)} collective-permute-done((bf16[16,1536]{1,0:T(8,128)(2,1)S(1)}, bf16[16,1536]{1,0:T(8,128)(2,1)S(1)}, u32[]{:S(2)}, u32[]{:S(2)}) %collective-permute-start.6) | collective-permute-done | bytes 49184 | tf_op jit(solution)/shard_map/ppermute | solution.py:22
  26.3 1.4 %collective-permute-done.7 = bf16[64,1536]{1,0:T(8,128)(2,1)S(1)} collective-permute-done((bf16[64,1536]{1,0:T(8,128)(2,1)S(1)}, bf16[64,1536]{1,0:T(8,128)(2,1)S(1)}, u32[]{:S(2)}, u32[]{:S(2)}) %collective-permute-start.7) | collective-permute-done | bytes 196640 | tf_op jit(solution)/shard_map/ppermute | solution.py:22
  27.7 0.7 collective-permute-start.3
  28.5 1.3 %copy-done.1 = bf16[256,2,1536]{2,1,0:T(2,128)(2,1)S(1)} copy-done((bf16[256,2,1536]{2,1,0:T(2,128)(2,1)S(1)}, bf16[256,2,1536]{2,1,0:T(2,128)(2,1)}, u32[]{:S(2)}) %copy-start.1) | copy-done | bytes 1572888
  29.8 0.2 copy-done.2
  30.0 0.2 copy-done.3
  30.3 10.2 %attention.2 = (bf16[256,1536]{1,0:T(8,128)(2,1)}, f32[6,512,128]{2,1,0:T(8,128)S(1)}, bf16[6,256,128]{2,1,0:T(8,128)(2,1)S(1)}, bf16[6,256,128]{2,1,0:T(8,128)(...) custom-call(s32[1]{0:T(128)} %bitcast.pos_ref, ...), custom_call_target="tpu_custom_call" | custom-call | flops 1384120320 | bytes 6488064 | tf_op jit(solution)/shard_map/attention/pallas_call | solution.py:197
  40.5 2.7 %collective-permute-start.11 = (bf16[6,256,128]{2,1,0:T(8,128)(2,1)S(1)}, bf16[6,256,128]{2,1,0:T(8,128)(2,1)S(1)}, u32[]{:S(2)}, u32[]{:S(2)}) collective-permute-start(bf16[6,256,128]{2,1,0:T(8,128)(2,1)S(1)} %get-tuple-element.79), channel_id=1, source_target_pairs={{0,2},{2,0},{4,6},{6,4},{8,10},{10,8},{12,14},{14,12},{1,3},{3,1},... | collective-permute-start | bytes 1179656 | tf_op jit(solution)/shard_map/ppermute | solution.py:41
  43.3 0.7 collective-permute-start.12
  44.0 10.4 %attention.3 = (bf16[256,1536]{1,0:T(8,128)(2,1)}, f32[6,512,128]{2,1,0:T(8,128)S(1)}, bf16[6,256,128]{2,1,0:T(8,128)(2,1)S(1)}, bf16[6,256,128]{2,1,0:T(8,128)(...) custom-call(s32[1]{0:T(128)} %bitcast.pos_ref, ...), custom_call_target="tpu_custom_call", output_to_operand_aliasing={{0}: (10, {}), {5}: (11, {})} | custom-call | flops 1384120320 | bytes 6488064 | tf_op jit(solution)/shard_map/attention/pallas_call | solution.py:197
  54.6 0.6 fusion.2
  55.3 0.5 collective-permute-start.10
  55.9 4.2 %collective-permute-done.11.refs_0_ = bf16[6,256,128]{2,1,0:T(8,128)(2,1)S(1)} collective-permute-done((bf16[6,256,128]{2,1,0:T(8,128)(2,1)S(1)}, bf16[6,256,128]{2,1,0:T(8,128)(2,1)S(1)}, u32[]{:S(2)}, u32[]{:S(2)}) %collective-permute-start.11) | collective-permute-done | bytes 393248 | tf_op jit(solution)/shard_map/ppermute | solution.py:41
  60.1 0.7 copy-done.6
  60.8 0.8 copy-done.8
  61.6 0.7 copy-done.10
  62.4 2.5 %collective-permute-start.19 = (bf16[6,256,128]{2,1,0:T(8,128)(2,1)S(1)}, bf16[6,256,128]{2,1,0:T(8,128)(2,1)S(1)}, u32[]{:S(2)}, u32[]{:S(2)}) collective-permute-start(bf16[6,256,128]{2,1,0:T(8,128)(2,1)S(1)} %get-tuple-element.96), channel_id=1, source_target_pairs={{0,2},{2,0},{4,6},{6,4},{8,10},{10,8},{12,14},{14,12},{1,3},{3,1},... | collective-permute-start | bytes 1179656 | tf_op jit(solution)/shard_map/ppermute | solution.py:41
  64.8 0.7 collective-permute-start.20
  65.5 0.7 slice_add_fusion.3
  66.2 0.8 slice_add_fusion
  67.1 1.0 %fusion.3 = (f32[16,1536]{1,0:T(8,128)S(1)}, f32[16,1536]{1,0:T(8,128)S(1)}, f32[16,1536]{1,0:T(8,128)S(1)}) fusion(f32[64,1536]{1,0:T(8,128)} %slice_add_fusion), kind=kLoop, calls=%fused_computation.24 | loop fusion | bytes 589824 | tf_op jit(solution)/shard_map/slice | solution.py:346
  68.1 2.8 %collective-permute-start.15 = (f32[16,1664]{1,0:T(8,128)S(1)}, f32[16,1664]{1,0:T(8,128)S(1)}, u32[]{:S(2)}, u32[]{:S(2)}) collective-permute-start(f32[16,1664]{1,0:T(8,128)S(1)} %get-tuple-element.111), channel_id=1, source_target_pairs={{0,4},{1,5},{2,6},{3,7},{4,0},{5,1},{6,2},{7,3},{8,12},{9,13},{10,... | collective-permute-start | bytes 319496 | tf_op jit(solution)/shard_map/ppermute | solution.py:22
  70.9 3.5 %collective-permute-start.16 = (f32[16,1664]{1,0:T(8,128)S(1)}, f32[16,1664]{1,0:T(8,128)S(1)}, u32[]{:S(2)}, u32[]{:S(2)}) collective-permute-start(f32[16,1664]{1,0:T(8,128)S(1)} %get-tuple-element.110), channel_id=1, source_target_pairs={{0,8},{1,9},{2,10},{3,11},{4,12},{5,13},{6,14},{7,15},{8,0},{9,1},... | collective-permute-start | bytes 319496 | tf_op jit(solution)/shard_map/ppermute | solution.py:22
  74.4 1.0 %copy-done.7 = bf16[6,256,128]{2,1,0:T(8,128)(2,1)S(1)} copy-done((bf16[6,256,128]{2,1,0:T(8,128)(2,1)S(1)}, bf16[6,256,128]{2,1,0:T(8,128)(2,1)}, u32[]{:S(2)}) %copy-start.7) | copy-done | bytes 393240
  75.4 1.0 %copy-done.9 = bf16[6,256,128]{2,1,0:T(8,128)(2,1)S(1)} copy-done((bf16[6,256,128]{2,1,0:T(8,128)(2,1)S(1)}, bf16[6,256,128]{2,1,0:T(8,128)(2,1)}, u32[]{:S(2)}) %copy-start.9) | copy-done | bytes 393240
  76.4 1.0 %copy-done.11 = bf16[6,256,128]{2,1,0:T(8,128)(2,1)S(1)} copy-done((bf16[6,256,128]{2,1,0:T(8,128)(2,1)S(1)}, bf16[6,256,128]{2,1,0:T(8,128)(2,1)}, u32[]{:S(2)}) %copy-start.11) | copy-done | bytes 393240
  77.4 1.4 %copy-done.13 = f32[6,512,128]{2,1,0:T(8,128)S(1)} copy-done((f32[6,512,128]{2,1,0:T(8,128)S(1)}, f32[6,512,128]{2,1,0:T(8,128)}, u32[]{:S(2)}) %copy-start.13) | copy-done | bytes 1572888
  78.8 1.7 %combine.3.rest_0_ = bf16[256,2,1536]{2,1,0:T(2,128)(2,1)} custom-call(s32[1]{0:T(128)} %bitcast.pos_ref, s32[3,1]{1,0:T(4,128)S(1)} %copy.20.sent_ref, f32[6,512,128]{2,1,0:T(8,128)S(1)} %copy-done.13, bf16[6,256,128]{2,1,0:T(8,128)(2,1)S(1)} %copy-done.7, bf16[6,256,128]{2,1,0:T(8,128)(2,1)S(1)} %copy-done.9, bf16[6,256,128]{2,1,0:T(8,128)(2,1)S(1)} %copy-done.11), custom_call_target="tpu_custom_call" | custom-call | flops 6291456000 | bytes 1769472 | tf_op jit(solution)/shard_map/combine/pallas_call | solution.py:265
  80.5 1.7 %collective-permute-done.15 = f32[16,1664]{1,0:T(8,128)S(1)} collective-permute-done((f32[16,1664]{1,0:T(8,128)S(1)}, f32[16,1664]{1,0:T(8,128)S(1)}, u32[]{:S(2)}, u32[]{:S(2)}) %collective-permute-start.15) | collective-permute-done | bytes 106528 | tf_op jit(solution)/shard_map/ppermute | solution.py:22
  82.2 0.5 collective-permute-done.16
  82.6 4.7 %collective-permute-done.17 = f32[16,1664]{1,0:T(8,128)S(1)} collective-permute-done((f32[16,1664]{1,0:T(8,128)S(1)}, f32[16,1664]{1,0:T(8,128)S(1)}, u32[]{:S(2)}, u32[]{:S(2)}) %collective-permute-start.17) | collective-permute-done | bytes 106528 | tf_op jit(solution)/shard_map/ppermute | solution.py:22
  87.3 0.9 fusion.1
  88.4 1.7 %combine.4.rest_0_ = bf16[256,2,1536]{2,1,0:T(2,128)(2,1)} custom-call(s32[1]{0:T(128)} %bitcast.pos_ref, s32[3,1]{1,0:T(4,128)S(1)} %copy.20.sent_ref, f32[6,512,128]{2,1,0:T(8,128)S(1)} %copy-done.14, bf16[6,256,128]{2,1,0:T(8,128)(2,1)S(1)} %copy-done.7, bf16[6,256,128]{2,1,0:T(8,128)(2,1)S(1)} %copy-done.9, ...), custom_call_target="tpu_custom_call", output_to_operand_aliasing={{}: (6, {})} | custom-call | flops 6291456000 | bytes 1769472 | tf_op jit(solution)/shard_map/combine/pallas_call | solution.py:265
  90.1 2.2 %combine.5 = bf16[256,2,1536]{2,1,0:T(2,128)(2,1)} custom-call(s32[1]{0:T(128)} %bitcast.pos_ref, s32[3,1]{1,0:T(4,128)S(1)} %copy.20.sent_ref, f32[6,512,128]{2,1,0:T(8,128)S(1)} %get-tuple-element.95.own_ref, bf16[6,256,128]{2,1,0:T(8,128)(2,1)S(1)} %collective-permute-done.19.dir_ref, ...), custom_call_target="tpu_custom_call", output_to_operand_aliasing={{}: (6, {})} | custom-call | bytes 3538944 | tf_op jit(solution)/shard_map/combine/pallas_call | solution.py:265
  92.5 0.6 finish.1
  93.1 0.5 slice_bitcast_fusion
  (63 shorter events, 1.0 us)
Async XLA Ops:
  1.4 8.0 %collective-permute-start.1 = (bf16[8,1536]{1,0:T(8,128)(2,1)S(1)}, bf16[8,1536]{1,0:T(8,128)(2,1)S(1)}, u32[]{:S(2)}, u32[]{:S(2)}) collective-permute-start(bf16[8,1536]{1,0:T(8,128)(2,1)S(1)} %reshape.53), channel_id=1, source_target_pairs={{0,2},{1,3},{2,0},{3,1},{4,6},{5,7},{6,4},{7,5},{8,10},{9,11},{10,... | collective-permute-start | bytes 73736 | tf_op jit(solution)/shard_map/ppermute | solution.py:22
  5.1 1.4 %copy-start = (bf16[256,2,1536]{2,1,0:T(2,128)(2,1)S(1)}, bf16[256,2,1536]{2,1,0:T(2,128)(2,1)}, u32[]{:S(2)}) copy-start(bf16[256,2,1536]{2,1,0:T(2,128)(2,1)} %own_ref.3) | copy-start | bytes 4718596
  7.2 21.3 %collective-permute-start.8 = (bf16[128,2,768]{2,1,0:T(2,128)(2,1)S(1)}, bf16[128,2,768]{2,1,0:T(2,128)(2,1)S(1)}, u32[]{:S(2)}, u32[]{:S(2)}) collective-permute-start(bf16[128,2,768]{2,1,0:T(2,128)(2,1)S(1)} %get-tuple-element.66), channel_id=1, source_target_pairs={{0,2},{2,0},{4,6},{6,4},{8,10},{10,8},{12,14},{14,12},{1,3},{3,1},... | collective-permute-start | bytes 1179656 | tf_op jit(solution)/shard_map/ppermute | solution.py:41
  7.3 21.2 %collective-permute-start.9 = (bf16[128,2,768]{2,1,0:T(2,128)(2,1)S(1)}, bf16[128,2,768]{2,1,0:T(2,128)(2,1)S(1)}, u32[]{:S(2)}, u32[]{:S(2)}) collective-permute-start(bf16[128,2,768]{2,1,0:T(2,128)(2,1)S(1)} %get-tuple-element.67), channel_id=1, source_target_pairs={{2,4},{4,2},{6,8},{8,6},{10,12},{12,10},{3,5},{5,3},{7,9},{9,7},{1... | collective-permute-start | bytes 1179656 | tf_op jit(solution)/shard_map/ppermute | solution.py:41
  9.4 13.2 %collective-permute-start.4 = (bf16[16,1536]{1,0:T(8,128)(2,1)S(1)}, bf16[16,1536]{1,0:T(8,128)(2,1)S(1)}, u32[]{:S(2)}, u32[]{:S(2)}) collective-permute-start(bf16[16,1536]{1,0:T(8,128)(2,1)S(1)} %pad_maximum_fusion.6), channel_id=1, source_target_pairs={{0,4},{1,5},{2,6},{3,7},{4,0},{5,1},{6,2},{7,3},{8,12},{9,13},{10,... | collective-permute-start | bytes 147464 | tf_op jit(solution)/shard_map/ppermute | solution.py:22
  14.2 10.5 %collective-permute-start.5 = (bf16[16,1536]{1,0:T(8,128)(2,1)S(1)}, bf16[16,1536]{1,0:T(8,128)(2,1)S(1)}, u32[]{:S(2)}, u32[]{:S(2)}) collective-permute-start(bf16[16,1536]{1,0:T(8,128)(2,1)S(1)} %pad_maximum_fusion.6), channel_id=1, source_target_pairs={{0,8},{1,9},{2,10},{3,11},{4,12},{5,13},{6,14},{7,15},{8,0},{9,1},... | collective-permute-start | bytes 147464 | tf_op jit(solution)/shard_map/ppermute | solution.py:22
  16.7 9.5 %collective-permute-start.6 = (bf16[16,1536]{1,0:T(8,128)(2,1)S(1)}, bf16[16,1536]{1,0:T(8,128)(2,1)S(1)}, u32[]{:S(2)}, u32[]{:S(2)}) collective-permute-start(bf16[16,1536]{1,0:T(8,128)(2,1)S(1)} %pad_maximum_fusion.6), channel_id=1, source_target_pairs={{0,12},{1,13},{2,14},{3,15},{4,8},{5,9},{6,10},{7,11},{8,4},{9,5},... | collective-permute-start | bytes 147464 | tf_op jit(solution)/shard_map/ppermute | solution.py:22
  22.6 6.0 %collective-permute-start = (bf16[128,2,1536]{2,1,0:T(2,128)(2,1)S(1)}, bf16[128,2,1536]{2,1,0:T(2,128)(2,1)S(1)}, u32[]{:S(2)}, u32[]{:S(2)}) collective-permute-start(bf16[128,2,1536]{2,1,0:T(2,128)(2,1)S(1)} %get-tuple-element.60), channel_id=1, source_target_pairs={{0,1},{1,0},{2,3},{3,2},{4,5},{5,4},{6,7},{7,6},{8,9},{9,8},{10,11... | collective-permute-start | bytes 2359304 | tf_op jit(solution)/shard_map/ppermute | solution.py:22
  24.6 19.4 %collective-permute-start.2 = (bf16[128,2,768]{2,1,0:T(2,128)(2,1)S(1)}, bf16[128,2,768]{2,1,0:T(2,128)(2,1)S(1)}, u32[]{:S(2)}, u32[]{:S(2)}) collective-permute-start(bf16[128,2,768]{2,1,0:T(2,128)(2,1)S(1)} %get-tuple-element.63), channel_id=1, source_target_pairs={{0,2},{2,0},{4,6},{6,4},{8,10},{10,8},{12,14},{14,12},{1,3},{3,1},... | collective-permute-start | bytes 1179656 | tf_op jit(solution)/shard_map/ppermute | solution.py:41
  26.2 1.5 %collective-permute-start.7 = (bf16[64,1536]{1,0:T(8,128)(2,1)S(1)}, bf16[64,1536]{1,0:T(8,128)(2,1)S(1)}, u32[]{:S(2)}, u32[]{:S(2)}) collective-permute-start(bf16[64,1536]{1,0:T(8,128)(2,1)S(1)} %pad_maximum_fusion.1), channel_id=1, source_target_pairs={{0,1},{1,0},{2,3},{3,2},{4,5},{5,4},{6,7},{7,6},{8,9},{9,8},{10,11... | collective-permute-start | bytes 589832 | tf_op jit(solution)/shard_map/ppermute | solution.py:22
  27.7 16.3 %collective-permute-start.3 = (bf16[128,2,768]{2,1,0:T(2,128)(2,1)S(1)}, bf16[128,2,768]{2,1,0:T(2,128)(2,1)S(1)}, u32[]{:S(2)}, u32[]{:S(2)}) collective-permute-start(bf16[128,2,768]{2,1,0:T(2,128)(2,1)S(1)} %get-tuple-element.64), channel_id=1, source_target_pairs={{2,4},{4,2},{6,8},{8,6},{10,12},{12,10},{3,5},{5,3},{7,9},{9,7},{1... | collective-permute-start | bytes 1179656 | tf_op jit(solution)/shard_map/ppermute | solution.py:41
  28.4 1.4 %copy-start.1 = (bf16[256,2,1536]{2,1,0:T(2,128)(2,1)S(1)}, bf16[256,2,1536]{2,1,0:T(2,128)(2,1)}, u32[]{:S(2)}) copy-start(bf16[256,2,1536]{2,1,0:T(2,128)(2,1)} %own_ref.3) | copy-start | bytes 4718596
  28.4 1.6 %copy-start.2 = (bf16[256,1536]{1,0:T(8,128)(2,1)S(1)}, bf16[256,1536]{1,0:T(8,128)(2,1)}, u32[]{:S(2)}) copy-start(bf16[256,1536]{1,0:T(8,128)(2,1)} %q_ref.3) | copy-start | bytes 2359300
  28.5 1.8 %copy-start.3 = (bf16[256,1536]{1,0:T(8,128)(2,1)S(1)}, bf16[256,1536]{1,0:T(8,128)(2,1)}, u32[]{:S(2)}) copy-start(bf16[256,1536]{1,0:T(8,128)(2,1)} %g_ref.3) | copy-start | bytes 2359300
  28.5 1.8 %copy-start.4 = (s32[1,2,5]{2,1,0:T(2,128)S(1)}, s32[1,2,5]{2,1,0:T(2,128)}, u32[]{:S(2)}) copy-start(s32[1,2,5]{2,1,0:T(2,128)} %param.15) | copy-start | bytes 124
  28.5 1.8 %copy-start.5 = (f32[12]{0:T(128)S(1)}, f32[12]{0:T(128)}, u32[]{:S(2)}) copy-start(f32[12]{0:T(128)} %warm_ref.3) | copy-start | bytes 148
  40.5 13.9 %copy-start.12 = (f32[6,512,128]{2,1,0:T(8,128)}, f32[6,512,128]{2,1,0:T(8,128)S(1)}, u32[]{:S(2)}) copy-start(f32[6,512,128]{2,1,0:T(8,128)S(1)} %get-tuple-element.88.own_ref) | copy-start | bytes 4718596
  40.5 19.6 %collective-permute-start.11 = (bf16[6,256,128]{2,1,0:T(8,128)(2,1)S(1)}, bf16[6,256,128]{2,1,0:T(8,128)(2,1)S(1)}, u32[]{:S(2)}, u32[]{:S(2)}) collective-permute-start(bf16[6,256,128]{2,1,0:T(8,128)(2,1)S(1)} %get-tuple-element.79), channel_id=1, source_target_pairs={{0,2},{2,0},{4,6},{6,4},{8,10},{10,8},{12,14},{14,12},{1,3},{3,1},... | collective-permute-start | bytes 1179656 | tf_op jit(solution)/shard_map/ppermute | solution.py:41
  43.3 16.8 %collective-permute-start.12 = (bf16[6,256,128]{2,1,0:T(8,128)(2,1)S(1)}, bf16[6,256,128]{2,1,0:T(8,128)(2,1)S(1)}, u32[]{:S(2)}, u32[]{:S(2)}) collective-permute-start(bf16[6,256,128]{2,1,0:T(8,128)(2,1)S(1)} %get-tuple-element.80), channel_id=1, source_target_pairs={{2,4},{4,2},{6,8},{8,6},{10,12},{12,10},{3,5},{5,3},{7,9},{9,7},{1... | collective-permute-start | bytes 1179656 | tf_op jit(solution)/shard_map/ppermute | solution.py:41
  43.9 16.1 %collective-permute-start.13 = (bf16[6,256,128]{2,1,0:T(8,128)(2,1)S(1)}, bf16[6,256,128]{2,1,0:T(8,128)(2,1)S(1)}, u32[]{:S(2)}, u32[]{:S(2)}) collective-permute-start(bf16[6,256,128]{2,1,0:T(8,128)(2,1)S(1)} %get-tuple-element.81), channel_id=1, source_target_pairs={{0,1},{1,0},{2,3},{3,2},{4,5},{5,4},{6,7},{7,6},{8,9},{9,8},{10,11... | collective-permute-start | bytes 1179656 | tf_op jit(solution)/shard_map/ppermute | solution.py:22
  55.3 7.0 %collective-permute-start.10 = (f32[64,1664]{1,0:T(8,128)S(1)}, f32[64,1664]{1,0:T(8,128)S(1)}, u32[]{:S(2)}, u32[]{:S(2)}) collective-permute-start(f32[64,1664]{1,0:T(8,128)S(1)} %pad_maximum_fusion), channel_id=1, source_target_pairs={{0,1},{1,0},{2,3},{3,2},{4,5},{5,4},{6,7},{7,6},{8,9},{9,8},{10,11... | collective-permute-start | bytes 1277960 | tf_op jit(solution)/shard_map/ppermute | solution.py:22
  60.1 0.7 copy-start.6
  60.8 0.8 copy-start.8
  61.6 0.7 copy-start.10
  62.4 3.2 %collective-permute-start.14 = (bf16[6,256,128]{2,1,0:T(8,128)(2,1)S(1)}, bf16[6,256,128]{2,1,0:T(8,128)(2,1)S(1)}, u32[]{:S(2)}, u32[]{:S(2)}) collective-permute-start(bf16[6,256,128]{2,1,0:T(8,128)(2,1)S(1)} %get-tuple-element.86), channel_id=1, source_target_pairs={{0,1},{1,0},{2,3},{3,2},{4,5},{5,4},{6,7},{7,6},{8,9},{9,8},{10,11... | collective-permute-start | bytes 1179656 | tf_op jit(solution)/shard_map/ppermute | solution.py:22
  62.4 27.8 %collective-permute-start.19 = (bf16[6,256,128]{2,1,0:T(8,128)(2,1)S(1)}, bf16[6,256,128]{2,1,0:T(8,128)(2,1)S(1)}, u32[]{:S(2)}, u32[]{:S(2)}) collective-permute-start(bf16[6,256,128]{2,1,0:T(8,128)(2,1)S(1)} %get-tuple-element.96), channel_id=1, source_target_pairs={{0,2},{2,0},{4,6},{6,4},{8,10},{10,8},{12,14},{14,12},{1,3},{3,1},... | collective-permute-start | bytes 1179656 | tf_op jit(solution)/shard_map/ppermute | solution.py:41
  64.8 25.3 %collective-permute-start.20 = (bf16[6,256,128]{2,1,0:T(8,128)(2,1)S(1)}, bf16[6,256,128]{2,1,0:T(8,128)(2,1)S(1)}, u32[]{:S(2)}, u32[]{:S(2)}) collective-permute-start(bf16[6,256,128]{2,1,0:T(8,128)(2,1)S(1)} %get-tuple-element.97), channel_id=1, source_target_pairs={{2,4},{4,2},{6,8},{8,6},{10,12},{12,10},{3,5},{5,3},{7,9},{9,7},{1... | collective-permute-start | bytes 1179656 | tf_op jit(solution)/shard_map/ppermute | solution.py:41
  68.1 14.0 %collective-permute-start.15 = (f32[16,1664]{1,0:T(8,128)S(1)}, f32[16,1664]{1,0:T(8,128)S(1)}, u32[]{:S(2)}, u32[]{:S(2)}) collective-permute-start(f32[16,1664]{1,0:T(8,128)S(1)} %get-tuple-element.111), channel_id=1, source_target_pairs={{0,4},{1,5},{2,6},{3,7},{4,0},{5,1},{6,2},{7,3},{8,12},{9,13},{10,... | collective-permute-start | bytes 319496 | tf_op jit(solution)/shard_map/ppermute | solution.py:22
  70.9 11.7 %collective-permute-start.16 = (f32[16,1664]{1,0:T(8,128)S(1)}, f32[16,1664]{1,0:T(8,128)S(1)}, u32[]{:S(2)}, u32[]{:S(2)}) collective-permute-start(f32[16,1664]{1,0:T(8,128)S(1)} %get-tuple-element.110), channel_id=1, source_target_pairs={{0,8},{1,9},{2,10},{3,11},{4,12},{5,13},{6,14},{7,15},{8,0},{9,1},... | collective-permute-start | bytes 319496 | tf_op jit(solution)/shard_map/ppermute | solution.py:22
  74.4 12.9 %collective-permute-start.17 = (f32[16,1664]{1,0:T(8,128)S(1)}, f32[16,1664]{1,0:T(8,128)S(1)}, u32[]{:S(2)}, u32[]{:S(2)}) collective-permute-start(f32[16,1664]{1,0:T(8,128)S(1)} %get-tuple-element.109), channel_id=1, source_target_pairs={{0,12},{1,13},{2,14},{3,15},{4,8},{5,9},{6,10},{7,11},{8,4},{9,5},... | collective-permute-start | bytes 319496 | tf_op jit(solution)/shard_map/ppermute | solution.py:22
  74.4 1.0 %copy-start.7 = (bf16[6,256,128]{2,1,0:T(8,128)(2,1)S(1)}, bf16[6,256,128]{2,1,0:T(8,128)(2,1)}, u32[]{:S(2)}) copy-start(bf16[6,256,128]{2,1,0:T(8,128)(2,1)} %copy-done.6) | copy-start | bytes 1179652
  75.4 1.0 %copy-start.9 = (bf16[6,256,128]{2,1,0:T(8,128)(2,1)S(1)}, bf16[6,256,128]{2,1,0:T(8,128)(2,1)}, u32[]{:S(2)}) copy-start(bf16[6,256,128]{2,1,0:T(8,128)(2,1)} %copy-done.8) | copy-start | bytes 1179652
  76.4 1.0 %copy-start.11 = (bf16[6,256,128]{2,1,0:T(8,128)(2,1)S(1)}, bf16[6,256,128]{2,1,0:T(8,128)(2,1)}, u32[]{:S(2)}) copy-start(bf16[6,256,128]{2,1,0:T(8,128)(2,1)} %copy-done.10) | copy-start | bytes 1179652
  77.4 1.4 %copy-start.13 = (f32[6,512,128]{2,1,0:T(8,128)S(1)}, f32[6,512,128]{2,1,0:T(8,128)}, u32[]{:S(2)}) copy-start(f32[6,512,128]{2,1,0:T(8,128)} %copy-done.12) | copy-start | bytes 4718596
  78.8 9.6 %copy-start.14 = (f32[6,512,128]{2,1,0:T(8,128)S(1)}, f32[6,512,128]{2,1,0:T(8,128)}, u32[]{:S(2)}) copy-start(f32[6,512,128]{2,1,0:T(8,128)} %copy-done.12) | copy-start | bytes 4718596
  88.3 4.2 %collective-permute-start.18 = (f32[8,1664]{1,0:T(8,128)S(1)}, f32[8,1664]{1,0:T(8,128)S(1)}, u32[]{:S(2)}, u32[]{:S(2)}) collective-permute-start(f32[8,1664]{1,0:T(8,128)S(1)} %pad_maximum_fusion.5), channel_id=1, source_target_pairs={{0,2},{1,3},{2,0},{3,1},{4,6},{5,7},{6,4},{7,5},{8,10},{9,11},{10,... | collective-permute-start | bytes 159752 | tf_op jit(solution)/shard_map/ppermute | solution.py:22

commit v8 on v7

--- a/solution.py
+++ b/solution.py
@@ -339,6 +339,8 @@
     temp = jnp.sum(jnp.concatenate(temps, axis=0), axis=(1, 2)) / math.sqrt(width)
     extra = jnp.zeros((1, LANES), F32).at[0, :total].set(temp)
     cell = None
+    anc, faces[-1], returned[-1] = lax.optimization_barrier((anc, faces[-1], returned[-1]))
+    returned.append(send_back(faces[-1]))
     for i, masks in enumerate(reversed(stages)):
         n = anc.shape[0] // (len(masks) + 1)
         wide = jnp.broadcast_to(extra, (n, LANES))
@@ -346,19 +348,8 @@
             swap_mask(jnp.concatenate([anc[k * n : (k + 1) * n], wide], axis=1), m)
             for k, m in enumerate(masks, 1)
         ]
-        if i == 0:
-            returned[-1] = hold(returned[-1], HOLD)
-            got, faces[-1], returned[-1] = lax.optimization_barrier((got, faces[-1], returned[-1]))
-            returned.append(send_back(faces[-1]))
-            got, returned[-1][2] = lax.optimization_barrier((got, returned[-1][2]))
-        head0, heads = chunks[-2]
-        half = heads // 2
-        part = {len(stages) - 2: (0, half), len(stages) - 1: (half, heads - half)}.get(i)
-        if part:
-            cell = combine(
-                pos, sent, owns[-2], returned[-2], head0, heads, feat, width, cell, part=part, weight=4000
-            )
         if i == len(stages) - 2:
+            cell = combine(pos, sent, owns[-2], returned[-2], *chunks[-2], feat, width, cell, weight=4000)
             got, cell = lax.optimization_barrier((got, cell))
         if i == len(stages) - 1:
             cell = combine(pos, sent, owns[-1], returned[-1], *chunks[-1], feat, width, cell, weight=0)

time: 94.2 us -> 91.2 us (0.968)
  local copies, waits for them, and re-layouts: 13 us -> 7.46 us
  waiting for transfers between devices: 22 us -> 27 us
  Pallas kernels: 28.3 us -> 27.1 us
    unnamed x34, local copies, waits for them, and re-layouts: 9.85 us -> 5.26 us
    ppermute x13, waiting for transfers between devices: 17.8 us -> 22.2 us  [swap_mask(): return lax.ppermute(x, ('gx', 'gy'), [(i, i ^ mask) for i in range(count)])]
    pallas_call x3 -> x2, Pallas kernels: 5.68 us -> 4.39 us  [combine(): pl.pallas_call(combine_kernel, grid=(heads // step,), in_specs=in_specs,...]
    slice x2, local copies, waits for them, and re-layouts: 1.04 us -> 0.05 us  [local(): anc[k * n:(k + 1) * n]]
  transfers between devices with their start and end apart: 21 -> 21, of which waited for: 9 -> 9; matrix products, arithmetic and copies ran while one was open for 6% -> 5% of each run, Pallas kernels for 30% -> 29%
where the time goes in v8:
time: 91.2 us; the launch traced here: 90.9 us
  Pallas kernels  27.1 us (30%)
  waiting for transfers between devices  27 us (30%)
  starting transfers between devices  24.9 us (27%)
  local copies, waits for them, and re-layouts  7.46 us (8%)
  other arithmetic  3.42 us (4%)
  between operations  1.05 us (1%)
    ppermute x13, waiting for transfers between devices, swap_mask(): return lax.ppermute(x, ('gx', 'gy'), [(i, i ^ mask) for i in range(count)])  22.2 us
    pallas_call x2, Pallas kernels, attention(): pl.pallas_call(functools.partial(attention_kernel, gx_count=lax.axis_size...  20.6 us
    ppermute x13, starting transfers between devices, swap_mask(): return lax.ppermute(x, ('gx', 'gy'), [(i, i ^ mask) for i in range(count)])  16.9 us
    ppermute x8, starting transfers between devices, swap_pairs(): return lax.ppermute(x, 'gx', route)  8 us
    unnamed x34, local copies, waits for them, and re-layouts  5.26 us
    ppermute x8, waiting for transfers between devices, swap_pairs(): return lax.ppermute(x, 'gx', route)  4.81 us
    pallas_call x2, Pallas kernels, combine(): pl.pallas_call(combine_kernel, grid=(heads // step,), in_specs=in_specs,...  4.39 us
  transfers between devices with their start and end apart: 21, of which 9 were waited for; matrix products, arithmetic and copies ran while one was open for 5% of the time, Pallas kernels for 29%

profile of v8, /device:TPU:0, one launch (start us, length us, event | category | flops | bytes accessed | tf_op | source)
XLA Modules:
  0.0 90.9 jit_solution(6816549140882849105)
XLA Ops:
  0.6 0.8 reshape.53
  1.4 3.0 %collective-permute-start.1 = (bf16[8,1536]{1,0:T(8,128)(2,1)S(1)}, bf16[8,1536]{1,0:T(8,128)(2,1)S(1)}, u32[]{:S(2)}, u32[]{:S(2)}) collective-permute-start(bf16[8,1536]{1,0:T(8,128)(2,1)S(1)} %reshape.53), channel_id=1, source_target_pairs={{0,2},{1,3},{2,0},{3,1},{4,6},{5,7},{6,4},{7,5},{8,10},{9,11},{10,... | collective-permute-start | bytes 73736 | tf_op jit(solution)/shard_map/ppermute | solution.py:22
  4.4 0.7 copy.16.sent_ref
  5.1 1.4 %copy-done = bf16[256,2,1536]{2,1,0:T(2,128)(2,1)S(1)} copy-done((bf16[256,2,1536]{2,1,0:T(2,128)(2,1)S(1)}, bf16[256,2,1536]{2,1,0:T(2,128)(2,1)}, u32[]{:S(2)}) %copy-start) | copy-done | bytes 1572888
  6.5 0.7 pick.3
  7.2 0.1 collective-permute-start.8
  7.3 0.7 collective-permute-start.9
  8.0 0.8 pick.2
  8.8 0.6 compare_reduce_fusion
  9.4 4.7 %collective-permute-start.4 = (bf16[16,1536]{1,0:T(8,128)(2,1)S(1)}, bf16[16,1536]{1,0:T(8,128)(2,1)S(1)}, u32[]{:S(2)}, u32[]{:S(2)}) collective-permute-start(bf16[16,1536]{1,0:T(8,128)(2,1)S(1)} %pad_maximum_fusion.6), channel_id=1, source_target_pairs={{0,4},{1,5},{2,6},{3,7},{4,0},{5,1},{6,2},{7,3},{8,12},{9,13},{10,... | collective-permute-start | bytes 147464 | tf_op jit(solution)/shard_map/ppermute | solution.py:22
  14.2 2.6 %collective-permute-start.5 = (bf16[16,1536]{1,0:T(8,128)(2,1)S(1)}, bf16[16,1536]{1,0:T(8,128)(2,1)S(1)}, u32[]{:S(2)}, u32[]{:S(2)}) collective-permute-start(bf16[16,1536]{1,0:T(8,128)(2,1)S(1)} %pad_maximum_fusion.6), channel_id=1, source_target_pairs={{0,8},{1,9},{2,10},{3,11},{4,12},{5,13},{6,14},{7,15},{8,0},{9,1},... | collective-permute-start | bytes 147464 | tf_op jit(solution)/shard_map/ppermute | solution.py:22
  16.8 5.8 %collective-permute-done.4 = bf16[16,1536]{1,0:T(8,128)(2,1)S(1)} collective-permute-done((bf16[16,1536]{1,0:T(8,128)(2,1)S(1)}, bf16[16,1536]{1,0:T(8,128)(2,1)S(1)}, u32[]{:S(2)}, u32[]{:S(2)}) %collective-permute-start.4) | collective-permute-done | bytes 49184 | tf_op jit(solution)/shard_map/ppermute | solution.py:22
  22.6 2.1 %collective-permute-done.5 = bf16[16,1536]{1,0:T(8,128)(2,1)S(1)} collective-permute-done((bf16[16,1536]{1,0:T(8,128)(2,1)S(1)}, bf16[16,1536]{1,0:T(8,128)(2,1)S(1)}, u32[]{:S(2)}, u32[]{:S(2)}) %collective-permute-start.5) | collective-permute-done | bytes 49184 | tf_op jit(solution)/shard_map/ppermute | solution.py:22
  24.6 1.6 %collective-permute-done.6 = bf16[16,1536]{1,0:T(8,128)(2,1)S(1)} collective-permute-done((bf16[16,1536]{1,0:T(8,128)(2,1)S(1)}, bf16[16,1536]{1,0:T(8,128)(2,1)S(1)}, u32[]{:S(2)}, u32[]{:S(2)}) %collective-permute-start.6) | collective-permute-done | bytes 49184 | tf_op jit(solution)/shard_map/ppermute | solution.py:22
  26.2 0.1 collective-permute-start.7
  26.3 1.4 %collective-permute-done.7 = bf16[64,1536]{1,0:T(8,128)(2,1)S(1)} collective-permute-done((bf16[64,1536]{1,0:T(8,128)(2,1)S(1)}, bf16[64,1536]{1,0:T(8,128)(2,1)S(1)}, u32[]{:S(2)}, u32[]{:S(2)}) %collective-permute-start.7) | collective-permute-done | bytes 196640 | tf_op jit(solution)/shard_map/ppermute | solution.py:22
  27.7 0.7 collective-permute-start.3
  28.5 1.3 %copy-done.1 = bf16[256,2,1536]{2,1,0:T(2,128)(2,1)S(1)} copy-done((bf16[256,2,1536]{2,1,0:T(2,128)(2,1)S(1)}, bf16[256,2,1536]{2,1,0:T(2,128)(2,1)}, u32[]{:S(2)}) %copy-start.1) | copy-done | bytes 1572888
  29.8 0.2 copy-done.2
  30.0 0.2 copy-done.3
  30.3 10.2 %attention.2 = (bf16[256,1536]{1,0:T(8,128)(2,1)}, f32[6,512,128]{2,1,0:T(8,128)S(1)}, bf16[6,256,128]{2,1,0:T(8,128)(2,1)S(1)}, bf16[6,256,128]{2,1,0:T(8,128)(...) custom-call(s32[1]{0:T(128)} %bitcast.pos_ref, ...), custom_call_target="tpu_custom_call" | custom-call | flops 1384120320 | bytes 6488064 | tf_op jit(solution)/shard_map/attention/pallas_call | solution.py:197
  40.5 2.7 %collective-permute-start.10 = (bf16[6,256,128]{2,1,0:T(8,128)(2,1)S(1)}, bf16[6,256,128]{2,1,0:T(8,128)(2,1)S(1)}, u32[]{:S(2)}, u32[]{:S(2)}) collective-permute-start(bf16[6,256,128]{2,1,0:T(8,128)(2,1)S(1)} %get-tuple-element.72), channel_id=1, source_target_pairs={{0,2},{2,0},{4,6},{6,4},{8,10},{10,8},{12,14},{14,12},{1,3},{3,1},... | collective-permute-start | bytes 1179656 | tf_op jit(solution)/shard_map/ppermute | solution.py:41
  43.3 0.7 collective-permute-start.11
  43.9 0.1 collective-permute-start.12
  44.0 10.4 %attention.3 = (bf16[256,1536]{1,0:T(8,128)(2,1)}, f32[6,512,128]{2,1,0:T(8,128)S(1)}, bf16[6,256,128]{2,1,0:T(8,128)(2,1)}, bf16[6,256,128]{2,1,0:T(8,128)(2,1)...) custom-call(s32[1]{0:T(128)} %bitcast.pos_ref, ...), custom_call_target="tpu_custom_call", output_to_operand_aliasing={{0}: (10, {}), {5}: (11, {})} | custom-call | flops 1384120320 | bytes 6488064 | tf_op jit(solution)/shard_map/attention/pallas_call | solution.py:197
  54.4 0.2 maximum_reduce_fusion
  54.6 0.6 fusion.2
  55.3 4.8 %collective-permute-done.10.dir_ref = bf16[6,256,128]{2,1,0:T(8,128)(2,1)S(1)} collective-permute-done((bf16[6,256,128]{2,1,0:T(8,128)(2,1)S(1)}, bf16[6,256,128]{2,1,0:T(8,128)(2,1)S(1)}, u32[]{:S(2)}, u32[]{:S(2)}) %collective-permute-start.10) | collective-permute-done | bytes 393248 | tf_op jit(solution)/shard_map/ppermute | solution.py:41
  60.2 0.1 collective-permute-start.13
  60.3 0.6 copy-done.6
  60.8 2.5 %collective-permute-start.18 = (bf16[6,256,128]{2,1,0:T(8,128)(2,1)}, bf16[6,256,128]{2,1,0:T(8,128)(2,1)S(1)}, u32[]{:S(2)}, u32[]{:S(2)}) collective-permute-start(bf16[6,256,128]{2,1,0:T(8,128)(2,1)} %get-tuple-element.86), channel_id=1, source_target_pairs={{0,2},{2,0},{4,6},{6,4},{8,10},{10,8},{12,14},{14,12},{1,3},{3,1},... | collective-permute-start | bytes 1179656 | tf_op jit(solution)/shard_map/ppermute | solution.py:41
  63.3 0.7 collective-permute-start.19
  64.0 0.7 slice_add_fusion.2
  64.7 0.1 copy-done.14
  64.8 0.1 add.30
  64.9 1.2 %slice_add_fusion = f32[64,1536]{1,0:T(8,128)S(1)} fusion(f32[64,1664]{1,0:T(8,128)} %copy-done.14, f32[128,1536]{1,0:T(8,128)S(1)} %get-tuple-element.75), kind=kLoop, calls=%fused_computation.1 | loop fusion | flops 98304 | bytes 1179648 | tf_op jit(solution)/shard_map/add | solution.py:359
  66.1 2.9 %collective-permute-start.14 = (f32[16,1664]{1,0:T(8,128)S(1)}, f32[16,1664]{1,0:T(8,128)S(1)}, u32[]{:S(2)}, u32[]{:S(2)}) collective-permute-start(f32[16,1664]{1,0:T(8,128)S(1)} %get-tuple-element.101), channel_id=1, source_target_pairs={{0,4},{1,5},{2,6},{3,7},{4,0},{5,1},{6,2},{7,3},{8,12},{9,13},{10,... | collective-permute-start | bytes 319496 | tf_op jit(solution)/shard_map/ppermute | solution.py:22
  69.0 3.3 %collective-permute-start.15 = (f32[16,1664]{1,0:T(8,128)S(1)}, f32[16,1664]{1,0:T(8,128)S(1)}, u32[]{:S(2)}, u32[]{:S(2)}) collective-permute-start(f32[16,1664]{1,0:T(8,128)S(1)} %get-tuple-element.100), channel_id=1, source_target_pairs={{0,8},{1,9},{2,10},{3,11},{4,12},{5,13},{6,14},{7,15},{8,0},{9,1},... | collective-permute-start | bytes 319496 | tf_op jit(solution)/shard_map/ppermute | solution.py:22
  72.4 1.4 %copy-done.13 = f32[6,512,128]{2,1,0:T(8,128)S(1)} copy-done((f32[6,512,128]{2,1,0:T(8,128)S(1)}, f32[6,512,128]{2,1,0:T(8,128)}, u32[]{:S(2)}) %copy-start.13) | copy-done | bytes 1572888
  73.8 2.2 %combine.2.rest_0_ = bf16[256,2,1536]{2,1,0:T(2,128)(2,1)} custom-call(s32[1]{0:T(128)} %bitcast.pos_ref, s32[3,1]{1,0:T(4,128)S(1)} %copy.16.sent_ref, f32[6,512,128]{2,1,0:T(8,128)S(1)} %copy-done.13, bf16[6,256,128]{2,1,0:T(8,128)(2,1)S(1)} %copy-done.7, bf16[6,256,128]{2,1,0:T(8,128)(2,1)S(1)} %copy-done.9, bf16[6,256,128]{2,1,0:T(8,128)(2,1)S(1)} %copy-done.11), custom_call_target="tpu_custom_call" | custom-call | flops 12582912000 | bytes 3538944 | tf_op jit(solution)/shard_map/combine/pallas_call | solution.py:265
  76.0 3.7 %collective-permute-done.14 = f32[16,1664]{1,0:T(8,128)S(1)} collective-permute-done((f32[16,1664]{1,0:T(8,128)S(1)}, f32[16,1664]{1,0:T(8,128)S(1)}, u32[]{:S(2)}, u32[]{:S(2)}) %collective-permute-start.14) | collective-permute-done | bytes 106528 | tf_op jit(solution)/shard_map/ppermute | solution.py:22
  79.7 2.5 %collective-permute-done.15 = f32[16,1664]{1,0:T(8,128)S(1)} collective-permute-done((f32[16,1664]{1,0:T(8,128)S(1)}, f32[16,1664]{1,0:T(8,128)S(1)}, u32[]{:S(2)}, u32[]{:S(2)}) %collective-permute-start.15) | collective-permute-done | bytes 106528 | tf_op jit(solution)/shard_map/ppermute | solution.py:22
  82.2 3.3 %collective-permute-done.16 = f32[16,1664]{1,0:T(8,128)S(1)} collective-permute-done((f32[16,1664]{1,0:T(8,128)S(1)}, f32[16,1664]{1,0:T(8,128)S(1)}, u32[]{:S(2)}, u32[]{:S(2)}) %collective-permute-start.16) | collective-permute-done | bytes 106528 | tf_op jit(solution)/shard_map/ppermute | solution.py:22
  85.5 0.1 collective-permute-start.17
  85.6 2.2 %combine.3 = bf16[256,2,1536]{2,1,0:T(2,128)(2,1)} custom-call(s32[1]{0:T(128)} %bitcast.pos_ref, s32[3,1]{1,0:T(4,128)S(1)} %copy.16.sent_ref, f32[6,512,128]{2,1,0:T(8,128)S(1)} %get-tuple-element.85.own_ref, bf16[6,256,128]{2,1,0:T(8,128)(2,1)S(1)} %collective-permute-done.18.dir_ref, ...), custom_call_target="tpu_custom_call", output_to_operand_aliasing={{}: (6, {})} | custom-call | bytes 3538944 | tf_op jit(solution)/shard_map/combine/pallas_call | solution.py:265
  87.8 1.9 %collective-permute-done.17.refs_0_ = f32[8,1664]{1,0:T(8,128)S(1)} collective-permute-done((f32[8,1664]{1,0:T(8,128)S(1)}, f32[8,1664]{1,0:T(8,128)S(1)}, u32[]{:S(2)}, u32[]{:S(2)}) %collective-permute-start.17) | collective-permute-done | bytes 53280 | tf_op jit(solution)/shard_map/ppermute | solution.py:22
  89.7 0.6 finish.1
  90.4 0.5 slice_bitcast_fusion
  (61 shorter events, 0.4 us)
Async XLA Ops:
  1.4 8.0 %collective-permute-start.1 = (bf16[8,1536]{1,0:T(8,128)(2,1)S(1)}, bf16[8,1536]{1,0:T(8,128)(2,1)S(1)}, u32[]{:S(2)}, u32[]{:S(2)}) collective-permute-start(bf16[8,1536]{1,0:T(8,128)(2,1)S(1)} %reshape.53), channel_id=1, source_target_pairs={{0,2},{1,3},{2,0},{3,1},{4,6},{5,7},{6,4},{7,5},{8,10},{9,11},{10,... | collective-permute-start | bytes 73736 | tf_op jit(solution)/shard_map/ppermute | solution.py:22
  5.1 1.4 %copy-start = (bf16[256,2,1536]{2,1,0:T(2,128)(2,1)S(1)}, bf16[256,2,1536]{2,1,0:T(2,128)(2,1)}, u32[]{:S(2)}) copy-start(bf16[256,2,1536]{2,1,0:T(2,128)(2,1)} %own_ref.3) | copy-start | bytes 4718596
  7.2 21.3 %collective-permute-start.8 = (bf16[128,2,768]{2,1,0:T(2,128)(2,1)S(1)}, bf16[128,2,768]{2,1,0:T(2,128)(2,1)S(1)}, u32[]{:S(2)}, u32[]{:S(2)}) collective-permute-start(bf16[128,2,768]{2,1,0:T(2,128)(2,1)S(1)} %get-tuple-element.61), channel_id=1, source_target_pairs={{0,2},{2,0},{4,6},{6,4},{8,10},{10,8},{12,14},{14,12},{1,3},{3,1},... | collective-permute-start | bytes 1179656 | tf_op jit(solution)/shard_map/ppermute | solution.py:41
  7.3 21.2 %collective-permute-start.9 = (bf16[128,2,768]{2,1,0:T(2,128)(2,1)S(1)}, bf16[128,2,768]{2,1,0:T(2,128)(2,1)S(1)}, u32[]{:S(2)}, u32[]{:S(2)}) collective-permute-start(bf16[128,2,768]{2,1,0:T(2,128)(2,1)S(1)} %get-tuple-element.62), channel_id=1, source_target_pairs={{2,4},{4,2},{6,8},{8,6},{10,12},{12,10},{3,5},{5,3},{7,9},{9,7},{1... | collective-permute-start | bytes 1179656 | tf_op jit(solution)/shard_map/ppermute | solution.py:41
  9.4 13.2 %collective-permute-start.4 = (bf16[16,1536]{1,0:T(8,128)(2,1)S(1)}, bf16[16,1536]{1,0:T(8,128)(2,1)S(1)}, u32[]{:S(2)}, u32[]{:S(2)}) collective-permute-start(bf16[16,1536]{1,0:T(8,128)(2,1)S(1)} %pad_maximum_fusion.6), channel_id=1, source_target_pairs={{0,4},{1,5},{2,6},{3,7},{4,0},{5,1},{6,2},{7,3},{8,12},{9,13},{10,... | collective-permute-start | bytes 147464 | tf_op jit(solution)/shard_map/ppermute | solution.py:22
  14.2 10.5 %collective-permute-start.5 = (bf16[16,1536]{1,0:T(8,128)(2,1)S(1)}, bf16[16,1536]{1,0:T(8,128)(2,1)S(1)}, u32[]{:S(2)}, u32[]{:S(2)}) collective-permute-start(bf16[16,1536]{1,0:T(8,128)(2,1)S(1)} %pad_maximum_fusion.6), channel_id=1, source_target_pairs={{0,8},{1,9},{2,10},{3,11},{4,12},{5,13},{6,14},{7,15},{8,0},{9,1},... | collective-permute-start | bytes 147464 | tf_op jit(solution)/shard_map/ppermute | solution.py:22
  16.7 9.5 %collective-permute-start.6 = (bf16[16,1536]{1,0:T(8,128)(2,1)S(1)}, bf16[16,1536]{1,0:T(8,128)(2,1)S(1)}, u32[]{:S(2)}, u32[]{:S(2)}) collective-permute-start(bf16[16,1536]{1,0:T(8,128)(2,1)S(1)} %pad_maximum_fusion.6), channel_id=1, source_target_pairs={{0,12},{1,13},{2,14},{3,15},{4,8},{5,9},{6,10},{7,11},{8,4},{9,5},... | collective-permute-start | bytes 147464 | tf_op jit(solution)/shard_map/ppermute | solution.py:22
  22.6 6.0 %collective-permute-start = (bf16[128,2,1536]{2,1,0:T(2,128)(2,1)S(1)}, bf16[128,2,1536]{2,1,0:T(2,128)(2,1)S(1)}, u32[]{:S(2)}, u32[]{:S(2)}) collective-permute-start(bf16[128,2,1536]{2,1,0:T(2,128)(2,1)S(1)} %get-tuple-element.55), channel_id=1, source_target_pairs={{0,1},{1,0},{2,3},{3,2},{4,5},{5,4},{6,7},{7,6},{8,9},{9,8},{10,11... | collective-permute-start | bytes 2359304 | tf_op jit(solution)/shard_map/ppermute | solution.py:22
  24.6 19.4 %collective-permute-start.2 = (bf16[128,2,768]{2,1,0:T(2,128)(2,1)S(1)}, bf16[128,2,768]{2,1,0:T(2,128)(2,1)S(1)}, u32[]{:S(2)}, u32[]{:S(2)}) collective-permute-start(bf16[128,2,768]{2,1,0:T(2,128)(2,1)S(1)} %get-tuple-element.58), channel_id=1, source_target_pairs={{0,2},{2,0},{4,6},{6,4},{8,10},{10,8},{12,14},{14,12},{1,3},{3,1},... | collective-permute-start | bytes 1179656 | tf_op jit(solution)/shard_map/ppermute | solution.py:41
  26.2 1.5 %collective-permute-start.7 = (bf16[64,1536]{1,0:T(8,128)(2,1)S(1)}, bf16[64,1536]{1,0:T(8,128)(2,1)S(1)}, u32[]{:S(2)}, u32[]{:S(2)}) collective-permute-start(bf16[64,1536]{1,0:T(8,128)(2,1)S(1)} %pad_maximum_fusion.1), channel_id=1, source_target_pairs={{0,1},{1,0},{2,3},{3,2},{4,5},{5,4},{6,7},{7,6},{8,9},{9,8},{10,11... | collective-permute-start | bytes 589832 | tf_op jit(solution)/shard_map/ppermute | solution.py:22
  27.7 16.3 %collective-permute-start.3 = (bf16[128,2,768]{2,1,0:T(2,128)(2,1)S(1)}, bf16[128,2,768]{2,1,0:T(2,128)(2,1)S(1)}, u32[]{:S(2)}, u32[]{:S(2)}) collective-permute-start(bf16[128,2,768]{2,1,0:T(2,128)(2,1)S(1)} %get-tuple-element.59), channel_id=1, source_target_pairs={{2,4},{4,2},{6,8},{8,6},{10,12},{12,10},{3,5},{5,3},{7,9},{9,7},{1... | collective-permute-start | bytes 1179656 | tf_op jit(solution)/shard_map/ppermute | solution.py:41
  28.4 1.4 %copy-start.1 = (bf16[256,2,1536]{2,1,0:T(2,128)(2,1)S(1)}, bf16[256,2,1536]{2,1,0:T(2,128)(2,1)}, u32[]{:S(2)}) copy-start(bf16[256,2,1536]{2,1,0:T(2,128)(2,1)} %own_ref.3) | copy-start | bytes 4718596
  28.4 1.6 %copy-start.2 = (bf16[256,1536]{1,0:T(8,128)(2,1)S(1)}, bf16[256,1536]{1,0:T(8,128)(2,1)}, u32[]{:S(2)}) copy-start(bf16[256,1536]{1,0:T(8,128)(2,1)} %q_ref.3) | copy-start | bytes 2359300
  28.5 1.8 %copy-start.3 = (bf16[256,1536]{1,0:T(8,128)(2,1)S(1)}, bf16[256,1536]{1,0:T(8,128)(2,1)}, u32[]{:S(2)}) copy-start(bf16[256,1536]{1,0:T(8,128)(2,1)} %g_ref.3) | copy-start | bytes 2359300
  28.5 1.8 %copy-start.4 = (s32[1,2,5]{2,1,0:T(2,128)S(1)}, s32[1,2,5]{2,1,0:T(2,128)}, u32[]{:S(2)}) copy-start(s32[1,2,5]{2,1,0:T(2,128)} %param.15) | copy-start | bytes 124
  28.5 1.8 %copy-start.5 = (f32[12]{0:T(128)S(1)}, f32[12]{0:T(128)}, u32[]{:S(2)}) copy-start(f32[12]{0:T(128)} %warm_ref.3) | copy-start | bytes 148
  40.5 13.9 %copy-start.12 = (f32[6,512,128]{2,1,0:T(8,128)}, f32[6,512,128]{2,1,0:T(8,128)S(1)}, u32[]{:S(2)}) copy-start(f32[6,512,128]{2,1,0:T(8,128)S(1)} %get-tuple-element.78.own_ref) | copy-start | bytes 4718596
  40.5 19.6 %collective-permute-start.10 = (bf16[6,256,128]{2,1,0:T(8,128)(2,1)S(1)}, bf16[6,256,128]{2,1,0:T(8,128)(2,1)S(1)}, u32[]{:S(2)}, u32[]{:S(2)}) collective-permute-start(bf16[6,256,128]{2,1,0:T(8,128)(2,1)S(1)} %get-tuple-element.72), channel_id=1, source_target_pairs={{0,2},{2,0},{4,6},{6,4},{8,10},{10,8},{12,14},{14,12},{1,3},{3,1},... | collective-permute-start | bytes 1179656 | tf_op jit(solution)/shard_map/ppermute | solution.py:41
  43.3 16.8 %collective-permute-start.11 = (bf16[6,256,128]{2,1,0:T(8,128)(2,1)S(1)}, bf16[6,256,128]{2,1,0:T(8,128)(2,1)S(1)}, u32[]{:S(2)}, u32[]{:S(2)}) collective-permute-start(bf16[6,256,128]{2,1,0:T(8,128)(2,1)S(1)} %get-tuple-element.73), channel_id=1, source_target_pairs={{2,4},{4,2},{6,8},{8,6},{10,12},{12,10},{3,5},{5,3},{7,9},{9,7},{1... | collective-permute-start | bytes 1179656 | tf_op jit(solution)/shard_map/ppermute | solution.py:41
  43.9 16.2 %collective-permute-start.12 = (bf16[6,256,128]{2,1,0:T(8,128)(2,1)S(1)}, bf16[6,256,128]{2,1,0:T(8,128)(2,1)S(1)}, u32[]{:S(2)}, u32[]{:S(2)}) collective-permute-start(bf16[6,256,128]{2,1,0:T(8,128)(2,1)S(1)} %get-tuple-element.74), channel_id=1, source_target_pairs={{0,1},{1,0},{2,3},{3,2},{4,5},{5,4},{6,7},{7,6},{8,9},{9,8},{10,11... | collective-permute-start | bytes 1179656 | tf_op jit(solution)/shard_map/ppermute | solution.py:22
  60.1 0.7 copy-start.6
  60.1 3.2 %copy-start.8 = (bf16[6,256,128]{2,1,0:T(8,128)(2,1)}, bf16[6,256,128]{2,1,0:T(8,128)(2,1)S(1)}, u32[]{:S(2)}) copy-start(bf16[6,256,128]{2,1,0:T(8,128)(2,1)S(1)} %collective-permute-done.11.dia_ref) | copy-start | bytes 1179652
  60.1 3.9 %copy-start.10 = (bf16[6,256,128]{2,1,0:T(8,128)(2,1)}, bf16[6,256,128]{2,1,0:T(8,128)(2,1)S(1)}, u32[]{:S(2)}) copy-start(bf16[6,256,128]{2,1,0:T(8,128)(2,1)S(1)} %collective-permute-done.12.par_ref) | copy-start | bytes 1179652
  60.2 3.8 %collective-permute-start.13 = (f32[64,1664]{1,0:T(8,128)S(1)}, f32[64,1664]{1,0:T(8,128)S(1)}, u32[]{:S(2)}, u32[]{:S(2)}) collective-permute-start(f32[64,1664]{1,0:T(8,128)S(1)} %pad_maximum_fusion), channel_id=1, source_target_pairs={{0,1},{1,0},{2,3},{3,2},{4,5},{5,4},{6,7},{7,6},{8,9},{9,8},{10,11... | collective-permute-start | bytes 1277960 | tf_op jit(solution)/shard_map/ppermute | solution.py:22
  60.8 24.8 %collective-permute-start.18 = (bf16[6,256,128]{2,1,0:T(8,128)(2,1)}, bf16[6,256,128]{2,1,0:T(8,128)(2,1)S(1)}, u32[]{:S(2)}, u32[]{:S(2)}) collective-permute-start(bf16[6,256,128]{2,1,0:T(8,128)(2,1)} %get-tuple-element.86), channel_id=1, source_target_pairs={{0,2},{2,0},{4,6},{6,4},{8,10},{10,8},{12,14},{14,12},{1,3},{3,1},... | collective-permute-start | bytes 1179656 | tf_op jit(solution)/shard_map/ppermute | solution.py:41
  63.3 22.3 %collective-permute-start.19 = (bf16[6,256,128]{2,1,0:T(8,128)(2,1)}, bf16[6,256,128]{2,1,0:T(8,128)(2,1)S(1)}, u32[]{:S(2)}, u32[]{:S(2)}) collective-permute-start(bf16[6,256,128]{2,1,0:T(8,128)(2,1)} %get-tuple-element.87), channel_id=1, source_target_pairs={{2,4},{4,2},{6,8},{8,6},{10,12},{12,10},{3,5},{5,3},{7,9},{9,7},{1... | collective-permute-start | bytes 1179656 | tf_op jit(solution)/shard_map/ppermute | solution.py:41
  64.0 0.8 copy-start.14
  64.9 7.5 %copy-start.7 = (bf16[6,256,128]{2,1,0:T(8,128)(2,1)S(1)}, bf16[6,256,128]{2,1,0:T(8,128)(2,1)}, u32[]{:S(2)}) copy-start(bf16[6,256,128]{2,1,0:T(8,128)(2,1)} %copy-done.6) | copy-start | bytes 1179652
  64.9 7.5 %copy-start.9 = (bf16[6,256,128]{2,1,0:T(8,128)(2,1)S(1)}, bf16[6,256,128]{2,1,0:T(8,128)(2,1)}, u32[]{:S(2)}) copy-start(bf16[6,256,128]{2,1,0:T(8,128)(2,1)} %copy-done.8) | copy-start | bytes 1179652
  64.9 7.5 %copy-start.11 = (bf16[6,256,128]{2,1,0:T(8,128)(2,1)S(1)}, bf16[6,256,128]{2,1,0:T(8,128)(2,1)}, u32[]{:S(2)}) copy-start(bf16[6,256,128]{2,1,0:T(8,128)(2,1)} %copy-done.10) | copy-start | bytes 1179652
  66.1 13.6 %collective-permute-start.14 = (f32[16,1664]{1,0:T(8,128)S(1)}, f32[16,1664]{1,0:T(8,128)S(1)}, u32[]{:S(2)}, u32[]{:S(2)}) collective-permute-start(f32[16,1664]{1,0:T(8,128)S(1)} %get-tuple-element.101), channel_id=1, source_target_pairs={{0,4},{1,5},{2,6},{3,7},{4,0},{5,1},{6,2},{7,3},{8,12},{9,13},{10,... | collective-permute-start | bytes 319496 | tf_op jit(solution)/shard_map/ppermute | solution.py:22
  69.0 13.1 %collective-permute-start.15 = (f32[16,1664]{1,0:T(8,128)S(1)}, f32[16,1664]{1,0:T(8,128)S(1)}, u32[]{:S(2)}, u32[]{:S(2)}) collective-permute-start(f32[16,1664]{1,0:T(8,128)S(1)} %get-tuple-element.100), channel_id=1, source_target_pairs={{0,8},{1,9},{2,10},{3,11},{4,12},{5,13},{6,14},{7,15},{8,0},{9,1},... | collective-permute-start | bytes 319496 | tf_op jit(solution)/shard_map/ppermute | solution.py:22
  72.4 13.1 %collective-permute-start.16 = (f32[16,1664]{1,0:T(8,128)S(1)}, f32[16,1664]{1,0:T(8,128)S(1)}, u32[]{:S(2)}, u32[]{:S(2)}) collective-permute-start(f32[16,1664]{1,0:T(8,128)S(1)} %get-tuple-element.99), channel_id=1, source_target_pairs={{0,12},{1,13},{2,14},{3,15},{4,8},{5,9},{6,10},{7,11},{8,4},{9,5},... | collective-permute-start | bytes 319496 | tf_op jit(solution)/shard_map/ppermute | solution.py:22
  72.4 1.4 %copy-start.13 = (f32[6,512,128]{2,1,0:T(8,128)S(1)}, f32[6,512,128]{2,1,0:T(8,128)}, u32[]{:S(2)}) copy-start(f32[6,512,128]{2,1,0:T(8,128)} %copy-done.12) | copy-start | bytes 4718596
  79.7 5.9 %collective-permute-start.20 = (bf16[6,256,128]{2,1,0:T(8,128)(2,1)S(1)}, bf16[6,256,128]{2,1,0:T(8,128)(2,1)S(1)}, u32[]{:S(2)}, u32[]{:S(2)}) collective-permute-start(bf16[6,256,128]{2,1,0:T(8,128)(2,1)S(1)} %get-tuple-element.88), channel_id=1, source_target_pairs={{0,1},{1,0},{2,3},{3,2},{4,5},{5,4},{6,7},{7,6},{8,9},{9,8},{10,11... | collective-permute-start | bytes 1179656 | tf_op jit(solution)/shard_map/ppermute | solution.py:22
  85.5 4.2 %collective-permute-start.17 = (f32[8,1664]{1,0:T(8,128)S(1)}, f32[8,1664]{1,0:T(8,128)S(1)}, u32[]{:S(2)}, u32[]{:S(2)}) collective-permute-start(f32[8,1664]{1,0:T(8,128)S(1)} %pad_maximum_fusion.5), channel_id=1, source_target_pairs={{0,2},{1,3},{2,0},{3,1},{4,6},{5,7},{6,4},{7,5},{8,10},{9,11},{10,... | collective-permute-start | bytes 159752 | tf_op jit(solution)/shard_map/ppermute | solution.py:22

commit v9 on v8

--- a/solution.py
+++ b/solution.py
@@ -51,9 +51,9 @@
     outs = rest[:-1]
     odd = lax.rem(pos_ref[0], 2)
     spots = {
-        "direct": jnp.where(odd == 1, sent_ref[0, 0], sent_ref[1, 0]),
-        "diagonal": jnp.where(odd == 1, sent_ref[1, 0], sent_ref[0, 0]),
-        "partner": sent_ref[2, 0],
+        "direct": jnp.where(odd == 1, sent_ref[0], sent_ref[1]),
+        "diagonal": jnp.where(odd == 1, sent_ref[1], sent_ref[0]),
+        "partner": sent_ref[2],
     }
     started = []
     for i, (out, (which, head0)) in enumerate(zip(outs, copies)):
@@ -75,7 +75,7 @@
         out_specs=[vmem] * len(copies),
         out_shape=[jax.ShapeDtypeStruct((BLOCK, 2, heads * width), BF16) for _, _, heads in copies],
         scratch_shapes=[pltpu.SemaphoreType.DMA((len(copies),))],
-        compiler_params=pltpu.CompilerParams(vmem_limit_bytes=8 << 20),
+        compiler_params=pltpu.CompilerParams(vmem_limit_bytes=60 << 20),
         cost_estimate=pl.CostEstimate(flops=0, transcendentals=0, bytes_accessed=1 << 20),
         name="pick",
     )(pos, sent, mesh_kv)
@@ -116,7 +116,7 @@
     own_rows = own_ref.shape[0]
     blocks = own_rows // BLOCK
     near = own_rows + 3 * BLOCK
-    keys = near + anc_ref.shape[0] // 2
+    keys = near + anc_ref.shape[0]
 
     row = 0
     for ref in (own_ref, par_ref, dir_ref, dia_ref, anc_ref):
@@ -178,7 +178,7 @@
     rows, feat = q.shape
     own_rows = mesh_kv.shape[0]
     width = feat // warm.shape[0]
-    a_rows = anchors.shape[0] // 2
+    a_rows = anchors.shape[0]
     keys = own_rows + 3 * BLOCK + a_rows
     smem = pl.BlockSpec(memory_space=SMEM)
     full = lambda n: pl.BlockSpec((n, 2, width), lambda h: (0, 0, head0 + h))
@@ -186,7 +186,7 @@
     back = pl.BlockSpec((None, 2 * BLOCK, width), lambda h: (h, 0, 0))
     cols = pl.BlockSpec((rows, width), lambda h: (0, head0 + h))
     in_specs = [smem, smem, smem, cols, cols, full(own_rows), full(BLOCK), part, part]
-    in_specs += [pl.BlockSpec((2 * a_rows, width), lambda h: (0, head0 + h))]
+    in_specs += [full(a_rows)]
     args = [pos, filt, warm, q, g, mesh_kv, partner, *halo, anchors]
     alias = {}
     if dq_prev is not None:
@@ -233,9 +233,9 @@
     odd = lax.rem(pos_ref[0], 2)
     blocks = out_ref.shape[0] // BLOCK
     spots = (
-        jnp.where(odd == 1, sent_ref[0, 0], sent_ref[1, 0]),
-        jnp.where(odd == 1, sent_ref[1, 0], sent_ref[0, 0]),
-        sent_ref[2, 0],
+        jnp.where(odd == 1, sent_ref[0], sent_ref[1]),
+        jnp.where(odd == 1, sent_ref[1], sent_ref[0]),
+        sent_ref[2],
     )
     width = own_ref.shape[2]
     for h in range(own_ref.shape[0]):
@@ -307,7 +307,7 @@
     stages = levels(lax.axis_size(("gx", "gy")))
     gx = lax.axis_index("gx")
     pos = jnp.full((1,), gx, jnp.int32)
-    sent = exported[0]
+    sent = exported.reshape(-1)
     filt = filt[0]
     sizes = split_heads(total)
     chunks = [(sum(sizes[:i]), n) for i, n in enumerate(sizes)]
@@ -317,7 +317,7 @@
     others = list(pick(pos, sent, mesh_kv, width, others + [("partner", 0, total)]))
     partner = swap_mask(others.pop(), 1)
     picks += [others[2 * i : 2 * i + 2] for i in range(len(chunks) - 1)]
-    anchors = landmark.reshape(2 * landmark.shape[0], feat)
+    anchors = landmark
     for i, masks in enumerate(stages):
         if i == 1:
             anchors, picks[1] = lax.optimization_barrier((anchors, picks[1]))

time: 91.2 us -> 91.3 us (level)
  Pallas kernels: 27.1 us -> 32.2 us
  waiting for transfers between devices: 27 us -> 24.2 us
  local copies, waits for them, and re-layouts: 7.46 us -> 4.86 us
    pallas_call x2, Pallas kernels: 1.44 us -> 6.26 us  [pick(): pl.pallas_call(functools.partial(pick_kernel, copies=[c[:2] for c in copi...]
    ppermute x13, waiting for transfers between devices: 22.2 us -> 19.6 us  [swap_mask(): return lax.ppermute(x, ('gx', 'gy'), [(i, i ^ mask) for i in range(count)])]
    unnamed x34 -> x36, local copies, waits for them, and re-layouts: 5.26 us -> 4.02 us
  transfers between devices with their start and end apart: 21 -> 21, of which waited for: 9 -> 9; matrix products, arithmetic and copies ran while one was open for 5% -> 5% of each run, Pallas kernels for 29% -> 35%
where the time goes in v9:
time: 91.3 us; the launch traced here: 90.9 us
  Pallas kernels  32.2 us (35%)
  starting transfers between devices  24.8 us (27%)
  waiting for transfers between devices  24.2 us (27%)
  local copies, waits for them, and re-layouts  4.86 us (5%)
  other arithmetic  3.75 us (4%)
  between operations  1.08 us (1%)
    pallas_call x2, Pallas kernels, attention(): pl.pallas_call(functools.partial(attention_kernel, gx_count=lax.axis_size...  21 us
    ppermute x13, waiting for transfers between devices, swap_mask(): return lax.ppermute(x, ('gx', 'gy'), [(i, i ^ mask) for i in range(count)])  19.6 us
    ppermute x13, starting transfers between devices, swap_mask(): return lax.ppermute(x, ('gx', 'gy'), [(i, i ^ mask) for i in range(count)])  16.8 us
    ppermute x8, starting transfers between devices, swap_pairs(): return lax.ppermute(x, 'gx', route)  7.99 us
    pallas_call x2, Pallas kernels, pick(): pl.pallas_call(functools.partial(pick_kernel, copies=[c[:2] for c in copi...  6.26 us
    ppermute x8, waiting for transfers between devices, swap_pairs(): return lax.ppermute(x, 'gx', route)  4.62 us
    pallas_call x2, Pallas kernels, combine(): pl.pallas_call(combine_kernel, grid=(heads // step,), in_specs=in_specs,...  4.34 us
    unnamed x36, local copies, waits for them, and re-layouts  4.02 us
  transfers between devices with their start and end apart: 21, of which 9 were waited for; matrix products, arithmetic and copies ran while one was open for 5% of the time, Pallas kernels for 35%

profile of v9, /device:TPU:0, one launch (start us, length us, event | category | flops | bytes accessed | tf_op | source)
XLA Modules:
  0.0 90.9 jit_solution(2534830413734723289)
XLA Ops:
  0.6 3.0 %collective-permute-start.1 = (bf16[4,2,1536]{2,1,0:T(2,128)(2,1)}, bf16[4,2,1536]{2,1,0:T(2,128)(2,1)S(1)}, u32[]{:S(2)}, u32[]{:S(2)}) collective-permute-start(bf16[4,2,1536]{2,1,0:T(2,128)(2,1)} %param.11), channel_id=1, source_target_pairs={{0,2},{1,3},{2,0},{3,1},{4,6},{5,7},{6,4},{7,5},{8,10},{9,11},{10,... | collective-permute-start | bytes 73736 | tf_op jit(solution)/shard_map/ppermute | solution.py:22
  3.6 2.9 %pick.3 = (bf16[128,2,768]{2,1,0:T(2,128)(2,1)}, bf16[128,2,768]{2,1,0:T(2,128)(2,1)}) custom-call(s32[1]{0:T(128)} %bitcast.pos_ref, s32[3]{0:T(128)} %bitcast.13, bf16[256,2,1536]{2,1,0:T(2,128)(2,1)} %own_ref.3), custom_call_target="tpu_custom_call" | custom-call | bytes 1048576 | tf_op jit(solution)/shard_map/pick/pallas_call | solution.py:72
  6.5 0.1 collective-permute-start.8
  6.6 0.7 collective-permute-start.9
  7.3 3.4 %pick.2 = (bf16[128,2,768]{2,1,0:T(2,128)(2,1)}, bf16[128,2,768]{2,1,0:T(2,128)(2,1)}, bf16[128,2,1536]{2,1,0:T(2,128)(2,1)}) custom-call(s32[1]{0:T(128)} %bitcast.pos_ref, s32[3]{0:T(128)} %bitcast.14, bf16[256,2,1536]{2,1,0:T(2,128)(2,1)} %own_ref.3), custom_call_target="tpu_custom_call" | custom-call | bytes 1048576 | tf_op jit(solution)/shard_map/pick/pallas_call | solution.py:72
  10.7 0.6 compare_reduce_fusion
  11.4 4.8 %collective-permute-start.4 = (bf16[8,2,1536]{2,1,0:T(2,128)(2,1)S(1)}, bf16[8,2,1536]{2,1,0:T(2,128)(2,1)S(1)}, u32[]{:S(2)}, u32[]{:S(2)}) collective-permute-start(bf16[8,2,1536]{2,1,0:T(2,128)(2,1)S(1)} %pad_maximum_fusion.6), channel_id=1, source_target_pairs={{0,4},{1,5},{2,6},{3,7},{4,0},{5,1},{6,2},{7,3},{8,12},{9,13},{10,... | collective-permute-start | bytes 147464 | tf_op jit(solution)/shard_map/ppermute | solution.py:22
  16.2 2.3 %collective-permute-start.5 = (bf16[8,2,1536]{2,1,0:T(2,128)(2,1)S(1)}, bf16[8,2,1536]{2,1,0:T(2,128)(2,1)S(1)}, u32[]{:S(2)}, u32[]{:S(2)}) collective-permute-start(bf16[8,2,1536]{2,1,0:T(2,128)(2,1)S(1)} %pad_maximum_fusion.6), channel_id=1, source_target_pairs={{0,8},{1,9},{2,10},{3,11},{4,12},{5,13},{6,14},{7,15},{8,0},{9,1},... | collective-permute-start | bytes 147464 | tf_op jit(solution)/shard_map/ppermute | solution.py:22
  18.5 0.2 collective-permute-start.6
  18.7 3.3 %collective-permute-done.4 = bf16[8,2,1536]{2,1,0:T(2,128)(2,1)S(1)} collective-permute-done((bf16[8,2,1536]{2,1,0:T(2,128)(2,1)S(1)}, bf16[8,2,1536]{2,1,0:T(2,128)(2,1)S(1)}, u32[]{:S(2)}, u32[]{:S(2)}) %collective-permute-start.4) | collective-permute-done | bytes 49184 | tf_op jit(solution)/shard_map/ppermute | solution.py:22
  22.0 2.1 %collective-permute-done.5 = bf16[8,2,1536]{2,1,0:T(2,128)(2,1)S(1)} collective-permute-done((bf16[8,2,1536]{2,1,0:T(2,128)(2,1)S(1)}, bf16[8,2,1536]{2,1,0:T(2,128)(2,1)S(1)}, u32[]{:S(2)}, u32[]{:S(2)}) %collective-permute-start.5) | collective-permute-done | bytes 49184 | tf_op jit(solution)/shard_map/ppermute | solution.py:22
  24.1 1.6 %collective-permute-done.6 = bf16[8,2,1536]{2,1,0:T(2,128)(2,1)S(1)} collective-permute-done((bf16[8,2,1536]{2,1,0:T(2,128)(2,1)S(1)}, bf16[8,2,1536]{2,1,0:T(2,128)(2,1)S(1)}, u32[]{:S(2)}, u32[]{:S(2)}) %collective-permute-start.6) | collective-permute-done | bytes 49184 | tf_op jit(solution)/shard_map/ppermute | solution.py:22
  25.7 0.3 pad_maximum_fusion.1
  25.9 0.1 collective-permute-start.7
  26.2 1.3 %collective-permute-done.7 = bf16[32,2,1536]{2,1,0:T(2,128)(2,1)S(1)} collective-permute-done((bf16[32,2,1536]{2,1,0:T(2,128)(2,1)S(1)}, bf16[32,2,1536]{2,1,0:T(2,128)(2,1)S(1)}, u32[]{:S(2)}, u32[]{:S(2)}) %collective-permute-start.7) | collective-permute-done | bytes 196640 | tf_op jit(solution)/shard_map/ppermute | solution.py:22
  27.5 0.7 collective-permute-start.3
  28.1 0.2 constant_dynamic-update-slice_fusion.anc_ref
  28.4 1.3 %copy-done = bf16[256,2,1536]{2,1,0:T(2,128)(2,1)S(1)} copy-done((bf16[256,2,1536]{2,1,0:T(2,128)(2,1)S(1)}, bf16[256,2,1536]{2,1,0:T(2,128)(2,1)}, u32[]{:S(2)}) %copy-start) | copy-done | bytes 1572888
  29.7 0.2 copy-done.1
  29.9 0.2 copy-done.2
  30.1 10.4 %attention.2 = (bf16[256,1536]{1,0:T(8,128)(2,1)}, f32[6,512,128]{2,1,0:T(8,128)S(1)}, bf16[6,256,128]{2,1,0:T(8,128)(2,1)S(1)}, bf16[6,256,128]{2,1,0:T(8,128)(...) custom-call(s32[1]{0:T(128)} %bitcast.pos_ref, ...), custom_call_target="tpu_custom_call" | custom-call | flops 1384120320 | bytes 6488064 | tf_op jit(solution)/shard_map/attention/pallas_call | solution.py:197
  40.6 2.7 %collective-permute-start.10 = (bf16[6,256,128]{2,1,0:T(8,128)(2,1)S(1)}, bf16[6,256,128]{2,1,0:T(8,128)(2,1)S(1)}, u32[]{:S(2)}, u32[]{:S(2)}) collective-permute-start(bf16[6,256,128]{2,1,0:T(8,128)(2,1)S(1)} %get-tuple-element.72), channel_id=1, source_target_pairs={{0,2},{2,0},{4,6},{6,4},{8,10},{10,8},{12,14},{14,12},{1,3},{3,1},... | collective-permute-start | bytes 1179656 | tf_op jit(solution)/shard_map/ppermute | solution.py:41
  43.3 0.7 collective-permute-start.11
  44.0 0.1 collective-permute-start.12
  44.1 10.6 %attention.3 = (bf16[256,1536]{1,0:T(8,128)(2,1)}, f32[6,512,128]{2,1,0:T(8,128)S(1)}, bf16[6,256,128]{2,1,0:T(8,128)(2,1)}, bf16[6,256,128]{2,1,0:T(8,128)(2,1)...) custom-call(s32[1]{0:T(128)} %bitcast.pos_ref, ...), custom_call_target="tpu_custom_call", output_to_operand_aliasing={{0}: (10, {}), {5}: (11, {})} | custom-call | flops 1384120320 | bytes 6488064 | tf_op jit(solution)/shard_map/attention/pallas_call | solution.py:197
  54.7 0.2 maximum_reduce_fusion
  54.8 0.6 fusion.2
  55.5 4.6 %collective-permute-done.10.dir_ref = bf16[6,256,128]{2,1,0:T(8,128)(2,1)S(1)} collective-permute-done((bf16[6,256,128]{2,1,0:T(8,128)(2,1)S(1)}, bf16[6,256,128]{2,1,0:T(8,128)(2,1)S(1)}, u32[]{:S(2)}, u32[]{:S(2)}) %collective-permute-start.10) | collective-permute-done | bytes 393248 | tf_op jit(solution)/shard_map/ppermute | solution.py:41
  60.2 0.1 collective-permute-start.13
  60.3 0.6 copy-done.6
  60.9 2.5 %collective-permute-start.18 = (bf16[6,256,128]{2,1,0:T(8,128)(2,1)}, bf16[6,256,128]{2,1,0:T(8,128)(2,1)S(1)}, u32[]{:S(2)}, u32[]{:S(2)}) collective-permute-start(bf16[6,256,128]{2,1,0:T(8,128)(2,1)} %get-tuple-element.86), channel_id=1, source_target_pairs={{0,2},{2,0},{4,6},{6,4},{8,10},{10,8},{12,14},{14,12},{1,3},{3,1},... | collective-permute-start | bytes 1179656 | tf_op jit(solution)/shard_map/ppermute | solution.py:41
  63.4 0.7 collective-permute-start.19
  64.1 0.7 slice_add_fusion.2
  64.8 0.1 copy-done.14
  64.8 0.1 add.30
  65.0 1.1 %slice_add_fusion = f32[64,1536]{1,0:T(8,128)S(1)} fusion(f32[64,1664]{1,0:T(8,128)} %copy-done.14, f32[128,1536]{1,0:T(8,128)S(1)} %get-tuple-element.75), kind=kLoop, calls=%fused_computation.1 | loop fusion | flops 98304 | bytes 1179648 | tf_op jit(solution)/shard_map/add | solution.py:359
  66.2 2.9 %collective-permute-start.14 = (f32[16,1664]{1,0:T(8,128)S(1)}, f32[16,1664]{1,0:T(8,128)S(1)}, u32[]{:S(2)}, u32[]{:S(2)}) collective-permute-start(f32[16,1664]{1,0:T(8,128)S(1)} %get-tuple-element.101), channel_id=1, source_target_pairs={{0,4},{1,5},{2,6},{3,7},{4,0},{5,1},{6,2},{7,3},{8,12},{9,13},{10,... | collective-permute-start | bytes 319496 | tf_op jit(solution)/shard_map/ppermute | solution.py:22
  69.1 3.4 %collective-permute-start.15 = (f32[16,1664]{1,0:T(8,128)S(1)}, f32[16,1664]{1,0:T(8,128)S(1)}, u32[]{:S(2)}, u32[]{:S(2)}) collective-permute-start(f32[16,1664]{1,0:T(8,128)S(1)} %get-tuple-element.100), channel_id=1, source_target_pairs={{0,8},{1,9},{2,10},{3,11},{4,12},{5,13},{6,14},{7,15},{8,0},{9,1},... | collective-permute-start | bytes 319496 | tf_op jit(solution)/shard_map/ppermute | solution.py:22
  72.5 1.4 %copy-done.13 = f32[6,512,128]{2,1,0:T(8,128)S(1)} copy-done((f32[6,512,128]{2,1,0:T(8,128)S(1)}, f32[6,512,128]{2,1,0:T(8,128)}, u32[]{:S(2)}) %copy-start.13) | copy-done | bytes 1572888
  73.9 2.2 %combine.2.rest_0_ = bf16[256,2,1536]{2,1,0:T(2,128)(2,1)} custom-call(s32[1]{0:T(128)} %bitcast.pos_ref, s32[3]{0:T(128)S(1)} %bitcast.15, f32[6,512,128]{2,1,0:T(8,128)S(1)} %copy-done.13, bf16[6,256,128]{2,1,0:T(8,128)(2,1)S(1)} %copy-done.7, bf16[6,256,128]{2,1,0:T(8,128)(2,1)S(1)} %copy-done.9, bf16[6,256,128]{2,1,0:T(8,128)(2,1)S(1)} %copy-done.11), custom_call_target="tpu_custom_call" | custom-call | flops 12582912000 | bytes 3538944 | tf_op jit(solution)/shard_map/combine/pallas_call | solution.py:265
  76.0 3.7 %collective-permute-done.14 = f32[16,1664]{1,0:T(8,128)S(1)} collective-permute-done((f32[16,1664]{1,0:T(8,128)S(1)}, f32[16,1664]{1,0:T(8,128)S(1)}, u32[]{:S(2)}, u32[]{:S(2)}) %collective-permute-start.14) | collective-permute-done | bytes 106528 | tf_op jit(solution)/shard_map/ppermute | solution.py:22
  79.8 2.5 %collective-permute-done.15 = f32[16,1664]{1,0:T(8,128)S(1)} collective-permute-done((f32[16,1664]{1,0:T(8,128)S(1)}, f32[16,1664]{1,0:T(8,128)S(1)}, u32[]{:S(2)}, u32[]{:S(2)}) %collective-permute-start.15) | collective-permute-done | bytes 106528 | tf_op jit(solution)/shard_map/ppermute | solution.py:22
  82.2 3.3 %collective-permute-done.16 = f32[16,1664]{1,0:T(8,128)S(1)} collective-permute-done((f32[16,1664]{1,0:T(8,128)S(1)}, f32[16,1664]{1,0:T(8,128)S(1)}, u32[]{:S(2)}, u32[]{:S(2)}) %collective-permute-start.16) | collective-permute-done | bytes 106528 | tf_op jit(solution)/shard_map/ppermute | solution.py:22
  85.6 0.1 collective-permute-start.17
  85.7 2.2 %combine.3 = bf16[256,2,1536]{2,1,0:T(2,128)(2,1)} custom-call(s32[1]{0:T(128)} %bitcast.pos_ref, s32[3]{0:T(128)S(1)} %bitcast.16, f32[6,512,128]{2,1,0:T(8,128)S(1)} %get-tuple-element.85.own_ref, bf16[6,256,128]{2,1,0:T(8,128)(2,1)S(1)} %collective-permute-done.18.dir_ref, ...), custom_call_target="tpu_custom_call", output_to_operand_aliasing={{}: (6, {})} | custom-call | bytes 3538944 | tf_op jit(solution)/shard_map/combine/pallas_call | solution.py:265
  87.9 1.9 %collective-permute-done.17.refs_0_ = f32[8,1664]{1,0:T(8,128)S(1)} collective-permute-done((f32[8,1664]{1,0:T(8,128)S(1)}, f32[8,1664]{1,0:T(8,128)S(1)}, u32[]{:S(2)}, u32[]{:S(2)}) %collective-permute-start.17) | collective-permute-done | bytes 53280 | tf_op jit(solution)/shard_map/ppermute | solution.py:22
  89.8 0.6 finish.1
  90.4 0.5 slice_bitcast_fusion
  (61 shorter events, 0.5 us)
Async XLA Ops:
  0.6 10.7 %collective-permute-start.1 = (bf16[4,2,1536]{2,1,0:T(2,128)(2,1)}, bf16[4,2,1536]{2,1,0:T(2,128)(2,1)S(1)}, u32[]{:S(2)}, u32[]{:S(2)}) collective-permute-start(bf16[4,2,1536]{2,1,0:T(2,128)(2,1)} %param.11), channel_id=1, source_target_pairs={{0,2},{1,3},{2,0},{3,1},{4,6},{5,7},{6,4},{7,5},{8,10},{9,11},{10,... | collective-permute-start | bytes 73736 | tf_op jit(solution)/shard_map/ppermute | solution.py:22
  3.6 7.7 %copy-start.15 = (bf16[4,2,1536]{2,1,0:T(2,128)(2,1)S(1)}, bf16[4,2,1536]{2,1,0:T(2,128)(2,1)}, u32[]{:S(2)}) copy-start(bf16[4,2,1536]{2,1,0:T(2,128)(2,1)} %param.11) | copy-start | bytes 73732
  6.5 21.9 %collective-permute-start.8 = (bf16[128,2,768]{2,1,0:T(2,128)(2,1)}, bf16[128,2,768]{2,1,0:T(2,128)(2,1)S(1)}, u32[]{:S(2)}, u32[]{:S(2)}) collective-permute-start(bf16[128,2,768]{2,1,0:T(2,128)(2,1)} %get-tuple-element.61), channel_id=1, source_target_pairs={{0,2},{2,0},{4,6},{6,4},{8,10},{10,8},{12,14},{14,12},{1,3},{3,1},... | collective-permute-start | bytes 1179656 | tf_op jit(solution)/shard_map/ppermute | solution.py:41
  6.6 21.8 %collective-permute-start.9 = (bf16[128,2,768]{2,1,0:T(2,128)(2,1)}, bf16[128,2,768]{2,1,0:T(2,128)(2,1)S(1)}, u32[]{:S(2)}, u32[]{:S(2)}) collective-permute-start(bf16[128,2,768]{2,1,0:T(2,128)(2,1)} %get-tuple-element.62), channel_id=1, source_target_pairs={{2,4},{4,2},{6,8},{8,6},{10,12},{12,10},{3,5},{5,3},{7,9},{9,7},{1... | collective-permute-start | bytes 1179656 | tf_op jit(solution)/shard_map/ppermute | solution.py:41
  11.4 10.6 %collective-permute-start.4 = (bf16[8,2,1536]{2,1,0:T(2,128)(2,1)S(1)}, bf16[8,2,1536]{2,1,0:T(2,128)(2,1)S(1)}, u32[]{:S(2)}, u32[]{:S(2)}) collective-permute-start(bf16[8,2,1536]{2,1,0:T(2,128)(2,1)S(1)} %pad_maximum_fusion.6), channel_id=1, source_target_pairs={{0,4},{1,5},{2,6},{3,7},{4,0},{5,1},{6,2},{7,3},{8,12},{9,13},{10,... | collective-permute-start | bytes 147464 | tf_op jit(solution)/shard_map/ppermute | solution.py:22
  16.2 7.8 %collective-permute-start.5 = (bf16[8,2,1536]{2,1,0:T(2,128)(2,1)S(1)}, bf16[8,2,1536]{2,1,0:T(2,128)(2,1)S(1)}, u32[]{:S(2)}, u32[]{:S(2)}) collective-permute-start(bf16[8,2,1536]{2,1,0:T(2,128)(2,1)S(1)} %pad_maximum_fusion.6), channel_id=1, source_target_pairs={{0,8},{1,9},{2,10},{3,11},{4,12},{5,13},{6,14},{7,15},{8,0},{9,1},... | collective-permute-start | bytes 147464 | tf_op jit(solution)/shard_map/ppermute | solution.py:22
  18.5 7.1 %collective-permute-start.6 = (bf16[8,2,1536]{2,1,0:T(2,128)(2,1)S(1)}, bf16[8,2,1536]{2,1,0:T(2,128)(2,1)S(1)}, u32[]{:S(2)}, u32[]{:S(2)}) collective-permute-start(bf16[8,2,1536]{2,1,0:T(2,128)(2,1)S(1)} %pad_maximum_fusion.6), channel_id=1, source_target_pairs={{0,12},{1,13},{2,14},{3,15},{4,8},{5,9},{6,10},{7,11},{8,4},{9,5},... | collective-permute-start | bytes 147464 | tf_op jit(solution)/shard_map/ppermute | solution.py:22
  22.0 6.4 %collective-permute-start = (bf16[128,2,1536]{2,1,0:T(2,128)(2,1)}, bf16[128,2,1536]{2,1,0:T(2,128)(2,1)S(1)}, u32[]{:S(2)}, u32[]{:S(2)}) collective-permute-start(bf16[128,2,1536]{2,1,0:T(2,128)(2,1)} %get-tuple-element.55), channel_id=1, source_target_pairs={{0,1},{1,0},{2,3},{3,2},{4,5},{5,4},{6,7},{7,6},{8,9},{9,8},{10,11... | collective-permute-start | bytes 2359304 | tf_op jit(solution)/shard_map/ppermute | solution.py:22
  24.1 20.0 %collective-permute-start.2 = (bf16[128,2,768]{2,1,0:T(2,128)(2,1)}, bf16[128,2,768]{2,1,0:T(2,128)(2,1)S(1)}, u32[]{:S(2)}, u32[]{:S(2)}) collective-permute-start(bf16[128,2,768]{2,1,0:T(2,128)(2,1)} %get-tuple-element.58), channel_id=1, source_target_pairs={{0,2},{2,0},{4,6},{6,4},{8,10},{10,8},{12,14},{14,12},{1,3},{3,1},... | collective-permute-start | bytes 1179656 | tf_op jit(solution)/shard_map/ppermute | solution.py:41
  25.9 1.5 %collective-permute-start.7 = (bf16[32,2,1536]{2,1,0:T(2,128)(2,1)S(1)}, bf16[32,2,1536]{2,1,0:T(2,128)(2,1)S(1)}, u32[]{:S(2)}, u32[]{:S(2)}) collective-permute-start(bf16[32,2,1536]{2,1,0:T(2,128)(2,1)S(1)} %pad_maximum_fusion.1), channel_id=1, source_target_pairs={{0,1},{1,0},{2,3},{3,2},{4,5},{5,4},{6,7},{7,6},{8,9},{9,8},{10,11... | collective-permute-start | bytes 589832 | tf_op jit(solution)/shard_map/ppermute | solution.py:22
  27.5 16.6 %collective-permute-start.3 = (bf16[128,2,768]{2,1,0:T(2,128)(2,1)}, bf16[128,2,768]{2,1,0:T(2,128)(2,1)S(1)}, u32[]{:S(2)}, u32[]{:S(2)}) collective-permute-start(bf16[128,2,768]{2,1,0:T(2,128)(2,1)} %get-tuple-element.59), channel_id=1, source_target_pairs={{2,4},{4,2},{6,8},{8,6},{10,12},{12,10},{3,5},{5,3},{7,9},{9,7},{1... | collective-permute-start | bytes 1179656 | tf_op jit(solution)/shard_map/ppermute | solution.py:41
  28.3 1.4 %copy-start = (bf16[256,2,1536]{2,1,0:T(2,128)(2,1)S(1)}, bf16[256,2,1536]{2,1,0:T(2,128)(2,1)}, u32[]{:S(2)}) copy-start(bf16[256,2,1536]{2,1,0:T(2,128)(2,1)} %own_ref.3) | copy-start | bytes 4718596
  28.3 1.6 %copy-start.1 = (bf16[256,1536]{1,0:T(8,128)(2,1)S(1)}, bf16[256,1536]{1,0:T(8,128)(2,1)}, u32[]{:S(2)}) copy-start(bf16[256,1536]{1,0:T(8,128)(2,1)} %q_ref.3) | copy-start | bytes 2359300
  28.3 1.8 %copy-start.2 = (bf16[256,1536]{1,0:T(8,128)(2,1)S(1)}, bf16[256,1536]{1,0:T(8,128)(2,1)}, u32[]{:S(2)}) copy-start(bf16[256,1536]{1,0:T(8,128)(2,1)} %g_ref.3) | copy-start | bytes 2359300
  28.3 1.8 %copy-start.4 = (s32[1,2,5]{2,1,0:T(2,128)S(1)}, s32[1,2,5]{2,1,0:T(2,128)}, u32[]{:S(2)}) copy-start(s32[1,2,5]{2,1,0:T(2,128)} %param.15) | copy-start | bytes 124
  28.3 1.8 %copy-start.5 = (f32[12]{0:T(128)S(1)}, f32[12]{0:T(128)}, u32[]{:S(2)}) copy-start(f32[12]{0:T(128)} %warm_ref.3) | copy-start | bytes 148
  40.6 14.1 %copy-start.12 = (f32[6,512,128]{2,1,0:T(8,128)}, f32[6,512,128]{2,1,0:T(8,128)S(1)}, u32[]{:S(2)}) copy-start(f32[6,512,128]{2,1,0:T(8,128)S(1)} %get-tuple-element.78.own_ref) | copy-start | bytes 4718596
  40.6 19.6 %collective-permute-start.10 = (bf16[6,256,128]{2,1,0:T(8,128)(2,1)S(1)}, bf16[6,256,128]{2,1,0:T(8,128)(2,1)S(1)}, u32[]{:S(2)}, u32[]{:S(2)}) collective-permute-start(bf16[6,256,128]{2,1,0:T(8,128)(2,1)S(1)} %get-tuple-element.72), channel_id=1, source_target_pairs={{0,2},{2,0},{4,6},{6,4},{8,10},{10,8},{12,14},{14,12},{1,3},{3,1},... | collective-permute-start | bytes 1179656 | tf_op jit(solution)/shard_map/ppermute | solution.py:41
  43.3 16.8 %collective-permute-start.11 = (bf16[6,256,128]{2,1,0:T(8,128)(2,1)S(1)}, bf16[6,256,128]{2,1,0:T(8,128)(2,1)S(1)}, u32[]{:S(2)}, u32[]{:S(2)}) collective-permute-start(bf16[6,256,128]{2,1,0:T(8,128)(2,1)S(1)} %get-tuple-element.73), channel_id=1, source_target_pairs={{2,4},{4,2},{6,8},{8,6},{10,12},{12,10},{3,5},{5,3},{7,9},{9,7},{1... | collective-permute-start | bytes 1179656 | tf_op jit(solution)/shard_map/ppermute | solution.py:41
  44.0 16.2 %collective-permute-start.12 = (bf16[6,256,128]{2,1,0:T(8,128)(2,1)S(1)}, bf16[6,256,128]{2,1,0:T(8,128)(2,1)S(1)}, u32[]{:S(2)}, u32[]{:S(2)}) collective-permute-start(bf16[6,256,128]{2,1,0:T(8,128)(2,1)S(1)} %get-tuple-element.74), channel_id=1, source_target_pairs={{0,1},{1,0},{2,3},{3,2},{4,5},{5,4},{6,7},{7,6},{8,9},{9,8},{10,11... | collective-permute-start | bytes 1179656 | tf_op jit(solution)/shard_map/ppermute | solution.py:22
  60.1 0.8 copy-start.6
  60.1 3.2 %copy-start.8 = (bf16[6,256,128]{2,1,0:T(8,128)(2,1)}, bf16[6,256,128]{2,1,0:T(8,128)(2,1)S(1)}, u32[]{:S(2)}) copy-start(bf16[6,256,128]{2,1,0:T(8,128)(2,1)S(1)} %collective-permute-done.11.dia_ref) | copy-start | bytes 1179652
  60.1 3.9 %copy-start.10 = (bf16[6,256,128]{2,1,0:T(8,128)(2,1)}, bf16[6,256,128]{2,1,0:T(8,128)(2,1)S(1)}, u32[]{:S(2)}) copy-start(bf16[6,256,128]{2,1,0:T(8,128)(2,1)S(1)} %collective-permute-done.12.par_ref) | copy-start | bytes 1179652
  60.2 12.2 %copy-start.3 = (s32[1,3,1]{1,2,0:T(1,128)S(1)}, s32[1,3,1]{1,2,0:T(1,128)}, u32[]{:S(2)}) copy-start(s32[1,3,1]{1,2,0:T(1,128)} %param.14) | copy-start | bytes 40
  60.2 3.8 %collective-permute-start.13 = (f32[64,1664]{1,0:T(8,128)S(1)}, f32[64,1664]{1,0:T(8,128)S(1)}, u32[]{:S(2)}, u32[]{:S(2)}) collective-permute-start(f32[64,1664]{1,0:T(8,128)S(1)} %pad_maximum_fusion), channel_id=1, source_target_pairs={{0,1},{1,0},{2,3},{3,2},{4,5},{5,4},{6,7},{7,6},{8,9},{9,8},{10,11... | collective-permute-start | bytes 1277960 | tf_op jit(solution)/shard_map/ppermute | solution.py:22
  60.9 24.8 %collective-permute-start.18 = (bf16[6,256,128]{2,1,0:T(8,128)(2,1)}, bf16[6,256,128]{2,1,0:T(8,128)(2,1)S(1)}, u32[]{:S(2)}, u32[]{:S(2)}) collective-permute-start(bf16[6,256,128]{2,1,0:T(8,128)(2,1)} %get-tuple-element.86), channel_id=1, source_target_pairs={{0,2},{2,0},{4,6},{6,4},{8,10},{10,8},{12,14},{14,12},{1,3},{3,1},... | collective-permute-start | bytes 1179656 | tf_op jit(solution)/shard_map/ppermute | solution.py:41
  63.4 22.3 %collective-permute-start.19 = (bf16[6,256,128]{2,1,0:T(8,128)(2,1)}, bf16[6,256,128]{2,1,0:T(8,128)(2,1)S(1)}, u32[]{:S(2)}, u32[]{:S(2)}) collective-permute-start(bf16[6,256,128]{2,1,0:T(8,128)(2,1)} %get-tuple-element.87), channel_id=1, source_target_pairs={{2,4},{4,2},{6,8},{8,6},{10,12},{12,10},{3,5},{5,3},{7,9},{9,7},{1... | collective-permute-start | bytes 1179656 | tf_op jit(solution)/shard_map/ppermute | solution.py:41
  64.1 0.8 copy-start.14
  64.9 7.5 %copy-start.7 = (bf16[6,256,128]{2,1,0:T(8,128)(2,1)S(1)}, bf16[6,256,128]{2,1,0:T(8,128)(2,1)}, u32[]{:S(2)}) copy-start(bf16[6,256,128]{2,1,0:T(8,128)(2,1)} %copy-done.6) | copy-start | bytes 1179652
  65.0 7.5 %copy-start.9 = (bf16[6,256,128]{2,1,0:T(8,128)(2,1)S(1)}, bf16[6,256,128]{2,1,0:T(8,128)(2,1)}, u32[]{:S(2)}) copy-start(bf16[6,256,128]{2,1,0:T(8,128)(2,1)} %copy-done.8) | copy-start | bytes 1179652
  65.0 7.5 %copy-start.11 = (bf16[6,256,128]{2,1,0:T(8,128)(2,1)S(1)}, bf16[6,256,128]{2,1,0:T(8,128)(2,1)}, u32[]{:S(2)}) copy-start(bf16[6,256,128]{2,1,0:T(8,128)(2,1)} %copy-done.10) | copy-start | bytes 1179652
  66.2 13.6 %collective-permute-start.14 = (f32[16,1664]{1,0:T(8,128)S(1)}, f32[16,1664]{1,0:T(8,128)S(1)}, u32[]{:S(2)}, u32[]{:S(2)}) collective-permute-start(f32[16,1664]{1,0:T(8,128)S(1)} %get-tuple-element.101), channel_id=1, source_target_pairs={{0,4},{1,5},{2,6},{3,7},{4,0},{5,1},{6,2},{7,3},{8,12},{9,13},{10,... | collective-permute-start | bytes 319496 | tf_op jit(solution)/shard_map/ppermute | solution.py:22
  69.1 13.2 %collective-permute-start.15 = (f32[16,1664]{1,0:T(8,128)S(1)}, f32[16,1664]{1,0:T(8,128)S(1)}, u32[]{:S(2)}, u32[]{:S(2)}) collective-permute-start(f32[16,1664]{1,0:T(8,128)S(1)} %get-tuple-element.100), channel_id=1, source_target_pairs={{0,8},{1,9},{2,10},{3,11},{4,12},{5,13},{6,14},{7,15},{8,0},{9,1},... | collective-permute-start | bytes 319496 | tf_op jit(solution)/shard_map/ppermute | solution.py:22
  72.4 13.1 %collective-permute-start.16 = (f32[16,1664]{1,0:T(8,128)S(1)}, f32[16,1664]{1,0:T(8,128)S(1)}, u32[]{:S(2)}, u32[]{:S(2)}) collective-permute-start(f32[16,1664]{1,0:T(8,128)S(1)} %get-tuple-element.99), channel_id=1, source_target_pairs={{0,12},{1,13},{2,14},{3,15},{4,8},{5,9},{6,10},{7,11},{8,4},{9,5},... | collective-permute-start | bytes 319496 | tf_op jit(solution)/shard_map/ppermute | solution.py:22
  72.5 1.4 %copy-start.13 = (f32[6,512,128]{2,1,0:T(8,128)S(1)}, f32[6,512,128]{2,1,0:T(8,128)}, u32[]{:S(2)}) copy-start(f32[6,512,128]{2,1,0:T(8,128)} %copy-done.12) | copy-start | bytes 4718596
  79.8 5.9 %collective-permute-start.20 = (bf16[6,256,128]{2,1,0:T(8,128)(2,1)S(1)}, bf16[6,256,128]{2,1,0:T(8,128)(2,1)S(1)}, u32[]{:S(2)}, u32[]{:S(2)}) collective-permute-start(bf16[6,256,128]{2,1,0:T(8,128)(2,1)S(1)} %get-tuple-element.88), channel_id=1, source_target_pairs={{0,1},{1,0},{2,3},{3,2},{4,5},{5,4},{6,7},{7,6},{8,9},{9,8},{10,11... | collective-permute-start | bytes 1179656 | tf_op jit(solution)/shard_map/ppermute | solution.py:22
  85.6 4.2 %collective-permute-start.17 = (f32[8,1664]{1,0:T(8,128)S(1)}, f32[8,1664]{1,0:T(8,128)S(1)}, u32[]{:S(2)}, u32[]{:S(2)}) collective-permute-start(f32[8,1664]{1,0:T(8,128)S(1)} %pad_maximum_fusion.5), channel_id=1, source_target_pairs={{0,2},{1,3},{2,0},{3,1},{4,6},{5,7},{6,4},{7,5},{8,10},{9,11},{10,... | collective-permute-start | bytes 159752 | tf_op jit(solution)/shard_map/ppermute | solution.py:22

commit v10 on v9

--- a/solution.py
+++ b/solution.py
@@ -75,7 +75,7 @@
         out_specs=[vmem] * len(copies),
         out_shape=[jax.ShapeDtypeStruct((BLOCK, 2, heads * width), BF16) for _, _, heads in copies],
         scratch_shapes=[pltpu.SemaphoreType.DMA((len(copies),))],
-        compiler_params=pltpu.CompilerParams(vmem_limit_bytes=60 << 20),
+        compiler_params=pltpu.CompilerParams(vmem_limit_bytes=8 << 20),
         cost_estimate=pl.CostEstimate(flops=0, transcendentals=0, bytes_accessed=1 << 20),
         name="pick",
     )(pos, sent, mesh_kv)
@@ -340,14 +340,18 @@
     extra = jnp.zeros((1, LANES), F32).at[0, :total].set(temp)
     cell = None
     anc, faces[-1], returned[-1] = lax.optimization_barrier((anc, faces[-1], returned[-1]))
-    returned.append(send_back(faces[-1]))
+    direct, diagonal, partner = faces[-1]
+    returned.append([swap_pairs(direct, 0), None, swap_mask(partner, 1)])
     for i, masks in enumerate(reversed(stages)):
         n = anc.shape[0] // (len(masks) + 1)
         wide = jnp.broadcast_to(extra, (n, LANES))
-        got = [
-            swap_mask(jnp.concatenate([anc[k * n : (k + 1) * n], wide], axis=1), m)
-            for k, m in enumerate(masks, 1)
+        out = [
+            jnp.concatenate([anc[k * n : (k + 1) * n], wide], axis=1) for k in range(1, len(masks) + 1)
         ]
+        if i == 1:
+            out, diagonal, returned[-1][2] = lax.optimization_barrier((out, diagonal, returned[-1][2]))
+            returned[-1][1] = swap_pairs(diagonal, 1)
+        got = [swap_mask(x, m) for x, m in zip(out, masks)]
         if i == len(stages) - 2:
             cell = combine(pos, sent, owns[-2], returned[-2], *chunks[-2], feat, width, cell, weight=4000)
             got, cell = lax.optimization_barrier((got, cell))

time: 91.3 us -> 89.9 us (0.985)
  the two profiles are of different devices: /device:TPU:0 before, /device:TPU:16 now
where the time goes in v10:
time: 89.9 us; the launch traced here: 89.6 us
  starting transfers between devices  27.6 us (31%)
  Pallas kernels  27.3 us (30%)
  waiting for transfers between devices  22.9 us (25%)
  local copies, waits for them, and re-layouts  7.04 us (8%)
  other arithmetic  3.72 us (4%)
  between operations  1.03 us (1%)
    pallas_call x2, Pallas kernels, attention(): pl.pallas_call(functools.partial(attention_kernel, gx_count=lax.axis_size...  21 us
    ppermute x8, starting transfers between devices, swap_pairs(): return lax.ppermute(x, 'gx', route)  17 us
    ppermute x13, waiting for transfers between devices, swap_mask(): return lax.ppermute(x, ('gx', 'gy'), [(i, i ^ mask) for i in range(count)])  11.7 us
    ppermute x8, waiting for transfers between devices, swap_pairs(): return lax.ppermute(x, 'gx', route)  11.2 us
    ppermute x13, starting transfers between devices, swap_mask(): return lax.ppermute(x, ('gx', 'gy'), [(i, i ^ mask) for i in range(count)])  10.6 us
    unnamed x40, local copies, waits for them, and re-layouts  6.22 us
    pallas_call x2, Pallas kernels, combine(): pl.pallas_call(combine_kernel, grid=(heads // step,), in_specs=in_specs,...  4.31 us
  transfers between devices with their start and end apart: 21, of which 5 were waited for; matrix products, arithmetic and copies ran while one was open for 5% of the time, Pallas kernels for 30%

profile of v10, /device:TPU:16, one launch (start us, length us, event | category | flops | bytes accessed | tf_op | source)
XLA Modules:
  0.0 89.6 jit_solution(5455236348423928502)
XLA Ops:
  0.6 1.6 %collective-permute-start.1 = (bf16[4,2,1536]{2,1,0:T(2,128)(2,1)}, bf16[4,2,1536]{2,1,0:T(2,128)(2,1)S(1)}, u32[]{:S(2)}, u32[]{:S(2)}) collective-permute-start(bf16[4,2,1536]{2,1,0:T(2,128)(2,1)} %param.11), channel_id=1, source_target_pairs={{0,2},{1,3},{2,0},{3,1},{4,6},{5,7},{6,4},{7,5},{8,10},{9,11},{10,... | collective-permute-start | bytes 73736 | tf_op jit(solution)/shard_map/ppermute | solution.py:22
  2.2 1.4 %copy-done = bf16[256,2,1536]{2,1,0:T(2,128)(2,1)S(1)} copy-done((bf16[256,2,1536]{2,1,0:T(2,128)(2,1)S(1)}, bf16[256,2,1536]{2,1,0:T(2,128)(2,1)}, u32[]{:S(2)}) %copy-start) | copy-done | bytes 1572888
  3.6 0.7 copy-done.4
  4.3 0.7 pick.3
  4.9 0.6 collective-permute-start.8
  5.5 3.3 %collective-permute-start.9 = (bf16[128,2,768]{2,1,0:T(2,128)(2,1)S(1)}, bf16[128,2,768]{2,1,0:T(2,128)(2,1)S(1)}, u32[]{:S(2)}, u32[]{:S(2)}) collective-permute-start(bf16[128,2,768]{2,1,0:T(2,128)(2,1)S(1)} %get-tuple-element.67), channel_id=1, source_target_pairs={{2,4},{4,2},{6,8},{8,6},{10,12},{12,10},{3,5},{5,3},{7,9},{9,7},{1... | collective-permute-start | bytes 1179656 | tf_op jit(solution)/shard_map/ppermute | solution.py:41
  8.8 0.7 pick.2
  9.5 0.6 compare_reduce_fusion
  10.3 1.6 %collective-permute-start.4 = (bf16[8,2,1536]{2,1,0:T(2,128)(2,1)S(1)}, bf16[8,2,1536]{2,1,0:T(2,128)(2,1)S(1)}, u32[]{:S(2)}, u32[]{:S(2)}) collective-permute-start(bf16[8,2,1536]{2,1,0:T(2,128)(2,1)S(1)} %pad_maximum_fusion.6), channel_id=1, source_target_pairs={{0,4},{1,5},{2,6},{3,7},{4,0},{5,1},{6,2},{7,3},{8,12},{9,13},{10,... | collective-permute-start | bytes 147464 | tf_op jit(solution)/shard_map/ppermute | solution.py:22
  11.9 0.3 collective-permute-start.5
  12.2 1.6 %collective-permute-start.6 = (bf16[8,2,1536]{2,1,0:T(2,128)(2,1)S(1)}, bf16[8,2,1536]{2,1,0:T(2,128)(2,1)S(1)}, u32[]{:S(2)}, u32[]{:S(2)}) collective-permute-start(bf16[8,2,1536]{2,1,0:T(2,128)(2,1)S(1)} %pad_maximum_fusion.6), channel_id=1, source_target_pairs={{0,12},{1,13},{2,14},{3,15},{4,8},{5,9},{6,10},{7,11},{8,4},{9,5},... | collective-permute-start | bytes 147464 | tf_op jit(solution)/shard_map/ppermute | solution.py:22
  13.8 6.9 %collective-permute-done.4 = bf16[8,2,1536]{2,1,0:T(2,128)(2,1)S(1)} collective-permute-done((bf16[8,2,1536]{2,1,0:T(2,128)(2,1)S(1)}, bf16[8,2,1536]{2,1,0:T(2,128)(2,1)S(1)}, u32[]{:S(2)}, u32[]{:S(2)}) %collective-permute-start.4) | collective-permute-done | bytes 49184 | tf_op jit(solution)/shard_map/ppermute | solution.py:22
  20.8 1.0 %collective-permute-start.2 = (bf16[128,2,768]{2,1,0:T(2,128)(2,1)S(1)}, bf16[128,2,768]{2,1,0:T(2,128)(2,1)S(1)}, u32[]{:S(2)}, u32[]{:S(2)}) collective-permute-start(bf16[128,2,768]{2,1,0:T(2,128)(2,1)S(1)} %get-tuple-element.63), channel_id=1, source_target_pairs={{0,2},{2,0},{4,6},{6,4},{8,10},{10,8},{12,14},{14,12},{1,3},{3,1},... | collective-permute-start | bytes 1179656 | tf_op jit(solution)/shard_map/ppermute | solution.py:41
  21.8 0.3 pad_maximum_fusion.1
  22.1 0.1 collective-permute-start.7
  22.4 1.3 %collective-permute-done.7 = bf16[32,2,1536]{2,1,0:T(2,128)(2,1)S(1)} collective-permute-done((bf16[32,2,1536]{2,1,0:T(2,128)(2,1)S(1)}, bf16[32,2,1536]{2,1,0:T(2,128)(2,1)S(1)}, u32[]{:S(2)}, u32[]{:S(2)}) %collective-permute-start.7) | collective-permute-done | bytes 196640 | tf_op jit(solution)/shard_map/ppermute | solution.py:22
  23.6 4.3 %collective-permute-start.3 = (bf16[128,2,768]{2,1,0:T(2,128)(2,1)S(1)}, bf16[128,2,768]{2,1,0:T(2,128)(2,1)S(1)}, u32[]{:S(2)}, u32[]{:S(2)}) collective-permute-start(bf16[128,2,768]{2,1,0:T(2,128)(2,1)S(1)} %get-tuple-element.64), channel_id=1, source_target_pairs={{2,4},{4,2},{6,8},{8,6},{10,12},{12,10},{3,5},{5,3},{7,9},{9,7},{1... | collective-permute-start | bytes 1179656 | tf_op jit(solution)/shard_map/ppermute | solution.py:41
  28.0 0.2 constant_dynamic-update-slice_fusion.anc_ref
  28.2 1.3 %copy-done.1 = bf16[256,2,1536]{2,1,0:T(2,128)(2,1)S(1)} copy-done((bf16[256,2,1536]{2,1,0:T(2,128)(2,1)S(1)}, bf16[256,2,1536]{2,1,0:T(2,128)(2,1)}, u32[]{:S(2)}) %copy-start.1) | copy-done | bytes 1572888
  29.6 0.2 copy-done.2
  29.8 0.2 copy-done.3
  30.0 10.4 %attention.2 = (bf16[256,1536]{1,0:T(8,128)(2,1)}, f32[6,512,128]{2,1,0:T(8,128)S(1)}, bf16[6,256,128]{2,1,0:T(8,128)(2,1)S(1)}, bf16[6,256,128]{2,1,0:T(8,128)(...) custom-call(s32[1]{0:T(128)} %bitcast.pos_ref, ...), custom_call_target="tpu_custom_call" | custom-call | flops 1384120320 | bytes 6488064 | tf_op jit(solution)/shard_map/attention/pallas_call | solution.py:197
  40.4 1.6 %collective-permute-start.10 = (bf16[6,256,128]{2,1,0:T(8,128)(2,1)S(1)}, bf16[6,256,128]{2,1,0:T(8,128)(2,1)S(1)}, u32[]{:S(2)}, u32[]{:S(2)}) collective-permute-start(bf16[6,256,128]{2,1,0:T(8,128)(2,1)S(1)} %get-tuple-element.77), channel_id=1, source_target_pairs={{0,2},{2,0},{4,6},{6,4},{8,10},{10,8},{12,14},{14,12},{1,3},{3,1},... | collective-permute-start | bytes 1179656 | tf_op jit(solution)/shard_map/ppermute | solution.py:41
  42.0 2.2 %collective-permute-start.11 = (bf16[6,256,128]{2,1,0:T(8,128)(2,1)S(1)}, bf16[6,256,128]{2,1,0:T(8,128)(2,1)S(1)}, u32[]{:S(2)}, u32[]{:S(2)}) collective-permute-start(bf16[6,256,128]{2,1,0:T(8,128)(2,1)S(1)} %get-tuple-element.78), channel_id=1, source_target_pairs={{2,4},{4,2},{6,8},{8,6},{10,12},{12,10},{3,5},{5,3},{7,9},{9,7},{1... | collective-permute-start | bytes 1179656 | tf_op jit(solution)/shard_map/ppermute | solution.py:41
  44.3 10.6 %attention.3 = (bf16[256,1536]{1,0:T(8,128)(2,1)}, f32[6,512,128]{2,1,0:T(8,128)S(1)}, bf16[6,256,128]{2,1,0:T(8,128)(2,1)}, bf16[6,256,128]{2,1,0:T(8,128)(2,1)...) custom-call(s32[1]{0:T(128)} %bitcast.pos_ref, ...), custom_call_target="tpu_custom_call", output_to_operand_aliasing={{0}: (10, {}), {5}: (11, {})} | custom-call | flops 1384120320 | bytes 6488064 | tf_op jit(solution)/shard_map/attention/pallas_call | solution.py:197
  54.9 0.2 maximum_reduce_fusion
  55.1 0.6 fusion.2
  55.7 4.0 %collective-permute-done.10.dir_ref = bf16[6,256,128]{2,1,0:T(8,128)(2,1)S(1)} collective-permute-done((bf16[6,256,128]{2,1,0:T(8,128)(2,1)S(1)}, bf16[6,256,128]{2,1,0:T(8,128)(2,1)S(1)}, u32[]{:S(2)}, u32[]{:S(2)}) %collective-permute-start.10) | collective-permute-done | bytes 393248 | tf_op jit(solution)/shard_map/ppermute | solution.py:41
  59.8 0.1 collective-permute-start.13
  59.9 0.6 copy-done.8
  60.5 0.1 copy-done.10
  60.6 1.5 %collective-permute-start.19 = (bf16[6,256,128]{2,1,0:T(8,128)(2,1)}, bf16[6,256,128]{2,1,0:T(8,128)(2,1)S(1)}, u32[]{:S(2)}, u32[]{:S(2)}) collective-permute-start(bf16[6,256,128]{2,1,0:T(8,128)(2,1)} %get-tuple-element.96), channel_id=1, source_target_pairs={{0,2},{2,0},{4,6},{6,4},{8,10},{10,8},{12,14},{14,12},{1,3},{3,1},... | collective-permute-start | bytes 1179656 | tf_op jit(solution)/shard_map/ppermute | solution.py:41
  62.2 0.7 slice_add_fusion.2
  62.8 0.1 copy-done.16
  62.9 0.1 add.30
  63.0 1.1 %slice_add_fusion = f32[64,1536]{1,0:T(8,128)S(1)} fusion(f32[64,1664]{1,0:T(8,128)} %copy-done.16, f32[128,1536]{1,0:T(8,128)S(1)} %get-tuple-element.80), kind=kLoop, calls=%fused_computation.1 | loop fusion | flops 98304 | bytes 1179648 | tf_op jit(solution)/shard_map/add | solution.py:363
  64.3 0.2 collective-permute-start.15
  64.5 1.3 %collective-permute-start.16 = (f32[16,1664]{1,0:T(8,128)S(1)}, f32[16,1664]{1,0:T(8,128)S(1)}, u32[]{:S(2)}, u32[]{:S(2)}) collective-permute-start(f32[16,1664]{1,0:T(8,128)S(1)} %get-tuple-element.86), channel_id=1, source_target_pairs={{0,8},{1,9},{2,10},{3,11},{4,12},{5,13},{6,14},{7,15},{8,0},{9,1},... | collective-permute-start | bytes 319496 | tf_op jit(solution)/shard_map/ppermute | solution.py:22
  65.7 2.1 %collective-permute-start.17 = (f32[16,1664]{1,0:T(8,128)S(1)}, f32[16,1664]{1,0:T(8,128)S(1)}, u32[]{:S(2)}, u32[]{:S(2)}) collective-permute-start(f32[16,1664]{1,0:T(8,128)S(1)} %get-tuple-element.87), channel_id=1, source_target_pairs={{0,12},{1,13},{2,14},{3,15},{4,8},{5,9},{6,10},{7,11},{8,4},{9,5},... | collective-permute-start | bytes 319496 | tf_op jit(solution)/shard_map/ppermute | solution.py:22
  67.8 1.4 %copy-done.15 = f32[6,512,128]{2,1,0:T(8,128)S(1)} copy-done((f32[6,512,128]{2,1,0:T(8,128)S(1)}, f32[6,512,128]{2,1,0:T(8,128)}, u32[]{:S(2)}) %copy-start.15) | copy-done | bytes 1572888
  69.2 2.2 %combine.2.rest_0_ = bf16[256,2,1536]{2,1,0:T(2,128)(2,1)} custom-call(s32[1]{0:T(128)} %bitcast.pos_ref, s32[3]{0:T(128)S(1)} %bitcast.15, f32[6,512,128]{2,1,0:T(8,128)S(1)} %copy-done.15, bf16[6,256,128]{2,1,0:T(8,128)(2,1)S(1)} %copy-done.9, bf16[6,256,128]{2,1,0:T(8,128)(2,1)S(1)} %copy-done.11, bf16[6,256,128]{2,1,0:T(8,128)(2,1)S(1)} %copy-done.13), custom_call_target="tpu_custom_call" | custom-call | flops 12582912000 | bytes 3538944 | tf_op jit(solution)/shard_map/combine/pallas_call | solution.py:265
  71.4 2.4 %collective-permute-start.20 = (bf16[6,256,128]{2,1,0:T(8,128)(2,1)S(1)}, bf16[6,256,128]{2,1,0:T(8,128)(2,1)S(1)}, u32[]{:S(2)}, u32[]{:S(2)}) collective-permute-start(bf16[6,256,128]{2,1,0:T(8,128)(2,1)S(1)} %get-tuple-element.97), channel_id=1, source_target_pairs={{2,4},{4,2},{6,8},{8,6},{10,12},{12,10},{3,5},{5,3},{7,9},{9,7},{1... | collective-permute-start | bytes 1179656 | tf_op jit(solution)/shard_map/ppermute | solution.py:41
  73.8 3.4 %collective-permute-done.17 = f32[16,1664]{1,0:T(8,128)S(1)} collective-permute-done((f32[16,1664]{1,0:T(8,128)S(1)}, f32[16,1664]{1,0:T(8,128)S(1)}, u32[]{:S(2)}, u32[]{:S(2)}) %collective-permute-start.17) | collective-permute-done | bytes 106528 | tf_op jit(solution)/shard_map/ppermute | solution.py:22
  77.3 1.7 %collective-permute-start.18 = (f32[8,1664]{1,0:T(8,128)S(1)}, f32[8,1664]{1,0:T(8,128)S(1)}, u32[]{:S(2)}, u32[]{:S(2)}) collective-permute-start(f32[8,1664]{1,0:T(8,128)S(1)} %pad_maximum_fusion.5), channel_id=1, source_target_pairs={{0,2},{1,3},{2,0},{3,1},{4,6},{5,7},{6,4},{7,5},{8,10},{9,11},{10,... | collective-permute-start | bytes 159752 | tf_op jit(solution)/shard_map/ppermute | solution.py:22
  79.1 7.2 %collective-permute-done.20.dia_ref = bf16[6,256,128]{2,1,0:T(8,128)(2,1)S(1)} collective-permute-done((bf16[6,256,128]{2,1,0:T(8,128)(2,1)S(1)}, bf16[6,256,128]{2,1,0:T(8,128)(2,1)S(1)}, u32[]{:S(2)}, u32[]{:S(2)}) %collective-permute-start.20) | collective-permute-done | bytes 393248 | tf_op jit(solution)/shard_map/ppermute | solution.py:41
  86.3 2.2 %combine.3 = bf16[256,2,1536]{2,1,0:T(2,128)(2,1)} custom-call(s32[1]{0:T(128)} %bitcast.pos_ref, s32[3]{0:T(128)S(1)} %bitcast.16, f32[6,512,128]{2,1,0:T(8,128)S(1)} %get-tuple-element.95.own_ref, bf16[6,256,128]{2,1,0:T(8,128)(2,1)S(1)} %collective-permute-done.19.dir_ref, ...), custom_call_target="tpu_custom_call", output_to_operand_aliasing={{}: (6, {})} | custom-call | bytes 3538944 | tf_op jit(solution)/shard_map/combine/pallas_call | solution.py:265
  88.5 0.6 finish.1
  89.1 0.5 slice_bitcast_fusion
  (65 shorter events, 0.6 us)
Async XLA Ops:
  0.6 9.6 %collective-permute-start.1 = (bf16[4,2,1536]{2,1,0:T(2,128)(2,1)}, bf16[4,2,1536]{2,1,0:T(2,128)(2,1)S(1)}, u32[]{:S(2)}, u32[]{:S(2)}) collective-permute-start(bf16[4,2,1536]{2,1,0:T(2,128)(2,1)} %param.11), channel_id=1, source_target_pairs={{0,2},{1,3},{2,0},{3,1},{4,6},{5,7},{6,4},{7,5},{8,10},{9,11},{10,... | collective-permute-start | bytes 73736 | tf_op jit(solution)/shard_map/ppermute | solution.py:22
  2.2 1.4 %copy-start = (bf16[256,2,1536]{2,1,0:T(2,128)(2,1)S(1)}, bf16[256,2,1536]{2,1,0:T(2,128)(2,1)}, u32[]{:S(2)}) copy-start(bf16[256,2,1536]{2,1,0:T(2,128)(2,1)} %own_ref.3) | copy-start | bytes 4718596
  3.6 0.7 copy-start.4
  4.3 5.9 %copy-start.17 = (bf16[4,2,1536]{2,1,0:T(2,128)(2,1)S(1)}, bf16[4,2,1536]{2,1,0:T(2,128)(2,1)}, u32[]{:S(2)}) copy-start(bf16[4,2,1536]{2,1,0:T(2,128)(2,1)} %param.11) | copy-start | bytes 73732
  4.9 23.3 %collective-permute-start.8 = (bf16[128,2,768]{2,1,0:T(2,128)(2,1)S(1)}, bf16[128,2,768]{2,1,0:T(2,128)(2,1)S(1)}, u32[]{:S(2)}, u32[]{:S(2)}) collective-permute-start(bf16[128,2,768]{2,1,0:T(2,128)(2,1)S(1)} %get-tuple-element.66), channel_id=1, source_target_pairs={{0,2},{2,0},{4,6},{6,4},{8,10},{10,8},{12,14},{14,12},{1,3},{3,1},... | collective-permute-start | bytes 1179656 | tf_op jit(solution)/shard_map/ppermute | solution.py:41
  5.5 22.7 %collective-permute-start.9 = (bf16[128,2,768]{2,1,0:T(2,128)(2,1)S(1)}, bf16[128,2,768]{2,1,0:T(2,128)(2,1)S(1)}, u32[]{:S(2)}, u32[]{:S(2)}) collective-permute-start(bf16[128,2,768]{2,1,0:T(2,128)(2,1)S(1)} %get-tuple-element.67), channel_id=1, source_target_pairs={{2,4},{4,2},{6,8},{8,6},{10,12},{12,10},{3,5},{5,3},{7,9},{9,7},{1... | collective-permute-start | bytes 1179656 | tf_op jit(solution)/shard_map/ppermute | solution.py:41
  10.3 10.5 %collective-permute-start.4 = (bf16[8,2,1536]{2,1,0:T(2,128)(2,1)S(1)}, bf16[8,2,1536]{2,1,0:T(2,128)(2,1)S(1)}, u32[]{:S(2)}, u32[]{:S(2)}) collective-permute-start(bf16[8,2,1536]{2,1,0:T(2,128)(2,1)S(1)} %pad_maximum_fusion.6), channel_id=1, source_target_pairs={{0,4},{1,5},{2,6},{3,7},{4,0},{5,1},{6,2},{7,3},{8,12},{9,13},{10,... | collective-permute-start | bytes 147464 | tf_op jit(solution)/shard_map/ppermute | solution.py:22
  11.9 8.9 %collective-permute-start.5 = (bf16[8,2,1536]{2,1,0:T(2,128)(2,1)S(1)}, bf16[8,2,1536]{2,1,0:T(2,128)(2,1)S(1)}, u32[]{:S(2)}, u32[]{:S(2)}) collective-permute-start(bf16[8,2,1536]{2,1,0:T(2,128)(2,1)S(1)} %pad_maximum_fusion.6), channel_id=1, source_target_pairs={{0,8},{1,9},{2,10},{3,11},{4,12},{5,13},{6,14},{7,15},{8,0},{9,1},... | collective-permute-start | bytes 147464 | tf_op jit(solution)/shard_map/ppermute | solution.py:22
  12.2 9.6 %collective-permute-start.6 = (bf16[8,2,1536]{2,1,0:T(2,128)(2,1)S(1)}, bf16[8,2,1536]{2,1,0:T(2,128)(2,1)S(1)}, u32[]{:S(2)}, u32[]{:S(2)}) collective-permute-start(bf16[8,2,1536]{2,1,0:T(2,128)(2,1)S(1)} %pad_maximum_fusion.6), channel_id=1, source_target_pairs={{0,12},{1,13},{2,14},{3,15},{4,8},{5,9},{6,10},{7,11},{8,4},{9,5},... | collective-permute-start | bytes 147464 | tf_op jit(solution)/shard_map/ppermute | solution.py:22
  20.8 7.5 %collective-permute-start = (bf16[128,2,1536]{2,1,0:T(2,128)(2,1)S(1)}, bf16[128,2,1536]{2,1,0:T(2,128)(2,1)S(1)}, u32[]{:S(2)}, u32[]{:S(2)}) collective-permute-start(bf16[128,2,1536]{2,1,0:T(2,128)(2,1)S(1)} %get-tuple-element.60), channel_id=1, source_target_pairs={{0,1},{1,0},{2,3},{3,2},{4,5},{5,4},{6,7},{7,6},{8,9},{9,8},{10,11... | collective-permute-start | bytes 2359304 | tf_op jit(solution)/shard_map/ppermute | solution.py:22
  20.8 23.5 %collective-permute-start.2 = (bf16[128,2,768]{2,1,0:T(2,128)(2,1)S(1)}, bf16[128,2,768]{2,1,0:T(2,128)(2,1)S(1)}, u32[]{:S(2)}, u32[]{:S(2)}) collective-permute-start(bf16[128,2,768]{2,1,0:T(2,128)(2,1)S(1)} %get-tuple-element.63), channel_id=1, source_target_pairs={{0,2},{2,0},{4,6},{6,4},{8,10},{10,8},{12,14},{14,12},{1,3},{3,1},... | collective-permute-start | bytes 1179656 | tf_op jit(solution)/shard_map/ppermute | solution.py:41
  22.1 1.5 %collective-permute-start.7 = (bf16[32,2,1536]{2,1,0:T(2,128)(2,1)S(1)}, bf16[32,2,1536]{2,1,0:T(2,128)(2,1)S(1)}, u32[]{:S(2)}, u32[]{:S(2)}) collective-permute-start(bf16[32,2,1536]{2,1,0:T(2,128)(2,1)S(1)} %pad_maximum_fusion.1), channel_id=1, source_target_pairs={{0,1},{1,0},{2,3},{3,2},{4,5},{5,4},{6,7},{7,6},{8,9},{9,8},{10,11... | collective-permute-start | bytes 589832 | tf_op jit(solution)/shard_map/ppermute | solution.py:22
  23.6 20.7 %collective-permute-start.3 = (bf16[128,2,768]{2,1,0:T(2,128)(2,1)S(1)}, bf16[128,2,768]{2,1,0:T(2,128)(2,1)S(1)}, u32[]{:S(2)}, u32[]{:S(2)}) collective-permute-start(bf16[128,2,768]{2,1,0:T(2,128)(2,1)S(1)} %get-tuple-element.64), channel_id=1, source_target_pairs={{2,4},{4,2},{6,8},{8,6},{10,12},{12,10},{3,5},{5,3},{7,9},{9,7},{1... | collective-permute-start | bytes 1179656 | tf_op jit(solution)/shard_map/ppermute | solution.py:41
  28.1 1.4 %copy-start.1 = (bf16[256,2,1536]{2,1,0:T(2,128)(2,1)S(1)}, bf16[256,2,1536]{2,1,0:T(2,128)(2,1)}, u32[]{:S(2)}) copy-start(bf16[256,2,1536]{2,1,0:T(2,128)(2,1)} %own_ref.3) | copy-start | bytes 4718596
  28.2 1.6 %copy-start.2 = (bf16[256,1536]{1,0:T(8,128)(2,1)S(1)}, bf16[256,1536]{1,0:T(8,128)(2,1)}, u32[]{:S(2)}) copy-start(bf16[256,1536]{1,0:T(8,128)(2,1)} %q_ref.3) | copy-start | bytes 2359300
  28.2 1.8 %copy-start.3 = (bf16[256,1536]{1,0:T(8,128)(2,1)S(1)}, bf16[256,1536]{1,0:T(8,128)(2,1)}, u32[]{:S(2)}) copy-start(bf16[256,1536]{1,0:T(8,128)(2,1)} %g_ref.3) | copy-start | bytes 2359300
  28.2 1.8 %copy-start.6 = (s32[1,2,5]{2,1,0:T(2,128)S(1)}, s32[1,2,5]{2,1,0:T(2,128)}, u32[]{:S(2)}) copy-start(s32[1,2,5]{2,1,0:T(2,128)} %param.15) | copy-start | bytes 124
  28.2 1.8 %copy-start.7 = (f32[12]{0:T(128)S(1)}, f32[12]{0:T(128)}, u32[]{:S(2)}) copy-start(f32[12]{0:T(128)} %warm_ref.3) | copy-start | bytes 148
  40.4 14.5 %copy-start.14 = (f32[6,512,128]{2,1,0:T(8,128)}, f32[6,512,128]{2,1,0:T(8,128)S(1)}, u32[]{:S(2)}) copy-start(f32[6,512,128]{2,1,0:T(8,128)S(1)} %get-tuple-element.88.own_ref) | copy-start | bytes 4718596
  40.4 19.3 %collective-permute-start.10 = (bf16[6,256,128]{2,1,0:T(8,128)(2,1)S(1)}, bf16[6,256,128]{2,1,0:T(8,128)(2,1)S(1)}, u32[]{:S(2)}, u32[]{:S(2)}) collective-permute-start(bf16[6,256,128]{2,1,0:T(8,128)(2,1)S(1)} %get-tuple-element.77), channel_id=1, source_target_pairs={{0,2},{2,0},{4,6},{6,4},{8,10},{10,8},{12,14},{14,12},{1,3},{3,1},... | collective-permute-start | bytes 1179656 | tf_op jit(solution)/shard_map/ppermute | solution.py:41
  42.0 17.8 %collective-permute-start.11 = (bf16[6,256,128]{2,1,0:T(8,128)(2,1)S(1)}, bf16[6,256,128]{2,1,0:T(8,128)(2,1)S(1)}, u32[]{:S(2)}, u32[]{:S(2)}) collective-permute-start(bf16[6,256,128]{2,1,0:T(8,128)(2,1)S(1)} %get-tuple-element.78), channel_id=1, source_target_pairs={{2,4},{4,2},{6,8},{8,6},{10,12},{12,10},{3,5},{5,3},{7,9},{9,7},{1... | collective-permute-start | bytes 1179656 | tf_op jit(solution)/shard_map/ppermute | solution.py:41
  44.2 15.5 %collective-permute-start.12 = (bf16[6,256,128]{2,1,0:T(8,128)(2,1)S(1)}, bf16[6,256,128]{2,1,0:T(8,128)(2,1)S(1)}, u32[]{:S(2)}, u32[]{:S(2)}) collective-permute-start(bf16[6,256,128]{2,1,0:T(8,128)(2,1)S(1)} %get-tuple-element.79), channel_id=1, source_target_pairs={{0,1},{1,0},{2,3},{3,2},{4,5},{5,4},{6,7},{7,6},{8,9},{9,8},{10,11... | collective-permute-start | bytes 1179656 | tf_op jit(solution)/shard_map/ppermute | solution.py:22
  59.7 0.8 copy-start.8
  59.7 0.9 copy-start.10
  59.7 2.4 %copy-start.12 = (bf16[6,256,128]{2,1,0:T(8,128)(2,1)}, bf16[6,256,128]{2,1,0:T(8,128)(2,1)S(1)}, u32[]{:S(2)}) copy-start(bf16[6,256,128]{2,1,0:T(8,128)(2,1)S(1)} %collective-permute-done.12.par_ref) | copy-start | bytes 1179652
  59.8 8.0 %copy-start.5 = (s32[1,3,1]{1,2,0:T(1,128)S(1)}, s32[1,3,1]{1,2,0:T(1,128)}, u32[]{:S(2)}) copy-start(s32[1,3,1]{1,2,0:T(1,128)} %param.14) | copy-start | bytes 40
  59.8 2.3 %collective-permute-start.13 = (f32[64,1664]{1,0:T(8,128)S(1)}, f32[64,1664]{1,0:T(8,128)S(1)}, u32[]{:S(2)}, u32[]{:S(2)}) collective-permute-start(f32[64,1664]{1,0:T(8,128)S(1)} %pad_maximum_fusion), channel_id=1, source_target_pairs={{0,1},{1,0},{2,3},{3,2},{4,5},{5,4},{6,7},{7,6},{8,9},{9,8},{10,11... | collective-permute-start | bytes 1277960 | tf_op jit(solution)/shard_map/ppermute | solution.py:22
  60.5 3.8 %collective-permute-start.14 = (bf16[6,256,128]{2,1,0:T(8,128)(2,1)}, bf16[6,256,128]{2,1,0:T(8,128)(2,1)S(1)}, u32[]{:S(2)}, u32[]{:S(2)}) collective-permute-start(bf16[6,256,128]{2,1,0:T(8,128)(2,1)} %get-tuple-element.84), channel_id=1, source_target_pairs={{0,1},{1,0},{2,3},{3,2},{4,5},{5,4},{6,7},{7,6},{8,9},{9,8},{10,11... | collective-permute-start | bytes 1179656 | tf_op jit(solution)/shard_map/ppermute | solution.py:22
  60.6 18.5 %collective-permute-start.19 = (bf16[6,256,128]{2,1,0:T(8,128)(2,1)}, bf16[6,256,128]{2,1,0:T(8,128)(2,1)S(1)}, u32[]{:S(2)}, u32[]{:S(2)}) collective-permute-start(bf16[6,256,128]{2,1,0:T(8,128)(2,1)} %get-tuple-element.96), channel_id=1, source_target_pairs={{0,2},{2,0},{4,6},{6,4},{8,10},{10,8},{12,14},{14,12},{1,3},{3,1},... | collective-permute-start | bytes 1179656 | tf_op jit(solution)/shard_map/ppermute | solution.py:41
  62.2 0.8 copy-start.16
  63.0 4.8 %copy-start.9 = (bf16[6,256,128]{2,1,0:T(8,128)(2,1)S(1)}, bf16[6,256,128]{2,1,0:T(8,128)(2,1)}, u32[]{:S(2)}) copy-start(bf16[6,256,128]{2,1,0:T(8,128)(2,1)} %copy-done.8) | copy-start | bytes 1179652
  63.0 4.8 %copy-start.11 = (bf16[6,256,128]{2,1,0:T(8,128)(2,1)S(1)}, bf16[6,256,128]{2,1,0:T(8,128)(2,1)}, u32[]{:S(2)}) copy-start(bf16[6,256,128]{2,1,0:T(8,128)(2,1)} %copy-done.10) | copy-start | bytes 1179652
  63.0 4.8 %copy-start.13 = (bf16[6,256,128]{2,1,0:T(8,128)(2,1)S(1)}, bf16[6,256,128]{2,1,0:T(8,128)(2,1)}, u32[]{:S(2)}) copy-start(bf16[6,256,128]{2,1,0:T(8,128)(2,1)} %copy-done.12) | copy-start | bytes 1179652
  64.3 9.6 %collective-permute-start.15 = (f32[16,1664]{1,0:T(8,128)S(1)}, f32[16,1664]{1,0:T(8,128)S(1)}, u32[]{:S(2)}, u32[]{:S(2)}) collective-permute-start(f32[16,1664]{1,0:T(8,128)S(1)} %get-tuple-element.85), channel_id=1, source_target_pairs={{0,4},{1,5},{2,6},{3,7},{4,0},{5,1},{6,2},{7,3},{8,12},{9,13},{10,... | collective-permute-start | bytes 319496 | tf_op jit(solution)/shard_map/ppermute | solution.py:22
  64.5 9.4 %collective-permute-start.16 = (f32[16,1664]{1,0:T(8,128)S(1)}, f32[16,1664]{1,0:T(8,128)S(1)}, u32[]{:S(2)}, u32[]{:S(2)}) collective-permute-start(f32[16,1664]{1,0:T(8,128)S(1)} %get-tuple-element.86), channel_id=1, source_target_pairs={{0,8},{1,9},{2,10},{3,11},{4,12},{5,13},{6,14},{7,15},{8,0},{9,1},... | collective-permute-start | bytes 319496 | tf_op jit(solution)/shard_map/ppermute | solution.py:22
  65.7 11.5 %collective-permute-start.17 = (f32[16,1664]{1,0:T(8,128)S(1)}, f32[16,1664]{1,0:T(8,128)S(1)}, u32[]{:S(2)}, u32[]{:S(2)}) collective-permute-start(f32[16,1664]{1,0:T(8,128)S(1)} %get-tuple-element.87), channel_id=1, source_target_pairs={{0,12},{1,13},{2,14},{3,15},{4,8},{5,9},{6,10},{7,11},{8,4},{9,5},... | collective-permute-start | bytes 319496 | tf_op jit(solution)/shard_map/ppermute | solution.py:22
  67.8 1.4 %copy-start.15 = (f32[6,512,128]{2,1,0:T(8,128)S(1)}, f32[6,512,128]{2,1,0:T(8,128)}, u32[]{:S(2)}) copy-start(f32[6,512,128]{2,1,0:T(8,128)} %copy-done.14) | copy-start | bytes 4718596
  71.4 14.9 %collective-permute-start.20 = (bf16[6,256,128]{2,1,0:T(8,128)(2,1)S(1)}, bf16[6,256,128]{2,1,0:T(8,128)(2,1)S(1)}, u32[]{:S(2)}, u32[]{:S(2)}) collective-permute-start(bf16[6,256,128]{2,1,0:T(8,128)(2,1)S(1)} %get-tuple-element.97), channel_id=1, source_target_pairs={{2,4},{4,2},{6,8},{8,6},{10,12},{12,10},{3,5},{5,3},{7,9},{9,7},{1... | collective-permute-start | bytes 1179656 | tf_op jit(solution)/shard_map/ppermute | solution.py:41
  77.3 11.1 %collective-permute-start.18 = (f32[8,1664]{1,0:T(8,128)S(1)}, f32[8,1664]{1,0:T(8,128)S(1)}, u32[]{:S(2)}, u32[]{:S(2)}) collective-permute-start(f32[8,1664]{1,0:T(8,128)S(1)} %pad_maximum_fusion.5), channel_id=1, source_target_pairs={{0,2},{1,3},{2,0},{3,1},{4,6},{5,7},{6,4},{7,5},{8,10},{9,11},{10,... | collective-permute-start | bytes 159752 | tf_op jit(solution)/shard_map/ppermute | solution.py:22

commit v11 on v10

--- a/solution.py
+++ b/solution.py
@@ -351,11 +351,10 @@
         if i == 1:
             out, diagonal, returned[-1][2] = lax.optimization_barrier((out, diagonal, returned[-1][2]))
             returned[-1][1] = swap_pairs(diagonal, 1)
+            (extra,) = hold([extra], HOLD)
         got = [swap_mask(x, m) for x, m in zip(out, masks)]
-        if i == len(stages) - 2:
+        if i == len(stages) - 1:
             cell = combine(pos, sent, owns[-2], returned[-2], *chunks[-2], feat, width, cell, weight=4000)
-            got, cell = lax.optimization_barrier((got, cell))
-        if i == len(stages) - 1:
             cell = combine(pos, sent, owns[-1], returned[-1], *chunks[-1], feat, width, cell, weight=0)
             got, cell = lax.optimization_barrier((got, cell))
             anchor_grad, temp = finish(anc[:n], extra, got, landmark.shape)

time: 89.9 us -> 89.9 us (level)
  local copies, waits for them, and re-layouts: 7.04 us -> 4.96 us
  waiting for transfers between devices: 22.9 us -> 24.3 us
    ppermute x13, waiting for transfers between devices: 11.7 us -> 14.9 us  [swap_mask(): return lax.ppermute(x, ('gx', 'gy'), [(i, i ^ mask) for i in range(count)])]
    unnamed x40, local copies, waits for them, and re-layouts: 6.22 us -> 4.12 us
    ppermute x8, waiting for transfers between devices: 11.2 us -> 9.41 us  [swap_pairs(): return lax.ppermute(x, 'gx', route)]
  transfers between devices with their start and end apart: 21 -> 21, of which waited for: 5 -> 6; matrix products, arithmetic and copies ran while one was open for 5% -> 5% of each run, Pallas kernels for 30% -> 30%
where the time goes in v11:
time: 89.9 us; the launch traced here: 89.6 us
  starting transfers between devices  28.3 us (31%)
  Pallas kernels  27.4 us (30%)
  waiting for transfers between devices  24.3 us (27%)
  local copies, waits for them, and re-layouts  4.96 us (6%)
  other arithmetic  3.62 us (4%)
  between operations  1.04 us (1%)
    pallas_call x2, Pallas kernels, attention(): pl.pallas_call(functools.partial(attention_kernel, gx_count=lax.axis_size...  21 us
    ppermute x8, starting transfers between devices, swap_pairs(): return lax.ppermute(x, 'gx', route)  17.2 us
    ppermute x13, waiting for transfers between devices, swap_mask(): return lax.ppermute(x, ('gx', 'gy'), [(i, i ^ mask) for i in range(count)])  14.9 us
    ppermute x13, starting transfers between devices, swap_mask(): return lax.ppermute(x, ('gx', 'gy'), [(i, i ^ mask) for i in range(count)])  11.2 us
    ppermute x8, waiting for transfers between devices, swap_pairs(): return lax.ppermute(x, 'gx', route)  9.41 us
    pallas_call x2, Pallas kernels, combine(): pl.pallas_call(combine_kernel, grid=(heads // step,), in_specs=in_specs,...  4.34 us
    unnamed x40, local copies, waits for them, and re-layouts  4.12 us
  transfers between devices with their start and end apart: 21, of which 6 were waited for; matrix products, arithmetic and copies ran while one was open for 5% of the time, Pallas kernels for 30%

profile of v11, /device:TPU:16, one launch (start us, length us, event | category | flops | bytes accessed | tf_op | source)
XLA Modules:
  0.0 89.6 jit_solution(4582769972837370127)
XLA Ops:
  0.6 1.6 %collective-permute-start.1 = (bf16[4,2,1536]{2,1,0:T(2,128)(2,1)}, bf16[4,2,1536]{2,1,0:T(2,128)(2,1)S(1)}, u32[]{:S(2)}, u32[]{:S(2)}) collective-permute-start(bf16[4,2,1536]{2,1,0:T(2,128)(2,1)} %param.11), channel_id=1, source_target_pairs={{0,2},{1,3},{2,0},{3,1},{4,6},{5,7},{6,4},{7,5},{8,10},{9,11},{10,... | collective-permute-start | bytes 73736 | tf_op jit(solution)/shard_map/ppermute | solution.py:22
  2.2 1.4 %copy-done = bf16[256,2,1536]{2,1,0:T(2,128)(2,1)S(1)} copy-done((bf16[256,2,1536]{2,1,0:T(2,128)(2,1)S(1)}, bf16[256,2,1536]{2,1,0:T(2,128)(2,1)}, u32[]{:S(2)}) %copy-start) | copy-done | bytes 1572888
  3.6 0.7 copy-done.4
  4.3 0.7 pick.3
  4.9 0.6 collective-permute-start.8
  5.5 3.3 %collective-permute-start.9 = (bf16[128,2,768]{2,1,0:T(2,128)(2,1)S(1)}, bf16[128,2,768]{2,1,0:T(2,128)(2,1)S(1)}, u32[]{:S(2)}, u32[]{:S(2)}) collective-permute-start(bf16[128,2,768]{2,1,0:T(2,128)(2,1)S(1)} %get-tuple-element.63), channel_id=1, source_target_pairs={{2,4},{4,2},{6,8},{8,6},{10,12},{12,10},{3,5},{5,3},{7,9},{9,7},{1... | collective-permute-start | bytes 1179656 | tf_op jit(solution)/shard_map/ppermute | solution.py:41
  8.8 0.7 pick.2
  9.5 0.6 compare_reduce_fusion
  10.3 1.6 %collective-permute-start.4 = (bf16[8,2,1536]{2,1,0:T(2,128)(2,1)S(1)}, bf16[8,2,1536]{2,1,0:T(2,128)(2,1)S(1)}, u32[]{:S(2)}, u32[]{:S(2)}) collective-permute-start(bf16[8,2,1536]{2,1,0:T(2,128)(2,1)S(1)} %pad_maximum_fusion.6), channel_id=1, source_target_pairs={{0,4},{1,5},{2,6},{3,7},{4,0},{5,1},{6,2},{7,3},{8,12},{9,13},{10,... | collective-permute-start | bytes 147464 | tf_op jit(solution)/shard_map/ppermute | solution.py:22
  11.9 0.3 collective-permute-start.5
  12.2 1.6 %collective-permute-start.6 = (bf16[8,2,1536]{2,1,0:T(2,128)(2,1)S(1)}, bf16[8,2,1536]{2,1,0:T(2,128)(2,1)S(1)}, u32[]{:S(2)}, u32[]{:S(2)}) collective-permute-start(bf16[8,2,1536]{2,1,0:T(2,128)(2,1)S(1)} %pad_maximum_fusion.6), channel_id=1, source_target_pairs={{0,12},{1,13},{2,14},{3,15},{4,8},{5,9},{6,10},{7,11},{8,4},{9,5},... | collective-permute-start | bytes 147464 | tf_op jit(solution)/shard_map/ppermute | solution.py:22
  13.8 6.9 %collective-permute-done.4 = bf16[8,2,1536]{2,1,0:T(2,128)(2,1)S(1)} collective-permute-done((bf16[8,2,1536]{2,1,0:T(2,128)(2,1)S(1)}, bf16[8,2,1536]{2,1,0:T(2,128)(2,1)S(1)}, u32[]{:S(2)}, u32[]{:S(2)}) %collective-permute-start.4) | collective-permute-done | bytes 49184 | tf_op jit(solution)/shard_map/ppermute | solution.py:22
  20.8 1.0 %collective-permute-start.2 = (bf16[128,2,768]{2,1,0:T(2,128)(2,1)S(1)}, bf16[128,2,768]{2,1,0:T(2,128)(2,1)S(1)}, u32[]{:S(2)}, u32[]{:S(2)}) collective-permute-start(bf16[128,2,768]{2,1,0:T(2,128)(2,1)S(1)} %get-tuple-element.59), channel_id=1, source_target_pairs={{0,2},{2,0},{4,6},{6,4},{8,10},{10,8},{12,14},{14,12},{1,3},{3,1},... | collective-permute-start | bytes 1179656 | tf_op jit(solution)/shard_map/ppermute | solution.py:41
  21.8 0.3 pad_maximum_fusion.1
  22.1 0.1 collective-permute-start.7
  22.4 1.3 %collective-permute-done.7 = bf16[32,2,1536]{2,1,0:T(2,128)(2,1)S(1)} collective-permute-done((bf16[32,2,1536]{2,1,0:T(2,128)(2,1)S(1)}, bf16[32,2,1536]{2,1,0:T(2,128)(2,1)S(1)}, u32[]{:S(2)}, u32[]{:S(2)}) %collective-permute-start.7) | collective-permute-done | bytes 196640 | tf_op jit(solution)/shard_map/ppermute | solution.py:22
  23.6 4.3 %collective-permute-start.3 = (bf16[128,2,768]{2,1,0:T(2,128)(2,1)S(1)}, bf16[128,2,768]{2,1,0:T(2,128)(2,1)S(1)}, u32[]{:S(2)}, u32[]{:S(2)}) collective-permute-start(bf16[128,2,768]{2,1,0:T(2,128)(2,1)S(1)} %get-tuple-element.60), channel_id=1, source_target_pairs={{2,4},{4,2},{6,8},{8,6},{10,12},{12,10},{3,5},{5,3},{7,9},{9,7},{1... | collective-permute-start | bytes 1179656 | tf_op jit(solution)/shard_map/ppermute | solution.py:41
  28.0 0.2 constant_dynamic-update-slice_fusion.anc_ref
  28.2 1.3 %copy-done.1 = bf16[256,2,1536]{2,1,0:T(2,128)(2,1)S(1)} copy-done((bf16[256,2,1536]{2,1,0:T(2,128)(2,1)S(1)}, bf16[256,2,1536]{2,1,0:T(2,128)(2,1)}, u32[]{:S(2)}) %copy-start.1) | copy-done | bytes 1572888
  29.6 0.2 copy-done.2
  29.8 0.2 copy-done.3
  30.0 10.4 %attention.2 = (bf16[256,1536]{1,0:T(8,128)(2,1)}, f32[6,512,128]{2,1,0:T(8,128)S(1)}, bf16[6,256,128]{2,1,0:T(8,128)(2,1)S(1)}, bf16[6,256,128]{2,1,0:T(8,128)(...) custom-call(s32[1]{0:T(128)} %bitcast.pos_ref, ...), custom_call_target="tpu_custom_call" | custom-call | flops 1384120320 | bytes 6488064 | tf_op jit(solution)/shard_map/attention/pallas_call | solution.py:197
  40.4 1.6 %collective-permute-start.10 = (bf16[6,256,128]{2,1,0:T(8,128)(2,1)S(1)}, bf16[6,256,128]{2,1,0:T(8,128)(2,1)S(1)}, u32[]{:S(2)}, u32[]{:S(2)}) collective-permute-start(bf16[6,256,128]{2,1,0:T(8,128)(2,1)S(1)} %get-tuple-element.73), channel_id=1, source_target_pairs={{0,2},{2,0},{4,6},{6,4},{8,10},{10,8},{12,14},{14,12},{1,3},{3,1},... | collective-permute-start | bytes 1179656 | tf_op jit(solution)/shard_map/ppermute | solution.py:41
  42.0 2.2 %collective-permute-start.11 = (bf16[6,256,128]{2,1,0:T(8,128)(2,1)S(1)}, bf16[6,256,128]{2,1,0:T(8,128)(2,1)S(1)}, u32[]{:S(2)}, u32[]{:S(2)}) collective-permute-start(bf16[6,256,128]{2,1,0:T(8,128)(2,1)S(1)} %get-tuple-element.74), channel_id=1, source_target_pairs={{2,4},{4,2},{6,8},{8,6},{10,12},{12,10},{3,5},{5,3},{7,9},{9,7},{1... | collective-permute-start | bytes 1179656 | tf_op jit(solution)/shard_map/ppermute | solution.py:41
  44.2 0.1 collective-permute-start.12
  44.3 10.6 %attention.3 = (bf16[256,1536]{1,0:T(8,128)(2,1)}, f32[6,512,128]{2,1,0:T(8,128)S(1)}, bf16[6,256,128]{2,1,0:T(8,128)(2,1)}, bf16[6,256,128]{2,1,0:T(8,128)(2,1)...) custom-call(s32[1]{0:T(128)} %bitcast.pos_ref, ...), custom_call_target="tpu_custom_call", output_to_operand_aliasing={{0}: (10, {}), {5}: (11, {})} | custom-call | flops 1384120320 | bytes 6488064 | tf_op jit(solution)/shard_map/attention/pallas_call | solution.py:197
  54.9 0.2 maximum_reduce_fusion
  55.1 0.6 fusion
  55.7 4.0 %collective-permute-done.10.dir_ref = bf16[6,256,128]{2,1,0:T(8,128)(2,1)S(1)} collective-permute-done((bf16[6,256,128]{2,1,0:T(8,128)(2,1)S(1)}, bf16[6,256,128]{2,1,0:T(8,128)(2,1)S(1)}, u32[]{:S(2)}, u32[]{:S(2)}) %collective-permute-start.10) | collective-permute-done | bytes 393248 | tf_op jit(solution)/shard_map/ppermute | solution.py:41
  59.8 0.1 collective-permute-start.13
  59.9 0.5 collective-permute-start.14
  60.4 1.5 %collective-permute-start.19 = (bf16[6,256,128]{2,1,0:T(8,128)(2,1)}, bf16[6,256,128]{2,1,0:T(8,128)(2,1)S(1)}, u32[]{:S(2)}, u32[]{:S(2)}) collective-permute-start(bf16[6,256,128]{2,1,0:T(8,128)(2,1)} %get-tuple-element.85), channel_id=1, source_target_pairs={{0,2},{2,0},{4,6},{6,4},{8,10},{10,8},{12,14},{14,12},{1,3},{3,1},... | collective-permute-start | bytes 1179656 | tf_op jit(solution)/shard_map/ppermute | solution.py:41
  62.0 0.7 slice_add_fusion.7
  62.6 0.1 copy-done.16
  62.7 0.1 add.30.refs_0_
  62.8 1.0 %slice_add_fusion = f32[64,1536]{1,0:T(8,128)S(1)} fusion(f32[64,1664]{1,0:T(8,128)} %copy-done.16, f32[128,1536]{1,0:T(8,128)S(1)} %get-tuple-element.76), kind=kLoop, calls=%fused_computation.1 | loop fusion | flops 98304 | bytes 1179648 | tf_op jit(solution)/shard_map/add | solution.py:362
  64.0 0.4 collective-permute-start.15
  64.4 1.3 %collective-permute-start.16 = (f32[16,1664]{1,0:T(8,128)S(1)}, f32[16,1664]{1,0:T(8,128)S(1)}, u32[]{:S(2)}, u32[]{:S(2)}) collective-permute-start(f32[16,1664]{1,0:T(8,128)S(1)} %get-tuple-element.82), channel_id=1, source_target_pairs={{0,8},{1,9},{2,10},{3,11},{4,12},{5,13},{6,14},{7,15},{8,0},{9,1},... | collective-permute-start | bytes 319496 | tf_op jit(solution)/shard_map/ppermute | solution.py:22
  65.6 1.9 %collective-permute-start.17 = (f32[16,1664]{1,0:T(8,128)S(1)}, f32[16,1664]{1,0:T(8,128)S(1)}, u32[]{:S(2)}, u32[]{:S(2)}) collective-permute-start(f32[16,1664]{1,0:T(8,128)S(1)} %get-tuple-element.83), channel_id=1, source_target_pairs={{0,12},{1,13},{2,14},{3,15},{4,8},{5,9},{6,10},{7,11},{8,4},{9,5},... | collective-permute-start | bytes 319496 | tf_op jit(solution)/shard_map/ppermute | solution.py:22
  67.6 2.6 %collective-permute-start.20 = (bf16[6,256,128]{2,1,0:T(8,128)(2,1)S(1)}, bf16[6,256,128]{2,1,0:T(8,128)(2,1)S(1)}, u32[]{:S(2)}, u32[]{:S(2)}) collective-permute-start(bf16[6,256,128]{2,1,0:T(8,128)(2,1)S(1)} %copy-done.13), channel_id=1, source_target_pairs={{2,4},{4,2},{6,8},{8,6},{10,12},{12,10},{3,5},{5,3},{7,9},{9,7},{1... | collective-permute-start | bytes 1179656 | tf_op jit(solution)/shard_map/ppermute | solution.py:41
  70.2 2.9 %collective-permute-done.16 = f32[16,1664]{1,0:T(8,128)S(1)} collective-permute-done((f32[16,1664]{1,0:T(8,128)S(1)}, f32[16,1664]{1,0:T(8,128)S(1)}, u32[]{:S(2)}, u32[]{:S(2)}) %collective-permute-start.16) | collective-permute-done | bytes 106528 | tf_op jit(solution)/shard_map/ppermute | solution.py:22
  73.0 3.8 %collective-permute-done.17 = f32[16,1664]{1,0:T(8,128)S(1)} collective-permute-done((f32[16,1664]{1,0:T(8,128)S(1)}, f32[16,1664]{1,0:T(8,128)S(1)}, u32[]{:S(2)}, u32[]{:S(2)}) %collective-permute-start.17) | collective-permute-done | bytes 106528 | tf_op jit(solution)/shard_map/ppermute | solution.py:22
  76.9 1.8 %collective-permute-start.18 = (f32[8,1664]{1,0:T(8,128)S(1)}, f32[8,1664]{1,0:T(8,128)S(1)}, u32[]{:S(2)}, u32[]{:S(2)}) collective-permute-start(f32[8,1664]{1,0:T(8,128)S(1)} %pad_maximum_fusion.5), channel_id=1, source_target_pairs={{0,2},{1,3},{2,0},{3,1},{4,6},{5,7},{6,4},{7,5},{8,10},{9,11},{10,... | collective-permute-start | bytes 159752 | tf_op jit(solution)/shard_map/ppermute | solution.py:22
  78.7 2.2 %combine.2.rest_0_ = bf16[256,2,1536]{2,1,0:T(2,128)(2,1)} custom-call(s32[1]{0:T(128)} %bitcast.pos_ref, s32[3]{0:T(128)S(1)} %bitcast.15, f32[6,512,128]{2,1,0:T(8,128)S(1)} %copy-done.15, bf16[6,256,128]{2,1,0:T(8,128)(2,1)S(1)} %collective-permute-done.10.dir_ref, bf16[6,256,128]{2,1,0:T(8,128)(2,1)S(1)} %copy-done.9, bf16[6,256,128]{2,1,0:T(8,128)(2,1)S(1)} %copy-done.11), custom_call_target="tpu_custom_call" | custom-call | flops 12582912000 | bytes 3538944 | tf_op jit(solution)/shard_map/combine/pallas_call | solution.py:265
  80.9 5.4 %collective-permute-done.20.dia_ref = bf16[6,256,128]{2,1,0:T(8,128)(2,1)S(1)} collective-permute-done((bf16[6,256,128]{2,1,0:T(8,128)(2,1)S(1)}, bf16[6,256,128]{2,1,0:T(8,128)(2,1)S(1)}, u32[]{:S(2)}, u32[]{:S(2)}) %collective-permute-start.20) | collective-permute-done | bytes 393248 | tf_op jit(solution)/shard_map/ppermute | solution.py:41
  86.3 2.2 %combine.3 = bf16[256,2,1536]{2,1,0:T(2,128)(2,1)} custom-call(s32[1]{0:T(128)} %bitcast.pos_ref, s32[3]{0:T(128)S(1)} %bitcast.16, f32[6,512,128]{2,1,0:T(8,128)S(1)} %get-tuple-element.84.own_ref, bf16[6,256,128]{2,1,0:T(8,128)(2,1)S(1)} %collective-permute-done.19.dir_ref, ...), custom_call_target="tpu_custom_call", output_to_operand_aliasing={{}: (6, {})} | custom-call | bytes 3538944 | tf_op jit(solution)/shard_map/combine/pallas_call | solution.py:265
  88.4 0.6 finish.1
  89.1 0.5 slice_bitcast_fusion
  (66 shorter events, 0.6 us)
Async XLA Ops:
  0.6 9.6 %collective-permute-start.1 = (bf16[4,2,1536]{2,1,0:T(2,128)(2,1)}, bf16[4,2,1536]{2,1,0:T(2,128)(2,1)S(1)}, u32[]{:S(2)}, u32[]{:S(2)}) collective-permute-start(bf16[4,2,1536]{2,1,0:T(2,128)(2,1)} %param.11), channel_id=1, source_target_pairs={{0,2},{1,3},{2,0},{3,1},{4,6},{5,7},{6,4},{7,5},{8,10},{9,11},{10,... | collective-permute-start | bytes 73736 | tf_op jit(solution)/shard_map/ppermute | solution.py:22
  2.2 1.4 %copy-start = (bf16[256,2,1536]{2,1,0:T(2,128)(2,1)S(1)}, bf16[256,2,1536]{2,1,0:T(2,128)(2,1)}, u32[]{:S(2)}) copy-start(bf16[256,2,1536]{2,1,0:T(2,128)(2,1)} %own_ref.3) | copy-start | bytes 4718596
  3.6 0.7 copy-start.4
  4.3 5.9 %copy-start.17 = (bf16[4,2,1536]{2,1,0:T(2,128)(2,1)S(1)}, bf16[4,2,1536]{2,1,0:T(2,128)(2,1)}, u32[]{:S(2)}) copy-start(bf16[4,2,1536]{2,1,0:T(2,128)(2,1)} %param.11) | copy-start | bytes 73732
  4.9 23.3 %collective-permute-start.8 = (bf16[128,2,768]{2,1,0:T(2,128)(2,1)S(1)}, bf16[128,2,768]{2,1,0:T(2,128)(2,1)S(1)}, u32[]{:S(2)}, u32[]{:S(2)}) collective-permute-start(bf16[128,2,768]{2,1,0:T(2,128)(2,1)S(1)} %get-tuple-element.62), channel_id=1, source_target_pairs={{0,2},{2,0},{4,6},{6,4},{8,10},{10,8},{12,14},{14,12},{1,3},{3,1},... | collective-permute-start | bytes 1179656 | tf_op jit(solution)/shard_map/ppermute | solution.py:41
  5.5 22.7 %collective-permute-start.9 = (bf16[128,2,768]{2,1,0:T(2,128)(2,1)S(1)}, bf16[128,2,768]{2,1,0:T(2,128)(2,1)S(1)}, u32[]{:S(2)}, u32[]{:S(2)}) collective-permute-start(bf16[128,2,768]{2,1,0:T(2,128)(2,1)S(1)} %get-tuple-element.63), channel_id=1, source_target_pairs={{2,4},{4,2},{6,8},{8,6},{10,12},{12,10},{3,5},{5,3},{7,9},{9,7},{1... | collective-permute-start | bytes 1179656 | tf_op jit(solution)/shard_map/ppermute | solution.py:41
  10.3 10.5 %collective-permute-start.4 = (bf16[8,2,1536]{2,1,0:T(2,128)(2,1)S(1)}, bf16[8,2,1536]{2,1,0:T(2,128)(2,1)S(1)}, u32[]{:S(2)}, u32[]{:S(2)}) collective-permute-start(bf16[8,2,1536]{2,1,0:T(2,128)(2,1)S(1)} %pad_maximum_fusion.6), channel_id=1, source_target_pairs={{0,4},{1,5},{2,6},{3,7},{4,0},{5,1},{6,2},{7,3},{8,12},{9,13},{10,... | collective-permute-start | bytes 147464 | tf_op jit(solution)/shard_map/ppermute | solution.py:22
  11.9 8.9 %collective-permute-start.5 = (bf16[8,2,1536]{2,1,0:T(2,128)(2,1)S(1)}, bf16[8,2,1536]{2,1,0:T(2,128)(2,1)S(1)}, u32[]{:S(2)}, u32[]{:S(2)}) collective-permute-start(bf16[8,2,1536]{2,1,0:T(2,128)(2,1)S(1)} %pad_maximum_fusion.6), channel_id=1, source_target_pairs={{0,8},{1,9},{2,10},{3,11},{4,12},{5,13},{6,14},{7,15},{8,0},{9,1},... | collective-permute-start | bytes 147464 | tf_op jit(solution)/shard_map/ppermute | solution.py:22
  12.2 9.6 %collective-permute-start.6 = (bf16[8,2,1536]{2,1,0:T(2,128)(2,1)S(1)}, bf16[8,2,1536]{2,1,0:T(2,128)(2,1)S(1)}, u32[]{:S(2)}, u32[]{:S(2)}) collective-permute-start(bf16[8,2,1536]{2,1,0:T(2,128)(2,1)S(1)} %pad_maximum_fusion.6), channel_id=1, source_target_pairs={{0,12},{1,13},{2,14},{3,15},{4,8},{5,9},{6,10},{7,11},{8,4},{9,5},... | collective-permute-start | bytes 147464 | tf_op jit(solution)/shard_map/ppermute | solution.py:22
  20.8 7.5 %collective-permute-start = (bf16[128,2,1536]{2,1,0:T(2,128)(2,1)S(1)}, bf16[128,2,1536]{2,1,0:T(2,128)(2,1)S(1)}, u32[]{:S(2)}, u32[]{:S(2)}) collective-permute-start(bf16[128,2,1536]{2,1,0:T(2,128)(2,1)S(1)} %get-tuple-element.56), channel_id=1, source_target_pairs={{0,1},{1,0},{2,3},{3,2},{4,5},{5,4},{6,7},{7,6},{8,9},{9,8},{10,11... | collective-permute-start | bytes 2359304 | tf_op jit(solution)/shard_map/ppermute | solution.py:22
  20.8 23.5 %collective-permute-start.2 = (bf16[128,2,768]{2,1,0:T(2,128)(2,1)S(1)}, bf16[128,2,768]{2,1,0:T(2,128)(2,1)S(1)}, u32[]{:S(2)}, u32[]{:S(2)}) collective-permute-start(bf16[128,2,768]{2,1,0:T(2,128)(2,1)S(1)} %get-tuple-element.59), channel_id=1, source_target_pairs={{0,2},{2,0},{4,6},{6,4},{8,10},{10,8},{12,14},{14,12},{1,3},{3,1},... | collective-permute-start | bytes 1179656 | tf_op jit(solution)/shard_map/ppermute | solution.py:41
  22.1 1.5 %collective-permute-start.7 = (bf16[32,2,1536]{2,1,0:T(2,128)(2,1)S(1)}, bf16[32,2,1536]{2,1,0:T(2,128)(2,1)S(1)}, u32[]{:S(2)}, u32[]{:S(2)}) collective-permute-start(bf16[32,2,1536]{2,1,0:T(2,128)(2,1)S(1)} %pad_maximum_fusion.1), channel_id=1, source_target_pairs={{0,1},{1,0},{2,3},{3,2},{4,5},{5,4},{6,7},{7,6},{8,9},{9,8},{10,11... | collective-permute-start | bytes 589832 | tf_op jit(solution)/shard_map/ppermute | solution.py:22
  23.6 20.7 %collective-permute-start.3 = (bf16[128,2,768]{2,1,0:T(2,128)(2,1)S(1)}, bf16[128,2,768]{2,1,0:T(2,128)(2,1)S(1)}, u32[]{:S(2)}, u32[]{:S(2)}) collective-permute-start(bf16[128,2,768]{2,1,0:T(2,128)(2,1)S(1)} %get-tuple-element.60), channel_id=1, source_target_pairs={{2,4},{4,2},{6,8},{8,6},{10,12},{12,10},{3,5},{5,3},{7,9},{9,7},{1... | collective-permute-start | bytes 1179656 | tf_op jit(solution)/shard_map/ppermute | solution.py:41
  28.1 1.4 %copy-start.1 = (bf16[256,2,1536]{2,1,0:T(2,128)(2,1)S(1)}, bf16[256,2,1536]{2,1,0:T(2,128)(2,1)}, u32[]{:S(2)}) copy-start(bf16[256,2,1536]{2,1,0:T(2,128)(2,1)} %own_ref.3) | copy-start | bytes 4718596
  28.2 1.6 %copy-start.2 = (bf16[256,1536]{1,0:T(8,128)(2,1)S(1)}, bf16[256,1536]{1,0:T(8,128)(2,1)}, u32[]{:S(2)}) copy-start(bf16[256,1536]{1,0:T(8,128)(2,1)} %q_ref.3) | copy-start | bytes 2359300
  28.2 1.8 %copy-start.3 = (bf16[256,1536]{1,0:T(8,128)(2,1)S(1)}, bf16[256,1536]{1,0:T(8,128)(2,1)}, u32[]{:S(2)}) copy-start(bf16[256,1536]{1,0:T(8,128)(2,1)} %g_ref.3) | copy-start | bytes 2359300
  28.2 1.8 %copy-start.6 = (s32[1,2,5]{2,1,0:T(2,128)S(1)}, s32[1,2,5]{2,1,0:T(2,128)}, u32[]{:S(2)}) copy-start(s32[1,2,5]{2,1,0:T(2,128)} %param.15) | copy-start | bytes 124
  28.2 1.8 %copy-start.7 = (f32[12]{0:T(128)S(1)}, f32[12]{0:T(128)}, u32[]{:S(2)}) copy-start(f32[12]{0:T(128)} %warm_ref.3) | copy-start | bytes 148
  40.4 14.5 %copy-start.14 = (f32[6,512,128]{2,1,0:T(8,128)}, f32[6,512,128]{2,1,0:T(8,128)S(1)}, u32[]{:S(2)}) copy-start(f32[6,512,128]{2,1,0:T(8,128)S(1)} %get-tuple-element.88.own_ref) | copy-start | bytes 4718596
  40.4 19.3 %collective-permute-start.10 = (bf16[6,256,128]{2,1,0:T(8,128)(2,1)S(1)}, bf16[6,256,128]{2,1,0:T(8,128)(2,1)S(1)}, u32[]{:S(2)}, u32[]{:S(2)}) collective-permute-start(bf16[6,256,128]{2,1,0:T(8,128)(2,1)S(1)} %get-tuple-element.73), channel_id=1, source_target_pairs={{0,2},{2,0},{4,6},{6,4},{8,10},{10,8},{12,14},{14,12},{1,3},{3,1},... | collective-permute-start | bytes 1179656 | tf_op jit(solution)/shard_map/ppermute | solution.py:41
  42.0 17.8 %collective-permute-start.11 = (bf16[6,256,128]{2,1,0:T(8,128)(2,1)S(1)}, bf16[6,256,128]{2,1,0:T(8,128)(2,1)S(1)}, u32[]{:S(2)}, u32[]{:S(2)}) collective-permute-start(bf16[6,256,128]{2,1,0:T(8,128)(2,1)S(1)} %get-tuple-element.74), channel_id=1, source_target_pairs={{2,4},{4,2},{6,8},{8,6},{10,12},{12,10},{3,5},{5,3},{7,9},{9,7},{1... | collective-permute-start | bytes 1179656 | tf_op jit(solution)/shard_map/ppermute | solution.py:41
  44.2 15.5 %collective-permute-start.12 = (bf16[6,256,128]{2,1,0:T(8,128)(2,1)S(1)}, bf16[6,256,128]{2,1,0:T(8,128)(2,1)S(1)}, u32[]{:S(2)}, u32[]{:S(2)}) collective-permute-start(bf16[6,256,128]{2,1,0:T(8,128)(2,1)S(1)} %get-tuple-element.75), channel_id=1, source_target_pairs={{0,1},{1,0},{2,3},{3,2},{4,5},{5,4},{6,7},{7,6},{8,9},{9,8},{10,11... | collective-permute-start | bytes 1179656 | tf_op jit(solution)/shard_map/ppermute | solution.py:22
  54.9 7.7 %copy-start.12 = (bf16[6,256,128]{2,1,0:T(8,128)(2,1)}, bf16[6,256,128]{2,1,0:T(8,128)(2,1)S(1)}, u32[]{:S(2)}) copy-start(bf16[6,256,128]{2,1,0:T(8,128)(2,1)S(1)} %get-tuple-element.86) | copy-start | bytes 1179652
  59.7 2.9 %copy-start.8 = (bf16[6,256,128]{2,1,0:T(8,128)(2,1)}, bf16[6,256,128]{2,1,0:T(8,128)(2,1)S(1)}, u32[]{:S(2)}) copy-start(bf16[6,256,128]{2,1,0:T(8,128)(2,1)S(1)} %collective-permute-done.11.dia_ref) | copy-start | bytes 1179652
  59.7 2.9 %copy-start.10 = (bf16[6,256,128]{2,1,0:T(8,128)(2,1)}, bf16[6,256,128]{2,1,0:T(8,128)(2,1)S(1)}, u32[]{:S(2)}) copy-start(bf16[6,256,128]{2,1,0:T(8,128)(2,1)S(1)} %collective-permute-done.12.par_ref) | copy-start | bytes 1179652
  59.8 2.1 %collective-permute-start.13 = (f32[64,1664]{1,0:T(8,128)S(1)}, f32[64,1664]{1,0:T(8,128)S(1)}, u32[]{:S(2)}, u32[]{:S(2)}) collective-permute-start(f32[64,1664]{1,0:T(8,128)S(1)} %pad_maximum_fusion), channel_id=1, source_target_pairs={{0,1},{1,0},{2,3},{3,2},{4,5},{5,4},{6,7},{7,6},{8,9},{9,8},{10,11... | collective-permute-start | bytes 1277960 | tf_op jit(solution)/shard_map/ppermute | solution.py:22
  59.9 4.0 %collective-permute-start.14 = (bf16[6,256,128]{2,1,0:T(8,128)(2,1)}, bf16[6,256,128]{2,1,0:T(8,128)(2,1)S(1)}, u32[]{:S(2)}, u32[]{:S(2)}) collective-permute-start(bf16[6,256,128]{2,1,0:T(8,128)(2,1)} %get-tuple-element.80), channel_id=1, source_target_pairs={{0,1},{1,0},{2,3},{3,2},{4,5},{5,4},{6,7},{7,6},{8,9},{9,8},{10,11... | collective-permute-start | bytes 1179656 | tf_op jit(solution)/shard_map/ppermute | solution.py:22
  60.4 20.5 %collective-permute-start.19 = (bf16[6,256,128]{2,1,0:T(8,128)(2,1)}, bf16[6,256,128]{2,1,0:T(8,128)(2,1)S(1)}, u32[]{:S(2)}, u32[]{:S(2)}) collective-permute-start(bf16[6,256,128]{2,1,0:T(8,128)(2,1)} %get-tuple-element.85), channel_id=1, source_target_pairs={{0,2},{2,0},{4,6},{6,4},{8,10},{10,8},{12,14},{14,12},{1,3},{3,1},... | collective-permute-start | bytes 1179656 | tf_op jit(solution)/shard_map/ppermute | solution.py:41
  62.0 0.8 copy-start.16
  63.9 3.6 %copy-start.13 = (bf16[6,256,128]{2,1,0:T(8,128)(2,1)S(1)}, bf16[6,256,128]{2,1,0:T(8,128)(2,1)}, u32[]{:S(2)}) copy-start(bf16[6,256,128]{2,1,0:T(8,128)(2,1)} %copy-done.12) | copy-start | bytes 1179652
  64.0 14.7 %copy-start.5 = (s32[1,3,1]{1,2,0:T(1,128)S(1)}, s32[1,3,1]{1,2,0:T(1,128)}, u32[]{:S(2)}) copy-start(s32[1,3,1]{1,2,0:T(1,128)} %param.14) | copy-start | bytes 40
  64.0 14.7 %copy-start.9 = (bf16[6,256,128]{2,1,0:T(8,128)(2,1)S(1)}, bf16[6,256,128]{2,1,0:T(8,128)(2,1)}, u32[]{:S(2)}) copy-start(bf16[6,256,128]{2,1,0:T(8,128)(2,1)} %copy-done.8) | copy-start | bytes 1179652
  64.0 14.7 %copy-start.11 = (bf16[6,256,128]{2,1,0:T(8,128)(2,1)S(1)}, bf16[6,256,128]{2,1,0:T(8,128)(2,1)}, u32[]{:S(2)}) copy-start(bf16[6,256,128]{2,1,0:T(8,128)(2,1)} %copy-done.10) | copy-start | bytes 1179652
  64.0 14.7 %copy-start.15 = (f32[6,512,128]{2,1,0:T(8,128)S(1)}, f32[6,512,128]{2,1,0:T(8,128)}, u32[]{:S(2)}) copy-start(f32[6,512,128]{2,1,0:T(8,128)} %copy-done.14) | copy-start | bytes 4718596
  64.0 6.2 %collective-permute-start.15 = (f32[16,1664]{1,0:T(8,128)S(1)}, f32[16,1664]{1,0:T(8,128)S(1)}, u32[]{:S(2)}, u32[]{:S(2)}) collective-permute-start(f32[16,1664]{1,0:T(8,128)S(1)} %get-tuple-element.81), channel_id=1, source_target_pairs={{0,4},{1,5},{2,6},{3,7},{4,0},{5,1},{6,2},{7,3},{8,12},{9,13},{10,... | collective-permute-start | bytes 319496 | tf_op jit(solution)/shard_map/ppermute | solution.py:22
  64.4 8.7 %collective-permute-start.16 = (f32[16,1664]{1,0:T(8,128)S(1)}, f32[16,1664]{1,0:T(8,128)S(1)}, u32[]{:S(2)}, u32[]{:S(2)}) collective-permute-start(f32[16,1664]{1,0:T(8,128)S(1)} %get-tuple-element.82), channel_id=1, source_target_pairs={{0,8},{1,9},{2,10},{3,11},{4,12},{5,13},{6,14},{7,15},{8,0},{9,1},... | collective-permute-start | bytes 319496 | tf_op jit(solution)/shard_map/ppermute | solution.py:22
  65.6 11.2 %collective-permute-start.17 = (f32[16,1664]{1,0:T(8,128)S(1)}, f32[16,1664]{1,0:T(8,128)S(1)}, u32[]{:S(2)}, u32[]{:S(2)}) collective-permute-start(f32[16,1664]{1,0:T(8,128)S(1)} %get-tuple-element.83), channel_id=1, source_target_pairs={{0,12},{1,13},{2,14},{3,15},{4,8},{5,9},{6,10},{7,11},{8,4},{9,5},... | collective-permute-start | bytes 319496 | tf_op jit(solution)/shard_map/ppermute | solution.py:22
  67.6 18.7 %collective-permute-start.20 = (bf16[6,256,128]{2,1,0:T(8,128)(2,1)S(1)}, bf16[6,256,128]{2,1,0:T(8,128)(2,1)S(1)}, u32[]{:S(2)}, u32[]{:S(2)}) collective-permute-start(bf16[6,256,128]{2,1,0:T(8,128)(2,1)S(1)} %copy-done.13), channel_id=1, source_target_pairs={{2,4},{4,2},{6,8},{8,6},{10,12},{12,10},{3,5},{5,3},{7,9},{9,7},{1... | collective-permute-start | bytes 1179656 | tf_op jit(solution)/shard_map/ppermute | solution.py:41
  76.9 11.5 %collective-permute-start.18 = (f32[8,1664]{1,0:T(8,128)S(1)}, f32[8,1664]{1,0:T(8,128)S(1)}, u32[]{:S(2)}, u32[]{:S(2)}) collective-permute-start(f32[8,1664]{1,0:T(8,128)S(1)} %pad_maximum_fusion.5), channel_id=1, source_target_pairs={{0,2},{1,3},{2,0},{3,1},{4,6},{5,7},{6,4},{7,5},{8,10},{9,11},{10,... | collective-permute-start | bytes 159752 | tf_op jit(solution)/shard_map/ppermute | solution.py:22

commit v12 on v11

--- a/solution.py
+++ b/solution.py
@@ -13,6 +13,7 @@
 BF16 = jnp.bfloat16
 SMEM = pltpu.MemorySpace.SMEM
 COMBINE_STEPS = (3, 2, 1)
+HEAD_STEPS = (3, 2, 1)
 LANES = 128
 HOLD = 20_000_000_000
 
@@ -108,8 +109,21 @@
     pos_ref, filt_ref, warm_ref, q_ref, g_ref, own_ref, par_ref, dir_ref, dia_ref, anc_ref, *rest,
     gx_count, head0, width,
 ):
-    (dq_ref, own_out, dir_out, dia_out, par_out, anc_out, temp_out, pair_ref) = rest[-8:]
-    head = pl.program_id(0)
+    for i in range(q_ref.shape[1] // width):
+        one_head(
+            pos_ref, filt_ref, warm_ref, q_ref, g_ref, own_ref, par_ref, dir_ref, dia_ref, anc_ref, *rest,
+            gx_count=gx_count, head0=head0, width=width, i=i,
+        )
+
+
+def one_head(
+    pos_ref, filt_ref, warm_ref, q_ref, g_ref, own_ref, par_ref, dir_ref, dia_ref, anc_ref, *rest,
+    gx_count, head0, width, i,
+):
+    (dq_ref, own_out, dir_out, dia_out, par_out, anc_out, temp_out, pairs_ref) = rest[-8:]
+    lanes = slice(i * width, (i + 1) * width)
+    pair_ref = pairs_ref.at[i]
+    head = pl.program_id(0) * (q_ref.shape[1] // width) + i
     gx = pos_ref[0]
     odd = lax.rem(gx, 2)
     queries = q_ref.shape[0]
@@ -120,14 +134,14 @@
 
     row = 0
     for ref in (own_ref, par_ref, dir_ref, dia_ref, anc_ref):
-        block = ref[...] if len(ref.shape) == 2 else ref[...].reshape(2 * ref.shape[0], width)
+        block = ref[:, :, lanes].reshape(2 * ref.shape[0], width)
         pair_ref[row : row + block.shape[0], :] = block.astype(F32)
         row += block.shape[0]
     k = pair_ref[pl.ds(0, keys, stride=2), :].astype(BF16)
     v = pair_ref[pl.ds(1, keys, stride=2), :].astype(BF16)
 
-    q = q_ref[...]
-    g = g_ref[...]
+    q = q_ref[:, lanes]
+    g = g_ref[:, lanes]
     nt = (((1,), (1,)), ((), ()))
     s = lax.dot_general(k, q, nt, preferred_element_type=F32)
     dp = lax.dot_general(v, g, nt, preferred_element_type=F32)
@@ -158,20 +172,20 @@
     pb = p.astype(BF16)
     delta = jnp.sum(pb.astype(F32) * dp, axis=0, keepdims=True)
     ds = p * (dp - delta)
-    temp_out[0] = jnp.sum(ds * s, axis=0, keepdims=True)
+    temp_out[i] = jnp.sum(ds * s, axis=0, keepdims=True)
     dsb = (ds * mult).astype(BF16)
     nn = (((1,), (0,)), ((), ()))
     dv = lax.dot_general(pb, g, nn, preferred_element_type=F32)
     dk = lax.dot_general(dsb, q, nn, preferred_element_type=F32)
     dq = lax.dot_general(dsb, k, (((0,), (0,)), ((), ())), preferred_element_type=F32)
-    dq_ref[...] = dq.astype(BF16)
+    dq_ref[:, lanes] = dq.astype(BF16)
     pair_ref[pl.ds(0, keys, stride=2), :] = dk
     pair_ref[pl.ds(1, keys, stride=2), :] = dv
-    own_out[...] = pair_ref[: 2 * own_rows, :]
-    for i, ref in enumerate((par_out, dir_out, dia_out)):
-        at = 2 * (own_rows + i * BLOCK)
-        ref[...] = pair_ref[at : at + 2 * BLOCK, :].astype(BF16)
-    anc_out[...] = pair_ref[2 * near :, :]
+    own_out[i] = pair_ref[: 2 * own_rows, :]
+    for b, ref in enumerate((par_out, dir_out, dia_out)):
+        at = 2 * (own_rows + b * BLOCK)
+        ref[i] = pair_ref[at : at + 2 * BLOCK, :].astype(BF16)
+    anc_out[:, lanes] = pair_ref[2 * near :, :]
 
 
 def attention(pos, filt, warm, q, g, mesh_kv, partner, halo, anchors, head0, heads, dq_prev, anc_prev):
@@ -180,11 +194,13 @@
     width = feat // warm.shape[0]
     a_rows = anchors.shape[0]
     keys = own_rows + 3 * BLOCK + a_rows
+    step = next(n for n in HEAD_STEPS if heads % n == 0 and head0 % n == 0)
+    first, wide = head0 // step, step * width
     smem = pl.BlockSpec(memory_space=SMEM)
-    full = lambda n: pl.BlockSpec((n, 2, width), lambda h: (0, 0, head0 + h))
-    part = pl.BlockSpec((BLOCK, 2, width), lambda h: (0, 0, h))
-    back = pl.BlockSpec((None, 2 * BLOCK, width), lambda h: (h, 0, 0))
-    cols = pl.BlockSpec((rows, width), lambda h: (0, head0 + h))
+    full = lambda n: pl.BlockSpec((n, 2, wide), lambda h: (0, 0, first + h))
+    part = pl.BlockSpec((BLOCK, 2, wide), lambda h: (0, 0, h))
+    back = pl.BlockSpec((step, 2 * BLOCK, width), lambda h: (h, 0, 0))
+    cols = pl.BlockSpec((rows, wide), lambda h: (0, first + h))
     in_specs = [smem, smem, smem, cols, cols, full(own_rows), full(BLOCK), part, part]
     in_specs += [full(a_rows)]
     args = [pos, filt, warm, q, g, mesh_kv, partner, *halo, anchors]
@@ -196,16 +212,16 @@
     face = jax.ShapeDtypeStruct((heads, 2 * BLOCK, width), BF16)
     return pl.pallas_call(
         functools.partial(attention_kernel, gx_count=lax.axis_size("gx"), head0=head0, width=width),
-        grid=(heads,),
+        grid=(heads // step,),
         in_specs=in_specs,
         out_specs=[
             cols,
-            pl.BlockSpec((None, 2 * own_rows, width), lambda h: (h, 0, 0)),
+            pl.BlockSpec((step, 2 * own_rows, width), lambda h: (h, 0, 0)),
             back,
             back,
             back,
-            pl.BlockSpec((2 * a_rows, width), lambda h: (0, head0 + h)),
-            pl.BlockSpec((1, 1, rows), lambda h: (h, 0, 0)),
+            pl.BlockSpec((2 * a_rows, wide), lambda h: (0, first + h)),
+            pl.BlockSpec((step, 1, rows), lambda h: (h, 0, 0)),
         ],
         out_shape=[
             jax.ShapeDtypeStruct(q.shape, BF16),
@@ -216,7 +232,7 @@
             jax.ShapeDtypeStruct((2 * a_rows, feat), F32),
             jax.ShapeDtypeStruct((heads, 1, rows), F32),
         ],
-        scratch_shapes=[pltpu.VMEM((2 * keys, width), F32)],
+        scratch_shapes=[pltpu.VMEM((step, 2 * keys, width), F32)],
         input_output_aliases=alias,
         compiler_params=pltpu.CompilerParams(vmem_limit_bytes=24 << 20),
         cost_estimate=pl.CostEstimate(

time: 89.9 us -> 88 us (0.979)
  the two profiles are of different devices: /device:TPU:16 before, /device:TPU:20 now
where the time goes in v12:
time: 88 us; the launch traced here: 87.7 us
  starting transfers between devices  28.3 us (32%)
  waiting for transfers between devices  26.2 us (30%)
  Pallas kernels  23.5 us (27%)
  local copies, waits for them, and re-layouts  4.96 us (6%)
  other arithmetic  3.62 us (4%)
  between operations  1.04 us (1%)
    ppermute x8, starting transfers between devices, swap_pairs(): return lax.ppermute(x, 'gx', route)  17.2 us
    pallas_call x2, Pallas kernels, attention(): pl.pallas_call(functools.partial(attention_kernel, gx_count=lax.axis_size...  17.1 us
    ppermute x13, waiting for transfers between devices, swap_mask(): return lax.ppermute(x, ('gx', 'gy'), [(i, i ^ mask) for i in range(count)])  14.9 us
    ppermute x8, waiting for transfers between devices, swap_pairs(): return lax.ppermute(x, 'gx', route)  11.3 us
    ppermute x13, starting transfers between devices, swap_mask(): return lax.ppermute(x, ('gx', 'gy'), [(i, i ^ mask) for i in range(count)])  11.2 us
    pallas_call x2, Pallas kernels, combine(): pl.pallas_call(combine_kernel, grid=(heads // step,), in_specs=in_specs,...  4.34 us
    unnamed x40, local copies, waits for them, and re-layouts  4.12 us
  transfers between devices with their start and end apart: 21, of which 6 were waited for; matrix products, arithmetic and copies ran while one was open for 5% of the time, Pallas kernels for 26%

profile of v12, /device:TPU:20, one launch (start us, length us, event | category | flops | bytes accessed | tf_op | source)
XLA Modules:
  0.0 87.7 jit_solution(2171205172334696223)
XLA Ops:
  0.6 1.6 %collective-permute-start.1 = (bf16[4,2,1536]{2,1,0:T(2,128)(2,1)}, bf16[4,2,1536]{2,1,0:T(2,128)(2,1)S(1)}, u32[]{:S(2)}, u32[]{:S(2)}) collective-permute-start(bf16[4,2,1536]{2,1,0:T(2,128)(2,1)} %param.11), channel_id=1, source_target_pairs={{0,2},{1,3},{2,0},{3,1},{4,6},{5,7},{6,4},{7,5},{8,10},{9,11},{10,... | collective-permute-start | bytes 73736 | tf_op jit(solution)/shard_map/ppermute | solution.py:23
  2.2 1.4 %copy-done = bf16[256,2,1536]{2,1,0:T(2,128)(2,1)S(1)} copy-done((bf16[256,2,1536]{2,1,0:T(2,128)(2,1)S(1)}, bf16[256,2,1536]{2,1,0:T(2,128)(2,1)}, u32[]{:S(2)}) %copy-start) | copy-done | bytes 1572888
  3.6 0.7 copy-done.4
  4.3 0.7 pick.3
  4.9 0.6 collective-permute-start.8
  5.5 3.3 %collective-permute-start.9 = (bf16[128,2,768]{2,1,0:T(2,128)(2,1)S(1)}, bf16[128,2,768]{2,1,0:T(2,128)(2,1)S(1)}, u32[]{:S(2)}, u32[]{:S(2)}) collective-permute-start(bf16[128,2,768]{2,1,0:T(2,128)(2,1)S(1)} %get-tuple-element.63), channel_id=1, source_target_pairs={{2,4},{4,2},{6,8},{8,6},{10,12},{12,10},{3,5},{5,3},{7,9},{9,7},{1... | collective-permute-start | bytes 1179656 | tf_op jit(solution)/shard_map/ppermute | solution.py:42
  8.8 0.7 pick.2
  9.5 0.6 compare_reduce_fusion
  10.3 1.6 %collective-permute-start.4 = (bf16[8,2,1536]{2,1,0:T(2,128)(2,1)S(1)}, bf16[8,2,1536]{2,1,0:T(2,128)(2,1)S(1)}, u32[]{:S(2)}, u32[]{:S(2)}) collective-permute-start(bf16[8,2,1536]{2,1,0:T(2,128)(2,1)S(1)} %pad_maximum_fusion.6), channel_id=1, source_target_pairs={{0,4},{1,5},{2,6},{3,7},{4,0},{5,1},{6,2},{7,3},{8,12},{9,13},{10,... | collective-permute-start | bytes 147464 | tf_op jit(solution)/shard_map/ppermute | solution.py:23
  11.9 0.3 collective-permute-start.5
  12.2 1.6 %collective-permute-start.6 = (bf16[8,2,1536]{2,1,0:T(2,128)(2,1)S(1)}, bf16[8,2,1536]{2,1,0:T(2,128)(2,1)S(1)}, u32[]{:S(2)}, u32[]{:S(2)}) collective-permute-start(bf16[8,2,1536]{2,1,0:T(2,128)(2,1)S(1)} %pad_maximum_fusion.6), channel_id=1, source_target_pairs={{0,12},{1,13},{2,14},{3,15},{4,8},{5,9},{6,10},{7,11},{8,4},{9,5},... | collective-permute-start | bytes 147464 | tf_op jit(solution)/shard_map/ppermute | solution.py:23
  13.8 6.9 %collective-permute-done.4 = bf16[8,2,1536]{2,1,0:T(2,128)(2,1)S(1)} collective-permute-done((bf16[8,2,1536]{2,1,0:T(2,128)(2,1)S(1)}, bf16[8,2,1536]{2,1,0:T(2,128)(2,1)S(1)}, u32[]{:S(2)}, u32[]{:S(2)}) %collective-permute-start.4) | collective-permute-done | bytes 49184 | tf_op jit(solution)/shard_map/ppermute | solution.py:23
  20.8 1.0 %collective-permute-start.2 = (bf16[128,2,768]{2,1,0:T(2,128)(2,1)S(1)}, bf16[128,2,768]{2,1,0:T(2,128)(2,1)S(1)}, u32[]{:S(2)}, u32[]{:S(2)}) collective-permute-start(bf16[128,2,768]{2,1,0:T(2,128)(2,1)S(1)} %get-tuple-element.59), channel_id=1, source_target_pairs={{0,2},{2,0},{4,6},{6,4},{8,10},{10,8},{12,14},{14,12},{1,3},{3,1},... | collective-permute-start | bytes 1179656 | tf_op jit(solution)/shard_map/ppermute | solution.py:42
  21.8 0.3 pad_maximum_fusion.1
  22.1 0.1 collective-permute-start.7
  22.4 1.3 %collective-permute-done.7 = bf16[32,2,1536]{2,1,0:T(2,128)(2,1)S(1)} collective-permute-done((bf16[32,2,1536]{2,1,0:T(2,128)(2,1)S(1)}, bf16[32,2,1536]{2,1,0:T(2,128)(2,1)S(1)}, u32[]{:S(2)}, u32[]{:S(2)}) %collective-permute-start.7) | collective-permute-done | bytes 196640 | tf_op jit(solution)/shard_map/ppermute | solution.py:23
  23.6 4.3 %collective-permute-start.3 = (bf16[128,2,768]{2,1,0:T(2,128)(2,1)S(1)}, bf16[128,2,768]{2,1,0:T(2,128)(2,1)S(1)}, u32[]{:S(2)}, u32[]{:S(2)}) collective-permute-start(bf16[128,2,768]{2,1,0:T(2,128)(2,1)S(1)} %get-tuple-element.60), channel_id=1, source_target_pairs={{2,4},{4,2},{6,8},{8,6},{10,12},{12,10},{3,5},{5,3},{7,9},{9,7},{1... | collective-permute-start | bytes 1179656 | tf_op jit(solution)/shard_map/ppermute | solution.py:42
  28.0 0.2 constant_dynamic-update-slice_fusion.anc_ref
  28.2 1.3 %copy-done.1 = bf16[256,2,1536]{2,1,0:T(2,128)(2,1)S(1)} copy-done((bf16[256,2,1536]{2,1,0:T(2,128)(2,1)S(1)}, bf16[256,2,1536]{2,1,0:T(2,128)(2,1)}, u32[]{:S(2)}) %copy-start.1) | copy-done | bytes 1572888
  29.6 0.2 copy-done.2
  29.8 0.2 copy-done.3
  30.0 8.5 %attention.2 = (bf16[256,1536]{1,0:T(8,128)(2,1)}, f32[6,512,128]{2,1,0:T(8,128)S(1)}, bf16[6,256,128]{2,1,0:T(8,128)(2,1)S(1)}, bf16[6,256,128]{2,1,0:T(8,128)(...) custom-call(s32[1]{0:T(128)} %bitcast.pos_ref, ...), custom_call_target="tpu_custom_call" | custom-call | flops 1384120320 | bytes 6488064 | tf_op jit(solution)/shard_map/attention/pallas_call | solution.py:213
  38.5 1.5 %collective-permute-start.10 = (bf16[6,256,128]{2,1,0:T(8,128)(2,1)S(1)}, bf16[6,256,128]{2,1,0:T(8,128)(2,1)S(1)}, u32[]{:S(2)}, u32[]{:S(2)}) collective-permute-start(bf16[6,256,128]{2,1,0:T(8,128)(2,1)S(1)} %get-tuple-element.73), channel_id=1, source_target_pairs={{0,2},{2,0},{4,6},{6,4},{8,10},{10,8},{12,14},{14,12},{1,3},{3,1},... | collective-permute-start | bytes 1179656 | tf_op jit(solution)/shard_map/ppermute | solution.py:42
  40.1 2.2 %collective-permute-start.11 = (bf16[6,256,128]{2,1,0:T(8,128)(2,1)S(1)}, bf16[6,256,128]{2,1,0:T(8,128)(2,1)S(1)}, u32[]{:S(2)}, u32[]{:S(2)}) collective-permute-start(bf16[6,256,128]{2,1,0:T(8,128)(2,1)S(1)} %get-tuple-element.74), channel_id=1, source_target_pairs={{2,4},{4,2},{6,8},{8,6},{10,12},{12,10},{3,5},{5,3},{7,9},{9,7},{1... | collective-permute-start | bytes 1179656 | tf_op jit(solution)/shard_map/ppermute | solution.py:42
  42.3 0.1 collective-permute-start.12
  42.4 8.6 %attention.3 = (bf16[256,1536]{1,0:T(8,128)(2,1)}, f32[6,512,128]{2,1,0:T(8,128)S(1)}, bf16[6,256,128]{2,1,0:T(8,128)(2,1)}, bf16[6,256,128]{2,1,0:T(8,128)(2,1)...) custom-call(s32[1]{0:T(128)} %bitcast.pos_ref, ...), custom_call_target="tpu_custom_call", output_to_operand_aliasing={{0}: (10, {}), {5}: (11, {})} | custom-call | flops 1384120320 | bytes 6488064 | tf_op jit(solution)/shard_map/attention/pallas_call | solution.py:213
  51.0 0.2 maximum_reduce_fusion
  51.2 0.6 fusion
  51.9 5.9 %collective-permute-done.10.dir_ref = bf16[6,256,128]{2,1,0:T(8,128)(2,1)S(1)} collective-permute-done((bf16[6,256,128]{2,1,0:T(8,128)(2,1)S(1)}, bf16[6,256,128]{2,1,0:T(8,128)(2,1)S(1)}, u32[]{:S(2)}, u32[]{:S(2)}) %collective-permute-start.10) | collective-permute-done | bytes 393248 | tf_op jit(solution)/shard_map/ppermute | solution.py:42
  57.9 0.1 collective-permute-start.13
  58.0 0.5 collective-permute-start.14
  58.5 1.6 %collective-permute-start.19 = (bf16[6,256,128]{2,1,0:T(8,128)(2,1)}, bf16[6,256,128]{2,1,0:T(8,128)(2,1)S(1)}, u32[]{:S(2)}, u32[]{:S(2)}) collective-permute-start(bf16[6,256,128]{2,1,0:T(8,128)(2,1)} %get-tuple-element.85), channel_id=1, source_target_pairs={{0,2},{2,0},{4,6},{6,4},{8,10},{10,8},{12,14},{14,12},{1,3},{3,1},... | collective-permute-start | bytes 1179656 | tf_op jit(solution)/shard_map/ppermute | solution.py:42
  60.0 0.7 slice_add_fusion.7
  60.7 0.1 copy-done.16
  60.8 0.1 add.30.refs_0_
  60.9 1.0 %slice_add_fusion = f32[64,1536]{1,0:T(8,128)S(1)} fusion(f32[64,1664]{1,0:T(8,128)} %copy-done.16, f32[128,1536]{1,0:T(8,128)S(1)} %get-tuple-element.76), kind=kLoop, calls=%fused_computation.1 | loop fusion | flops 98304 | bytes 1179648 | tf_op jit(solution)/shard_map/add | solution.py:378
  62.1 1.2 %collective-permute-start.15 = (f32[16,1664]{1,0:T(8,128)S(1)}, f32[16,1664]{1,0:T(8,128)S(1)}, u32[]{:S(2)}, u32[]{:S(2)}) collective-permute-start(f32[16,1664]{1,0:T(8,128)S(1)} %get-tuple-element.81), channel_id=1, source_target_pairs={{0,4},{1,5},{2,6},{3,7},{4,0},{5,1},{6,2},{7,3},{8,12},{9,13},{10,... | collective-permute-start | bytes 319496 | tf_op jit(solution)/shard_map/ppermute | solution.py:23
  63.3 0.4 collective-permute-start.16
  63.7 1.9 %collective-permute-start.17 = (f32[16,1664]{1,0:T(8,128)S(1)}, f32[16,1664]{1,0:T(8,128)S(1)}, u32[]{:S(2)}, u32[]{:S(2)}) collective-permute-start(f32[16,1664]{1,0:T(8,128)S(1)} %get-tuple-element.83), channel_id=1, source_target_pairs={{0,12},{1,13},{2,14},{3,15},{4,8},{5,9},{6,10},{7,11},{8,4},{9,5},... | collective-permute-start | bytes 319496 | tf_op jit(solution)/shard_map/ppermute | solution.py:23
  65.6 2.6 %collective-permute-start.20 = (bf16[6,256,128]{2,1,0:T(8,128)(2,1)S(1)}, bf16[6,256,128]{2,1,0:T(8,128)(2,1)S(1)}, u32[]{:S(2)}, u32[]{:S(2)}) collective-permute-start(bf16[6,256,128]{2,1,0:T(8,128)(2,1)S(1)} %copy-done.13), channel_id=1, source_target_pairs={{2,4},{4,2},{6,8},{8,6},{10,12},{12,10},{3,5},{5,3},{7,9},{9,7},{1... | collective-permute-start | bytes 1179656 | tf_op jit(solution)/shard_map/ppermute | solution.py:42
  68.3 3.0 %collective-permute-done.16 = f32[16,1664]{1,0:T(8,128)S(1)} collective-permute-done((f32[16,1664]{1,0:T(8,128)S(1)}, f32[16,1664]{1,0:T(8,128)S(1)}, u32[]{:S(2)}, u32[]{:S(2)}) %collective-permute-start.16) | collective-permute-done | bytes 106528 | tf_op jit(solution)/shard_map/ppermute | solution.py:23
  71.3 3.6 %collective-permute-done.17 = f32[16,1664]{1,0:T(8,128)S(1)} collective-permute-done((f32[16,1664]{1,0:T(8,128)S(1)}, f32[16,1664]{1,0:T(8,128)S(1)}, u32[]{:S(2)}, u32[]{:S(2)}) %collective-permute-start.17) | collective-permute-done | bytes 106528 | tf_op jit(solution)/shard_map/ppermute | solution.py:23
  75.0 1.8 %collective-permute-start.18 = (f32[8,1664]{1,0:T(8,128)S(1)}, f32[8,1664]{1,0:T(8,128)S(1)}, u32[]{:S(2)}, u32[]{:S(2)}) collective-permute-start(f32[8,1664]{1,0:T(8,128)S(1)} %pad_maximum_fusion.5), channel_id=1, source_target_pairs={{0,2},{1,3},{2,0},{3,1},{4,6},{5,7},{6,4},{7,5},{8,10},{9,11},{10,... | collective-permute-start | bytes 159752 | tf_op jit(solution)/shard_map/ppermute | solution.py:23
  76.8 2.2 %combine.2.rest_0_ = bf16[256,2,1536]{2,1,0:T(2,128)(2,1)} custom-call(s32[1]{0:T(128)} %bitcast.pos_ref, s32[3]{0:T(128)S(1)} %bitcast.15, f32[6,512,128]{2,1,0:T(8,128)S(1)} %copy-done.15, bf16[6,256,128]{2,1,0:T(8,128)(2,1)S(1)} %collective-permute-done.10.dir_ref, bf16[6,256,128]{2,1,0:T(8,128)(2,1)S(1)} %copy-done.9, bf16[6,256,128]{2,1,0:T(8,128)(2,1)S(1)} %copy-done.11), custom_call_target="tpu_custom_call" | custom-call | flops 12582912000 | bytes 3538944 | tf_op jit(solution)/shard_map/combine/pallas_call | solution.py:281
  79.0 5.4 %collective-permute-done.20.dia_ref = bf16[6,256,128]{2,1,0:T(8,128)(2,1)S(1)} collective-permute-done((bf16[6,256,128]{2,1,0:T(8,128)(2,1)S(1)}, bf16[6,256,128]{2,1,0:T(8,128)(2,1)S(1)}, u32[]{:S(2)}, u32[]{:S(2)}) %collective-permute-start.20) | collective-permute-done | bytes 393248 | tf_op jit(solution)/shard_map/ppermute | solution.py:42
  84.4 2.2 %combine.3 = bf16[256,2,1536]{2,1,0:T(2,128)(2,1)} custom-call(s32[1]{0:T(128)} %bitcast.pos_ref, s32[3]{0:T(128)S(1)} %bitcast.16, f32[6,512,128]{2,1,0:T(8,128)S(1)} %get-tuple-element.84.own_ref, bf16[6,256,128]{2,1,0:T(8,128)(2,1)S(1)} %collective-permute-done.19.dir_ref, ...), custom_call_target="tpu_custom_call", output_to_operand_aliasing={{}: (6, {})} | custom-call | bytes 3538944 | tf_op jit(solution)/shard_map/combine/pallas_call | solution.py:281
  86.5 0.6 finish.1
  87.1 0.5 slice_bitcast_fusion
  (66 shorter events, 0.6 us)
Async XLA Ops:
  0.6 9.6 %collective-permute-start.1 = (bf16[4,2,1536]{2,1,0:T(2,128)(2,1)}, bf16[4,2,1536]{2,1,0:T(2,128)(2,1)S(1)}, u32[]{:S(2)}, u32[]{:S(2)}) collective-permute-start(bf16[4,2,1536]{2,1,0:T(2,128)(2,1)} %param.11), channel_id=1, source_target_pairs={{0,2},{1,3},{2,0},{3,1},{4,6},{5,7},{6,4},{7,5},{8,10},{9,11},{10,... | collective-permute-start | bytes 73736 | tf_op jit(solution)/shard_map/ppermute | solution.py:23
  2.2 1.4 %copy-start = (bf16[256,2,1536]{2,1,0:T(2,128)(2,1)S(1)}, bf16[256,2,1536]{2,1,0:T(2,128)(2,1)}, u32[]{:S(2)}) copy-start(bf16[256,2,1536]{2,1,0:T(2,128)(2,1)} %own_ref.3) | copy-start | bytes 4718596
  3.6 0.7 copy-start.4
  4.3 5.9 %copy-start.17 = (bf16[4,2,1536]{2,1,0:T(2,128)(2,1)S(1)}, bf16[4,2,1536]{2,1,0:T(2,128)(2,1)}, u32[]{:S(2)}) copy-start(bf16[4,2,1536]{2,1,0:T(2,128)(2,1)} %param.11) | copy-start | bytes 73732
  4.9 23.3 %collective-permute-start.8 = (bf16[128,2,768]{2,1,0:T(2,128)(2,1)S(1)}, bf16[128,2,768]{2,1,0:T(2,128)(2,1)S(1)}, u32[]{:S(2)}, u32[]{:S(2)}) collective-permute-start(bf16[128,2,768]{2,1,0:T(2,128)(2,1)S(1)} %get-tuple-element.62), channel_id=1, source_target_pairs={{0,2},{2,0},{4,6},{6,4},{8,10},{10,8},{12,14},{14,12},{1,3},{3,1},... | collective-permute-start | bytes 1179656 | tf_op jit(solution)/shard_map/ppermute | solution.py:42
  5.5 22.7 %collective-permute-start.9 = (bf16[128,2,768]{2,1,0:T(2,128)(2,1)S(1)}, bf16[128,2,768]{2,1,0:T(2,128)(2,1)S(1)}, u32[]{:S(2)}, u32[]{:S(2)}) collective-permute-start(bf16[128,2,768]{2,1,0:T(2,128)(2,1)S(1)} %get-tuple-element.63), channel_id=1, source_target_pairs={{2,4},{4,2},{6,8},{8,6},{10,12},{12,10},{3,5},{5,3},{7,9},{9,7},{1... | collective-permute-start | bytes 1179656 | tf_op jit(solution)/shard_map/ppermute | solution.py:42
  10.3 10.5 %collective-permute-start.4 = (bf16[8,2,1536]{2,1,0:T(2,128)(2,1)S(1)}, bf16[8,2,1536]{2,1,0:T(2,128)(2,1)S(1)}, u32[]{:S(2)}, u32[]{:S(2)}) collective-permute-start(bf16[8,2,1536]{2,1,0:T(2,128)(2,1)S(1)} %pad_maximum_fusion.6), channel_id=1, source_target_pairs={{0,4},{1,5},{2,6},{3,7},{4,0},{5,1},{6,2},{7,3},{8,12},{9,13},{10,... | collective-permute-start | bytes 147464 | tf_op jit(solution)/shard_map/ppermute | solution.py:23
  11.9 8.9 %collective-permute-start.5 = (bf16[8,2,1536]{2,1,0:T(2,128)(2,1)S(1)}, bf16[8,2,1536]{2,1,0:T(2,128)(2,1)S(1)}, u32[]{:S(2)}, u32[]{:S(2)}) collective-permute-start(bf16[8,2,1536]{2,1,0:T(2,128)(2,1)S(1)} %pad_maximum_fusion.6), channel_id=1, source_target_pairs={{0,8},{1,9},{2,10},{3,11},{4,12},{5,13},{6,14},{7,15},{8,0},{9,1},... | collective-permute-start | bytes 147464 | tf_op jit(solution)/shard_map/ppermute | solution.py:23
  12.2 9.6 %collective-permute-start.6 = (bf16[8,2,1536]{2,1,0:T(2,128)(2,1)S(1)}, bf16[8,2,1536]{2,1,0:T(2,128)(2,1)S(1)}, u32[]{:S(2)}, u32[]{:S(2)}) collective-permute-start(bf16[8,2,1536]{2,1,0:T(2,128)(2,1)S(1)} %pad_maximum_fusion.6), channel_id=1, source_target_pairs={{0,12},{1,13},{2,14},{3,15},{4,8},{5,9},{6,10},{7,11},{8,4},{9,5},... | collective-permute-start | bytes 147464 | tf_op jit(solution)/shard_map/ppermute | solution.py:23
  20.8 7.5 %collective-permute-start = (bf16[128,2,1536]{2,1,0:T(2,128)(2,1)S(1)}, bf16[128,2,1536]{2,1,0:T(2,128)(2,1)S(1)}, u32[]{:S(2)}, u32[]{:S(2)}) collective-permute-start(bf16[128,2,1536]{2,1,0:T(2,128)(2,1)S(1)} %get-tuple-element.56), channel_id=1, source_target_pairs={{0,1},{1,0},{2,3},{3,2},{4,5},{5,4},{6,7},{7,6},{8,9},{9,8},{10,11... | collective-permute-start | bytes 2359304 | tf_op jit(solution)/shard_map/ppermute | solution.py:23
  20.8 21.6 %collective-permute-start.2 = (bf16[128,2,768]{2,1,0:T(2,128)(2,1)S(1)}, bf16[128,2,768]{2,1,0:T(2,128)(2,1)S(1)}, u32[]{:S(2)}, u32[]{:S(2)}) collective-permute-start(bf16[128,2,768]{2,1,0:T(2,128)(2,1)S(1)} %get-tuple-element.59), channel_id=1, source_target_pairs={{0,2},{2,0},{4,6},{6,4},{8,10},{10,8},{12,14},{14,12},{1,3},{3,1},... | collective-permute-start | bytes 1179656 | tf_op jit(solution)/shard_map/ppermute | solution.py:42
  22.1 1.5 %collective-permute-start.7 = (bf16[32,2,1536]{2,1,0:T(2,128)(2,1)S(1)}, bf16[32,2,1536]{2,1,0:T(2,128)(2,1)S(1)}, u32[]{:S(2)}, u32[]{:S(2)}) collective-permute-start(bf16[32,2,1536]{2,1,0:T(2,128)(2,1)S(1)} %pad_maximum_fusion.1), channel_id=1, source_target_pairs={{0,1},{1,0},{2,3},{3,2},{4,5},{5,4},{6,7},{7,6},{8,9},{9,8},{10,11... | collective-permute-start | bytes 589832 | tf_op jit(solution)/shard_map/ppermute | solution.py:23
  23.6 18.7 %collective-permute-start.3 = (bf16[128,2,768]{2,1,0:T(2,128)(2,1)S(1)}, bf16[128,2,768]{2,1,0:T(2,128)(2,1)S(1)}, u32[]{:S(2)}, u32[]{:S(2)}) collective-permute-start(bf16[128,2,768]{2,1,0:T(2,128)(2,1)S(1)} %get-tuple-element.60), channel_id=1, source_target_pairs={{2,4},{4,2},{6,8},{8,6},{10,12},{12,10},{3,5},{5,3},{7,9},{9,7},{1... | collective-permute-start | bytes 1179656 | tf_op jit(solution)/shard_map/ppermute | solution.py:42
  28.1 1.4 %copy-start.1 = (bf16[256,2,1536]{2,1,0:T(2,128)(2,1)S(1)}, bf16[256,2,1536]{2,1,0:T(2,128)(2,1)}, u32[]{:S(2)}) copy-start(bf16[256,2,1536]{2,1,0:T(2,128)(2,1)} %own_ref.3) | copy-start | bytes 4718596
  28.2 1.6 %copy-start.2 = (bf16[256,1536]{1,0:T(8,128)(2,1)S(1)}, bf16[256,1536]{1,0:T(8,128)(2,1)}, u32[]{:S(2)}) copy-start(bf16[256,1536]{1,0:T(8,128)(2,1)} %q_ref.3) | copy-start | bytes 2359300
  28.2 1.8 %copy-start.3 = (bf16[256,1536]{1,0:T(8,128)(2,1)S(1)}, bf16[256,1536]{1,0:T(8,128)(2,1)}, u32[]{:S(2)}) copy-start(bf16[256,1536]{1,0:T(8,128)(2,1)} %g_ref.3) | copy-start | bytes 2359300
  28.2 1.8 %copy-start.6 = (s32[1,2,5]{2,1,0:T(2,128)S(1)}, s32[1,2,5]{2,1,0:T(2,128)}, u32[]{:S(2)}) copy-start(s32[1,2,5]{2,1,0:T(2,128)} %param.15) | copy-start | bytes 124
  28.2 1.8 %copy-start.7 = (f32[12]{0:T(128)S(1)}, f32[12]{0:T(128)}, u32[]{:S(2)}) copy-start(f32[12]{0:T(128)} %warm_ref.3) | copy-start | bytes 148
  38.5 12.5 %copy-start.14 = (f32[6,512,128]{2,1,0:T(8,128)}, f32[6,512,128]{2,1,0:T(8,128)S(1)}, u32[]{:S(2)}) copy-start(f32[6,512,128]{2,1,0:T(8,128)S(1)} %get-tuple-element.88.own_ref) | copy-start | bytes 4718596
  38.5 19.3 %collective-permute-start.10 = (bf16[6,256,128]{2,1,0:T(8,128)(2,1)S(1)}, bf16[6,256,128]{2,1,0:T(8,128)(2,1)S(1)}, u32[]{:S(2)}, u32[]{:S(2)}) collective-permute-start(bf16[6,256,128]{2,1,0:T(8,128)(2,1)S(1)} %get-tuple-element.73), channel_id=1, source_target_pairs={{0,2},{2,0},{4,6},{6,4},{8,10},{10,8},{12,14},{14,12},{1,3},{3,1},... | collective-permute-start | bytes 1179656 | tf_op jit(solution)/shard_map/ppermute | solution.py:42
  40.1 17.8 %collective-permute-start.11 = (bf16[6,256,128]{2,1,0:T(8,128)(2,1)S(1)}, bf16[6,256,128]{2,1,0:T(8,128)(2,1)S(1)}, u32[]{:S(2)}, u32[]{:S(2)}) collective-permute-start(bf16[6,256,128]{2,1,0:T(8,128)(2,1)S(1)} %get-tuple-element.74), channel_id=1, source_target_pairs={{2,4},{4,2},{6,8},{8,6},{10,12},{12,10},{3,5},{5,3},{7,9},{9,7},{1... | collective-permute-start | bytes 1179656 | tf_op jit(solution)/shard_map/ppermute | solution.py:42
  42.3 15.5 %collective-permute-start.12 = (bf16[6,256,128]{2,1,0:T(8,128)(2,1)S(1)}, bf16[6,256,128]{2,1,0:T(8,128)(2,1)S(1)}, u32[]{:S(2)}, u32[]{:S(2)}) collective-permute-start(bf16[6,256,128]{2,1,0:T(8,128)(2,1)S(1)} %get-tuple-element.75), channel_id=1, source_target_pairs={{0,1},{1,0},{2,3},{3,2},{4,5},{5,4},{6,7},{7,6},{8,9},{9,8},{10,11... | collective-permute-start | bytes 1179656 | tf_op jit(solution)/shard_map/ppermute | solution.py:23
  51.0 9.7 %copy-start.12 = (bf16[6,256,128]{2,1,0:T(8,128)(2,1)}, bf16[6,256,128]{2,1,0:T(8,128)(2,1)S(1)}, u32[]{:S(2)}) copy-start(bf16[6,256,128]{2,1,0:T(8,128)(2,1)S(1)} %get-tuple-element.86) | copy-start | bytes 1179652
  57.8 2.9 %copy-start.8 = (bf16[6,256,128]{2,1,0:T(8,128)(2,1)}, bf16[6,256,128]{2,1,0:T(8,128)(2,1)S(1)}, u32[]{:S(2)}) copy-start(bf16[6,256,128]{2,1,0:T(8,128)(2,1)S(1)} %collective-permute-done.11.dia_ref) | copy-start | bytes 1179652
  57.8 2.9 %copy-start.10 = (bf16[6,256,128]{2,1,0:T(8,128)(2,1)}, bf16[6,256,128]{2,1,0:T(8,128)(2,1)S(1)}, u32[]{:S(2)}) copy-start(bf16[6,256,128]{2,1,0:T(8,128)(2,1)S(1)} %collective-permute-done.12.par_ref) | copy-start | bytes 1179652
  57.9 2.1 %collective-permute-start.13 = (f32[64,1664]{1,0:T(8,128)S(1)}, f32[64,1664]{1,0:T(8,128)S(1)}, u32[]{:S(2)}, u32[]{:S(2)}) collective-permute-start(f32[64,1664]{1,0:T(8,128)S(1)} %pad_maximum_fusion), channel_id=1, source_target_pairs={{0,1},{1,0},{2,3},{3,2},{4,5},{5,4},{6,7},{7,6},{8,9},{9,8},{10,11... | collective-permute-start | bytes 1277960 | tf_op jit(solution)/shard_map/ppermute | solution.py:23
  58.0 4.0 %collective-permute-start.14 = (bf16[6,256,128]{2,1,0:T(8,128)(2,1)}, bf16[6,256,128]{2,1,0:T(8,128)(2,1)S(1)}, u32[]{:S(2)}, u32[]{:S(2)}) collective-permute-start(bf16[6,256,128]{2,1,0:T(8,128)(2,1)} %get-tuple-element.80), channel_id=1, source_target_pairs={{0,1},{1,0},{2,3},{3,2},{4,5},{5,4},{6,7},{7,6},{8,9},{9,8},{10,11... | collective-permute-start | bytes 1179656 | tf_op jit(solution)/shard_map/ppermute | solution.py:23
  58.5 20.5 %collective-permute-start.19 = (bf16[6,256,128]{2,1,0:T(8,128)(2,1)}, bf16[6,256,128]{2,1,0:T(8,128)(2,1)S(1)}, u32[]{:S(2)}, u32[]{:S(2)}) collective-permute-start(bf16[6,256,128]{2,1,0:T(8,128)(2,1)} %get-tuple-element.85), channel_id=1, source_target_pairs={{0,2},{2,0},{4,6},{6,4},{8,10},{10,8},{12,14},{14,12},{1,3},{3,1},... | collective-permute-start | bytes 1179656 | tf_op jit(solution)/shard_map/ppermute | solution.py:42
  60.0 0.8 copy-start.16
  62.0 3.6 %copy-start.13 = (bf16[6,256,128]{2,1,0:T(8,128)(2,1)S(1)}, bf16[6,256,128]{2,1,0:T(8,128)(2,1)}, u32[]{:S(2)}) copy-start(bf16[6,256,128]{2,1,0:T(8,128)(2,1)} %copy-done.12) | copy-start | bytes 1179652
  62.0 14.7 %copy-start.5 = (s32[1,3,1]{1,2,0:T(1,128)S(1)}, s32[1,3,1]{1,2,0:T(1,128)}, u32[]{:S(2)}) copy-start(s32[1,3,1]{1,2,0:T(1,128)} %param.14) | copy-start | bytes 40
  62.1 14.7 %copy-start.9 = (bf16[6,256,128]{2,1,0:T(8,128)(2,1)S(1)}, bf16[6,256,128]{2,1,0:T(8,128)(2,1)}, u32[]{:S(2)}) copy-start(bf16[6,256,128]{2,1,0:T(8,128)(2,1)} %copy-done.8) | copy-start | bytes 1179652
  62.1 14.7 %copy-start.11 = (bf16[6,256,128]{2,1,0:T(8,128)(2,1)S(1)}, bf16[6,256,128]{2,1,0:T(8,128)(2,1)}, u32[]{:S(2)}) copy-start(bf16[6,256,128]{2,1,0:T(8,128)(2,1)} %copy-done.10) | copy-start | bytes 1179652
  62.1 14.7 %copy-start.15 = (f32[6,512,128]{2,1,0:T(8,128)S(1)}, f32[6,512,128]{2,1,0:T(8,128)}, u32[]{:S(2)}) copy-start(f32[6,512,128]{2,1,0:T(8,128)} %copy-done.14) | copy-start | bytes 4718596
  62.1 6.2 %collective-permute-start.15 = (f32[16,1664]{1,0:T(8,128)S(1)}, f32[16,1664]{1,0:T(8,128)S(1)}, u32[]{:S(2)}, u32[]{:S(2)}) collective-permute-start(f32[16,1664]{1,0:T(8,128)S(1)} %get-tuple-element.81), channel_id=1, source_target_pairs={{0,4},{1,5},{2,6},{3,7},{4,0},{5,1},{6,2},{7,3},{8,12},{9,13},{10,... | collective-permute-start | bytes 319496 | tf_op jit(solution)/shard_map/ppermute | solution.py:23
  63.3 7.9 %collective-permute-start.16 = (f32[16,1664]{1,0:T(8,128)S(1)}, f32[16,1664]{1,0:T(8,128)S(1)}, u32[]{:S(2)}, u32[]{:S(2)}) collective-permute-start(f32[16,1664]{1,0:T(8,128)S(1)} %get-tuple-element.82), channel_id=1, source_target_pairs={{0,8},{1,9},{2,10},{3,11},{4,12},{5,13},{6,14},{7,15},{8,0},{9,1},... | collective-permute-start | bytes 319496 | tf_op jit(solution)/shard_map/ppermute | solution.py:23
  63.7 11.2 %collective-permute-start.17 = (f32[16,1664]{1,0:T(8,128)S(1)}, f32[16,1664]{1,0:T(8,128)S(1)}, u32[]{:S(2)}, u32[]{:S(2)}) collective-permute-start(f32[16,1664]{1,0:T(8,128)S(1)} %get-tuple-element.83), channel_id=1, source_target_pairs={{0,12},{1,13},{2,14},{3,15},{4,8},{5,9},{6,10},{7,11},{8,4},{9,5},... | collective-permute-start | bytes 319496 | tf_op jit(solution)/shard_map/ppermute | solution.py:23
  65.6 18.7 %collective-permute-start.20 = (bf16[6,256,128]{2,1,0:T(8,128)(2,1)S(1)}, bf16[6,256,128]{2,1,0:T(8,128)(2,1)S(1)}, u32[]{:S(2)}, u32[]{:S(2)}) collective-permute-start(bf16[6,256,128]{2,1,0:T(8,128)(2,1)S(1)} %copy-done.13), channel_id=1, source_target_pairs={{2,4},{4,2},{6,8},{8,6},{10,12},{12,10},{3,5},{5,3},{7,9},{9,7},{1... | collective-permute-start | bytes 1179656 | tf_op jit(solution)/shard_map/ppermute | solution.py:42
  75.0 11.5 %collective-permute-start.18 = (f32[8,1664]{1,0:T(8,128)S(1)}, f32[8,1664]{1,0:T(8,128)S(1)}, u32[]{:S(2)}, u32[]{:S(2)}) collective-permute-start(f32[8,1664]{1,0:T(8,128)S(1)} %pad_maximum_fusion.5), channel_id=1, source_target_pairs={{0,2},{1,3},{2,0},{3,1},{4,6},{5,7},{6,4},{7,5},{8,10},{9,11},{10,... | collective-permute-start | bytes 159752 | tf_op jit(solution)/shard_map/ppermute | solution.py:23

commit v13 on v12

--- a/solution.py
+++ b/solution.py
@@ -358,25 +358,31 @@
     anc, faces[-1], returned[-1] = lax.optimization_barrier((anc, faces[-1], returned[-1]))
     direct, diagonal, partner = faces[-1]
     returned.append([swap_pairs(direct, 0), None, swap_mask(partner, 1)])
-    for i, masks in enumerate(reversed(stages)):
-        n = anc.shape[0] // (len(masks) + 1)
-        wide = jnp.broadcast_to(extra, (n, LANES))
-        out = [
-            jnp.concatenate([anc[k * n : (k + 1) * n], wide], axis=1) for k in range(1, len(masks) + 1)
-        ]
+    steps = []
+    for masks in reversed(stages):
+        steps += [(masks[0], True), (masks[1], False)] if len(masks) == 3 else [(masks[0], False)]
+    for i, (mask, inner) in enumerate(steps):
+        n = anc.shape[0] // 2
+        if inner:
+            halves = anc.reshape(2, 2, n // 2, feat)
+            mine, theirs = halves[:, 0].reshape(n, feat), halves[:, 1].reshape(n, feat)
+        else:
+            mine, theirs = anc[:n], anc[n:]
+        out = jnp.concatenate([theirs, jnp.broadcast_to(extra, (n, LANES))], axis=1)
         if i == 1:
             out, diagonal, returned[-1][2] = lax.optimization_barrier((out, diagonal, returned[-1][2]))
             returned[-1][1] = swap_pairs(diagonal, 1)
+        if 0 < i < len(steps) - 1:
             (extra,) = hold([extra], HOLD)
-        got = [swap_mask(x, m) for x, m in zip(out, masks)]
-        if i == len(stages) - 1:
+        got = swap_mask(out, mask)
+        if i == len(steps) - 1:
             cell = combine(pos, sent, owns[-2], returned[-2], *chunks[-2], feat, width, cell, weight=4000)
             cell = combine(pos, sent, owns[-1], returned[-1], *chunks[-1], feat, width, cell, weight=0)
             got, cell = lax.optimization_barrier((got, cell))
-            anchor_grad, temp = finish(anc[:n], extra, got, landmark.shape)
+            anchor_grad, temp = finish(mine, extra, [got], landmark.shape)
             break
-        anc = sum([x[:, :feat] for x in got], anc[:n])
-        extra = sum([x[:1, feat:] for x in got], extra)
+        anc = mine + got[:, :feat]
+        extra = extra + got[:1, feat:]
     return (dq, cell, anchor_grad, temp[0, :total])
 
 

time: 88 us -> 88 us (level)
  the two profiles are of different devices: /device:TPU:20 before, /device:TPU:0 now
where the time goes in v13:
time: 88 us; the launch traced here: 86.8 us
  waiting for transfers between devices  30 us (34%)
  starting transfers between devices  23.5 us (27%)
  Pallas kernels  23.5 us (27%)
  local copies, waits for them, and re-layouts  4.98 us (6%)
  other arithmetic  3.65 us (4%)
  between operations  1.08 us (1%)
    ppermute x12, waiting for transfers between devices, swap_mask(): return lax.ppermute(x, ('gx', 'gy'), [(i, i ^ mask) for i in range(count)])  23.5 us
    pallas_call x2, Pallas kernels, attention(): pl.pallas_call(functools.partial(attention_kernel, gx_count=lax.axis_size...  17.1 us
    ppermute x12, starting transfers between devices, swap_mask(): return lax.ppermute(x, ('gx', 'gy'), [(i, i ^ mask) for i in range(count)])  15.5 us
    ppermute x8, starting transfers between devices, swap_pairs(): return lax.ppermute(x, 'gx', route)  8.01 us
    ppermute x8, waiting for transfers between devices, swap_pairs(): return lax.ppermute(x, 'gx', route)  6.55 us
    pallas_call x2, Pallas kernels, combine(): pl.pallas_call(combine_kernel, grid=(heads // step,), in_specs=in_specs,...  4.36 us
    unnamed x40, local copies, waits for them, and re-layouts  4.12 us
  transfers between devices with their start and end apart: 20, of which 7 were waited for; matrix products, arithmetic and copies ran while one was open for 5% of the time, Pallas kernels for 26%

profile of v13, /device:TPU:0, one launch (start us, length us, event | category | flops | bytes accessed | tf_op | source)
XLA Modules:
  0.0 86.8 jit_solution(2900988040428039121)
XLA Ops:
  0.6 3.0 %collective-permute-start.1 = (bf16[4,2,1536]{2,1,0:T(2,128)(2,1)}, bf16[4,2,1536]{2,1,0:T(2,128)(2,1)S(1)}, u32[]{:S(2)}, u32[]{:S(2)}) collective-permute-start(bf16[4,2,1536]{2,1,0:T(2,128)(2,1)} %param.11), channel_id=1, source_target_pairs={{0,2},{1,3},{2,0},{3,1},{4,6},{5,7},{6,4},{7,5},{8,10},{9,11},{10,... | collective-permute-start | bytes 73736 | tf_op jit(solution)/shard_map/ppermute | solution.py:23
  3.6 1.4 %copy-done = bf16[256,2,1536]{2,1,0:T(2,128)(2,1)S(1)} copy-done((bf16[256,2,1536]{2,1,0:T(2,128)(2,1)S(1)}, bf16[256,2,1536]{2,1,0:T(2,128)(2,1)}, u32[]{:S(2)}) %copy-start) | copy-done | bytes 1572888
  5.0 0.7 copy-done.4
  5.7 0.7 pick.3
  6.4 0.1 collective-permute-start.8
  6.5 0.7 collective-permute-start.9
  7.1 0.7 pick.2
  7.9 0.6 compare_reduce_fusion
  8.5 0.1 pad_maximum_fusion.5
  8.6 4.8 %collective-permute-start.4 = (bf16[8,2,1536]{2,1,0:T(2,128)(2,1)S(1)}, bf16[8,2,1536]{2,1,0:T(2,128)(2,1)S(1)}, u32[]{:S(2)}, u32[]{:S(2)}) collective-permute-start(bf16[8,2,1536]{2,1,0:T(2,128)(2,1)S(1)} %pad_maximum_fusion.5), channel_id=1, source_target_pairs={{0,4},{1,5},{2,6},{3,7},{4,0},{5,1},{6,2},{7,3},{8,12},{9,13},{10,... | collective-permute-start | bytes 147464 | tf_op jit(solution)/shard_map/ppermute | solution.py:23
  13.3 2.6 %collective-permute-start.5 = (bf16[8,2,1536]{2,1,0:T(2,128)(2,1)S(1)}, bf16[8,2,1536]{2,1,0:T(2,128)(2,1)S(1)}, u32[]{:S(2)}, u32[]{:S(2)}) collective-permute-start(bf16[8,2,1536]{2,1,0:T(2,128)(2,1)S(1)} %pad_maximum_fusion.5), channel_id=1, source_target_pairs={{0,8},{1,9},{2,10},{3,11},{4,12},{5,13},{6,14},{7,15},{8,0},{9,1},... | collective-permute-start | bytes 147464 | tf_op jit(solution)/shard_map/ppermute | solution.py:23
  16.0 5.7 %collective-permute-done.4 = bf16[8,2,1536]{2,1,0:T(2,128)(2,1)S(1)} collective-permute-done((bf16[8,2,1536]{2,1,0:T(2,128)(2,1)S(1)}, bf16[8,2,1536]{2,1,0:T(2,128)(2,1)S(1)}, u32[]{:S(2)}, u32[]{:S(2)}) %collective-permute-start.4) | collective-permute-done | bytes 49184 | tf_op jit(solution)/shard_map/ppermute | solution.py:23
  21.7 2.1 %collective-permute-done.5 = bf16[8,2,1536]{2,1,0:T(2,128)(2,1)S(1)} collective-permute-done((bf16[8,2,1536]{2,1,0:T(2,128)(2,1)S(1)}, bf16[8,2,1536]{2,1,0:T(2,128)(2,1)S(1)}, u32[]{:S(2)}, u32[]{:S(2)}) %collective-permute-start.5) | collective-permute-done | bytes 49184 | tf_op jit(solution)/shard_map/ppermute | solution.py:23
  23.8 1.6 %collective-permute-done.6 = bf16[8,2,1536]{2,1,0:T(2,128)(2,1)S(1)} collective-permute-done((bf16[8,2,1536]{2,1,0:T(2,128)(2,1)S(1)}, bf16[8,2,1536]{2,1,0:T(2,128)(2,1)S(1)}, u32[]{:S(2)}, u32[]{:S(2)}) %collective-permute-start.6) | collective-permute-done | bytes 49184 | tf_op jit(solution)/shard_map/ppermute | solution.py:23
  25.3 0.3 pad_maximum_fusion.2
  25.6 0.1 collective-permute-start.7
  25.9 1.3 %collective-permute-done.7 = bf16[32,2,1536]{2,1,0:T(2,128)(2,1)S(1)} collective-permute-done((bf16[32,2,1536]{2,1,0:T(2,128)(2,1)S(1)}, bf16[32,2,1536]{2,1,0:T(2,128)(2,1)S(1)}, u32[]{:S(2)}, u32[]{:S(2)}) %collective-permute-start.7) | collective-permute-done | bytes 196640 | tf_op jit(solution)/shard_map/ppermute | solution.py:23
  27.1 0.7 collective-permute-start.3
  27.8 0.2 constant_dynamic-update-slice_fusion.anc_ref
  28.0 0.0 copy-start.3
  28.1 1.3 %copy-done.1 = bf16[256,2,1536]{2,1,0:T(2,128)(2,1)S(1)} copy-done((bf16[256,2,1536]{2,1,0:T(2,128)(2,1)S(1)}, bf16[256,2,1536]{2,1,0:T(2,128)(2,1)}, u32[]{:S(2)}) %copy-start.1) | copy-done | bytes 1572888
  29.4 0.2 copy-done.2
  29.6 0.2 copy-done.3
  29.8 8.5 %attention.2 = (bf16[256,1536]{1,0:T(8,128)(2,1)}, f32[6,512,128]{2,1,0:T(8,128)S(1)}, bf16[6,256,128]{2,1,0:T(8,128)(2,1)S(1)}, bf16[6,256,128]{2,1,0:T(8,128)(...) custom-call(s32[1]{0:T(128)} %bitcast.pos_ref, ...), custom_call_target="tpu_custom_call" | custom-call | flops 1384120320 | bytes 6488064 | tf_op jit(solution)/shard_map/attention/pallas_call | solution.py:213
  38.3 2.7 %collective-permute-start.10 = (bf16[6,256,128]{2,1,0:T(8,128)(2,1)S(1)}, bf16[6,256,128]{2,1,0:T(8,128)(2,1)S(1)}, u32[]{:S(2)}, u32[]{:S(2)}) collective-permute-start(bf16[6,256,128]{2,1,0:T(8,128)(2,1)S(1)} %get-tuple-element.71), channel_id=1, source_target_pairs={{0,2},{2,0},{4,6},{6,4},{8,10},{10,8},{12,14},{14,12},{1,3},{3,1},... | collective-permute-start | bytes 1179656 | tf_op jit(solution)/shard_map/ppermute | solution.py:42
  41.1 0.7 collective-permute-start.11
  41.8 0.1 collective-permute-start.12
  41.9 8.6 %attention.3 = (bf16[256,1536]{1,0:T(8,128)(2,1)}, f32[6,512,128]{2,1,0:T(8,128)S(1)}, bf16[6,256,128]{2,1,0:T(8,128)(2,1)}, bf16[6,256,128]{2,1,0:T(8,128)(2,1)...) custom-call(s32[1]{0:T(128)} %bitcast.pos_ref, ...), custom_call_target="tpu_custom_call", output_to_operand_aliasing={{0}: (10, {}), {5}: (11, {})} | custom-call | flops 1384120320 | bytes 6488064 | tf_op jit(solution)/shard_map/attention/pallas_call | solution.py:213
  50.5 0.2 maximum_reduce_fusion
  50.7 0.6 fusion
  51.4 6.5 %collective-permute-done.10.dir_ref = bf16[6,256,128]{2,1,0:T(8,128)(2,1)S(1)} collective-permute-done((bf16[6,256,128]{2,1,0:T(8,128)(2,1)S(1)}, bf16[6,256,128]{2,1,0:T(8,128)(2,1)S(1)}, u32[]{:S(2)}, u32[]{:S(2)}) %collective-permute-start.10) | collective-permute-done | bytes 393248 | tf_op jit(solution)/shard_map/ppermute | solution.py:42
  58.0 0.1 collective-permute-start.13
  58.1 0.5 collective-permute-start.14
  58.6 2.5 %collective-permute-start.18 = (bf16[6,256,128]{2,1,0:T(8,128)(2,1)}, bf16[6,256,128]{2,1,0:T(8,128)(2,1)S(1)}, u32[]{:S(2)}, u32[]{:S(2)}) collective-permute-start(bf16[6,256,128]{2,1,0:T(8,128)(2,1)} %get-tuple-element.81), channel_id=1, source_target_pairs={{0,2},{2,0},{4,6},{6,4},{8,10},{10,8},{12,14},{14,12},{1,3},{3,1},... | collective-permute-start | bytes 1179656 | tf_op jit(solution)/shard_map/ppermute | solution.py:42
  61.1 0.7 slice_add_fusion.5
  61.8 0.1 copy-done.16
  61.8 0.1 add.24.refs_0_
  61.9 1.0 %slice_add_fusion = f32[64,1536]{1,0:T(8,128)S(1)} fusion(f32[64,1664]{1,0:T(8,128)} %copy-done.16, f32[128,1536]{1,0:T(8,128)S(1)} %get-tuple-element.74), kind=kLoop, calls=%fused_computation.1 | loop fusion | flops 98304 | bytes 1179648 | tf_op jit(solution)/shard_map/add | solution.py:384
  63.1 1.7 %collective-permute-start.15 = (f32[32,1664]{1,0:T(8,128)S(1)}, f32[32,1664]{1,0:T(8,128)S(1)}, u32[]{:S(2)}, u32[]{:S(2)}) collective-permute-start(f32[32,1664]{1,0:T(8,128)S(1)} %pad_maximum_fusion.1), channel_id=1, source_target_pairs={{0,4},{1,5},{2,6},{3,7},{4,0},{5,1},{6,2},{7,3},{8,12},{9,13},{10,... | collective-permute-start | bytes 638984 | tf_op jit(solution)/shard_map/ppermute | solution.py:23
  64.8 0.7 collective-permute-start.19
  65.5 5.8 %collective-permute-done.15 = f32[32,1664]{1,0:T(8,128)S(1)} collective-permute-done((f32[32,1664]{1,0:T(8,128)S(1)}, f32[32,1664]{1,0:T(8,128)S(1)}, u32[]{:S(2)}, u32[]{:S(2)}) %collective-permute-start.15) | collective-permute-done | bytes 213024 | tf_op jit(solution)/shard_map/ppermute | solution.py:23
  71.4 2.7 %collective-permute-start.16 = (f32[16,1664]{1,0:T(8,128)S(1)}, f32[16,1664]{1,0:T(8,128)S(1)}, u32[]{:S(2)}, u32[]{:S(2)}) collective-permute-start(f32[16,1664]{1,0:T(8,128)S(1)} %pad_maximum_fusion.3), channel_id=1, source_target_pairs={{0,8},{1,9},{2,10},{3,11},{4,12},{5,13},{6,14},{7,15},{8,0},{9,1},... | collective-permute-start | bytes 319496 | tf_op jit(solution)/shard_map/ppermute | solution.py:23
  74.0 7.0 %collective-permute-done.16 = f32[16,1664]{1,0:T(8,128)S(1)} collective-permute-done((f32[16,1664]{1,0:T(8,128)S(1)}, f32[16,1664]{1,0:T(8,128)S(1)}, u32[]{:S(2)}, u32[]{:S(2)}) %collective-permute-start.16) | collective-permute-done | bytes 106528 | tf_op jit(solution)/shard_map/ppermute | solution.py:23
  81.2 0.1 collective-permute-start.17
  81.3 2.2 %combine.2.rest_0_ = bf16[256,2,1536]{2,1,0:T(2,128)(2,1)} custom-call(s32[1]{0:T(128)} %bitcast.pos_ref, s32[3]{0:T(128)S(1)} %bitcast.24, f32[6,512,128]{2,1,0:T(8,128)S(1)} %copy-done.15, bf16[6,256,128]{2,1,0:T(8,128)(2,1)S(1)} %collective-permute-done.10.dir_ref, bf16[6,256,128]{2,1,0:T(8,128)(2,1)S(1)} %copy-done.9, bf16[6,256,128]{2,1,0:T(8,128)(2,1)S(1)} %copy-done.11), custom_call_target="tpu_custom_call" | custom-call | flops 12582912000 | bytes 3538944 | tf_op jit(solution)/shard_map/combine/pallas_call | solution.py:281
  83.5 2.2 %combine.3 = bf16[256,2,1536]{2,1,0:T(2,128)(2,1)} custom-call(s32[1]{0:T(128)} %bitcast.pos_ref, s32[3]{0:T(128)S(1)} %bitcast.25, f32[6,512,128]{2,1,0:T(8,128)S(1)} %get-tuple-element.80.own_ref, bf16[6,256,128]{2,1,0:T(8,128)(2,1)S(1)} %collective-permute-done.18.dir_ref, ...), custom_call_target="tpu_custom_call", output_to_operand_aliasing={{}: (6, {})} | custom-call | bytes 3538944 | tf_op jit(solution)/shard_map/combine/pallas_call | solution.py:281
  85.6 0.6 finish.1
  86.3 0.5 slice_bitcast_fusion
  (70 shorter events, 0.5 us)
Async XLA Ops:
  0.6 7.9 %collective-permute-start.1 = (bf16[4,2,1536]{2,1,0:T(2,128)(2,1)}, bf16[4,2,1536]{2,1,0:T(2,128)(2,1)S(1)}, u32[]{:S(2)}, u32[]{:S(2)}) collective-permute-start(bf16[4,2,1536]{2,1,0:T(2,128)(2,1)} %param.11), channel_id=1, source_target_pairs={{0,2},{1,3},{2,0},{3,1},{4,6},{5,7},{6,4},{7,5},{8,10},{9,11},{10,... | collective-permute-start | bytes 73736 | tf_op jit(solution)/shard_map/ppermute | solution.py:23
  3.6 1.4 %copy-start = (bf16[256,2,1536]{2,1,0:T(2,128)(2,1)S(1)}, bf16[256,2,1536]{2,1,0:T(2,128)(2,1)}, u32[]{:S(2)}) copy-start(bf16[256,2,1536]{2,1,0:T(2,128)(2,1)} %own_ref.3) | copy-start | bytes 4718596
  5.0 0.7 copy-start.4
  5.7 2.8 %copy-start.17 = (bf16[4,2,1536]{2,1,0:T(2,128)(2,1)S(1)}, bf16[4,2,1536]{2,1,0:T(2,128)(2,1)}, u32[]{:S(2)}) copy-start(bf16[4,2,1536]{2,1,0:T(2,128)(2,1)} %param.11) | copy-start | bytes 73732
  6.4 21.7 %collective-permute-start.8 = (bf16[128,2,768]{2,1,0:T(2,128)(2,1)S(1)}, bf16[128,2,768]{2,1,0:T(2,128)(2,1)S(1)}, u32[]{:S(2)}, u32[]{:S(2)}) collective-permute-start(bf16[128,2,768]{2,1,0:T(2,128)(2,1)S(1)} %get-tuple-element.60), channel_id=1, source_target_pairs={{0,2},{2,0},{4,6},{6,4},{8,10},{10,8},{12,14},{14,12},{1,3},{3,1},... | collective-permute-start | bytes 1179656 | tf_op jit(solution)/shard_map/ppermute | solution.py:42
  6.5 21.6 %collective-permute-start.9 = (bf16[128,2,768]{2,1,0:T(2,128)(2,1)S(1)}, bf16[128,2,768]{2,1,0:T(2,128)(2,1)S(1)}, u32[]{:S(2)}, u32[]{:S(2)}) collective-permute-start(bf16[128,2,768]{2,1,0:T(2,128)(2,1)S(1)} %get-tuple-element.61), channel_id=1, source_target_pairs={{2,4},{4,2},{6,8},{8,6},{10,12},{12,10},{3,5},{5,3},{7,9},{9,7},{1... | collective-permute-start | bytes 1179656 | tf_op jit(solution)/shard_map/ppermute | solution.py:42
  8.6 13.1 %collective-permute-start.4 = (bf16[8,2,1536]{2,1,0:T(2,128)(2,1)S(1)}, bf16[8,2,1536]{2,1,0:T(2,128)(2,1)S(1)}, u32[]{:S(2)}, u32[]{:S(2)}) collective-permute-start(bf16[8,2,1536]{2,1,0:T(2,128)(2,1)S(1)} %pad_maximum_fusion.5), channel_id=1, source_target_pairs={{0,4},{1,5},{2,6},{3,7},{4,0},{5,1},{6,2},{7,3},{8,12},{9,13},{10,... | collective-permute-start | bytes 147464 | tf_op jit(solution)/shard_map/ppermute | solution.py:23
  13.3 10.4 %collective-permute-start.5 = (bf16[8,2,1536]{2,1,0:T(2,128)(2,1)S(1)}, bf16[8,2,1536]{2,1,0:T(2,128)(2,1)S(1)}, u32[]{:S(2)}, u32[]{:S(2)}) collective-permute-start(bf16[8,2,1536]{2,1,0:T(2,128)(2,1)S(1)} %pad_maximum_fusion.5), channel_id=1, source_target_pairs={{0,8},{1,9},{2,10},{3,11},{4,12},{5,13},{6,14},{7,15},{8,0},{9,1},... | collective-permute-start | bytes 147464 | tf_op jit(solution)/shard_map/ppermute | solution.py:23
  15.9 9.4 %collective-permute-start.6 = (bf16[8,2,1536]{2,1,0:T(2,128)(2,1)S(1)}, bf16[8,2,1536]{2,1,0:T(2,128)(2,1)S(1)}, u32[]{:S(2)}, u32[]{:S(2)}) collective-permute-start(bf16[8,2,1536]{2,1,0:T(2,128)(2,1)S(1)} %pad_maximum_fusion.5), channel_id=1, source_target_pairs={{0,12},{1,13},{2,14},{3,15},{4,8},{5,9},{6,10},{7,11},{8,4},{9,5},... | collective-permute-start | bytes 147464 | tf_op jit(solution)/shard_map/ppermute | solution.py:23
  21.7 6.4 %collective-permute-start = (bf16[128,2,1536]{2,1,0:T(2,128)(2,1)S(1)}, bf16[128,2,1536]{2,1,0:T(2,128)(2,1)S(1)}, u32[]{:S(2)}, u32[]{:S(2)}) collective-permute-start(bf16[128,2,1536]{2,1,0:T(2,128)(2,1)S(1)} %get-tuple-element.54), channel_id=1, source_target_pairs={{0,1},{1,0},{2,3},{3,2},{4,5},{5,4},{6,7},{7,6},{8,9},{9,8},{10,11... | collective-permute-start | bytes 2359304 | tf_op jit(solution)/shard_map/ppermute | solution.py:23
  23.8 18.1 %collective-permute-start.2 = (bf16[128,2,768]{2,1,0:T(2,128)(2,1)S(1)}, bf16[128,2,768]{2,1,0:T(2,128)(2,1)S(1)}, u32[]{:S(2)}, u32[]{:S(2)}) collective-permute-start(bf16[128,2,768]{2,1,0:T(2,128)(2,1)S(1)} %get-tuple-element.57), channel_id=1, source_target_pairs={{0,2},{2,0},{4,6},{6,4},{8,10},{10,8},{12,14},{14,12},{1,3},{3,1},... | collective-permute-start | bytes 1179656 | tf_op jit(solution)/shard_map/ppermute | solution.py:42
  25.6 1.5 %collective-permute-start.7 = (bf16[32,2,1536]{2,1,0:T(2,128)(2,1)S(1)}, bf16[32,2,1536]{2,1,0:T(2,128)(2,1)S(1)}, u32[]{:S(2)}, u32[]{:S(2)}) collective-permute-start(bf16[32,2,1536]{2,1,0:T(2,128)(2,1)S(1)} %pad_maximum_fusion.2), channel_id=1, source_target_pairs={{0,1},{1,0},{2,3},{3,2},{4,5},{5,4},{6,7},{7,6},{8,9},{9,8},{10,11... | collective-permute-start | bytes 589832 | tf_op jit(solution)/shard_map/ppermute | solution.py:23
  27.1 14.7 %collective-permute-start.3 = (bf16[128,2,768]{2,1,0:T(2,128)(2,1)S(1)}, bf16[128,2,768]{2,1,0:T(2,128)(2,1)S(1)}, u32[]{:S(2)}, u32[]{:S(2)}) collective-permute-start(bf16[128,2,768]{2,1,0:T(2,128)(2,1)S(1)} %get-tuple-element.58), channel_id=1, source_target_pairs={{2,4},{4,2},{6,8},{8,6},{10,12},{12,10},{3,5},{5,3},{7,9},{9,7},{1... | collective-permute-start | bytes 1179656 | tf_op jit(solution)/shard_map/ppermute | solution.py:42
  28.0 1.4 %copy-start.1 = (bf16[256,2,1536]{2,1,0:T(2,128)(2,1)S(1)}, bf16[256,2,1536]{2,1,0:T(2,128)(2,1)}, u32[]{:S(2)}) copy-start(bf16[256,2,1536]{2,1,0:T(2,128)(2,1)} %own_ref.3) | copy-start | bytes 4718596
  28.0 1.6 %copy-start.2 = (bf16[256,1536]{1,0:T(8,128)(2,1)S(1)}, bf16[256,1536]{1,0:T(8,128)(2,1)}, u32[]{:S(2)}) copy-start(bf16[256,1536]{1,0:T(8,128)(2,1)} %q_ref.3) | copy-start | bytes 2359300
  28.0 1.8 %copy-start.3 = (bf16[256,1536]{1,0:T(8,128)(2,1)S(1)}, bf16[256,1536]{1,0:T(8,128)(2,1)}, u32[]{:S(2)}) copy-start(bf16[256,1536]{1,0:T(8,128)(2,1)} %g_ref.3) | copy-start | bytes 2359300
  28.0 1.8 %copy-start.6 = (s32[1,2,5]{2,1,0:T(2,128)S(1)}, s32[1,2,5]{2,1,0:T(2,128)}, u32[]{:S(2)}) copy-start(s32[1,2,5]{2,1,0:T(2,128)} %param.15) | copy-start | bytes 124
  28.0 1.8 %copy-start.7 = (f32[12]{0:T(128)S(1)}, f32[12]{0:T(128)}, u32[]{:S(2)}) copy-start(f32[12]{0:T(128)} %warm_ref.3) | copy-start | bytes 148
  38.3 12.2 %copy-start.14 = (f32[6,512,128]{2,1,0:T(8,128)}, f32[6,512,128]{2,1,0:T(8,128)S(1)}, u32[]{:S(2)}) copy-start(f32[6,512,128]{2,1,0:T(8,128)S(1)} %get-tuple-element.84.own_ref) | copy-start | bytes 4718596
  38.3 19.6 %collective-permute-start.10 = (bf16[6,256,128]{2,1,0:T(8,128)(2,1)S(1)}, bf16[6,256,128]{2,1,0:T(8,128)(2,1)S(1)}, u32[]{:S(2)}, u32[]{:S(2)}) collective-permute-start(bf16[6,256,128]{2,1,0:T(8,128)(2,1)S(1)} %get-tuple-element.71), channel_id=1, source_target_pairs={{0,2},{2,0},{4,6},{6,4},{8,10},{10,8},{12,14},{14,12},{1,3},{3,1},... | collective-permute-start | bytes 1179656 | tf_op jit(solution)/shard_map/ppermute | solution.py:42
  41.1 16.8 %collective-permute-start.11 = (bf16[6,256,128]{2,1,0:T(8,128)(2,1)S(1)}, bf16[6,256,128]{2,1,0:T(8,128)(2,1)S(1)}, u32[]{:S(2)}, u32[]{:S(2)}) collective-permute-start(bf16[6,256,128]{2,1,0:T(8,128)(2,1)S(1)} %get-tuple-element.72), channel_id=1, source_target_pairs={{2,4},{4,2},{6,8},{8,6},{10,12},{12,10},{3,5},{5,3},{7,9},{9,7},{1... | collective-permute-start | bytes 1179656 | tf_op jit(solution)/shard_map/ppermute | solution.py:42
  41.8 16.1 %collective-permute-start.12 = (bf16[6,256,128]{2,1,0:T(8,128)(2,1)S(1)}, bf16[6,256,128]{2,1,0:T(8,128)(2,1)S(1)}, u32[]{:S(2)}, u32[]{:S(2)}) collective-permute-start(bf16[6,256,128]{2,1,0:T(8,128)(2,1)S(1)} %get-tuple-element.73), channel_id=1, source_target_pairs={{0,1},{1,0},{2,3},{3,2},{4,5},{5,4},{6,7},{7,6},{8,9},{9,8},{10,11... | collective-permute-start | bytes 1179656 | tf_op jit(solution)/shard_map/ppermute | solution.py:23
  50.5 11.2 %copy-start.12 = (bf16[6,256,128]{2,1,0:T(8,128)(2,1)}, bf16[6,256,128]{2,1,0:T(8,128)(2,1)S(1)}, u32[]{:S(2)}) copy-start(bf16[6,256,128]{2,1,0:T(8,128)(2,1)S(1)} %get-tuple-element.82) | copy-start | bytes 1179652
  57.9 3.8 %copy-start.8 = (bf16[6,256,128]{2,1,0:T(8,128)(2,1)}, bf16[6,256,128]{2,1,0:T(8,128)(2,1)S(1)}, u32[]{:S(2)}) copy-start(bf16[6,256,128]{2,1,0:T(8,128)(2,1)S(1)} %collective-permute-done.11.dia_ref) | copy-start | bytes 1179652
  57.9 3.8 %copy-start.10 = (bf16[6,256,128]{2,1,0:T(8,128)(2,1)}, bf16[6,256,128]{2,1,0:T(8,128)(2,1)S(1)}, u32[]{:S(2)}) copy-start(bf16[6,256,128]{2,1,0:T(8,128)(2,1)S(1)} %collective-permute-done.12.par_ref) | copy-start | bytes 1179652
  58.0 3.1 %collective-permute-start.13 = (f32[64,1664]{1,0:T(8,128)S(1)}, f32[64,1664]{1,0:T(8,128)S(1)}, u32[]{:S(2)}, u32[]{:S(2)}) collective-permute-start(f32[64,1664]{1,0:T(8,128)S(1)} %pad_maximum_fusion), channel_id=1, source_target_pairs={{0,1},{1,0},{2,3},{3,2},{4,5},{5,4},{6,7},{7,6},{8,9},{9,8},{10,11... | collective-permute-start | bytes 1277960 | tf_op jit(solution)/shard_map/ppermute | solution.py:23
  58.1 5.0 %collective-permute-start.14 = (bf16[6,256,128]{2,1,0:T(8,128)(2,1)}, bf16[6,256,128]{2,1,0:T(8,128)(2,1)S(1)}, u32[]{:S(2)}, u32[]{:S(2)}) collective-permute-start(bf16[6,256,128]{2,1,0:T(8,128)(2,1)} %get-tuple-element.78), channel_id=1, source_target_pairs={{0,1},{1,0},{2,3},{3,2},{4,5},{5,4},{6,7},{7,6},{8,9},{9,8},{10,11... | collective-permute-start | bytes 1179656 | tf_op jit(solution)/shard_map/ppermute | solution.py:23
  58.6 24.9 %collective-permute-start.18 = (bf16[6,256,128]{2,1,0:T(8,128)(2,1)}, bf16[6,256,128]{2,1,0:T(8,128)(2,1)S(1)}, u32[]{:S(2)}, u32[]{:S(2)}) collective-permute-start(bf16[6,256,128]{2,1,0:T(8,128)(2,1)} %get-tuple-element.81), channel_id=1, source_target_pairs={{0,2},{2,0},{4,6},{6,4},{8,10},{10,8},{12,14},{14,12},{1,3},{3,1},... | collective-permute-start | bytes 1179656 | tf_op jit(solution)/shard_map/ppermute | solution.py:42
  61.1 0.8 copy-start.16
  63.0 1.7 %copy-start.13 = (bf16[6,256,128]{2,1,0:T(8,128)(2,1)S(1)}, bf16[6,256,128]{2,1,0:T(8,128)(2,1)}, u32[]{:S(2)}) copy-start(bf16[6,256,128]{2,1,0:T(8,128)(2,1)} %copy-done.12) | copy-start | bytes 1179652
  63.1 8.2 %collective-permute-start.15 = (f32[32,1664]{1,0:T(8,128)S(1)}, f32[32,1664]{1,0:T(8,128)S(1)}, u32[]{:S(2)}, u32[]{:S(2)}) collective-permute-start(f32[32,1664]{1,0:T(8,128)S(1)} %pad_maximum_fusion.1), channel_id=1, source_target_pairs={{0,4},{1,5},{2,6},{3,7},{4,0},{5,1},{6,2},{7,3},{8,12},{9,13},{10,... | collective-permute-start | bytes 638984 | tf_op jit(solution)/shard_map/ppermute | solution.py:23
  64.8 18.7 %collective-permute-start.19 = (bf16[6,256,128]{2,1,0:T(8,128)(2,1)S(1)}, bf16[6,256,128]{2,1,0:T(8,128)(2,1)S(1)}, u32[]{:S(2)}, u32[]{:S(2)}) collective-permute-start(bf16[6,256,128]{2,1,0:T(8,128)(2,1)S(1)} %copy-done.13), channel_id=1, source_target_pairs={{2,4},{4,2},{6,8},{8,6},{10,12},{12,10},{3,5},{5,3},{7,9},{9,7},{1... | collective-permute-start | bytes 1179656 | tf_op jit(solution)/shard_map/ppermute | solution.py:42
  71.3 9.9 %copy-start.5 = (s32[1,3,1]{1,2,0:T(1,128)S(1)}, s32[1,3,1]{1,2,0:T(1,128)}, u32[]{:S(2)}) copy-start(s32[1,3,1]{1,2,0:T(1,128)} %param.14) | copy-start | bytes 40
  71.3 9.9 %copy-start.9 = (bf16[6,256,128]{2,1,0:T(8,128)(2,1)S(1)}, bf16[6,256,128]{2,1,0:T(8,128)(2,1)}, u32[]{:S(2)}) copy-start(bf16[6,256,128]{2,1,0:T(8,128)(2,1)} %copy-done.8) | copy-start | bytes 1179652
  71.3 9.9 %copy-start.11 = (bf16[6,256,128]{2,1,0:T(8,128)(2,1)S(1)}, bf16[6,256,128]{2,1,0:T(8,128)(2,1)}, u32[]{:S(2)}) copy-start(bf16[6,256,128]{2,1,0:T(8,128)(2,1)} %copy-done.10) | copy-start | bytes 1179652
  71.3 9.9 %copy-start.15 = (f32[6,512,128]{2,1,0:T(8,128)S(1)}, f32[6,512,128]{2,1,0:T(8,128)}, u32[]{:S(2)}) copy-start(f32[6,512,128]{2,1,0:T(8,128)} %copy-done.14) | copy-start | bytes 4718596
  71.4 9.7 %collective-permute-start.16 = (f32[16,1664]{1,0:T(8,128)S(1)}, f32[16,1664]{1,0:T(8,128)S(1)}, u32[]{:S(2)}, u32[]{:S(2)}) collective-permute-start(f32[16,1664]{1,0:T(8,128)S(1)} %pad_maximum_fusion.3), channel_id=1, source_target_pairs={{0,8},{1,9},{2,10},{3,11},{4,12},{5,13},{6,14},{7,15},{8,0},{9,1},... | collective-permute-start | bytes 319496 | tf_op jit(solution)/shard_map/ppermute | solution.py:23
  81.2 4.5 %collective-permute-start.17 = (f32[8,1664]{1,0:T(8,128)S(1)}, f32[8,1664]{1,0:T(8,128)S(1)}, u32[]{:S(2)}, u32[]{:S(2)}) collective-permute-start(f32[8,1664]{1,0:T(8,128)S(1)} %pad_maximum_fusion.4), channel_id=1, source_target_pairs={{0,2},{1,3},{2,0},{3,1},{4,6},{5,7},{6,4},{7,5},{8,10},{9,11},{10,... | collective-permute-start | bytes 159752 | tf_op jit(solution)/shard_map/ppermute | solution.py:23

commit v14 on v13

--- a/solution.py
+++ b/solution.py
@@ -372,11 +372,13 @@
         if i == 1:
             out, diagonal, returned[-1][2] = lax.optimization_barrier((out, diagonal, returned[-1][2]))
             returned[-1][1] = swap_pairs(diagonal, 1)
-        if 0 < i < len(steps) - 1:
+        if 0 < i < len(steps) - 2:
             (extra,) = hold([extra], HOLD)
         got = swap_mask(out, mask)
+        if i == len(steps) - 2:
+            cell = combine(pos, sent, owns[-2], returned[-2], *chunks[-2], feat, width, cell, weight=4000)
+            got, cell = lax.optimization_barrier((got, cell))
         if i == len(steps) - 1:
-            cell = combine(pos, sent, owns[-2], returned[-2], *chunks[-2], feat, width, cell, weight=4000)
             cell = combine(pos, sent, owns[-1], returned[-1], *chunks[-1], feat, width, cell, weight=0)
             got, cell = lax.optimization_barrier((got, cell))
             anchor_grad, temp = finish(mine, extra, [got], landmark.shape)

time: 88 us -> 90.7 us (1.031)
  starting transfers between devices: 23.5 us -> 26.2 us
    ppermute x12, starting transfers between devices: 15.5 us -> 18.2 us  [swap_mask(): return lax.ppermute(x, ('gx', 'gy'), [(i, i ^ mask) for i in range(count)])]
  transfers between devices with their start and end apart: 20 -> 20, of which waited for: 7 -> 8; matrix products, arithmetic and copies ran while one was open for 5% -> 5% of each run, Pallas kernels for 26% -> 26%
where the time goes in v14:
time: 90.7 us; the launch traced here: 89.7 us
  waiting for transfers between devices  30.3 us (33%)
  starting transfers between devices  26.2 us (29%)
  Pallas kernels  23.5 us (26%)
  local copies, waits for them, and re-layouts  4.98 us (5%)
  other arithmetic  3.65 us (4%)
  between operations  1.06 us (1%)
    ppermute x12, waiting for transfers between devices, swap_mask(): return lax.ppermute(x, ('gx', 'gy'), [(i, i ^ mask) for i in range(count)])  23.8 us
    ppermute x12, starting transfers between devices, swap_mask(): return lax.ppermute(x, ('gx', 'gy'), [(i, i ^ mask) for i in range(count)])  18.2 us
    pallas_call x2, Pallas kernels, attention(): pl.pallas_call(functools.partial(attention_kernel, gx_count=lax.axis_size...  17.1 us
    ppermute x8, starting transfers between devices, swap_pairs(): return lax.ppermute(x, 'gx', route)  8 us
    ppermute x8, waiting for transfers between devices, swap_pairs(): return lax.ppermute(x, 'gx', route)  6.56 us
    pallas_call x2, Pallas kernels, combine(): pl.pallas_call(combine_kernel, grid=(heads // step,), in_specs=in_specs,...  4.36 us
    unnamed x40, local copies, waits for them, and re-layouts  4.12 us
  transfers between devices with their start and end apart: 20, of which 8 were waited for; matrix products, arithmetic and copies ran while one was open for 5% of the time, Pallas kernels for 26%

profile of v14, /device:TPU:0, one launch (start us, length us, event | category | flops | bytes accessed | tf_op | source)
XLA Modules:
  0.0 89.7 jit_solution(10214791880047780202)
XLA Ops:
  0.6 3.0 %collective-permute-start.1 = (bf16[4,2,1536]{2,1,0:T(2,128)(2,1)}, bf16[4,2,1536]{2,1,0:T(2,128)(2,1)S(1)}, u32[]{:S(2)}, u32[]{:S(2)}) collective-permute-start(bf16[4,2,1536]{2,1,0:T(2,128)(2,1)} %param.11), channel_id=1, source_target_pairs={{0,2},{1,3},{2,0},{3,1},{4,6},{5,7},{6,4},{7,5},{8,10},{9,11},{10,... | collective-permute-start | bytes 73736 | tf_op jit(solution)/shard_map/ppermute | solution.py:23
  3.6 1.4 %copy-done = bf16[256,2,1536]{2,1,0:T(2,128)(2,1)S(1)} copy-done((bf16[256,2,1536]{2,1,0:T(2,128)(2,1)S(1)}, bf16[256,2,1536]{2,1,0:T(2,128)(2,1)}, u32[]{:S(2)}) %copy-start) | copy-done | bytes 1572888
  5.0 0.7 copy-done.4
  5.7 0.7 pick.3
  6.4 0.1 collective-permute-start.8
  6.5 0.7 collective-permute-start.9
  7.1 0.7 pick.2
  7.9 0.6 compare_reduce_fusion
  8.5 0.1 pad_maximum_fusion.5
  8.6 4.8 %collective-permute-start.4 = (bf16[8,2,1536]{2,1,0:T(2,128)(2,1)S(1)}, bf16[8,2,1536]{2,1,0:T(2,128)(2,1)S(1)}, u32[]{:S(2)}, u32[]{:S(2)}) collective-permute-start(bf16[8,2,1536]{2,1,0:T(2,128)(2,1)S(1)} %pad_maximum_fusion.5), channel_id=1, source_target_pairs={{0,4},{1,5},{2,6},{3,7},{4,0},{5,1},{6,2},{7,3},{8,12},{9,13},{10,... | collective-permute-start | bytes 147464 | tf_op jit(solution)/shard_map/ppermute | solution.py:23
  13.3 2.6 %collective-permute-start.5 = (bf16[8,2,1536]{2,1,0:T(2,128)(2,1)S(1)}, bf16[8,2,1536]{2,1,0:T(2,128)(2,1)S(1)}, u32[]{:S(2)}, u32[]{:S(2)}) collective-permute-start(bf16[8,2,1536]{2,1,0:T(2,128)(2,1)S(1)} %pad_maximum_fusion.5), channel_id=1, source_target_pairs={{0,8},{1,9},{2,10},{3,11},{4,12},{5,13},{6,14},{7,15},{8,0},{9,1},... | collective-permute-start | bytes 147464 | tf_op jit(solution)/shard_map/ppermute | solution.py:23
  16.0 5.7 %collective-permute-done.4 = bf16[8,2,1536]{2,1,0:T(2,128)(2,1)S(1)} collective-permute-done((bf16[8,2,1536]{2,1,0:T(2,128)(2,1)S(1)}, bf16[8,2,1536]{2,1,0:T(2,128)(2,1)S(1)}, u32[]{:S(2)}, u32[]{:S(2)}) %collective-permute-start.4) | collective-permute-done | bytes 49184 | tf_op jit(solution)/shard_map/ppermute | solution.py:23
  21.7 2.1 %collective-permute-done.5 = bf16[8,2,1536]{2,1,0:T(2,128)(2,1)S(1)} collective-permute-done((bf16[8,2,1536]{2,1,0:T(2,128)(2,1)S(1)}, bf16[8,2,1536]{2,1,0:T(2,128)(2,1)S(1)}, u32[]{:S(2)}, u32[]{:S(2)}) %collective-permute-start.5) | collective-permute-done | bytes 49184 | tf_op jit(solution)/shard_map/ppermute | solution.py:23
  23.8 1.6 %collective-permute-done.6 = bf16[8,2,1536]{2,1,0:T(2,128)(2,1)S(1)} collective-permute-done((bf16[8,2,1536]{2,1,0:T(2,128)(2,1)S(1)}, bf16[8,2,1536]{2,1,0:T(2,128)(2,1)S(1)}, u32[]{:S(2)}, u32[]{:S(2)}) %collective-permute-start.6) | collective-permute-done | bytes 49184 | tf_op jit(solution)/shard_map/ppermute | solution.py:23
  25.3 0.3 pad_maximum_fusion.2
  25.6 0.1 collective-permute-start.7
  25.9 1.3 %collective-permute-done.7 = bf16[32,2,1536]{2,1,0:T(2,128)(2,1)S(1)} collective-permute-done((bf16[32,2,1536]{2,1,0:T(2,128)(2,1)S(1)}, bf16[32,2,1536]{2,1,0:T(2,128)(2,1)S(1)}, u32[]{:S(2)}, u32[]{:S(2)}) %collective-permute-start.7) | collective-permute-done | bytes 196640 | tf_op jit(solution)/shard_map/ppermute | solution.py:23
  27.1 0.7 collective-permute-start.3
  27.8 0.2 constant_dynamic-update-slice_fusion.anc_ref
  28.1 1.3 %copy-done.1 = bf16[256,2,1536]{2,1,0:T(2,128)(2,1)S(1)} copy-done((bf16[256,2,1536]{2,1,0:T(2,128)(2,1)S(1)}, bf16[256,2,1536]{2,1,0:T(2,128)(2,1)}, u32[]{:S(2)}) %copy-start.1) | copy-done | bytes 1572888
  29.4 0.2 copy-done.2
  29.6 0.2 copy-done.3
  29.8 8.5 %attention.2 = (bf16[256,1536]{1,0:T(8,128)(2,1)}, f32[6,512,128]{2,1,0:T(8,128)S(1)}, bf16[6,256,128]{2,1,0:T(8,128)(2,1)S(1)}, bf16[6,256,128]{2,1,0:T(8,128)(...) custom-call(s32[1]{0:T(128)} %bitcast.pos_ref, ...), custom_call_target="tpu_custom_call" | custom-call | flops 1384120320 | bytes 6488064 | tf_op jit(solution)/shard_map/attention/pallas_call | solution.py:213
  38.3 2.7 %collective-permute-start.10 = (bf16[6,256,128]{2,1,0:T(8,128)(2,1)S(1)}, bf16[6,256,128]{2,1,0:T(8,128)(2,1)S(1)}, u32[]{:S(2)}, u32[]{:S(2)}) collective-permute-start(bf16[6,256,128]{2,1,0:T(8,128)(2,1)S(1)} %get-tuple-element.73), channel_id=1, source_target_pairs={{0,2},{2,0},{4,6},{6,4},{8,10},{10,8},{12,14},{14,12},{1,3},{3,1},... | collective-permute-start | bytes 1179656 | tf_op jit(solution)/shard_map/ppermute | solution.py:42
  41.1 0.7 collective-permute-start.11
  41.8 0.1 collective-permute-start.12
  41.9 8.6 %attention.3 = (bf16[256,1536]{1,0:T(8,128)(2,1)}, f32[6,512,128]{2,1,0:T(8,128)S(1)}, bf16[6,256,128]{2,1,0:T(8,128)(2,1)}, bf16[6,256,128]{2,1,0:T(8,128)(2,1)...) custom-call(s32[1]{0:T(128)} %bitcast.pos_ref, ...), custom_call_target="tpu_custom_call", output_to_operand_aliasing={{0}: (10, {}), {5}: (11, {})} | custom-call | flops 1384120320 | bytes 6488064 | tf_op jit(solution)/shard_map/attention/pallas_call | solution.py:213
  50.5 0.2 maximum_reduce_fusion
  50.7 0.6 fusion
  51.4 6.5 %collective-permute-done.10.dir_ref = bf16[6,256,128]{2,1,0:T(8,128)(2,1)S(1)} collective-permute-done((bf16[6,256,128]{2,1,0:T(8,128)(2,1)S(1)}, bf16[6,256,128]{2,1,0:T(8,128)(2,1)S(1)}, u32[]{:S(2)}, u32[]{:S(2)}) %collective-permute-start.10) | collective-permute-done | bytes 393248 | tf_op jit(solution)/shard_map/ppermute | solution.py:42
  58.0 0.1 collective-permute-start.13
  58.1 0.5 collective-permute-start.14
  58.6 2.5 %collective-permute-start.18 = (bf16[6,256,128]{2,1,0:T(8,128)(2,1)}, bf16[6,256,128]{2,1,0:T(8,128)(2,1)S(1)}, u32[]{:S(2)}, u32[]{:S(2)}) collective-permute-start(bf16[6,256,128]{2,1,0:T(8,128)(2,1)} %get-tuple-element.88), channel_id=1, source_target_pairs={{0,2},{2,0},{4,6},{6,4},{8,10},{10,8},{12,14},{14,12},{1,3},{3,1},... | collective-permute-start | bytes 1179656 | tf_op jit(solution)/shard_map/ppermute | solution.py:42
  61.1 0.7 slice_add_fusion.4
  61.8 0.1 copy-done.16
  61.8 0.1 add.24.refs_0_
  61.9 1.0 %slice_add_fusion = f32[64,1536]{1,0:T(8,128)S(1)} fusion(f32[64,1664]{1,0:T(8,128)} %copy-done.16, f32[128,1536]{1,0:T(8,128)S(1)} %get-tuple-element.76), kind=kLoop, calls=%fused_computation.1 | loop fusion | flops 98304 | bytes 1179648 | tf_op jit(solution)/shard_map/add | solution.py:386
  63.1 1.7 %collective-permute-start.15 = (f32[32,1664]{1,0:T(8,128)S(1)}, f32[32,1664]{1,0:T(8,128)S(1)}, u32[]{:S(2)}, u32[]{:S(2)}) collective-permute-start(f32[32,1664]{1,0:T(8,128)S(1)} %pad_maximum_fusion.1), channel_id=1, source_target_pairs={{0,4},{1,5},{2,6},{3,7},{4,0},{5,1},{6,2},{7,3},{8,12},{9,13},{10,... | collective-permute-start | bytes 638984 | tf_op jit(solution)/shard_map/ppermute | solution.py:23
  64.8 5.6 %collective-permute-done.15 = f32[32,1664]{1,0:T(8,128)S(1)} collective-permute-done((f32[32,1664]{1,0:T(8,128)S(1)}, f32[32,1664]{1,0:T(8,128)S(1)}, u32[]{:S(2)}, u32[]{:S(2)}) %collective-permute-start.15) | collective-permute-done | bytes 213024 | tf_op jit(solution)/shard_map/ppermute | solution.py:23
  70.5 2.9 %collective-permute-start.16 = (f32[16,1664]{1,0:T(8,128)S(1)}, f32[16,1664]{1,0:T(8,128)S(1)}, u32[]{:S(2)}, u32[]{:S(2)}) collective-permute-start(f32[16,1664]{1,0:T(8,128)S(1)} %pad_maximum_fusion.3), channel_id=1, source_target_pairs={{0,8},{1,9},{2,10},{3,11},{4,12},{5,13},{6,14},{7,15},{8,0},{9,1},... | collective-permute-start | bytes 319496 | tf_op jit(solution)/shard_map/ppermute | solution.py:23
  73.4 2.2 %combine.2.rest_0_ = bf16[256,2,1536]{2,1,0:T(2,128)(2,1)} custom-call(s32[1]{0:T(128)} %bitcast.pos_ref, s32[3]{0:T(128)S(1)} %bitcast.25, f32[6,512,128]{2,1,0:T(8,128)S(1)} %copy-done.15, bf16[6,256,128]{2,1,0:T(8,128)(2,1)S(1)} %copy-done.9, bf16[6,256,128]{2,1,0:T(8,128)(2,1)S(1)} %copy-done.11, bf16[6,256,128]{2,1,0:T(8,128)(2,1)S(1)} %copy-done.13), custom_call_target="tpu_custom_call" | custom-call | flops 12582912000 | bytes 3538944 | tf_op jit(solution)/shard_map/combine/pallas_call | solution.py:281
  75.5 0.7 collective-permute-start.19
  76.2 1.7 %collective-permute-done.16 = f32[16,1664]{1,0:T(8,128)S(1)} collective-permute-done((f32[16,1664]{1,0:T(8,128)S(1)}, f32[16,1664]{1,0:T(8,128)S(1)}, u32[]{:S(2)}, u32[]{:S(2)}) %collective-permute-start.16) | collective-permute-done | bytes 106528 | tf_op jit(solution)/shard_map/ppermute | solution.py:23
  78.0 2.5 %collective-permute-start.17 = (f32[8,1664]{1,0:T(8,128)S(1)}, f32[8,1664]{1,0:T(8,128)S(1)}, u32[]{:S(2)}, u32[]{:S(2)}) collective-permute-start(f32[8,1664]{1,0:T(8,128)S(1)} %pad_maximum_fusion.4), channel_id=1, source_target_pairs={{0,2},{1,3},{2,0},{3,1},{4,6},{5,7},{6,4},{7,5},{8,10},{9,11},{10,... | collective-permute-start | bytes 159752 | tf_op jit(solution)/shard_map/ppermute | solution.py:23
  80.5 2.2 %combine.3 = bf16[256,2,1536]{2,1,0:T(2,128)(2,1)} custom-call(s32[1]{0:T(128)} %bitcast.pos_ref, s32[3]{0:T(128)S(1)} %bitcast.26, f32[6,512,128]{2,1,0:T(8,128)S(1)} %get-tuple-element.87.own_ref, bf16[6,256,128]{2,1,0:T(8,128)(2,1)S(1)} %collective-permute-done.18.dir_ref, ...), custom_call_target="tpu_custom_call", output_to_operand_aliasing={{}: (6, {})} | custom-call | bytes 3538944 | tf_op jit(solution)/shard_map/combine/pallas_call | solution.py:281
  82.7 5.9 %collective-permute-done.17.refs_0_ = f32[8,1664]{1,0:T(8,128)S(1)} collective-permute-done((f32[8,1664]{1,0:T(8,128)S(1)}, f32[8,1664]{1,0:T(8,128)S(1)}, u32[]{:S(2)}, u32[]{:S(2)}) %collective-permute-start.17) | collective-permute-done | bytes 53280 | tf_op jit(solution)/shard_map/ppermute | solution.py:23
  88.6 0.6 finish.1
  89.2 0.5 slice_bitcast_fusion
  (69 shorter events, 0.5 us)
Async XLA Ops:
  0.6 7.9 %collective-permute-start.1 = (bf16[4,2,1536]{2,1,0:T(2,128)(2,1)}, bf16[4,2,1536]{2,1,0:T(2,128)(2,1)S(1)}, u32[]{:S(2)}, u32[]{:S(2)}) collective-permute-start(bf16[4,2,1536]{2,1,0:T(2,128)(2,1)} %param.11), channel_id=1, source_target_pairs={{0,2},{1,3},{2,0},{3,1},{4,6},{5,7},{6,4},{7,5},{8,10},{9,11},{10,... | collective-permute-start | bytes 73736 | tf_op jit(solution)/shard_map/ppermute | solution.py:23
  3.6 1.4 %copy-start = (bf16[256,2,1536]{2,1,0:T(2,128)(2,1)S(1)}, bf16[256,2,1536]{2,1,0:T(2,128)(2,1)}, u32[]{:S(2)}) copy-start(bf16[256,2,1536]{2,1,0:T(2,128)(2,1)} %own_ref.3) | copy-start | bytes 4718596
  5.0 0.7 copy-start.4
  5.7 2.8 %copy-start.17 = (bf16[4,2,1536]{2,1,0:T(2,128)(2,1)S(1)}, bf16[4,2,1536]{2,1,0:T(2,128)(2,1)}, u32[]{:S(2)}) copy-start(bf16[4,2,1536]{2,1,0:T(2,128)(2,1)} %param.11) | copy-start | bytes 73732
  6.4 21.7 %collective-permute-start.8 = (bf16[128,2,768]{2,1,0:T(2,128)(2,1)S(1)}, bf16[128,2,768]{2,1,0:T(2,128)(2,1)S(1)}, u32[]{:S(2)}, u32[]{:S(2)}) collective-permute-start(bf16[128,2,768]{2,1,0:T(2,128)(2,1)S(1)} %get-tuple-element.62), channel_id=1, source_target_pairs={{0,2},{2,0},{4,6},{6,4},{8,10},{10,8},{12,14},{14,12},{1,3},{3,1},... | collective-permute-start | bytes 1179656 | tf_op jit(solution)/shard_map/ppermute | solution.py:42
  6.5 21.6 %collective-permute-start.9 = (bf16[128,2,768]{2,1,0:T(2,128)(2,1)S(1)}, bf16[128,2,768]{2,1,0:T(2,128)(2,1)S(1)}, u32[]{:S(2)}, u32[]{:S(2)}) collective-permute-start(bf16[128,2,768]{2,1,0:T(2,128)(2,1)S(1)} %get-tuple-element.63), channel_id=1, source_target_pairs={{2,4},{4,2},{6,8},{8,6},{10,12},{12,10},{3,5},{5,3},{7,9},{9,7},{1... | collective-permute-start | bytes 1179656 | tf_op jit(solution)/shard_map/ppermute | solution.py:42
  8.6 13.1 %collective-permute-start.4 = (bf16[8,2,1536]{2,1,0:T(2,128)(2,1)S(1)}, bf16[8,2,1536]{2,1,0:T(2,128)(2,1)S(1)}, u32[]{:S(2)}, u32[]{:S(2)}) collective-permute-start(bf16[8,2,1536]{2,1,0:T(2,128)(2,1)S(1)} %pad_maximum_fusion.5), channel_id=1, source_target_pairs={{0,4},{1,5},{2,6},{3,7},{4,0},{5,1},{6,2},{7,3},{8,12},{9,13},{10,... | collective-permute-start | bytes 147464 | tf_op jit(solution)/shard_map/ppermute | solution.py:23
  13.3 10.4 %collective-permute-start.5 = (bf16[8,2,1536]{2,1,0:T(2,128)(2,1)S(1)}, bf16[8,2,1536]{2,1,0:T(2,128)(2,1)S(1)}, u32[]{:S(2)}, u32[]{:S(2)}) collective-permute-start(bf16[8,2,1536]{2,1,0:T(2,128)(2,1)S(1)} %pad_maximum_fusion.5), channel_id=1, source_target_pairs={{0,8},{1,9},{2,10},{3,11},{4,12},{5,13},{6,14},{7,15},{8,0},{9,1},... | collective-permute-start | bytes 147464 | tf_op jit(solution)/shard_map/ppermute | solution.py:23
  15.9 9.4 %collective-permute-start.6 = (bf16[8,2,1536]{2,1,0:T(2,128)(2,1)S(1)}, bf16[8,2,1536]{2,1,0:T(2,128)(2,1)S(1)}, u32[]{:S(2)}, u32[]{:S(2)}) collective-permute-start(bf16[8,2,1536]{2,1,0:T(2,128)(2,1)S(1)} %pad_maximum_fusion.5), channel_id=1, source_target_pairs={{0,12},{1,13},{2,14},{3,15},{4,8},{5,9},{6,10},{7,11},{8,4},{9,5},... | collective-permute-start | bytes 147464 | tf_op jit(solution)/shard_map/ppermute | solution.py:23
  21.7 6.4 %collective-permute-start = (bf16[128,2,1536]{2,1,0:T(2,128)(2,1)S(1)}, bf16[128,2,1536]{2,1,0:T(2,128)(2,1)S(1)}, u32[]{:S(2)}, u32[]{:S(2)}) collective-permute-start(bf16[128,2,1536]{2,1,0:T(2,128)(2,1)S(1)} %get-tuple-element.56), channel_id=1, source_target_pairs={{0,1},{1,0},{2,3},{3,2},{4,5},{5,4},{6,7},{7,6},{8,9},{9,8},{10,11... | collective-permute-start | bytes 2359304 | tf_op jit(solution)/shard_map/ppermute | solution.py:23
  23.8 18.1 %collective-permute-start.2 = (bf16[128,2,768]{2,1,0:T(2,128)(2,1)S(1)}, bf16[128,2,768]{2,1,0:T(2,128)(2,1)S(1)}, u32[]{:S(2)}, u32[]{:S(2)}) collective-permute-start(bf16[128,2,768]{2,1,0:T(2,128)(2,1)S(1)} %get-tuple-element.59), channel_id=1, source_target_pairs={{0,2},{2,0},{4,6},{6,4},{8,10},{10,8},{12,14},{14,12},{1,3},{3,1},... | collective-permute-start | bytes 1179656 | tf_op jit(solution)/shard_map/ppermute | solution.py:42
  25.6 1.5 %collective-permute-start.7 = (bf16[32,2,1536]{2,1,0:T(2,128)(2,1)S(1)}, bf16[32,2,1536]{2,1,0:T(2,128)(2,1)S(1)}, u32[]{:S(2)}, u32[]{:S(2)}) collective-permute-start(bf16[32,2,1536]{2,1,0:T(2,128)(2,1)S(1)} %pad_maximum_fusion.2), channel_id=1, source_target_pairs={{0,1},{1,0},{2,3},{3,2},{4,5},{5,4},{6,7},{7,6},{8,9},{9,8},{10,11... | collective-permute-start | bytes 589832 | tf_op jit(solution)/shard_map/ppermute | solution.py:23
  27.1 14.7 %collective-permute-start.3 = (bf16[128,2,768]{2,1,0:T(2,128)(2,1)S(1)}, bf16[128,2,768]{2,1,0:T(2,128)(2,1)S(1)}, u32[]{:S(2)}, u32[]{:S(2)}) collective-permute-start(bf16[128,2,768]{2,1,0:T(2,128)(2,1)S(1)} %get-tuple-element.60), channel_id=1, source_target_pairs={{2,4},{4,2},{6,8},{8,6},{10,12},{12,10},{3,5},{5,3},{7,9},{9,7},{1... | collective-permute-start | bytes 1179656 | tf_op jit(solution)/shard_map/ppermute | solution.py:42
  28.0 1.4 %copy-start.1 = (bf16[256,2,1536]{2,1,0:T(2,128)(2,1)S(1)}, bf16[256,2,1536]{2,1,0:T(2,128)(2,1)}, u32[]{:S(2)}) copy-start(bf16[256,2,1536]{2,1,0:T(2,128)(2,1)} %own_ref.3) | copy-start | bytes 4718596
  28.0 1.6 %copy-start.2 = (bf16[256,1536]{1,0:T(8,128)(2,1)S(1)}, bf16[256,1536]{1,0:T(8,128)(2,1)}, u32[]{:S(2)}) copy-start(bf16[256,1536]{1,0:T(8,128)(2,1)} %q_ref.3) | copy-start | bytes 2359300
  28.0 1.8 %copy-start.3 = (bf16[256,1536]{1,0:T(8,128)(2,1)S(1)}, bf16[256,1536]{1,0:T(8,128)(2,1)}, u32[]{:S(2)}) copy-start(bf16[256,1536]{1,0:T(8,128)(2,1)} %g_ref.3) | copy-start | bytes 2359300
  28.0 1.8 %copy-start.6 = (s32[1,2,5]{2,1,0:T(2,128)S(1)}, s32[1,2,5]{2,1,0:T(2,128)}, u32[]{:S(2)}) copy-start(s32[1,2,5]{2,1,0:T(2,128)} %param.15) | copy-start | bytes 124
  28.0 1.8 %copy-start.7 = (f32[12]{0:T(128)S(1)}, f32[12]{0:T(128)}, u32[]{:S(2)}) copy-start(f32[12]{0:T(128)} %warm_ref.3) | copy-start | bytes 148
  38.3 12.2 %copy-start.14 = (f32[6,512,128]{2,1,0:T(8,128)}, f32[6,512,128]{2,1,0:T(8,128)S(1)}, u32[]{:S(2)}) copy-start(f32[6,512,128]{2,1,0:T(8,128)S(1)} %get-tuple-element.82.own_ref) | copy-start | bytes 4718596
  38.3 19.6 %collective-permute-start.10 = (bf16[6,256,128]{2,1,0:T(8,128)(2,1)S(1)}, bf16[6,256,128]{2,1,0:T(8,128)(2,1)S(1)}, u32[]{:S(2)}, u32[]{:S(2)}) collective-permute-start(bf16[6,256,128]{2,1,0:T(8,128)(2,1)S(1)} %get-tuple-element.73), channel_id=1, source_target_pairs={{0,2},{2,0},{4,6},{6,4},{8,10},{10,8},{12,14},{14,12},{1,3},{3,1},... | collective-permute-start | bytes 1179656 | tf_op jit(solution)/shard_map/ppermute | solution.py:42
  41.1 16.8 %collective-permute-start.11 = (bf16[6,256,128]{2,1,0:T(8,128)(2,1)S(1)}, bf16[6,256,128]{2,1,0:T(8,128)(2,1)S(1)}, u32[]{:S(2)}, u32[]{:S(2)}) collective-permute-start(bf16[6,256,128]{2,1,0:T(8,128)(2,1)S(1)} %get-tuple-element.74), channel_id=1, source_target_pairs={{2,4},{4,2},{6,8},{8,6},{10,12},{12,10},{3,5},{5,3},{7,9},{9,7},{1... | collective-permute-start | bytes 1179656 | tf_op jit(solution)/shard_map/ppermute | solution.py:42
  41.8 16.2 %collective-permute-start.12 = (bf16[6,256,128]{2,1,0:T(8,128)(2,1)S(1)}, bf16[6,256,128]{2,1,0:T(8,128)(2,1)S(1)}, u32[]{:S(2)}, u32[]{:S(2)}) collective-permute-start(bf16[6,256,128]{2,1,0:T(8,128)(2,1)S(1)} %get-tuple-element.75), channel_id=1, source_target_pairs={{0,1},{1,0},{2,3},{3,2},{4,5},{5,4},{6,7},{7,6},{8,9},{9,8},{10,11... | collective-permute-start | bytes 1179656 | tf_op jit(solution)/shard_map/ppermute | solution.py:23
  57.9 3.8 %copy-start.8 = (bf16[6,256,128]{2,1,0:T(8,128)(2,1)}, bf16[6,256,128]{2,1,0:T(8,128)(2,1)S(1)}, u32[]{:S(2)}) copy-start(bf16[6,256,128]{2,1,0:T(8,128)(2,1)S(1)} %collective-permute-done.10.dir_ref) | copy-start | bytes 1179652
  57.9 3.8 %copy-start.10 = (bf16[6,256,128]{2,1,0:T(8,128)(2,1)}, bf16[6,256,128]{2,1,0:T(8,128)(2,1)S(1)}, u32[]{:S(2)}) copy-start(bf16[6,256,128]{2,1,0:T(8,128)(2,1)S(1)} %collective-permute-done.11.dia_ref) | copy-start | bytes 1179652
  57.9 3.8 %copy-start.12 = (bf16[6,256,128]{2,1,0:T(8,128)(2,1)}, bf16[6,256,128]{2,1,0:T(8,128)(2,1)S(1)}, u32[]{:S(2)}) copy-start(bf16[6,256,128]{2,1,0:T(8,128)(2,1)S(1)} %collective-permute-done.12.par_ref) | copy-start | bytes 1179652
  58.0 3.1 %collective-permute-start.13 = (f32[64,1664]{1,0:T(8,128)S(1)}, f32[64,1664]{1,0:T(8,128)S(1)}, u32[]{:S(2)}, u32[]{:S(2)}) collective-permute-start(f32[64,1664]{1,0:T(8,128)S(1)} %pad_maximum_fusion), channel_id=1, source_target_pairs={{0,1},{1,0},{2,3},{3,2},{4,5},{5,4},{6,7},{7,6},{8,9},{9,8},{10,11... | collective-permute-start | bytes 1277960 | tf_op jit(solution)/shard_map/ppermute | solution.py:23
  58.1 5.0 %collective-permute-start.14 = (bf16[6,256,128]{2,1,0:T(8,128)(2,1)}, bf16[6,256,128]{2,1,0:T(8,128)(2,1)S(1)}, u32[]{:S(2)}, u32[]{:S(2)}) collective-permute-start(bf16[6,256,128]{2,1,0:T(8,128)(2,1)} %get-tuple-element.80), channel_id=1, source_target_pairs={{0,1},{1,0},{2,3},{3,2},{4,5},{5,4},{6,7},{7,6},{8,9},{9,8},{10,11... | collective-permute-start | bytes 1179656 | tf_op jit(solution)/shard_map/ppermute | solution.py:23
  58.6 21.9 %collective-permute-start.18 = (bf16[6,256,128]{2,1,0:T(8,128)(2,1)}, bf16[6,256,128]{2,1,0:T(8,128)(2,1)S(1)}, u32[]{:S(2)}, u32[]{:S(2)}) collective-permute-start(bf16[6,256,128]{2,1,0:T(8,128)(2,1)} %get-tuple-element.88), channel_id=1, source_target_pairs={{0,2},{2,0},{4,6},{6,4},{8,10},{10,8},{12,14},{14,12},{1,3},{3,1},... | collective-permute-start | bytes 1179656 | tf_op jit(solution)/shard_map/ppermute | solution.py:42
  61.1 0.8 copy-start.16
  63.0 10.3 %copy-start.5 = (s32[1,3,1]{1,2,0:T(1,128)S(1)}, s32[1,3,1]{1,2,0:T(1,128)}, u32[]{:S(2)}) copy-start(s32[1,3,1]{1,2,0:T(1,128)} %param.14) | copy-start | bytes 40
  63.1 10.3 %copy-start.9 = (bf16[6,256,128]{2,1,0:T(8,128)(2,1)S(1)}, bf16[6,256,128]{2,1,0:T(8,128)(2,1)}, u32[]{:S(2)}) copy-start(bf16[6,256,128]{2,1,0:T(8,128)(2,1)} %copy-done.8) | copy-start | bytes 1179652
  63.1 10.3 %copy-start.11 = (bf16[6,256,128]{2,1,0:T(8,128)(2,1)S(1)}, bf16[6,256,128]{2,1,0:T(8,128)(2,1)}, u32[]{:S(2)}) copy-start(bf16[6,256,128]{2,1,0:T(8,128)(2,1)} %copy-done.10) | copy-start | bytes 1179652
  63.1 10.3 %copy-start.13 = (bf16[6,256,128]{2,1,0:T(8,128)(2,1)S(1)}, bf16[6,256,128]{2,1,0:T(8,128)(2,1)}, u32[]{:S(2)}) copy-start(bf16[6,256,128]{2,1,0:T(8,128)(2,1)} %copy-done.12) | copy-start | bytes 1179652
  63.1 10.3 %copy-start.15 = (f32[6,512,128]{2,1,0:T(8,128)S(1)}, f32[6,512,128]{2,1,0:T(8,128)}, u32[]{:S(2)}) copy-start(f32[6,512,128]{2,1,0:T(8,128)} %copy-done.14) | copy-start | bytes 4718596
  63.1 7.3 %collective-permute-start.15 = (f32[32,1664]{1,0:T(8,128)S(1)}, f32[32,1664]{1,0:T(8,128)S(1)}, u32[]{:S(2)}, u32[]{:S(2)}) collective-permute-start(f32[32,1664]{1,0:T(8,128)S(1)} %pad_maximum_fusion.1), channel_id=1, source_target_pairs={{0,4},{1,5},{2,6},{3,7},{4,0},{5,1},{6,2},{7,3},{8,12},{9,13},{10,... | collective-permute-start | bytes 638984 | tf_op jit(solution)/shard_map/ppermute | solution.py:23
  70.5 7.5 %collective-permute-start.16 = (f32[16,1664]{1,0:T(8,128)S(1)}, f32[16,1664]{1,0:T(8,128)S(1)}, u32[]{:S(2)}, u32[]{:S(2)}) collective-permute-start(f32[16,1664]{1,0:T(8,128)S(1)} %pad_maximum_fusion.3), channel_id=1, source_target_pairs={{0,8},{1,9},{2,10},{3,11},{4,12},{5,13},{6,14},{7,15},{8,0},{9,1},... | collective-permute-start | bytes 319496 | tf_op jit(solution)/shard_map/ppermute | solution.py:23
  75.5 5.0 %collective-permute-start.19 = (bf16[6,256,128]{2,1,0:T(8,128)(2,1)S(1)}, bf16[6,256,128]{2,1,0:T(8,128)(2,1)S(1)}, u32[]{:S(2)}, u32[]{:S(2)}) collective-permute-start(bf16[6,256,128]{2,1,0:T(8,128)(2,1)S(1)} %get-tuple-element.89), channel_id=1, source_target_pairs={{2,4},{4,2},{6,8},{8,6},{10,12},{12,10},{3,5},{5,3},{7,9},{9,7},{1... | collective-permute-start | bytes 1179656 | tf_op jit(solution)/shard_map/ppermute | solution.py:42
  78.0 10.6 %collective-permute-start.17 = (f32[8,1664]{1,0:T(8,128)S(1)}, f32[8,1664]{1,0:T(8,128)S(1)}, u32[]{:S(2)}, u32[]{:S(2)}) collective-permute-start(f32[8,1664]{1,0:T(8,128)S(1)} %pad_maximum_fusion.4), channel_id=1, source_target_pairs={{0,2},{1,3},{2,0},{3,1},{4,6},{5,7},{6,4},{7,5},{8,10},{9,11},{10,... | collective-permute-start | bytes 159752 | tf_op jit(solution)/shard_map/ppermute | solution.py:23

commit v15 on v13

--- a/solution.py
+++ b/solution.py
@@ -303,13 +303,13 @@
         total = total + ref[:, :feat]
         temp = temp + ref[:1, feat:]
     out_ref[...] = total.reshape(out_ref.shape)
-    sum_ref[...] = temp
-
-
-def finish(own, temp, got, shape):
+    sum_ref[...] = temp[:, : sum_ref.shape[1]]
+
+
+def finish(own, temp, got, shape, total):
     return pl.pallas_call(
         finish_kernel,
-        out_shape=[jax.ShapeDtypeStruct(shape, F32), jax.ShapeDtypeStruct(temp.shape, F32)],
+        out_shape=[jax.ShapeDtypeStruct(shape, F32), jax.ShapeDtypeStruct((1, total), F32)],
         compiler_params=pltpu.CompilerParams(vmem_limit_bytes=8 << 20),
         name="finish",
     )(own, temp, *got)
@@ -379,11 +379,11 @@
             cell = combine(pos, sent, owns[-2], returned[-2], *chunks[-2], feat, width, cell, weight=4000)
             cell = combine(pos, sent, owns[-1], returned[-1], *chunks[-1], feat, width, cell, weight=0)
             got, cell = lax.optimization_barrier((got, cell))
-            anchor_grad, temp = finish(mine, extra, [got], landmark.shape)
+            anchor_grad, temp = finish(mine, extra, [got], landmark.shape, total)
             break
         anc = mine + got[:, :feat]
         extra = extra + got[:1, feat:]
-    return (dq, cell, anchor_grad, temp[0, :total])
+    return (dq, cell, anchor_grad, temp.reshape(total))
 
 
 def solution(mesh):

time: 88 us -> 87.5 us (level)
  transfers between devices with their start and end apart: 20 -> 20, of which waited for: 7 -> 7; matrix products, arithmetic and copies ran while one was open for 5% -> 5% of each run, Pallas kernels for 26% -> 27%
where the time goes in v15:
time: 87.5 us; the launch traced here: 86.3 us
  waiting for transfers between devices  30 us (34%)
  starting transfers between devices  23.5 us (27%)
  Pallas kernels  23.5 us (27%)
  local copies, waits for them, and re-layouts  4.47 us (5%)
  other arithmetic  3.65 us (4%)
  between operations  1.08 us (1%)
    ppermute x12, waiting for transfers between devices, swap_mask(): return lax.ppermute(x, ('gx', 'gy'), [(i, i ^ mask) for i in range(count)])  23.5 us
    pallas_call x2, Pallas kernels, attention(): pl.pallas_call(functools.partial(attention_kernel, gx_count=lax.axis_size...  17.1 us
    ppermute x12, starting transfers between devices, swap_mask(): return lax.ppermute(x, ('gx', 'gy'), [(i, i ^ mask) for i in range(count)])  15.5 us
    ppermute x8, starting transfers between devices, swap_pairs(): return lax.ppermute(x, 'gx', route)  8.01 us
    ppermute x8, waiting for transfers between devices, swap_pairs(): return lax.ppermute(x, 'gx', route)  6.55 us
    pallas_call x2, Pallas kernels, combine(): pl.pallas_call(combine_kernel, grid=(heads // step,), in_specs=in_specs,...  4.36 us
    unnamed x40, local copies, waits for them, and re-layouts  4.12 us
  transfers between devices with their start and end apart: 20, of which 7 were waited for; matrix products, arithmetic and copies ran while one was open for 5% of the time, Pallas kernels for 27%

profile of v15, /device:TPU:0, one launch (start us, length us, event | category | flops | bytes accessed | tf_op | source)
XLA Modules:
  0.0 86.3 jit_solution(3114770690581901309)
XLA Ops:
  0.6 3.0 %collective-permute-start.1 = (bf16[4,2,1536]{2,1,0:T(2,128)(2,1)}, bf16[4,2,1536]{2,1,0:T(2,128)(2,1)S(1)}, u32[]{:S(2)}, u32[]{:S(2)}) collective-permute-start(bf16[4,2,1536]{2,1,0:T(2,128)(2,1)} %param.11), channel_id=1, source_target_pairs={{0,2},{1,3},{2,0},{3,1},{4,6},{5,7},{6,4},{7,5},{8,10},{9,11},{10,... | collective-permute-start | bytes 73736 | tf_op jit(solution)/shard_map/ppermute | solution.py:23
  3.6 1.4 %copy-done = bf16[256,2,1536]{2,1,0:T(2,128)(2,1)S(1)} copy-done((bf16[256,2,1536]{2,1,0:T(2,128)(2,1)S(1)}, bf16[256,2,1536]{2,1,0:T(2,128)(2,1)}, u32[]{:S(2)}) %copy-start) | copy-done | bytes 1572888
  5.0 0.7 copy-done.4
  5.7 0.7 pick.3
  6.4 0.1 collective-permute-start.8
  6.5 0.7 collective-permute-start.9
  7.1 0.7 pick.2
  7.9 0.6 compare_reduce_fusion
  8.5 0.1 pad_maximum_fusion.5
  8.6 4.8 %collective-permute-start.4 = (bf16[8,2,1536]{2,1,0:T(2,128)(2,1)S(1)}, bf16[8,2,1536]{2,1,0:T(2,128)(2,1)S(1)}, u32[]{:S(2)}, u32[]{:S(2)}) collective-permute-start(bf16[8,2,1536]{2,1,0:T(2,128)(2,1)S(1)} %pad_maximum_fusion.5), channel_id=1, source_target_pairs={{0,4},{1,5},{2,6},{3,7},{4,0},{5,1},{6,2},{7,3},{8,12},{9,13},{10,... | collective-permute-start | bytes 147464 | tf_op jit(solution)/shard_map/ppermute | solution.py:23
  13.3 2.6 %collective-permute-start.5 = (bf16[8,2,1536]{2,1,0:T(2,128)(2,1)S(1)}, bf16[8,2,1536]{2,1,0:T(2,128)(2,1)S(1)}, u32[]{:S(2)}, u32[]{:S(2)}) collective-permute-start(bf16[8,2,1536]{2,1,0:T(2,128)(2,1)S(1)} %pad_maximum_fusion.5), channel_id=1, source_target_pairs={{0,8},{1,9},{2,10},{3,11},{4,12},{5,13},{6,14},{7,15},{8,0},{9,1},... | collective-permute-start | bytes 147464 | tf_op jit(solution)/shard_map/ppermute | solution.py:23
  16.0 5.7 %collective-permute-done.4 = bf16[8,2,1536]{2,1,0:T(2,128)(2,1)S(1)} collective-permute-done((bf16[8,2,1536]{2,1,0:T(2,128)(2,1)S(1)}, bf16[8,2,1536]{2,1,0:T(2,128)(2,1)S(1)}, u32[]{:S(2)}, u32[]{:S(2)}) %collective-permute-start.4) | collective-permute-done | bytes 49184 | tf_op jit(solution)/shard_map/ppermute | solution.py:23
  21.7 2.1 %collective-permute-done.5 = bf16[8,2,1536]{2,1,0:T(2,128)(2,1)S(1)} collective-permute-done((bf16[8,2,1536]{2,1,0:T(2,128)(2,1)S(1)}, bf16[8,2,1536]{2,1,0:T(2,128)(2,1)S(1)}, u32[]{:S(2)}, u32[]{:S(2)}) %collective-permute-start.5) | collective-permute-done | bytes 49184 | tf_op jit(solution)/shard_map/ppermute | solution.py:23
  23.8 1.6 %collective-permute-done.6 = bf16[8,2,1536]{2,1,0:T(2,128)(2,1)S(1)} collective-permute-done((bf16[8,2,1536]{2,1,0:T(2,128)(2,1)S(1)}, bf16[8,2,1536]{2,1,0:T(2,128)(2,1)S(1)}, u32[]{:S(2)}, u32[]{:S(2)}) %collective-permute-start.6) | collective-permute-done | bytes 49184 | tf_op jit(solution)/shard_map/ppermute | solution.py:23
  25.3 0.3 pad_maximum_fusion.2
  25.6 0.1 collective-permute-start.7
  25.9 1.3 %collective-permute-done.7 = bf16[32,2,1536]{2,1,0:T(2,128)(2,1)S(1)} collective-permute-done((bf16[32,2,1536]{2,1,0:T(2,128)(2,1)S(1)}, bf16[32,2,1536]{2,1,0:T(2,128)(2,1)S(1)}, u32[]{:S(2)}, u32[]{:S(2)}) %collective-permute-start.7) | collective-permute-done | bytes 196640 | tf_op jit(solution)/shard_map/ppermute | solution.py:23
  27.1 0.7 collective-permute-start.3
  27.8 0.2 constant_dynamic-update-slice_fusion.anc_ref
  28.0 0.0 copy-start.1
  28.0 0.0 copy-start.2
  28.1 1.3 %copy-done.1 = bf16[256,2,1536]{2,1,0:T(2,128)(2,1)S(1)} copy-done((bf16[256,2,1536]{2,1,0:T(2,128)(2,1)S(1)}, bf16[256,2,1536]{2,1,0:T(2,128)(2,1)}, u32[]{:S(2)}) %copy-start.1) | copy-done | bytes 1572888
  29.4 0.2 copy-done.2
  29.6 0.2 copy-done.3
  29.8 8.5 %attention.2 = (bf16[256,1536]{1,0:T(8,128)(2,1)}, f32[6,512,128]{2,1,0:T(8,128)S(1)}, bf16[6,256,128]{2,1,0:T(8,128)(2,1)S(1)}, bf16[6,256,128]{2,1,0:T(8,128)(...) custom-call(s32[1]{0:T(128)} %bitcast.pos_ref, ...), custom_call_target="tpu_custom_call" | custom-call | flops 1384120320 | bytes 6488064 | tf_op jit(solution)/shard_map/attention/pallas_call | solution.py:213
  38.3 2.7 %collective-permute-start.10 = (bf16[6,256,128]{2,1,0:T(8,128)(2,1)S(1)}, bf16[6,256,128]{2,1,0:T(8,128)(2,1)S(1)}, u32[]{:S(2)}, u32[]{:S(2)}) collective-permute-start(bf16[6,256,128]{2,1,0:T(8,128)(2,1)S(1)} %get-tuple-element.71), channel_id=1, source_target_pairs={{0,2},{2,0},{4,6},{6,4},{8,10},{10,8},{12,14},{14,12},{1,3},{3,1},... | collective-permute-start | bytes 1179656 | tf_op jit(solution)/shard_map/ppermute | solution.py:42
  41.1 0.7 collective-permute-start.11
  41.8 0.1 collective-permute-start.12
  41.9 8.6 %attention.3 = (bf16[256,1536]{1,0:T(8,128)(2,1)}, f32[6,512,128]{2,1,0:T(8,128)S(1)}, bf16[6,256,128]{2,1,0:T(8,128)(2,1)}, bf16[6,256,128]{2,1,0:T(8,128)(2,1)...) custom-call(s32[1]{0:T(128)} %bitcast.pos_ref, ...), custom_call_target="tpu_custom_call", output_to_operand_aliasing={{0}: (10, {}), {5}: (11, {})} | custom-call | flops 1384120320 | bytes 6488064 | tf_op jit(solution)/shard_map/attention/pallas_call | solution.py:213
  50.5 0.2 maximum_reduce_fusion
  50.7 0.6 fusion
  51.4 6.5 %collective-permute-done.10.dir_ref = bf16[6,256,128]{2,1,0:T(8,128)(2,1)S(1)} collective-permute-done((bf16[6,256,128]{2,1,0:T(8,128)(2,1)S(1)}, bf16[6,256,128]{2,1,0:T(8,128)(2,1)S(1)}, u32[]{:S(2)}, u32[]{:S(2)}) %collective-permute-start.10) | collective-permute-done | bytes 393248 | tf_op jit(solution)/shard_map/ppermute | solution.py:42
  58.0 0.1 collective-permute-start.13
  58.1 0.5 collective-permute-start.14
  58.6 2.5 %collective-permute-start.18 = (bf16[6,256,128]{2,1,0:T(8,128)(2,1)}, bf16[6,256,128]{2,1,0:T(8,128)(2,1)S(1)}, u32[]{:S(2)}, u32[]{:S(2)}) collective-permute-start(bf16[6,256,128]{2,1,0:T(8,128)(2,1)} %get-tuple-element.81), channel_id=1, source_target_pairs={{0,2},{2,0},{4,6},{6,4},{8,10},{10,8},{12,14},{14,12},{1,3},{3,1},... | collective-permute-start | bytes 1179656 | tf_op jit(solution)/shard_map/ppermute | solution.py:42
  61.1 0.7 slice_add_fusion.5
  61.8 0.1 copy-done.16
  61.8 0.1 add.24.refs_0_
  61.9 1.0 %slice_add_fusion = f32[64,1536]{1,0:T(8,128)S(1)} fusion(f32[64,1664]{1,0:T(8,128)} %copy-done.16, f32[128,1536]{1,0:T(8,128)S(1)} %get-tuple-element.74), kind=kLoop, calls=%fused_computation.1 | loop fusion | flops 98304 | bytes 1179648 | tf_op jit(solution)/shard_map/add | solution.py:384
  63.1 1.7 %collective-permute-start.15 = (f32[32,1664]{1,0:T(8,128)S(1)}, f32[32,1664]{1,0:T(8,128)S(1)}, u32[]{:S(2)}, u32[]{:S(2)}) collective-permute-start(f32[32,1664]{1,0:T(8,128)S(1)} %pad_maximum_fusion.1), channel_id=1, source_target_pairs={{0,4},{1,5},{2,6},{3,7},{4,0},{5,1},{6,2},{7,3},{8,12},{9,13},{10,... | collective-permute-start | bytes 638984 | tf_op jit(solution)/shard_map/ppermute | solution.py:23
  64.8 0.7 collective-permute-start.19
  65.5 5.8 %collective-permute-done.15 = f32[32,1664]{1,0:T(8,128)S(1)} collective-permute-done((f32[32,1664]{1,0:T(8,128)S(1)}, f32[32,1664]{1,0:T(8,128)S(1)}, u32[]{:S(2)}, u32[]{:S(2)}) %collective-permute-start.15) | collective-permute-done | bytes 213024 | tf_op jit(solution)/shard_map/ppermute | solution.py:23
  71.4 2.7 %collective-permute-start.16 = (f32[16,1664]{1,0:T(8,128)S(1)}, f32[16,1664]{1,0:T(8,128)S(1)}, u32[]{:S(2)}, u32[]{:S(2)}) collective-permute-start(f32[16,1664]{1,0:T(8,128)S(1)} %pad_maximum_fusion.3), channel_id=1, source_target_pairs={{0,8},{1,9},{2,10},{3,11},{4,12},{5,13},{6,14},{7,15},{8,0},{9,1},... | collective-permute-start | bytes 319496 | tf_op jit(solution)/shard_map/ppermute | solution.py:23
  74.0 7.0 %collective-permute-done.16 = f32[16,1664]{1,0:T(8,128)S(1)} collective-permute-done((f32[16,1664]{1,0:T(8,128)S(1)}, f32[16,1664]{1,0:T(8,128)S(1)}, u32[]{:S(2)}, u32[]{:S(2)}) %collective-permute-start.16) | collective-permute-done | bytes 106528 | tf_op jit(solution)/shard_map/ppermute | solution.py:23
  81.2 0.1 collective-permute-start.17
  81.3 2.2 %combine.2.rest_0_ = bf16[256,2,1536]{2,1,0:T(2,128)(2,1)} custom-call(s32[1]{0:T(128)} %bitcast.pos_ref, s32[3]{0:T(128)S(1)} %bitcast.23, f32[6,512,128]{2,1,0:T(8,128)S(1)} %copy-done.15, bf16[6,256,128]{2,1,0:T(8,128)(2,1)S(1)} %collective-permute-done.10.dir_ref, bf16[6,256,128]{2,1,0:T(8,128)(2,1)S(1)} %copy-done.9, bf16[6,256,128]{2,1,0:T(8,128)(2,1)S(1)} %copy-done.11), custom_call_target="tpu_custom_call" | custom-call | flops 12582912000 | bytes 3538944 | tf_op jit(solution)/shard_map/combine/pallas_call | solution.py:281
  83.5 2.2 %combine.3 = bf16[256,2,1536]{2,1,0:T(2,128)(2,1)} custom-call(s32[1]{0:T(128)} %bitcast.pos_ref, s32[3]{0:T(128)S(1)} %bitcast.24, f32[6,512,128]{2,1,0:T(8,128)S(1)} %get-tuple-element.80.own_ref, bf16[6,256,128]{2,1,0:T(8,128)(2,1)S(1)} %collective-permute-done.18.dir_ref, ...), custom_call_target="tpu_custom_call", output_to_operand_aliasing={{}: (6, {})} | custom-call | bytes 3538944 | tf_op jit(solution)/shard_map/combine/pallas_call | solution.py:281
  85.6 0.6 finish.1
  (69 shorter events, 0.5 us)
Async XLA Ops:
  0.6 7.9 %collective-permute-start.1 = (bf16[4,2,1536]{2,1,0:T(2,128)(2,1)}, bf16[4,2,1536]{2,1,0:T(2,128)(2,1)S(1)}, u32[]{:S(2)}, u32[]{:S(2)}) collective-permute-start(bf16[4,2,1536]{2,1,0:T(2,128)(2,1)} %param.11), channel_id=1, source_target_pairs={{0,2},{1,3},{2,0},{3,1},{4,6},{5,7},{6,4},{7,5},{8,10},{9,11},{10,... | collective-permute-start | bytes 73736 | tf_op jit(solution)/shard_map/ppermute | solution.py:23
  3.6 1.4 %copy-start = (bf16[256,2,1536]{2,1,0:T(2,128)(2,1)S(1)}, bf16[256,2,1536]{2,1,0:T(2,128)(2,1)}, u32[]{:S(2)}) copy-start(bf16[256,2,1536]{2,1,0:T(2,128)(2,1)} %own_ref.3) | copy-start | bytes 4718596
  5.0 0.7 copy-start.4
  5.7 2.8 %copy-start.17 = (bf16[4,2,1536]{2,1,0:T(2,128)(2,1)S(1)}, bf16[4,2,1536]{2,1,0:T(2,128)(2,1)}, u32[]{:S(2)}) copy-start(bf16[4,2,1536]{2,1,0:T(2,128)(2,1)} %param.11) | copy-start | bytes 73732
  6.4 21.7 %collective-permute-start.8 = (bf16[128,2,768]{2,1,0:T(2,128)(2,1)S(1)}, bf16[128,2,768]{2,1,0:T(2,128)(2,1)S(1)}, u32[]{:S(2)}, u32[]{:S(2)}) collective-permute-start(bf16[128,2,768]{2,1,0:T(2,128)(2,1)S(1)} %get-tuple-element.60), channel_id=1, source_target_pairs={{0,2},{2,0},{4,6},{6,4},{8,10},{10,8},{12,14},{14,12},{1,3},{3,1},... | collective-permute-start | bytes 1179656 | tf_op jit(solution)/shard_map/ppermute | solution.py:42
  6.5 21.6 %collective-permute-start.9 = (bf16[128,2,768]{2,1,0:T(2,128)(2,1)S(1)}, bf16[128,2,768]{2,1,0:T(2,128)(2,1)S(1)}, u32[]{:S(2)}, u32[]{:S(2)}) collective-permute-start(bf16[128,2,768]{2,1,0:T(2,128)(2,1)S(1)} %get-tuple-element.61), channel_id=1, source_target_pairs={{2,4},{4,2},{6,8},{8,6},{10,12},{12,10},{3,5},{5,3},{7,9},{9,7},{1... | collective-permute-start | bytes 1179656 | tf_op jit(solution)/shard_map/ppermute | solution.py:42
  8.6 13.1 %collective-permute-start.4 = (bf16[8,2,1536]{2,1,0:T(2,128)(2,1)S(1)}, bf16[8,2,1536]{2,1,0:T(2,128)(2,1)S(1)}, u32[]{:S(2)}, u32[]{:S(2)}) collective-permute-start(bf16[8,2,1536]{2,1,0:T(2,128)(2,1)S(1)} %pad_maximum_fusion.5), channel_id=1, source_target_pairs={{0,4},{1,5},{2,6},{3,7},{4,0},{5,1},{6,2},{7,3},{8,12},{9,13},{10,... | collective-permute-start | bytes 147464 | tf_op jit(solution)/shard_map/ppermute | solution.py:23
  13.3 10.4 %collective-permute-start.5 = (bf16[8,2,1536]{2,1,0:T(2,128)(2,1)S(1)}, bf16[8,2,1536]{2,1,0:T(2,128)(2,1)S(1)}, u32[]{:S(2)}, u32[]{:S(2)}) collective-permute-start(bf16[8,2,1536]{2,1,0:T(2,128)(2,1)S(1)} %pad_maximum_fusion.5), channel_id=1, source_target_pairs={{0,8},{1,9},{2,10},{3,11},{4,12},{5,13},{6,14},{7,15},{8,0},{9,1},... | collective-permute-start | bytes 147464 | tf_op jit(solution)/shard_map/ppermute | solution.py:23
  15.9 9.4 %collective-permute-start.6 = (bf16[8,2,1536]{2,1,0:T(2,128)(2,1)S(1)}, bf16[8,2,1536]{2,1,0:T(2,128)(2,1)S(1)}, u32[]{:S(2)}, u32[]{:S(2)}) collective-permute-start(bf16[8,2,1536]{2,1,0:T(2,128)(2,1)S(1)} %pad_maximum_fusion.5), channel_id=1, source_target_pairs={{0,12},{1,13},{2,14},{3,15},{4,8},{5,9},{6,10},{7,11},{8,4},{9,5},... | collective-permute-start | bytes 147464 | tf_op jit(solution)/shard_map/ppermute | solution.py:23
  21.7 6.4 %collective-permute-start = (bf16[128,2,1536]{2,1,0:T(2,128)(2,1)S(1)}, bf16[128,2,1536]{2,1,0:T(2,128)(2,1)S(1)}, u32[]{:S(2)}, u32[]{:S(2)}) collective-permute-start(bf16[128,2,1536]{2,1,0:T(2,128)(2,1)S(1)} %get-tuple-element.54), channel_id=1, source_target_pairs={{0,1},{1,0},{2,3},{3,2},{4,5},{5,4},{6,7},{7,6},{8,9},{9,8},{10,11... | collective-permute-start | bytes 2359304 | tf_op jit(solution)/shard_map/ppermute | solution.py:23
  23.8 18.1 %collective-permute-start.2 = (bf16[128,2,768]{2,1,0:T(2,128)(2,1)S(1)}, bf16[128,2,768]{2,1,0:T(2,128)(2,1)S(1)}, u32[]{:S(2)}, u32[]{:S(2)}) collective-permute-start(bf16[128,2,768]{2,1,0:T(2,128)(2,1)S(1)} %get-tuple-element.57), channel_id=1, source_target_pairs={{0,2},{2,0},{4,6},{6,4},{8,10},{10,8},{12,14},{14,12},{1,3},{3,1},... | collective-permute-start | bytes 1179656 | tf_op jit(solution)/shard_map/ppermute | solution.py:42
  25.6 1.5 %collective-permute-start.7 = (bf16[32,2,1536]{2,1,0:T(2,128)(2,1)S(1)}, bf16[32,2,1536]{2,1,0:T(2,128)(2,1)S(1)}, u32[]{:S(2)}, u32[]{:S(2)}) collective-permute-start(bf16[32,2,1536]{2,1,0:T(2,128)(2,1)S(1)} %pad_maximum_fusion.2), channel_id=1, source_target_pairs={{0,1},{1,0},{2,3},{3,2},{4,5},{5,4},{6,7},{7,6},{8,9},{9,8},{10,11... | collective-permute-start | bytes 589832 | tf_op jit(solution)/shard_map/ppermute | solution.py:23
  27.1 14.7 %collective-permute-start.3 = (bf16[128,2,768]{2,1,0:T(2,128)(2,1)S(1)}, bf16[128,2,768]{2,1,0:T(2,128)(2,1)S(1)}, u32[]{:S(2)}, u32[]{:S(2)}) collective-permute-start(bf16[128,2,768]{2,1,0:T(2,128)(2,1)S(1)} %get-tuple-element.58), channel_id=1, source_target_pairs={{2,4},{4,2},{6,8},{8,6},{10,12},{12,10},{3,5},{5,3},{7,9},{9,7},{1... | collective-permute-start | bytes 1179656 | tf_op jit(solution)/shard_map/ppermute | solution.py:42
  28.0 1.4 %copy-start.1 = (bf16[256,2,1536]{2,1,0:T(2,128)(2,1)S(1)}, bf16[256,2,1536]{2,1,0:T(2,128)(2,1)}, u32[]{:S(2)}) copy-start(bf16[256,2,1536]{2,1,0:T(2,128)(2,1)} %own_ref.3) | copy-start | bytes 4718596
  28.0 1.6 %copy-start.2 = (bf16[256,1536]{1,0:T(8,128)(2,1)S(1)}, bf16[256,1536]{1,0:T(8,128)(2,1)}, u32[]{:S(2)}) copy-start(bf16[256,1536]{1,0:T(8,128)(2,1)} %q_ref.3) | copy-start | bytes 2359300
  28.0 1.8 %copy-start.3 = (bf16[256,1536]{1,0:T(8,128)(2,1)S(1)}, bf16[256,1536]{1,0:T(8,128)(2,1)}, u32[]{:S(2)}) copy-start(bf16[256,1536]{1,0:T(8,128)(2,1)} %g_ref.3) | copy-start | bytes 2359300
  28.0 1.8 %copy-start.6 = (s32[1,2,5]{2,1,0:T(2,128)S(1)}, s32[1,2,5]{2,1,0:T(2,128)}, u32[]{:S(2)}) copy-start(s32[1,2,5]{2,1,0:T(2,128)} %param.15) | copy-start | bytes 124
  28.0 1.8 %copy-start.7 = (f32[12]{0:T(128)S(1)}, f32[12]{0:T(128)}, u32[]{:S(2)}) copy-start(f32[12]{0:T(128)} %warm_ref.3) | copy-start | bytes 148
  38.3 12.2 %copy-start.14 = (f32[6,512,128]{2,1,0:T(8,128)}, f32[6,512,128]{2,1,0:T(8,128)S(1)}, u32[]{:S(2)}) copy-start(f32[6,512,128]{2,1,0:T(8,128)S(1)} %get-tuple-element.84.own_ref) | copy-start | bytes 4718596
  38.3 19.6 %collective-permute-start.10 = (bf16[6,256,128]{2,1,0:T(8,128)(2,1)S(1)}, bf16[6,256,128]{2,1,0:T(8,128)(2,1)S(1)}, u32[]{:S(2)}, u32[]{:S(2)}) collective-permute-start(bf16[6,256,128]{2,1,0:T(8,128)(2,1)S(1)} %get-tuple-element.71), channel_id=1, source_target_pairs={{0,2},{2,0},{4,6},{6,4},{8,10},{10,8},{12,14},{14,12},{1,3},{3,1},... | collective-permute-start | bytes 1179656 | tf_op jit(solution)/shard_map/ppermute | solution.py:42
  41.1 16.8 %collective-permute-start.11 = (bf16[6,256,128]{2,1,0:T(8,128)(2,1)S(1)}, bf16[6,256,128]{2,1,0:T(8,128)(2,1)S(1)}, u32[]{:S(2)}, u32[]{:S(2)}) collective-permute-start(bf16[6,256,128]{2,1,0:T(8,128)(2,1)S(1)} %get-tuple-element.72), channel_id=1, source_target_pairs={{2,4},{4,2},{6,8},{8,6},{10,12},{12,10},{3,5},{5,3},{7,9},{9,7},{1... | collective-permute-start | bytes 1179656 | tf_op jit(solution)/shard_map/ppermute | solution.py:42
  41.8 16.1 %collective-permute-start.12 = (bf16[6,256,128]{2,1,0:T(8,128)(2,1)S(1)}, bf16[6,256,128]{2,1,0:T(8,128)(2,1)S(1)}, u32[]{:S(2)}, u32[]{:S(2)}) collective-permute-start(bf16[6,256,128]{2,1,0:T(8,128)(2,1)S(1)} %get-tuple-element.73), channel_id=1, source_target_pairs={{0,1},{1,0},{2,3},{3,2},{4,5},{5,4},{6,7},{7,6},{8,9},{9,8},{10,11... | collective-permute-start | bytes 1179656 | tf_op jit(solution)/shard_map/ppermute | solution.py:23
  50.5 11.2 %copy-start.12 = (bf16[6,256,128]{2,1,0:T(8,128)(2,1)}, bf16[6,256,128]{2,1,0:T(8,128)(2,1)S(1)}, u32[]{:S(2)}) copy-start(bf16[6,256,128]{2,1,0:T(8,128)(2,1)S(1)} %get-tuple-element.82) | copy-start | bytes 1179652
  57.9 3.8 %copy-start.8 = (bf16[6,256,128]{2,1,0:T(8,128)(2,1)}, bf16[6,256,128]{2,1,0:T(8,128)(2,1)S(1)}, u32[]{:S(2)}) copy-start(bf16[6,256,128]{2,1,0:T(8,128)(2,1)S(1)} %collective-permute-done.11.dia_ref) | copy-start | bytes 1179652
  57.9 3.8 %copy-start.10 = (bf16[6,256,128]{2,1,0:T(8,128)(2,1)}, bf16[6,256,128]{2,1,0:T(8,128)(2,1)S(1)}, u32[]{:S(2)}) copy-start(bf16[6,256,128]{2,1,0:T(8,128)(2,1)S(1)} %collective-permute-done.12.par_ref) | copy-start | bytes 1179652
  58.0 3.1 %collective-permute-start.13 = (f32[64,1664]{1,0:T(8,128)S(1)}, f32[64,1664]{1,0:T(8,128)S(1)}, u32[]{:S(2)}, u32[]{:S(2)}) collective-permute-start(f32[64,1664]{1,0:T(8,128)S(1)} %pad_maximum_fusion), channel_id=1, source_target_pairs={{0,1},{1,0},{2,3},{3,2},{4,5},{5,4},{6,7},{7,6},{8,9},{9,8},{10,11... | collective-permute-start | bytes 1277960 | tf_op jit(solution)/shard_map/ppermute | solution.py:23
  58.1 5.0 %collective-permute-start.14 = (bf16[6,256,128]{2,1,0:T(8,128)(2,1)}, bf16[6,256,128]{2,1,0:T(8,128)(2,1)S(1)}, u32[]{:S(2)}, u32[]{:S(2)}) collective-permute-start(bf16[6,256,128]{2,1,0:T(8,128)(2,1)} %get-tuple-element.78), channel_id=1, source_target_pairs={{0,1},{1,0},{2,3},{3,2},{4,5},{5,4},{6,7},{7,6},{8,9},{9,8},{10,11... | collective-permute-start | bytes 1179656 | tf_op jit(solution)/shard_map/ppermute | solution.py:23
  58.6 24.9 %collective-permute-start.18 = (bf16[6,256,128]{2,1,0:T(8,128)(2,1)}, bf16[6,256,128]{2,1,0:T(8,128)(2,1)S(1)}, u32[]{:S(2)}, u32[]{:S(2)}) collective-permute-start(bf16[6,256,128]{2,1,0:T(8,128)(2,1)} %get-tuple-element.81), channel_id=1, source_target_pairs={{0,2},{2,0},{4,6},{6,4},{8,10},{10,8},{12,14},{14,12},{1,3},{3,1},... | collective-permute-start | bytes 1179656 | tf_op jit(solution)/shard_map/ppermute | solution.py:42
  61.1 0.8 copy-start.16
  63.0 1.7 %copy-start.13 = (bf16[6,256,128]{2,1,0:T(8,128)(2,1)S(1)}, bf16[6,256,128]{2,1,0:T(8,128)(2,1)}, u32[]{:S(2)}) copy-start(bf16[6,256,128]{2,1,0:T(8,128)(2,1)} %copy-done.12) | copy-start | bytes 1179652
  63.1 8.2 %collective-permute-start.15 = (f32[32,1664]{1,0:T(8,128)S(1)}, f32[32,1664]{1,0:T(8,128)S(1)}, u32[]{:S(2)}, u32[]{:S(2)}) collective-permute-start(f32[32,1664]{1,0:T(8,128)S(1)} %pad_maximum_fusion.1), channel_id=1, source_target_pairs={{0,4},{1,5},{2,6},{3,7},{4,0},{5,1},{6,2},{7,3},{8,12},{9,13},{10,... | collective-permute-start | bytes 638984 | tf_op jit(solution)/shard_map/ppermute | solution.py:23
  64.8 18.7 %collective-permute-start.19 = (bf16[6,256,128]{2,1,0:T(8,128)(2,1)S(1)}, bf16[6,256,128]{2,1,0:T(8,128)(2,1)S(1)}, u32[]{:S(2)}, u32[]{:S(2)}) collective-permute-start(bf16[6,256,128]{2,1,0:T(8,128)(2,1)S(1)} %copy-done.13), channel_id=1, source_target_pairs={{2,4},{4,2},{6,8},{8,6},{10,12},{12,10},{3,5},{5,3},{7,9},{9,7},{1... | collective-permute-start | bytes 1179656 | tf_op jit(solution)/shard_map/ppermute | solution.py:42
  71.3 9.9 %copy-start.5 = (s32[1,3,1]{1,2,0:T(1,128)S(1)}, s32[1,3,1]{1,2,0:T(1,128)}, u32[]{:S(2)}) copy-start(s32[1,3,1]{1,2,0:T(1,128)} %param.14) | copy-start | bytes 40
  71.3 9.9 %copy-start.9 = (bf16[6,256,128]{2,1,0:T(8,128)(2,1)S(1)}, bf16[6,256,128]{2,1,0:T(8,128)(2,1)}, u32[]{:S(2)}) copy-start(bf16[6,256,128]{2,1,0:T(8,128)(2,1)} %copy-done.8) | copy-start | bytes 1179652
  71.3 9.9 %copy-start.11 = (bf16[6,256,128]{2,1,0:T(8,128)(2,1)S(1)}, bf16[6,256,128]{2,1,0:T(8,128)(2,1)}, u32[]{:S(2)}) copy-start(bf16[6,256,128]{2,1,0:T(8,128)(2,1)} %copy-done.10) | copy-start | bytes 1179652
  71.3 9.9 %copy-start.15 = (f32[6,512,128]{2,1,0:T(8,128)S(1)}, f32[6,512,128]{2,1,0:T(8,128)}, u32[]{:S(2)}) copy-start(f32[6,512,128]{2,1,0:T(8,128)} %copy-done.14) | copy-start | bytes 4718596
  71.4 9.7 %collective-permute-start.16 = (f32[16,1664]{1,0:T(8,128)S(1)}, f32[16,1664]{1,0:T(8,128)S(1)}, u32[]{:S(2)}, u32[]{:S(2)}) collective-permute-start(f32[16,1664]{1,0:T(8,128)S(1)} %pad_maximum_fusion.3), channel_id=1, source_target_pairs={{0,8},{1,9},{2,10},{3,11},{4,12},{5,13},{6,14},{7,15},{8,0},{9,1},... | collective-permute-start | bytes 319496 | tf_op jit(solution)/shard_map/ppermute | solution.py:23
  81.2 4.5 %collective-permute-start.17 = (f32[8,1664]{1,0:T(8,128)S(1)}, f32[8,1664]{1,0:T(8,128)S(1)}, u32[]{:S(2)}, u32[]{:S(2)}) collective-permute-start(f32[8,1664]{1,0:T(8,128)S(1)} %pad_maximum_fusion.4), channel_id=1, source_target_pairs={{0,2},{1,3},{2,0},{3,1},{4,6},{5,7},{6,4},{7,5},{8,10},{9,11},{10,... | collective-permute-start | bytes 159752 | tf_op jit(solution)/shard_map/ppermute | solution.py:23
